TPU v7x, 32 devices: a whole 2x2x4 slice. The times are simulated.
32 devices in a mesh: dp: 16 (over z, y, core), seq: 2 (over x).
Axes of the slice: x: 2, y: 2, z: 4, core: 2. Of those that a mesh axis runs over, the one named last changes fastest.
Arguments:
- patches: bfloat16 [64, 448, 768], P(('dp', 'seq')), may hold values from -6 to 6
- masked_at: int32 [64, 448], P(('dp', 'seq')), may hold values from 0 to 1, as said below
- edge_w: float32 [768, 1536], P(('dp', 'seq')), may hold values from -0.21875 to 0.21875
- attn_w: float32 [768, 6144], P(('dp', 'seq')), may hold values from -0.21875 to 0.21875
- mlp_w: float32 [768, 12288], P(('dp', 'seq')), may hold values from -0.21875 to 0.21875
- posit_w: float32 [768, 448], P(('dp', 'seq')), may hold values from -1.2 to 1.2
- vecs_w: float32 [768, 6], P(('dp', 'seq')), may hold values from 0.5 to 1.5
- edge_m: float32 [768, 1536], P(('dp', 'seq')), may hold values from -6e-05 to 6e-05
- attn_m: float32 [768, 6144], P(('dp', 'seq')), may hold values from -6e-05 to 6e-05
- mlp_m: float32 [768, 12288], P(('dp', 'seq')), may hold values from -6e-05 to 6e-05
- posit_m: float32 [768, 448], P(('dp', 'seq')), may hold values from -6e-05 to 6e-05
- vecs_m: float32 [768, 6], P(('dp', 'seq')), may hold values from -6e-05 to 6e-05
- edge_v: float32 [768, 1536], P(('dp', 'seq')), may hold values from 1e-10 to 4e-10
- attn_v: float32 [768, 6144], P(('dp', 'seq')), may hold values from 1e-10 to 4e-10
- mlp_v: float32 [768, 12288], P(('dp', 'seq')), may hold values from 1e-10 to 4e-10
- posit_v: float32 [768, 448], P(('dp', 'seq')), may hold values from 1e-10 to 4e-10
- vecs_v: float32 [768, 6], P(('dp', 'seq')), may hold values from 1e-10 to 4e-10
- edge_t: float32 [768, 1536], P(('dp', 'seq')), may hold values from -0.21875 to 0.21875
- attn_t: float32 [768, 6144], P(('dp', 'seq')), may hold values from -0.21875 to 0.21875
- mlp_t: float32 [768, 12288], P(('dp', 'seq')), may hold values from -0.21875 to 0.21875
- posit_t: float32 [768, 448], P(('dp', 'seq')), may hold values from -1.2 to 1.2
- vecs_t: float32 [768, 6], P(('dp', 'seq')), may hold values from 0.5 to 1.5
Outputs:
- loss: float32 [], replicated
- new_edge_w: float32 [768, 1536], P(('dp', 'seq'))
- new_attn_w: float32 [768, 6144], P(('dp', 'seq'))
- new_mlp_w: float32 [768, 12288], P(('dp', 'seq'))
- new_posit_w: float32 [768, 448], P(('dp', 'seq'))
- new_vecs_w: float32 [768, 6], P(('dp', 'seq'))
- new_edge_m: float32 [768, 1536], P(('dp', 'seq'))
- new_attn_m: float32 [768, 6144], P(('dp', 'seq'))
- new_mlp_m: float32 [768, 12288], P(('dp', 'seq'))
- new_posit_m: float32 [768, 448], P(('dp', 'seq'))
- new_vecs_m: float32 [768, 6], P(('dp', 'seq'))
- new_edge_v: float32 [768, 1536], P(('dp', 'seq'))
- new_attn_v: float32 [768, 6144], P(('dp', 'seq'))
- new_mlp_v: float32 [768, 12288], P(('dp', 'seq'))
- new_posit_v: float32 [768, 448], P(('dp', 'seq'))
- new_vecs_v: float32 [768, 6], P(('dp', 'seq'))
- new_edge_t: float32 [768, 1536], P(('dp', 'seq'))
- new_attn_t: float32 [768, 6144], P(('dp', 'seq'))
- new_mlp_t: float32 [768, 12288], P(('dp', 'seq'))
- new_posit_t: float32 [768, 448], P(('dp', 'seq'))
- new_vecs_t: float32 [768, 6], P(('dp', 'seq'))
Inputs may be any that keep to these rules, and one draw needn't show every extreme that they name: `masked_at`: sequence s (counted from 0) has exactly 112 + (448 // 2 * s) // 63 masked tokens.
All inputs are finite; a program needn't handle non-finite values.
Results may differ from a plain program's by a relative error of at most 0.002.
The roundings to bfloat16 on the way count: a program that leaves them out, or rounds other values in their place, can miss the bound.
Values may be sent and summed in bfloat16 or wider, within the bound.
No kernel may reach another device: no remote copies, remote signals or barrier semaphores. Data moves between devices by JAX's collectives and lax.ppermute only.
A program may use at most 448 MiB of HBM per device.

v0:
```python
import jax
import jax.numpy as jnp
from jax import lax
from jax.sharding import PartitionSpec as P

HEADS = 12
HDIM = 64
LAYERS = 2
MICRO = 2
TOPK = 2


ln_eps = 1e-05
in_eps = 1e-05
learn_rate = 0.02
first_decay = 0.5
second_decay = 0.5
adam_eps = 1e-08
weight_decay = 0.1
teacher_keep = 0.5
huber_beta = 1.0
score_scale = 0.125
entry_clip = 1e-05
half_type = jnp.bfloat16


def gelu_exact(values):
    return jax.nn.gelu(values, approximate=False)


def contract_rows(left, right):
    return lax.dot_general(
        left, right, (((0,), (0,)), ((), ())), preferred_element_type=jnp.float32
    )


def contract_cols(left, right):
    return lax.dot_general(
        left, right, (((1,), (1,)), ((), ())), preferred_element_type=jnp.float32
    )


def normalize(values, gain_vec):
    centre = values - jnp.mean(values, axis=-1, keepdims=True)
    inv_scale = lax.rsqrt(jnp.mean(centre * centre, axis=-1, keepdims=True) + ln_eps)
    normed_unit = centre * inv_scale
    return (normed_unit * gain_vec, normed_unit, inv_scale)


def normalize_back(grad_out, gain_vec, normed_unit, inv_scale):
    grad_unit = grad_out * gain_vec
    inner_mean = jnp.mean(grad_unit, axis=-1, keepdims=True)
    along_mean = jnp.mean(grad_unit * normed_unit, axis=-1, keepdims=True)
    grad_in = (grad_unit - inner_mean - normed_unit * along_mean) * inv_scale
    return (grad_in, jnp.sum(grad_out * normed_unit, axis=0))


def split_heads(values):
    return values.reshape(values.shape[0], values.shape[1], HEADS, HDIM)


def attend(queries, keys_all, values_all):
    scores = (
        jnp.einsum(
            "sqhd,skhd->shqk",
            split_heads(queries),
            split_heads(keys_all),
            preferred_element_type=jnp.float32,
        )
        * score_scale
    )
    top_score = jnp.max(scores, axis=-1, keepdims=True)
    exp_scores = jnp.exp(scores - top_score)
    totals = jnp.sum(exp_scores, axis=-1, keepdims=True)
    soft_probs = (exp_scores / totals).astype(half_type)
    mixed_out = jnp.einsum(
        "shqk,skhd->sqhd", soft_probs, split_heads(values_all), preferred_element_type=jnp.float32
    )
    log_total = top_score + jnp.log(totals)
    return (mixed_out.reshape(queries.shape).astype(half_type), log_total)


def attend_back(queries, keys_all, values_all, log_total, grad_mixed):
    head_queries = split_heads(queries)
    head_keys = split_heads(keys_all)
    head_values = split_heads(values_all)
    head_grad = split_heads(grad_mixed)
    scores = (
        jnp.einsum("sqhd,skhd->shqk", head_queries, head_keys, preferred_element_type=jnp.float32)
        * score_scale
    )
    soft_probs = jnp.exp(scores - log_total)
    grad_values = jnp.einsum(
        "shqk,sqhd->skhd",
        soft_probs.astype(half_type),
        head_grad,
        preferred_element_type=jnp.float32,
    )
    grad_probs = jnp.einsum(
        "sqhd,skhd->shqk", head_grad, head_values, preferred_element_type=jnp.float32
    )
    grad_scores = (
        soft_probs * (grad_probs - jnp.sum(soft_probs * grad_probs, axis=-1, keepdims=True))
    ).astype(half_type)
    grad_queries = (
        jnp.einsum("shqk,skhd->sqhd", grad_scores, head_keys, preferred_element_type=jnp.float32)
        * score_scale
    )
    grad_keys = (
        jnp.einsum("shqk,sqhd->skhd", grad_scores, head_queries, preferred_element_type=jnp.float32)
        * score_scale
    )
    return (
        grad_queries.reshape(queries.shape),
        grad_keys.reshape(keys_all.shape),
        grad_values.reshape(values_all.shape),
    )


def layer_forward(hidden_in, attn_full, mlp_full, gain_one, gain_two):
    shape_in = hidden_in.shape
    model_width = shape_in[2]
    ff_width = mlp_full.shape[1] // 2
    flat_in = hidden_in.reshape(-1, model_width)
    normed_one, unit_one, scale_one = normalize(flat_in, gain_one)
    normed_one = normed_one.astype(half_type)
    projected = jnp.dot(
        normed_one, attn_full[:, : 3 * model_width], preferred_element_type=jnp.float32
    ).astype(half_type)
    projected = projected.reshape(shape_in[0], shape_in[1], 3 * model_width)
    queries = projected[:, :, :model_width]
    keys_all = projected[:, :, model_width : 2 * model_width]
    values_all = projected[:, :, 2 * model_width :]
    mixed_out, log_total = attend(queries, keys_all, values_all)
    flat_mixed = mixed_out.reshape(-1, model_width)
    middle = flat_in + jnp.dot(
        flat_mixed, attn_full[:, 3 * model_width :], preferred_element_type=jnp.float32
    )
    normed_two, unit_two, scale_two = normalize(middle, gain_two)
    normed_two = normed_two.astype(half_type)
    hidden_up = jnp.dot(normed_two, mlp_full[:, :ff_width], preferred_element_type=jnp.float32)
    active = gelu_exact(hidden_up).astype(half_type)
    hidden_out = middle + contract_cols(active, mlp_full[:, ff_width:])
    saved_parts = (
        unit_one,
        scale_one,
        normed_one,
        queries,
        keys_all,
        values_all,
        log_total,
        flat_mixed,
        unit_two,
        scale_two,
        normed_two,
        hidden_up,
        active,
    )
    return (hidden_out.reshape(shape_in), saved_parts)


def layer_backward(grad_out, saved_parts, attn_full, mlp_full, gain_one, gain_two):
    (
        unit_one,
        scale_one,
        normed_one,
        queries,
        keys_all,
        values_all,
        log_total,
        flat_mixed,
        unit_two,
        scale_two,
        normed_two,
        hidden_up,
        active,
    ) = saved_parts
    model_width = grad_out.shape[1]
    ff_width = mlp_full.shape[1] // 2
    grad_down = grad_out.astype(half_type)
    grad_wdown = contract_rows(grad_down, active)
    grad_active = jnp.dot(grad_down, mlp_full[:, ff_width:], preferred_element_type=jnp.float32)
    grad_hidden = jax.vjp(gelu_exact, hidden_up)[1](grad_active)[0].astype(half_type)
    grad_wup = contract_rows(normed_two, grad_hidden)
    grad_norm_two = contract_cols(grad_hidden, mlp_full[:, :ff_width])
    grad_middle, grad_gain_two = normalize_back(grad_norm_two, gain_two, unit_two, scale_two)
    grad_middle = grad_out + grad_middle
    grad_branch = grad_middle.astype(half_type)
    grad_wout = contract_rows(flat_mixed, grad_branch)
    grad_mixed = (
        contract_cols(grad_branch, attn_full[:, 3 * model_width :])
        .astype(half_type)
        .reshape(queries.shape)
    )
    grad_queries, grad_keys, grad_values = attend_back(
        queries, keys_all, values_all, log_total, grad_mixed
    )
    grad_proj = (
        jnp.concatenate([grad_queries, grad_keys, grad_values], axis=2)
        .astype(half_type)
        .reshape(-1, 3 * model_width)
    )
    grad_wqkv = contract_rows(normed_one, grad_proj)
    grad_norm_one = contract_cols(grad_proj, attn_full[:, : 3 * model_width])
    grad_in, grad_gain_one = normalize_back(grad_norm_one, gain_one, unit_one, scale_one)
    attn_grad = jnp.concatenate([grad_wqkv, grad_wout], axis=1)
    mlp_grad = jnp.concatenate([grad_wup, grad_wdown], axis=1)
    return (grad_middle + grad_in, attn_grad, mlp_grad, grad_gain_one, grad_gain_two)


def fetch_layer(attn_half, mlp_half, layer_idx):
    attn_cols = attn_half.shape[1] // LAYERS
    mlp_cols = mlp_half.shape[1] // LAYERS
    attn_piece = attn_half[:, layer_idx * attn_cols : (layer_idx + 1) * attn_cols]
    mlp_piece = mlp_half[:, layer_idx * mlp_cols : (layer_idx + 1) * mlp_cols]
    return (
        lax.all_gather(attn_piece, ("dp", "seq"), axis=0, tiled=True),
        lax.all_gather(mlp_piece, ("dp", "seq"), axis=0, tiled=True),
    )


def add_parts(left_parts, right_parts):
    return tuple((left_item + right_item for left_item, right_item in zip(left_parts, right_parts)))


def adam_step(weight, first_mom, second_mom, teacher, gradient):
    first_new = first_decay * first_mom + (1.0 - first_decay) * gradient
    second_new = second_decay * second_mom + (1.0 - second_decay) * gradient * gradient
    weight_new = weight - learn_rate * (
        first_new / (jnp.sqrt(second_new) + adam_eps) + weight_decay * weight
    )
    teacher_new = teacher_keep * teacher + (1.0 - teacher_keep) * weight_new
    return (weight_new, first_new, second_new, teacher_new)


def local(
    patches,
    masked_at,
    edge_w,
    attn_w,
    mlp_w,
    posit_w,
    vecs_w,
    edge_m,
    attn_m,
    mlp_m,
    posit_m,
    vecs_m,
    edge_v,
    attn_v,
    mlp_v,
    posit_v,
    vecs_v,
    edge_t,
    attn_t,
    mlp_t,
    posit_t,
    vecs_t,
):
    seq_count, tok_rows, model_width = patches.shape
    seq_group = seq_count // MICRO
    device_count = lax.axis_size("dp") * lax.axis_size("seq")
    total_masked = seq_count * device_count * tok_rows // 2
    attn_cols = attn_w.shape[1] // LAYERS
    mlp_cols = mlp_w.shape[1] // LAYERS
    edge_half = edge_w.astype(half_type)
    attn_half = attn_w.astype(half_type)
    mlp_half = mlp_w.astype(half_type)
    posit_half = posit_w.astype(half_type)
    vecs_half = vecs_w.astype(half_type)
    teach_edge_half = edge_t.astype(half_type)
    teach_attn_half = attn_t.astype(half_type)
    teach_mlp_half = mlp_t.astype(half_type)
    teach_posit_half = posit_t.astype(half_type)
    teach_vecs_half = vecs_t.astype(half_type)
    accum_parts = None
    shard_parts = None
    loss_local = jnp.zeros((), jnp.float32)
    for micro_idx in range(MICRO):
        rows_now = patches[micro_idx * seq_group : (micro_idx + 1) * seq_group]
        mask_now = masked_at[micro_idx * seq_group : (micro_idx + 1) * seq_group].astype(
            jnp.float32
        )[:, :, None]
        flat_patch = rows_now.reshape(-1, model_width)
        teach_edge, teach_attn, teach_mlp, teach_posit, teach_vecs = (
            lax.all_gather(teach_edge_half, ("dp", "seq"), axis=0, tiled=True),
            lax.all_gather(teach_attn_half, ("dp", "seq"), axis=0, tiled=True),
            lax.all_gather(teach_mlp_half, ("dp", "seq"), axis=0, tiled=True),
            lax.all_gather(teach_posit_half, ("dp", "seq"), axis=0, tiled=True),
            lax.all_gather(teach_vecs_half, ("dp", "seq"), axis=0, tiled=True),
        )
        teach_gains = teach_vecs.astype(jnp.float32)
        teach_state = jnp.dot(
            flat_patch, teach_edge[:, :model_width], preferred_element_type=jnp.float32
        ).reshape(seq_group, tok_rows, model_width)
        teach_state = teach_state + teach_posit.T.astype(jnp.float32)[None]
        outputs = []
        for layer_idx in range(LAYERS):
            teach_state, unused_saved = layer_forward(
                teach_state,
                teach_attn[:, layer_idx * attn_cols : (layer_idx + 1) * attn_cols],
                teach_mlp[:, layer_idx * mlp_cols : (layer_idx + 1) * mlp_cols],
                teach_gains[:, layer_idx],
                teach_gains[:, LAYERS + layer_idx],
            )
            outputs.append(teach_state)
        stacked = jnp.stack(outputs[LAYERS - TOPK :])
        centred = stacked - jnp.mean(stacked, axis=2, keepdims=True)
        variance = jnp.mean(centred * centred, axis=2, keepdims=True)
        target = jnp.mean(centred * lax.rsqrt(variance + in_eps), axis=0)
        stud_edge, stud_posit, stud_vecs = (
            lax.all_gather(edge_half, ("dp", "seq"), axis=0, tiled=True),
            lax.all_gather(posit_half, ("dp", "seq"), axis=0, tiled=True),
            lax.all_gather(vecs_half, ("dp", "seq"), axis=0, tiled=True),
        )
        gain_table = stud_vecs.astype(jnp.float32)
        embedded = jnp.dot(
            flat_patch, stud_edge[:, :model_width], preferred_element_type=jnp.float32
        ).reshape(seq_group, tok_rows, model_width)
        current = (
            embedded * (1.0 - mask_now)
            + mask_now * gain_table[:, 2 * LAYERS + 1]
            + stud_posit.T.astype(jnp.float32)[None]
        )
        kept_weights = []
        kept_saved = []
        for layer_idx in range(LAYERS):
            attn_full, mlp_full = fetch_layer(attn_half, mlp_half, layer_idx)
            kept_weights.append((attn_full, mlp_full))
            current, saved_parts = layer_forward(
                current,
                attn_full,
                mlp_full,
                gain_table[:, layer_idx],
                gain_table[:, LAYERS + layer_idx],
            )
            kept_saved.append(saved_parts)
        flat_state = current.reshape(-1, model_width)
        final_normed, final_unit, final_scale = normalize(flat_state, gain_table[:, 2 * LAYERS])
        final_normed = final_normed.astype(half_type)
        predicted = jnp.dot(
            final_normed, stud_edge[:, model_width:], preferred_element_type=jnp.float32
        )
        mask_flat = mask_now.reshape(-1, 1)
        differ = predicted - target.reshape(-1, model_width)
        magnitude = jnp.abs(differ)
        huber_terms = jnp.where(
            magnitude < huber_beta, 0.5 * differ * differ / huber_beta, magnitude - 0.5 * huber_beta
        )
        loss_local = loss_local + jnp.sum(huber_terms * mask_flat) / total_masked
        grad_pred = (mask_flat * jnp.clip(differ / huber_beta, -1.0, 1.0) / total_masked).astype(
            half_type
        )
        grad_head = contract_rows(final_normed, grad_pred)
        grad_flow, grad_gain_final = normalize_back(
            contract_cols(grad_pred, stud_edge[:, model_width:]),
            gain_table[:, 2 * LAYERS],
            final_unit,
            final_scale,
        )
        attn_grads = [None] * LAYERS
        mlp_grads = [None] * LAYERS
        gain_ones = [None] * LAYERS
        gain_twos = [None] * LAYERS
        for layer_idx in reversed(range(LAYERS)):
            attn_full, mlp_full = fetch_layer(attn_half, mlp_half, layer_idx)
            (
                grad_flow,
                attn_grads[layer_idx],
                mlp_grads[layer_idx],
                gain_ones[layer_idx],
                gain_twos[layer_idx],
            ) = layer_backward(
                grad_flow,
                kept_saved[layer_idx],
                attn_full,
                mlp_full,
                gain_table[:, layer_idx],
                gain_table[:, LAYERS + layer_idx],
            )
        grad_embed_in = grad_flow.reshape(seq_group, tok_rows, model_width)
        grad_maskvec = jnp.sum(grad_embed_in * mask_now, axis=(0, 1))
        grad_posit = jnp.sum(grad_embed_in, axis=0).T
        grad_embed = (grad_embed_in * (1.0 - mask_now)).astype(half_type).reshape(-1, model_width)
        grad_patch = contract_rows(flat_patch, grad_embed)
        micro_grads = (
            jnp.concatenate([grad_patch, grad_head], axis=1),
            jnp.concatenate(attn_grads, axis=1),
            jnp.concatenate(mlp_grads, axis=1),
            grad_posit,
            jnp.stack(gain_ones + gain_twos + [grad_gain_final, grad_maskvec], axis=1),
        )
        accum_parts = micro_grads if accum_parts is None else add_parts(accum_parts, micro_grads)
    shard_parts = (
        lax.psum_scatter(accum_parts[0], ("dp", "seq"), scatter_dimension=0, tiled=True),
        lax.psum_scatter(accum_parts[1], ("dp", "seq"), scatter_dimension=0, tiled=True),
        lax.psum_scatter(accum_parts[2], ("dp", "seq"), scatter_dimension=0, tiled=True),
        lax.psum_scatter(accum_parts[3], ("dp", "seq"), scatter_dimension=0, tiled=True),
        lax.psum_scatter(accum_parts[4], ("dp", "seq"), scatter_dimension=0, tiled=True),
    )
    square_sums = tuple((jnp.sum(part * part) for part in shard_parts))
    summed = lax.psum(
        (
            loss_local,
            square_sums[0],
            square_sums[1],
            square_sums[2],
            square_sums[3],
            square_sums[4],
        ),
        ("dp", "seq"),
    )
    total_loss = summed[0]
    clipped = []
    for group_idx in range(5):
        part = shard_parts[group_idx]
        limit = entry_clip * jnp.sqrt(jnp.float32(part.size * device_count))
        norm_value = jnp.sqrt(summed[group_idx + 1])
        clipped.append(part * (limit / jnp.maximum(norm_value, limit)))
    edge_new = adam_step(edge_w, edge_m, edge_v, edge_t, clipped[0])
    attn_new = adam_step(attn_w, attn_m, attn_v, attn_t, clipped[1])
    mlp_new = adam_step(mlp_w, mlp_m, mlp_v, mlp_t, clipped[2])
    posit_new = adam_step(posit_w, posit_m, posit_v, posit_t, clipped[3])
    vecs_new = adam_step(vecs_w, vecs_m, vecs_v, vecs_t, clipped[4])
    return (
        total_loss,
        edge_new[0],
        attn_new[0],
        mlp_new[0],
        posit_new[0],
        vecs_new[0],
        edge_new[1],
        attn_new[1],
        mlp_new[1],
        posit_new[1],
        vecs_new[1],
        edge_new[2],
        attn_new[2],
        mlp_new[2],
        posit_new[2],
        vecs_new[2],
        edge_new[3],
        attn_new[3],
        mlp_new[3],
        posit_new[3],
        vecs_new[3],
    )


def solution(mesh):
    in_specs = (
        P(("dp", "seq"), None, None),
        P(("dp", "seq"), None),
        P(("dp", "seq"), None),
        P(("dp", "seq"), None),
        P(("dp", "seq"), None),
        P(("dp", "seq"), None),
        P(("dp", "seq"), None),
        P(("dp", "seq"), None),
        P(("dp", "seq"), None),
        P(("dp", "seq"), None),
        P(("dp", "seq"), None),
        P(("dp", "seq"), None),
        P(("dp", "seq"), None),
        P(("dp", "seq"), None),
        P(("dp", "seq"), None),
        P(("dp", "seq"), None),
        P(("dp", "seq"), None),
        P(("dp", "seq"), None),
        P(("dp", "seq"), None),
        P(("dp", "seq"), None),
        P(("dp", "seq"), None),
        P(("dp", "seq"), None),
    )
    out_specs = (
        P(),
        P(("dp", "seq"), None),
        P(("dp", "seq"), None),
        P(("dp", "seq"), None),
        P(("dp", "seq"), None),
        P(("dp", "seq"), None),
        P(("dp", "seq"), None),
        P(("dp", "seq"), None),
        P(("dp", "seq"), None),
        P(("dp", "seq"), None),
        P(("dp", "seq"), None),
        P(("dp", "seq"), None),
        P(("dp", "seq"), None),
        P(("dp", "seq"), None),
        P(("dp", "seq"), None),
        P(("dp", "seq"), None),
        P(("dp", "seq"), None),
        P(("dp", "seq"), None),
        P(("dp", "seq"), None),
        P(("dp", "seq"), None),
        P(("dp", "seq"), None),
    )
    return jax.shard_map(local, mesh=mesh, in_specs=in_specs, out_specs=out_specs, check_vma=False)
```

profile of v0, /device:TPU:0, one launch (start us, length us, event | category | flops | bytes accessed | tf_op | source)
XLA Modules:
  0.0 1817.0 jit_solution(4598723160833695906)
XLA Ops:
  19.2 70.2 %all-gather.1 = bf16[32,24,6]{1,2,0:T(8,128)(2,1)S(1)} all-gather(bf16[1,24,6]{1,2,0:T(8,128)(2,1)S(1)} %convert_bitcast_fusion.1), channel_id=1, replica_groups=mesh['dp'=16,'seq'=2] {'dp','seq'}, dimensions={0}, use_global_device_ids=true | all-gather | bytes 9504 | tf_op jit(solution)/shard_map/all_gather | solution.py:290
  90.3 64.0 %all-gather = bf16[32,24,6]{1,2,0:T(8,128)(2,1)S(1)} all-gather(bf16[1,24,6]{1,2,0:T(8,128)(2,1)S(1)} %convert_bitcast_fusion.2), channel_id=1, replica_groups=mesh['dp'=16,'seq'=2] {'dp','seq'}, dimensions={0}, use_global_device_ids=true | all-gather | bytes 9504 | tf_op jit(solution)/shard_map/all_gather | solution.py:314
  155.3 72.2 %all_gather.64 = bf16[768,448]{1,0:T(8,128)(2,1)S(1)} all-gather(bf16[24,448]{1,0:T(8,128)(2,1)S(1)} %convert_element_type.455), channel_id=1, replica_groups=mesh['dp'=16,'seq'=2] {'dp','seq'}, dimensions={0}, use_global_device_ids=true | all-gather | bytes 709632 | tf_op jit(solution)/shard_map/all_gather | solution.py:289
  228.6 72.3 %all_gather.26 = bf16[768,448]{1,0:T(8,128)(2,1)S(1)} all-gather(bf16[24,448]{1,0:T(8,128)(2,1)S(1)} %convert_element_type.430), channel_id=1, replica_groups=mesh['dp'=16,'seq'=2] {'dp','seq'}, dimensions={0}, use_global_device_ids=true | all-gather | bytes 709632 | tf_op jit(solution)/shard_map/all_gather | solution.py:313
  383.7 17.3 multiply_convert_fusion.7
  404.9 37.2 %all-gather.17.cloned.1.call-done = bf16[768,3072]{1,0:T(8,128)(2,1)} async-done(((bf16[24,3072]{1,0:T(8,128)(2,1)}), bf16[768,3072]{1,0:T(8,128)(2,1)}) %all-gather.17.cloned.1.call-update) | async-done | bytes 4718608 | tf_op jit(solution)/shard_map/all_gather | solution.py:217
  453.6 17.3 multiply_convert_fusion.5
  489.7 9.0 fusion.726
  508.3 9.4 fusion.734
  538.7 17.4 multiply_convert_fusion.6
  574.2 16.4 multiply_convert_fusion.4
  598.7 54.6 %all-gather.25.cloned.1.call-done = bf16[768,12288]{1,0:T(8,128)(2,1)} async-done(((bf16[24,12288]{1,0:T(8,128)(2,1)}), bf16[768,12288]{1,0:T(8,128)(2,1)}) %all-gather.25.cloned.1.call-update) | async-done | bytes 18874384 | tf_op jit(solution)/shard_map/all_gather | solution.py:288
  653.2 19.1 %fusion.728 = (f32[448]{0:T(512)S(1)}, f32[448,768]{1,0:T(8,128)S(1)}) fusion(f32[448,768]{1,0:T(8,128)S(1)} %copy-done.95, bf16[768,12288]{1,0:T(8,128)(2,1)} %all-gather.25.cloned.1.call-done, f32[768]{0:T(1024)S(1)} %copy-done.312, f32[448]{0:T(512)S(1)} %add_rsqrt_fusion.13, f32[448]{0:T(512)S(1)} %copy-done.305), kind=kOutput, calls=%fused_computation.998 | convolution fusion | flops 4319378944 | bytes 13575936 | tf_op jit(solution)/shard_map/dot_general | solution.py:38
  679.2 8.8 fusion.731
  696.6 19.9 %fusion.357 = f32[1,1,448,768]{3,2,1,0:T(8,128)S(1)} fusion(f32[448,768]{1,0:T(8,128)} %copy-done.97, bf16[768,12288]{1,0:T(8,128)(2,1)} %all-gather.25.cloned.1.call-done, f32[768]{0:T(1024)S(1)} %copy-done.309, f32[448]{0:T(512)S(1)} %add_rsqrt_fusion.11, f32[448]{0:T(512)S(1)} %broadcast_multiply_fusion.31), kind=kOutput, calls=%fused_computation.463 | convolution fusion | flops 4319035392 | bytes 13572608 | tf_op jit(solution)/shard_map/dot_general | solution.py:38
  718.4 19.8 %fusion.736 = (f32[448]{0:T(512)S(1)}, f32[448,768]{1,0:T(8,128)S(1)}) fusion(f32[448,768]{1,0:T(8,128)} %copy-done.93, bf16[768,12288]{1,0:T(8,128)(2,1)} %all-gather.25.cloned.1.call-done, f32[448]{0:T(512)S(1)} %copy-done.327, f32[448]{0:T(512)S(1)} %copy-done.295, f32[768]{0:T(1024)S(1)} %copy-done.312), kind=kOutput, calls=%fused_computation.1004 | convolution fusion | flops 4319378944 | bytes 13574400 | tf_op jit(solution)/shard_map/dot_general | solution.py:38
  745.1 9.0 fusion.739
  762.6 20.0 %fusion.371 = f32[1,1,448,768]{3,2,1,0:T(8,128)S(1)} fusion(f32[448,768]{1,0:T(8,128)} %copy-done.96, bf16[768,12288]{1,0:T(8,128)(2,1)} %all-gather.25.cloned.1.call-done, f32[448]{0:T(512)S(1)} %add_rsqrt_fusion.2, f32[448]{0:T(512)S(1)} %broadcast_multiply_fusion.22, f32[768]{0:T(1024)S(1)} %copy-done.309), kind=kOutput, calls=%fused_computation.465 | convolution fusion | flops 4319035392 | bytes 13572608 | tf_op jit(solution)/shard_map/dot_general | solution.py:38
  825.0 8.3 multiply_reduce_fusion.3
  852.7 8.3 multiply_reduce_fusion.1
  876.4 9.1 add_convert_fusion
  889.2 7.4 add_convert_fusion.2
  905.9 7.2 fusion.389
  954.6 8.0 multiply_reduce_fusion.16
  964.0 9.7 fusion.406
  1021.0 16.2 maximum_add_fusion.1
  1078.1 31.8 %maximum_add_fusion = f32[768,12288]{1,0:T(8,128)} fusion(f32[768,3072]{1,0:T(8,128)S(1)} %fusion.542, f32[768,3072]{1,0:T(8,128)} %fusion.691, f32[768,3072]{1,0:T(8,128)} %fusion.536, f32[768,3072]{1,0:T(8,128)} %fusion.690, f32[768,3072]{1,0:T(8,128)S(1)} %fusion.530, f32[768,3072]{1,0:T(8,128)} %fusion.693, f32[768,3072]{1,0:T(8,128)} %fusion.524, ...), kind=kLoop, calls=%fused_computation.4 | loop fusion | flops 66060288 | bytes 113246208 | tf_op jit(solution)/shard_map/add | solution.py:223
  1112.2 39.7 %all-reduce = f32[768,6]{0,1:T(8,128)S(1)} all-reduce(f32[768,6]{0,1:T(8,128)S(1)} %add.584), channel_id=6, replica_groups=mesh['dp'=16,'seq'=2] {'dp','seq'}, use_global_device_ids=true, to_apply=%region_109.110.clone | all-reduce | flops 4608 | bytes 36864
  1154.2 29.3 %reduce-scatter.14.cloned.1.call-done = f32[24,1536]{1,0:T(8,128)} async-done(((f32[768,1536]{1,0:T(8,128)}), f32[24,1536]{1,0:T(8,128)}) %reduce-scatter.14.cloned.1.call-update) | async-done | bytes 147472 | tf_op jit(solution)/shard_map/reduce_scatter | solution.py:395
  1185.6 211.4 %reduce-scatter.10.cloned.1.call-done = f32[24,6144]{1,0:T(8,128)} async-done(((f32[768,6144]{1,0:T(8,128)}), f32[24,6144]{1,0:T(8,128)}) %reduce-scatter.10.cloned.1.call-update) | async-done | bytes 589840 | tf_op jit(solution)/shard_map/reduce_scatter | solution.py:396
  1398.8 353.2 %reduce-scatter.12.cloned.1.call-done = f32[24,12288]{1,0:T(8,128)} async-done(((f32[768,12288]{1,0:T(8,128)}), f32[24,12288]{1,0:T(8,128)}) %reduce-scatter.12.cloned.1.call-update) | async-done | bytes 1179664 | tf_op jit(solution)/shard_map/reduce_scatter | solution.py:397
  1754.3 40.1 %all-reduce.1 = (f32[]{:T(128)}, f32[]{:T(128)}, f32[]{:T(128)}, f32[]{:T(128)}, f32[]{:T(128)}, /*index=5*/f32[]{:T(128)}) all-reduce(f32[]{:T(128)S(6)} %multiply.377, f32[]{:T(128)} %multiply_reduce_fusion.67, f32[]{:T(128)} %multiply_reduce_fusion.68, f32[]{:T(128)} %multiply_reduce_fusion.56, ...), channel_id=1, replica_groups=mesh['dp'=16,'seq'=2] {'dp','seq'}, use_global_device_ids=true, to_apply=%region_60.61 | all-reduce | flops 6 | bytes 48 | tf_op jit(solution)/shard_map/psum | solution.py:402
  (1050 shorter events, 458.8 us)
Async XLA Ops:
  7.2 294.0 %all-gather.21.cloned.1.call-start = ((), (), s32[]{:S(2)}) async-start(), calls=%async_computation.9 | async-start | bytes 2433024 | tf_op jit(solution)/shard_map/all_gather | solution.py:286
  9.0 299.5 %all-gather.11.cloned.1.call-start = ((), (), s32[]{:S(2)}) async-start(), calls=%async_computation.4 | async-start | bytes 2433024 | tf_op jit(solution)/shard_map/all_gather | solution.py:312
  10.6 304.5 %all-gather.13.cloned.1.call-start = ((), (), s32[]{:S(2)}) async-start(), calls=%async_computation.5 | async-start | bytes 4866048 | tf_op jit(solution)/shard_map/all_gather | solution.py:217
  12.5 352.3 %all-gather.23.cloned.1.call-start = ((), (), s32[]{:S(2)}) async-start(), calls=%async_computation.10 | async-start | bytes 9732096 | tf_op jit(solution)/shard_map/all_gather | solution.py:287
  14.4 369.3 %all-gather.15.cloned.1.call-start = ((), (), s32[]{:S(2)}) async-start(), calls=%async_computation.6 | async-start | bytes 9732096 | tf_op jit(solution)/shard_map/all_gather | solution.py:218
  15.8 285.5 %copy-start.117 = (bf16[2,448,768]{2,1,0:T(8,128)(2,1)S(1)}, bf16[2,448,768]{2,1,0:T(8,128)(2,1)}, u32[]{:S(2)}) copy-start(bf16[2,448,768]{2,1,0:T(8,128)(2,1)} %param.22) | copy-start | bytes 4128772
  16.6 425.4 %all-gather.17.cloned.1.call-start = ((), (), s32[]{:S(2)}) async-start(), calls=%async_computation.7 | async-start | bytes 4866048 | tf_op jit(solution)/shard_map/all_gather | solution.py:217
  17.2 521.5 %all-gather.19.cloned.1.call-start = ((), (), s32[]{:S(2)}) async-start(), calls=%async_computation.8 | async-start | bytes 9732096 | tf_op jit(solution)/shard_map/all_gather | solution.py:218
  18.0 635.3 %all-gather.25.cloned.1.call-start = ((), (), s32[]{:S(2)}) async-start(), calls=%async_computation.11 | async-start | bytes 19464192 | tf_op jit(solution)/shard_map/all_gather | solution.py:288
  18.9 1133.7 %reduce-scatter.16.cloned.1.call-start = ((), (), s32[]{:S(2)}) async-start(), calls=%async_computation.15 | async-start | bytes 1622016 | tf_op jit(solution)/shard_map/reduce_scatter | solution.py:398
  19.0 291.5 %copy-start.179 = (f32[1,448]{1,0:T(1,128)}, f32[1,448]{1,0:T(1,128)S(1)}, u32[]{:S(2)}) copy-start(f32[1,448]{1,0:T(1,128)S(1)} %get-tuple-element.222) | copy-start | bytes 5380
  19.1 291.5 %copy-start.194 = (f32[1,448]{1,0:T(1,128)}, f32[1,448]{1,0:T(1,128)S(1)}, u32[]{:S(2)}) copy-start(f32[1,448]{1,0:T(1,128)S(1)} %get-tuple-element.221) | copy-start | bytes 5380
  19.1 289.4 %copy-start.278 = (f32[448]{0:T(512)}, f32[448]{0:T(512)S(1)}, u32[]{:S(2)}) copy-start(f32[448]{0:T(512)S(1)} %broadcast_subtract_fusion.1) | copy-start | bytes 5380
  19.1 291.4 %copy-start.237 = (f32[448]{0:T(512)}, f32[448]{0:T(512)S(1)}, u32[]{:S(2)}) copy-start(f32[448]{0:T(512)S(1)} %broadcast_subtract_fusion) | copy-start | bytes 5380
  155.3 155.2 %copy-start.199 = (f32[768]{0:T(1024)}, f32[768]{0:T(1024)S(1)}, u32[]{:S(2)}) copy-start(f32[768]{0:T(1024)S(1)} %get-tuple-element.119) | copy-start | bytes 9220
  155.3 171.2 %copy-start.209 = (f32[768]{0:T(1024)}, f32[768]{0:T(1024)S(1)}, u32[]{:S(2)}) copy-start(f32[768]{0:T(1024)S(1)} %get-tuple-element.118) | copy-start | bytes 9220
  155.3 298.3 %copy-start.201 = (f32[768]{0:T(1024)}, f32[768]{0:T(1024)S(1)}, u32[]{:S(2)}) copy-start(f32[768]{0:T(1024)S(1)} %get-tuple-element.117) | copy-start | bytes 9220
  155.3 322.7 %copy-start.213 = (f32[768]{0:T(1024)}, f32[768]{0:T(1024)S(1)}, u32[]{:S(2)}) copy-start(f32[768]{0:T(1024)S(1)} %get-tuple-element.116) | copy-start | bytes 9220
  352.0 101.6 %copy-start.239 = (f32[448]{0:T(512)}, f32[448]{0:T(512)S(1)}, u32[]{:S(2)}) copy-start(f32[448]{0:T(512)S(1)} %broadcast_multiply_fusion.29) | copy-start | bytes 5380
  352.3 101.3 %copy-start.280 = (f32[448]{0:T(512)}, f32[448]{0:T(512)S(1)}, u32[]{:S(2)}) copy-start(f32[448]{0:T(512)S(1)} %add_rsqrt_fusion.9) | copy-start | bytes 5380
  404.5 130.4 %copy-start.28 = (f32[448,768]{1,0:T(8,128)}, f32[448,768]{1,0:T(8,128)S(1)}, u32[]{:S(2)}) copy-start(f32[448,768]{1,0:T(8,128)S(1)} %get-tuple-element.177) | copy-start | bytes 4128772
  448.7 77.7 %copy-start.39 = (bf16[1,448,768]{1,2,0:T(8,128)(2,1)}, bf16[1,448,768]{1,2,0:T(8,128)(2,1)S(1)}, u32[]{:S(2)}) copy-start(bf16[1,448,768]{1,2,0:T(8,128)(2,1)S(1)} %copy.288) | copy-start | bytes 2064388
  484.9 75.5 %copy-start.41 = (bf16[1,448,768]{1,2,0:T(8,128)(2,1)}, bf16[1,448,768]{1,2,0:T(8,128)(2,1)S(1)}, u32[]{:S(2)}) copy-start(bf16[1,448,768]{1,2,0:T(8,128)(2,1)S(1)} %copy.307) | copy-start | bytes 2064388
  976.8 206.8 %reduce-scatter.14.cloned.1.call-start = ((), (), s32[]{:S(2)}) async-start(), calls=%async_computation.14 | async-start | bytes 4866048 | tf_op jit(solution)/shard_map/reduce_scatter | solution.py:395
  993.9 403.1 %reduce-scatter.10.cloned.1.call-start = ((), (), s32[]{:S(2)}) async-start(), calls=%async_computation.12 | async-start | bytes 19464192 | tf_op jit(solution)/shard_map/reduce_scatter | solution.py:396
  1037.2 714.9 %reduce-scatter.12.cloned.1.call-start = ((), (), s32[]{:S(2)}) async-start(), calls=%async_computation.13 | async-start | bytes 38928384 | tf_op jit(solution)/shard_map/reduce_scatter | solution.py:397
  1110.0 688.0 %copy-start.275 = (f32[24,6]{0,1:T(8,128)S(1)}, f32[24,6]{0,1:T(8,128)}, u32[]{:S(2)}) copy-start(f32[24,6]{0,1:T(8,128)} %param.43) | copy-start | bytes 1732
  1110.0 688.0 %copy-start.277 = (f32[24,6]{0,1:T(8,128)S(1)}, f32[24,6]{0,1:T(8,128)}, u32[]{:S(2)}) copy-start(f32[24,6]{0,1:T(8,128)} %param.28) | copy-start | bytes 1732
  1110.1 688.0 %copy-start.307 = (f32[24,6]{0,1:T(8,128)S(1)}, f32[24,6]{0,1:T(8,128)}, u32[]{:S(2)}) copy-start(f32[24,6]{0,1:T(8,128)} %param.38) | copy-start | bytes 1732
  1110.1 688.0 %copy-start.308 = (f32[24,6]{0,1:T(8,128)S(1)}, f32[24,6]{0,1:T(8,128)}, u32[]{:S(2)}) copy-start(f32[24,6]{0,1:T(8,128)} %param.33) | copy-start | bytes 1732
  1184.8 622.0 %copy-start.98 = (f32[24,12288]{1,0:T(8,128)S(1)}, f32[24,12288]{1,0:T(8,128)}, u32[]{:S(2)}) copy-start(f32[24,12288]{1,0:T(8,128)} %param.26) | copy-start | bytes 3538948
  1184.8 622.0 %copy-start.100 = (f32[24,12288]{1,0:T(8,128)S(1)}, f32[24,12288]{1,0:T(8,128)}, u32[]{:S(2)}) copy-start(f32[24,12288]{1,0:T(8,128)} %param.41) | copy-start | bytes 3538948
  (346 other events, 2546.0 us)
Sparse Core Ops, SparseCore 0:
  11.6 60.2 all-gather.20
  75.3 56.1 all-gather.10
  135.0 65.3 all-gather.12
  203.8 88.3 all-gather.22
  295.6 80.8 all-gather.14
  379.8 62.2 all-gather.16
  445.5 80.8 all-gather.18
  529.9 123.2 all-gather.24
  976.9 95.2 reduce-scatter.15
  1077.5 106.0 reduce-scatter.13
  1191.1 205.8 reduce-scatter.9
  1404.4 347.6 reduce-scatter.11
where the time goes:
time: 1830 us; the launch traced here: 1820 us
  waiting for transfers between devices  687 us (38%)
  matrix products  525 us (29%)
  blocking collectives  359 us (20%)
  other arithmetic  131 us (7%)
  local copies, waits for them, and re-layouts  88.9 us (5%)
  between operations  24.7 us (1%)
    reduce_scatter x1, waiting for transfers between devices, local(): lax.psum_scatter(accum_parts[2], ('dp', 'seq'), scatter_dimension=0, tile...  353 us
    reduce_scatter x1, waiting for transfers between devices, local(): lax.psum_scatter(accum_parts[1], ('dp', 'seq'), scatter_dimension=0, tile...  211 us
    dot_general x22, matrix products, contract_cols(): lax.dot_general(left, right, (((1,), (1,)), ((), ())), preferred_element_...  142 us
    all_gather x1, blocking collectives, local(): lax.all_gather(posit_half, ('dp', 'seq'), axis=0, tiled=True)  72.3 us
    all_gather x1, blocking collectives, local(): lax.all_gather(teach_posit_half, ('dp', 'seq'), axis=0, tiled=True)  72.2 us
    all_gather x1, blocking collectives, local(): lax.all_gather(teach_vecs_half, ('dp', 'seq'), axis=0, tiled=True)  70.2 us
    dot_general x20, matrix products, contract_rows(): lax.dot_general(left, right, (((0,), (0,)), ((), ())), preferred_element_...  69 us
    dot_general x4, matrix products, layer_forward(): jnp.dot(normed_two, mlp_full[:, :ff_width], preferred_element_type=jnp.fl...  68.4 us
  transfers between devices with their start and end apart: 12, of which 5 were waited for; matrix products, arithmetic and copies ran while one was open for 22% of the time, Pallas kernels for 0%

commit v1 on v0

v1 whole, which is shorter than its diff:
```python
import jax
import jax.numpy as jnp
from jax import lax
from jax.experimental import pallas as pl
from jax.experimental.pallas import tpu as pltpu
from jax.sharding import PartitionSpec as P

HDIM = 64
LAYERS = 2
TOPK = 2
LANES = 128

ln_eps = 1e-05
in_eps = 1e-05
learn_rate = 0.02
first_decay = 0.5
second_decay = 0.5
adam_eps = 1e-08
weight_decay = 0.1
teacher_keep = 0.5
huber_beta = 1.0
score_scale = 0.125
entry_clip = 1e-05
half_type = jnp.bfloat16
full_type = jnp.float32
AXES = ("dp", "seq")


def contract(left, right, left_dim, right_dim):
    return lax.dot_general(
        left,
        right,
        (((left_dim,), (right_dim,)), ((), ())),
        preferred_element_type=full_type,
    )


def head_mask(which, width):
    lane = lax.broadcasted_iota(jnp.int32, (1, width), 1)
    return (lane // HDIM) == which


def attend_kernel(q_ref, k_ref, v_ref, o_ref):
    queries = q_ref[0] * jnp.asarray(score_scale, half_type)
    keys_all = k_ref[0]
    values_all = v_ref[0]
    width = queries.shape[1]
    mixed = None
    for which in range(width // HDIM):
        mask = head_mask(which, width)
        head_q = jnp.where(mask, queries, jnp.zeros_like(queries))
        scores = contract(head_q, keys_all, 1, 1)
        exps = jnp.exp(scores - jnp.max(scores, axis=1, keepdims=True))
        probs = (exps * (1.0 / jnp.sum(exps, axis=1, keepdims=True))).astype(half_type)
        head_out = contract(probs, values_all, 1, 0)
        mixed = head_out if mixed is None else jnp.where(mask, head_out, mixed)
    o_ref[0] = mixed.astype(half_type)


def attend_back_kernel(q_ref, k_ref, v_ref, do_ref, dq_ref, dk_ref, dv_ref):
    queries = q_ref[0] * jnp.asarray(score_scale, half_type)
    keys_all = k_ref[0]
    values_all = v_ref[0]
    grad_out = do_ref[0]
    width = queries.shape[1]
    grad_k = None
    grad_v = None
    grad_q_rows = []
    for which in range(width // HDIM):
        mask = head_mask(which, width)
        head_q = jnp.where(mask, queries, jnp.zeros_like(queries))
        head_do = jnp.where(mask, grad_out, jnp.zeros_like(grad_out))
        scores = contract(keys_all, head_q, 1, 1)
        exps = jnp.exp(scores - jnp.max(scores, axis=0, keepdims=True))
        probs = exps * (1.0 / jnp.sum(exps, axis=0, keepdims=True))
        grad_probs = contract(values_all, head_do, 1, 1)
        prods = probs * grad_probs
        grad_scores = (prods - probs * jnp.sum(prods, axis=0, keepdims=True)).astype(half_type)
        head_dv = contract(probs.astype(half_type), grad_out, 1, 0)
        head_dk = contract(grad_scores, queries, 1, 0)
        head_dq = contract(keys_all, grad_scores, 0, 0)
        grad_q_rows.append(head_dq[which * HDIM : (which + 1) * HDIM])
        grad_v = head_dv if grad_v is None else jnp.where(mask, head_dv, grad_v)
        grad_k = head_dk if grad_k is None else jnp.where(mask, head_dk, grad_k)
    grad_q = jnp.concatenate(grad_q_rows, axis=0).T * score_scale
    dq_ref[0] = grad_q.astype(half_type)
    dk_ref[0] = grad_k.astype(half_type)
    dv_ref[0] = grad_v.astype(half_type)


def qkv_specs(tokens, blocks):
    return [
        pl.BlockSpec((1, tokens, LANES), lambda s, j, off=off: (s, 0, off * blocks + j))
        for off in range(3)
    ]


def attend(projected):
    seqs, tokens, width3 = projected.shape
    width = width3 // 3
    blocks = width // LANES
    return pl.pallas_call(
        attend_kernel,
        grid=(seqs, blocks),
        in_specs=qkv_specs(tokens, blocks),
        out_specs=pl.BlockSpec((1, tokens, LANES), lambda s, j: (s, 0, j)),
        out_shape=jax.ShapeDtypeStruct((seqs, tokens, width), half_type),
        cost_estimate=pl.CostEstimate(
            flops=16 * seqs * tokens * tokens * width,
            transcendentals=seqs * tokens * tokens * width // HDIM,
            bytes_accessed=8 * seqs * tokens * width,
        ),
        name="attend",
    )(projected, projected, projected)


def attend_back(projected, grad_mixed):
    seqs, tokens, width3 = projected.shape
    width = width3 // 3
    blocks = width // LANES
    block = pl.BlockSpec((1, tokens, LANES), lambda s, j: (s, 0, j))
    shape = jax.ShapeDtypeStruct((seqs, tokens, width), half_type)
    return pl.pallas_call(
        attend_back_kernel,
        grid=(seqs, blocks),
        in_specs=qkv_specs(tokens, blocks) + [block],
        out_specs=[block, block, block],
        out_shape=[shape, shape, shape],
        cost_estimate=pl.CostEstimate(
            flops=32 * seqs * tokens * tokens * width,
            transcendentals=seqs * tokens * tokens * width // HDIM,
            bytes_accessed=14 * seqs * tokens * width,
        ),
        name="attend_back",
    )(projected, projected, projected, grad_mixed)


def normalize(values, gain_vec):
    centre = values - jnp.mean(values, axis=-1, keepdims=True)
    inv_scale = lax.rsqrt(jnp.mean(centre * centre, axis=-1, keepdims=True) + ln_eps)
    normed_unit = centre * inv_scale
    return (normed_unit * gain_vec).astype(half_type), normed_unit, inv_scale


def normalize_back(grad_out, gain_vec, normed_unit, inv_scale):
    grad_unit = grad_out * gain_vec
    inner_mean = jnp.mean(grad_unit, axis=-1, keepdims=True)
    along_mean = jnp.mean(grad_unit * normed_unit, axis=-1, keepdims=True)
    grad_in = (grad_unit - inner_mean - normed_unit * along_mean) * inv_scale
    return grad_in, jnp.sum(grad_out * normed_unit, axis=0)


def normal_cdf(values):
    return 0.5 + 0.5 * lax.erf(values * (0.5**0.5))


def gelu_exact(values):
    return values * normal_cdf(values)


def gelu_slope(values):
    density = jnp.exp(-0.5 * values * values) * (0.5 / jnp.pi) ** 0.5
    return normal_cdf(values) + values * density


class Plan:
    def __init__(self):
        self.seq_size = lax.axis_size("seq")
        self.count = lax.axis_size("dp") * self.seq_size
        self.bits = self.count.bit_length() - 1
        self.early = list(range(self.bits - 1, 2, -1))

        def flips(pick):
            return [(i, i ^ (1 << pick((i >> 1) & 1))) for i in range(self.count)]

        self.stages = [flips(lambda core, b=b: b) for b in self.early]
        self.stages.append(flips(lambda core: 0 if core else 2))
        self.stages.append(flips(lambda core: 2 if core else 0))
        self.core_stage = flips(lambda core: 1)
        self.index = lax.axis_index("dp") * self.seq_size + lax.axis_index("seq")

    def swap(self, value, perm):
        return lax.ppermute(value, AXES, perm)

    def row_table(self, width):
        rows = width // self.count
        place = lax.broadcasted_iota(jnp.int32, (1, width), 1)
        spot = place // rows
        early_count = len(self.early)
        other = (spot >> (self.bits - 1)) & 1
        holder_core = ((self.index >> 1) & 1) ^ other
        block = self.index ^ (other << 1)
        for step, bit in enumerate(self.early):
            block = block ^ (((spot >> step) & 1) << bit)
        first = (spot >> early_count) & 1
        second = (spot >> (early_count + 1)) & 1
        block = block ^ jnp.where(holder_core == 0, first << 2, first)
        block = block ^ jnp.where(holder_core == 0, second, second << 2)
        return block * rows + place % rows

    def mover(self, width):
        table = self.row_table(width)
        whole = lax.broadcasted_iota(jnp.int32, (width, width), 0)
        return (whole == table).astype(half_type)


def to_relative(values, mover):
    return contract(values, mover, 1, 0).astype(half_type)


def to_whole(values, mover):
    return contract(values, mover, 1, 1).astype(half_type)


def gather_chunks(plan, chunks):
    done = []
    last = [None] * len(plan.stages)
    for parts in chunks:
        value = jnp.concatenate(parts, axis=1)
        for step, perm in enumerate(plan.stages):
            if last[step] is not None:
                value, _ = lax.optimization_barrier((value, last[step]))
            got = plan.swap(value, perm)
            last[step] = got
            value = jnp.concatenate([value, got], axis=0)
        got = plan.swap(value, plan.core_stage)
        outs = []
        start = 0
        for part in parts:
            stop = start + part.shape[1]
            outs.append(jnp.concatenate([value[:, start:stop], got[:, start:stop]], axis=0))
            start = stop
        done.append(outs)
    return done


def scatter_chunk(plan, pieces):
    gots = [plan.swap(far, plan.core_stage) for _, far in pieces]
    quarter = pieces[0][0].shape[0] // 2
    send = jnp.concatenate(
        [near[quarter:] + got[quarter:] for (near, _), got in zip(pieces, gots)], axis=1
    )
    keep = jnp.concatenate(
        [near[:quarter] + got[:quarter] for (near, _), got in zip(pieces, gots)], axis=1
    )
    stages = plan.stages[::-1]
    for step, perm in enumerate(stages):
        got = plan.swap(send, perm)
        if step == len(stages) - 1:
            return keep + got
        half = keep.shape[0] // 2
        send = keep[half:] + got[half:]
        keep = keep[:half] + got[:half]


def halves(left, right):
    half = left.shape[1] // 2
    return contract(left[:, :half], right, 0, 0), contract(left[:, half:], right, 0, 0)


def row_halves(value):
    half = value.shape[0] // 2
    return value[:half], value[half:]


def layer_forward(flat_in, seqs, weights, gain_one, gain_two):
    w_qkv, w_out, w_up, w_down = weights
    tokens = flat_in.shape[0] // seqs
    normed_one, unit_one, scale_one = normalize(flat_in, gain_one)
    projected = contract(normed_one, w_qkv, 1, 0).astype(half_type)
    projected = projected.reshape(seqs, tokens, projected.shape[1])
    mixed = attend(projected).reshape(flat_in.shape)
    middle = flat_in + contract(mixed, w_out, 1, 0)
    normed_two, unit_two, scale_two = normalize(middle, gain_two)
    hidden_up = contract(normed_two, w_up, 1, 0)
    active = gelu_exact(hidden_up).astype(half_type)
    out = middle + contract(active, w_down, 1, 1)
    saved = (
        unit_one,
        scale_one,
        normed_one,
        projected,
        mixed,
        unit_two,
        scale_two,
        normed_two,
        hidden_up,
        active,
    )
    return out, saved


def layer_backward(grad_out, saved, weights, gain_one, gain_two, mover):
    (
        unit_one,
        scale_one,
        normed_one,
        projected,
        mixed,
        unit_two,
        scale_two,
        normed_two,
        hidden_up,
        active,
    ) = saved
    w_qkv, w_out, w_up, w_down = weights
    grad_down = grad_out.astype(half_type)
    grad_active = contract(grad_down, w_down, 1, 0)
    grad_hidden = (grad_active * gelu_slope(hidden_up)).astype(half_type)
    mlp_pieces = [halves(normed_two, grad_hidden), halves(grad_down, active)]
    grad_norm_two = contract(grad_hidden, w_up, 1, 1)
    grad_middle, grad_gain_two = normalize_back(grad_norm_two, gain_two, unit_two, scale_two)
    grad_middle = grad_out + grad_middle
    grad_branch = grad_middle.astype(half_type)
    out_piece = halves(to_relative(mixed, mover), to_whole(grad_branch, mover))
    grad_mixed = contract(grad_branch, w_out, 1, 1).astype(half_type)
    grad_q, grad_k, grad_v = attend_back(
        projected, grad_mixed.reshape(projected.shape[0], projected.shape[1], -1)
    )
    grad_proj = jnp.concatenate([grad_q, grad_k, grad_v], axis=2).reshape(
        grad_out.shape[0], projected.shape[2]
    )
    qkv_piece = halves(normed_one, grad_proj)
    grad_norm_one = contract(grad_proj, w_qkv, 1, 1)
    grad_in, grad_gain_one = normalize_back(grad_norm_one, gain_one, unit_one, scale_one)
    return (
        grad_middle + grad_in,
        [qkv_piece, out_piece],
        mlp_pieces,
        grad_gain_one,
        grad_gain_two,
    )


def adam_step(weight, first_mom, second_mom, teacher, gradient):
    first_new = first_decay * first_mom + (1.0 - first_decay) * gradient
    second_new = second_decay * second_mom + (1.0 - second_decay) * gradient * gradient
    weight_new = weight - learn_rate * (
        first_new / (jnp.sqrt(second_new) + adam_eps) + weight_decay * weight
    )
    teacher_new = teacher_keep * teacher + (1.0 - teacher_keep) * weight_new
    return (weight_new, first_new, second_new, teacher_new)


def pad_lanes(value):
    extra = -value.shape[1] % LANES
    return jnp.pad(value, ((0, 0), (0, extra)))


def local(
    patches,
    masked_at,
    edge_w,
    attn_w,
    mlp_w,
    posit_w,
    vecs_w,
    edge_m,
    attn_m,
    mlp_m,
    posit_m,
    vecs_m,
    edge_v,
    attn_v,
    mlp_v,
    posit_v,
    vecs_v,
    edge_t,
    attn_t,
    mlp_t,
    posit_t,
    vecs_t,
):
    seqs, tokens, width = patches.shape
    plan = Plan()
    total_masked = seqs * plan.count * tokens // 2
    ff_width = mlp_w.shape[1] // (2 * LAYERS)
    small_cols = tokens + vecs_w.shape[1]
    flat_patch = patches.reshape(-1, width)
    mask_flat = masked_at.astype(full_type).reshape(-1, 1)

    def shards(edge, attn, mlp, posit, vecs):
        edge, attn, mlp, posit, vecs = (
            part.astype(half_type) for part in (edge, attn, mlp, posit, vecs)
        )
        small = pad_lanes(jnp.concatenate([posit, vecs], axis=1))
        attn_parts = []
        mlp_parts = []
        for layer in range(LAYERS):
            base = layer * 4 * width
            attn_parts.append(
                [attn[:, base : base + 3 * width], attn[:, base + 3 * width : base + 4 * width]]
            )
            base = layer * 2 * ff_width
            mlp_parts.append(
                [mlp[:, base : base + ff_width], mlp[:, base + ff_width : base + 2 * ff_width]]
            )
        return edge[:, :width], edge[:, width:], small, attn_parts, mlp_parts

    t_patch, _, t_small, t_attn, t_mlp = shards(edge_t, attn_t, mlp_t, posit_t, vecs_t)
    s_patch, s_head, s_small, s_attn, s_mlp = shards(edge_w, attn_w, mlp_w, posit_w, vecs_w)
    chunks = [
        [t_patch, t_small] + t_attn[0],
        t_mlp[0],
        t_attn[1] + t_mlp[1],
        [s_patch, s_small] + s_attn[0],
        s_mlp[0],
        s_attn[1] + [s_head],
        s_mlp[1],
    ]
    gathered = gather_chunks(plan, chunks)
    t_first, t_mlp0, t_second, s_first, s_mlp0, s_second, s_mlp1 = gathered

    mover = plan.mover(width)
    patch_rel = to_relative(flat_patch, mover)

    def both_sides(w_out):
        return contract(mover, to_relative(w_out, mover), 1, 0).astype(half_type)

    def ready(first, mlp0, attn1, mlp1):
        patch, small, qkv0, out0 = first
        qkv1, out1 = attn1
        vec_table = small[:, tokens:small_cols].astype(full_type).T
        posit = small[:, :tokens].astype(full_type).T
        layers = [
            (qkv0, both_sides(out0), mlp0[0], mlp0[1]),
            (qkv1, both_sides(out1), mlp1[0], mlp1[1]),
        ]
        return to_relative(patch, mover), posit, vec_table, layers

    t_embed, t_posit, t_vecs, t_layers = ready(t_first, t_mlp0, t_second[:2], t_second[2:])
    s_embed, s_posit, s_vecs, s_layers = ready(s_first, s_mlp0, s_second[:2], s_mlp1)
    head_rel = to_relative(s_second[2], mover)

    def spread(table):
        return jnp.broadcast_to(table[None], (seqs, tokens, width)).reshape(-1, width)

    state = contract(patch_rel, t_embed, 1, 0) + spread(t_posit)
    target = None
    for layer in range(LAYERS):
        state, _ = layer_forward(
            state, seqs, t_layers[layer], t_vecs[layer], t_vecs[LAYERS + layer]
        )
        if layer >= LAYERS - TOPK:
            by_seq = state.reshape(seqs, tokens, width)
            centred = by_seq - jnp.mean(by_seq, axis=1, keepdims=True)
            variance = jnp.mean(centred * centred, axis=1, keepdims=True)
            term = centred * lax.rsqrt(variance + in_eps)
            target = term if target is None else target + term
    target = (target / TOPK).reshape(-1, width)

    embedded = contract(patch_rel, s_embed, 1, 0)
    current = (
        embedded * (1.0 - mask_flat) + mask_flat * s_vecs[2 * LAYERS + 1] + spread(s_posit)
    )
    kept = []
    for layer in range(LAYERS):
        current, saved = layer_forward(
            current, seqs, s_layers[layer], s_vecs[layer], s_vecs[LAYERS + layer]
        )
        kept.append(saved)
    final_normed, final_unit, final_scale = normalize(current, s_vecs[2 * LAYERS])
    predicted = contract(final_normed, head_rel, 1, 0)
    differ = predicted - target
    magnitude = jnp.abs(differ)
    huber_terms = jnp.where(
        magnitude < huber_beta, 0.5 * differ * differ / huber_beta, magnitude - 0.5 * huber_beta
    )
    loss_local = jnp.sum(huber_terms * mask_flat) / total_masked
    grad_pred = (mask_flat * jnp.clip(differ / huber_beta, -1.0, 1.0) / total_masked).astype(
        half_type
    )
    head_piece = halves(final_normed, to_whole(grad_pred, mover))
    grad_flow, grad_gain_final = normalize_back(
        contract(grad_pred, head_rel, 1, 1), s_vecs[2 * LAYERS], final_unit, final_scale
    )
    gain_ones = [None] * LAYERS
    gain_twos = [None] * LAYERS
    attn_shards = [None] * LAYERS
    mlp_shards = [None] * LAYERS
    head_shard = None
    for layer in reversed(range(LAYERS)):
        grad_flow, attn_pieces, mlp_pieces, gain_ones[layer], gain_twos[layer] = layer_backward(
            grad_flow,
            kept[layer],
            s_layers[layer],
            s_vecs[layer],
            s_vecs[LAYERS + layer],
            mover,
        )
        mlp_shards[layer] = scatter_chunk(plan, mlp_pieces)
        if head_shard is None:
            summed = scatter_chunk(plan, [head_piece] + attn_pieces)
            head_shard = summed[:, :width]
            attn_shards[layer] = summed[:, width:]
        else:
            attn_shards[layer] = scatter_chunk(plan, attn_pieces)
    grad_maskvec = jnp.sum(grad_flow * mask_flat, axis=0)
    grad_posit = jnp.sum(grad_flow.reshape(seqs, tokens, width), axis=0).T
    grad_embed = to_whole((grad_flow * (1.0 - mask_flat)).astype(half_type), mover)
    patch_piece = halves(patch_rel, grad_embed)
    vec_grads = jnp.stack(gain_ones + gain_twos + [grad_gain_final, grad_maskvec], axis=1)
    small_grads = pad_lanes(jnp.concatenate([grad_posit, vec_grads], axis=1))
    summed = scatter_chunk(plan, [patch_piece, row_halves(small_grads)])
    raw = (
        jnp.concatenate([summed[:, :width], head_shard], axis=1),
        jnp.concatenate(attn_shards, axis=1),
        jnp.concatenate(mlp_shards, axis=1),
        summed[:, width : width + tokens],
        summed[:, width + tokens : width + small_cols],
    )
    totals = jnp.stack([loss_local] + [jnp.sum(part * part) for part in raw])
    totals = jnp.broadcast_to(totals[:, None], (totals.shape[0], LANES))
    for perm in [plan.core_stage] + plan.stages:
        totals = totals + plan.swap(totals, perm)
    total_loss = totals[0, 0]
    clipped = []
    for group, part in enumerate(raw):
        limit = entry_clip * jnp.sqrt(jnp.float32(part.size * plan.count))
        norm_value = jnp.sqrt(totals[group + 1, 0])
        clipped.append(part * (limit / jnp.maximum(norm_value, limit)))
    edge_new = adam_step(edge_w, edge_m, edge_v, edge_t, clipped[0])
    attn_new = adam_step(attn_w, attn_m, attn_v, attn_t, clipped[1])
    mlp_new = adam_step(mlp_w, mlp_m, mlp_v, mlp_t, clipped[2])
    posit_new = adam_step(posit_w, posit_m, posit_v, posit_t, clipped[3])
    vecs_new = adam_step(vecs_w, vecs_m, vecs_v, vecs_t, clipped[4])
    news = (edge_new, attn_new, mlp_new, posit_new, vecs_new)
    return (total_loss,) + tuple(group[part] for part in range(4) for group in news)


def solution(mesh):
    rows = P(AXES, None)
    in_specs = (P(AXES, None, None),) + (rows,) * 21
    out_specs = (P(),) + (rows,) * 20
    return jax.shard_map(local, mesh=mesh, in_specs=in_specs, out_specs=out_specs, check_vma=False)
```

time: 1830 us -> 1180 us (0.64)
  blocking collectives: 359 us -> 0 us
  matrix products: 525 us -> 265 us
  waiting for transfers between devices: 687 us -> 440 us
  Pallas kernels: 0 us -> 117 us
  local copies, waits for them, and re-layouts: 88.9 us -> 148 us
  starting transfers between devices: 1.34 us -> 58.2 us
    reduce_scatter x4 -> x0, waiting for transfers between devices: 594 us -> none  [the longest x1 353 us: local(): lax.psum_scatter(accum_parts[2], ('dp', 'seq'), scatter_dimension=0, tile...]
    ppermute x0 -> x71, waiting for transfers between devices: none -> 440 us  [swap(): return lax.ppermute(value, AXES, perm)]
    all_gather x4 -> x0, blocking collectives: 279 us -> none  [the longest x1 72.3 us: local(): lax.all_gather(posit_half, ('dp', 'seq'), axis=0, tiled=True)]
    dot_general x100 -> x59, matrix products: 489 us -> 265 us  [contract(): lax.dot_general(left, right, (((left_dim,), (right_dim,)), ((), ())), pre...]
    pallas_call x0 -> x6, Pallas kernels: none -> 117 us  [the longest x4 66.3 us: attend(): pl.pallas_call(attend_kernel, grid=(seqs, blocks), in_specs=qkv_specs(tok...]
    all_gather x8 -> x0, waiting for transfers between devices: 91.8 us -> none  [the longest x1 54.6 us: local(): lax.all_gather(teach_mlp_half, ('dp', 'seq'), axis=0, tiled=True)]
    ppermute x0 -> x71, starting transfers between devices: none -> 58.2 us  [swap(): return lax.ppermute(value, AXES, perm)]
    psum x1 -> x0, blocking collectives: 40.1 us -> none  [local(): lax.psum((loss_local, square_sums[0], square_sums[1], square_sums[2], squ...]
  transfers between devices with their start and end apart: 12 -> 71, of which waited for: 5 -> 34; matrix products, arithmetic and copies ran while one was open for 22% -> 30% of each run, Pallas kernels for 0% -> 6%
where the time goes in v1:
time: 1180 us; the launch traced here: 1170 us
  waiting for transfers between devices  440 us (37%)
  matrix products  265 us (22%)
  local copies, waits for them, and re-layouts  148 us (13%)
  other arithmetic  130 us (11%)
  Pallas kernels  117 us (10%)
  starting transfers between devices  58.2 us (5%)
    ppermute x71, waiting for transfers between devices, swap(): return lax.ppermute(value, AXES, perm)  440 us
    dot_general x59, matrix products, contract(): lax.dot_general(left, right, (((left_dim,), (right_dim,)), ((), ())), pre...  265 us
    pallas_call x4, Pallas kernels, attend(): pl.pallas_call(attend_kernel, grid=(seqs, blocks), in_specs=qkv_specs(tok...  66.3 us
    ppermute x71, starting transfers between devices, swap(): return lax.ppermute(value, AXES, perm)  58.2 us
    pallas_call x2, Pallas kernels, attend_back(): pl.pallas_call(attend_back_kernel, grid=(seqs, blocks), in_specs=qkv_spec...  50.3 us
    unnamed x365, local copies, waits for them, and re-layouts  47.4 us
    slice x14, local copies, waits for them, and re-layouts, gather_chunks(): value[:, start:stop]  34.9 us
    add x11, other arithmetic, scatter_chunk(): near[:quarter] + got[:quarter]  33.2 us
  transfers between devices with their start and end apart: 71, of which 34 were waited for; matrix products, arithmetic and copies ran while one was open for 30% of the time, Pallas kernels for 6%

profile of v1, /device:TPU:0, one launch (start us, length us, event | category | flops | bytes accessed | tf_op | source)
XLA Modules:
  0.0 1166.1 jit_solution(2096701481500483858)
XLA Ops:
  24.1 11.4 collective-permute-done.1
  42.5 13.9 %collective-permute-done.2 = bf16[24,9216]{1,0:T(8,128)(2,1)S(1)} collective-permute-done((bf16[24,9216]{1,0:T(8,128)(2,1)S(1)}, bf16[24,9216]{1,0:T(8,128)(2,1)S(1)}, u32[]{:S(2)}, u32[]{:S(2)}) %collective-permute-start.2) | collective-permute-done | bytes 442400 | tf_op jit(solution)/shard_map/ppermute | solution.py:183
  56.6 12.3 %collective-permute-done.3 = bf16[24,4352]{1,0:T(8,128)(2,1)S(1)} collective-permute-done((bf16[24,4352]{1,0:T(8,128)(2,1)S(1)}, bf16[24,4352]{1,0:T(8,128)(2,1)S(1)}, u32[]{:S(2)}, u32[]{:S(2)}) %collective-permute-start.3) | collective-permute-done | bytes 208928 | tf_op jit(solution)/shard_map/ppermute | solution.py:183
  73.6 11.3 collective-permute-done.17
  88.2 7.8 collective-permute-done.22
  99.5 15.3 %collective-permute-done.27 = bf16[24,6144]{1,0:T(8,128)(2,1)S(1)} collective-permute-done((bf16[24,6144]{1,0:T(8,128)(2,1)S(1)}, bf16[24,6144]{1,0:T(8,128)(2,1)S(1)}, u32[]{:S(2)}, u32[]{:S(2)}) %collective-permute-start.27) | collective-permute-done | bytes 294944 | tf_op jit(solution)/shard_map/ppermute | solution.py:183
  115.1 10.9 collective-permute-done.7
  127.9 11.8 %collective-permute-done.18 = bf16[48,6144]{1,0:T(8,128)(2,1)S(1)} collective-permute-done((bf16[48,6144]{1,0:T(8,128)(2,1)S(1)}, bf16[48,6144]{1,0:T(8,128)(2,1)S(1)}, u32[]{:S(2)}, u32[]{:S(2)}) %collective-permute-start.18) | collective-permute-done | bytes 589856 | tf_op jit(solution)/shard_map/ppermute | solution.py:183
  152.5 8.1 collective-permute-done.28
  164.7 18.4 %collective-permute-done.11 = bf16[96,4352]{1,0:T(8,128)(2,1)S(1)} collective-permute-done((bf16[96,4352]{1,0:T(8,128)(2,1)S(1)}, bf16[96,4352]{1,0:T(8,128)(2,1)S(1)}, u32[]{:S(2)}, u32[]{:S(2)}) %collective-permute-start.11) | collective-permute-done | bytes 835616 | tf_op jit(solution)/shard_map/ppermute | solution.py:183
  196.5 8.0 collective-permute-done.19
  231.1 16.3 %attend.6 = bf16[2,448,768]{2,1,0:T(8,128)(2,1)} custom-call(bf16[2,448,2304]{2,1,0:T(8,128)(2,1)} %bitcast.165, bf16[2,448,2304]{2,1,0:T(8,128)(2,1)} %bitcast.166, bf16[2,448,2304]{2,1,0:T(8,128)(2,1)} %bitcast.167), custom_call_target="tpu_custom_call" | custom-call | flops 4932501504 | bytes 5505024 | tf_op jit(solution)/shard_map/attend/pallas_call | solution.py:102
  288.7 16.0 %fusion.322 = (f32[896]{0:T(1024)S(1)}, f32[896,768]{1,0:T(8,128)}) fusion(f32[896,768]{1,0:T(8,128)} %copy-done.27, bf16[384,3072]{1,0:T(8,128)(2,1)} %get-tuple-element.277, bf16[384,3072]{1,0:T(8,128)(2,1)} %get-tuple-element.275, bf16[384,3072]{1,0:T(8,128)(2,1)} %get-tuple-element.276, bf16[384,3072]{1,0:T(8,128)(2,1)} %get-tuple-element.274, ...), kind=kOutput, calls=%fused_computation.555 | convolution fusion | flops 8492481536 | bytes 14956032 | tf_op jit(solution)/shard_map/dot_general | solution.py:30
  318.3 17.5 %collective-permute-done.20 = bf16[192,6144]{1,0:T(8,128)(2,1)S(1)} collective-permute-done((bf16[192,6144]{1,0:T(8,128)(2,1)}, bf16[192,6144]{1,0:T(8,128)(2,1)S(1)}, u32[]{:S(2)}, u32[]{:S(2)}) %collective-permute-start.20) | collective-permute-done | bytes 2359328 | tf_op jit(solution)/shard_map/ppermute | solution.py:183
  368.2 16.6 %attend.4 = bf16[2,448,768]{2,1,0:T(8,128)(2,1)} custom-call(bf16[2,448,2304]{2,1,0:T(8,128)(2,1)} %bitcast.150, bf16[2,448,2304]{2,1,0:T(8,128)(2,1)} %bitcast.151, bf16[2,448,2304]{2,1,0:T(8,128)(2,1)} %bitcast.152), custom_call_target="tpu_custom_call" | custom-call | flops 4932501504 | bytes 5505024 | tf_op jit(solution)/shard_map/attend/pallas_call | solution.py:102
  415.4 16.8 %attend.7 = bf16[2,448,768]{2,1,0:T(8,128)(2,1)} custom-call(bf16[2,448,2304]{2,1,0:T(8,128)(2,1)} %bitcast.162, bf16[2,448,2304]{2,1,0:T(8,128)(2,1)} %bitcast.163, bf16[2,448,2304]{2,1,0:T(8,128)(2,1)} %bitcast.164), custom_call_target="tpu_custom_call" | custom-call | flops 4932501504 | bytes 5505024 | tf_op jit(solution)/shard_map/attend/pallas_call | solution.py:102
  447.3 15.8 %fusion.82 = f32[896,768]{1,0:T(8,128)} fusion(f32[896,768]{1,0:T(8,128)} %copy-done.50, bf16[384,3072]{1,0:T(8,128)(2,1)} %get-tuple-element.257, bf16[384,3072]{1,0:T(8,128)(2,1)} %get-tuple-element.255, bf16[384,3072]{1,0:T(8,128)(2,1)} %get-tuple-element.256, bf16[384,3072]{1,0:T(8,128)(2,1)} %get-tuple-element.254, f32[768]{0:T(1024)S(1)} %copy-done.143, ...), kind=kOutput, calls=%fused_computation.189 | convolution fusion | flops 8491794432 | bytes 14952448 | tf_op jit(solution)/shard_map/dot_general | solution.py:30
  508.2 16.6 %attend.5 = bf16[2,448,768]{2,1,0:T(8,128)(2,1)} custom-call(bf16[2,448,2304]{2,1,0:T(8,128)(2,1)} %bitcast.156, bf16[2,448,2304]{2,1,0:T(8,128)(2,1)} %bitcast.157, bf16[2,448,2304]{2,1,0:T(8,128)(2,1)} %bitcast.158), custom_call_target="tpu_custom_call" | custom-call | flops 4932501504 | bytes 5505024 | tf_op jit(solution)/shard_map/attend/pallas_call | solution.py:102
  557.4 11.9 %fusion.5 = bf16[896,3072]{1,0:T(8,128)(2,1)S(1)} fusion(f32[896,3072]{1,0:T(8,128)} %get-tuple-element.351, bf16[896,768]{1,0:T(8,128)(2,1)S(1)} %get-tuple-element.236, bf16[384,3072]{1,0:T(8,128)(2,1)S(1)} %copy-done.77, bf16[384,3072]{1,0:T(8,128)(2,1)S(1)} %copy-done.73), kind=kOutput, calls=%fused_computation.7 | convolution fusion | flops 4264820736 | bytes 22609920 | tf_op jit(solution)/shard_map/dot_general | solution.py:30
  577.9 25.2 %attend_back.2 = (bf16[2,448,768]{2,1,0:T(8,128)(2,1)}, bf16[2,448,768]{2,1,0:T(8,128)(2,1)}, bf16[2,448,768]{2,1,0:T(8,128)(2,1)}) custom-call(bf16[2,448,2304]{2,1,0:T(8,128)(2,1)} %bitcast.159, bf16[2,448,2304]{2,1,0:T(8,128)(2,1)} %bitcast.160, bf16[2,448,2304]{2,1,0:T(8,128)(2,1)} %bitcast.161, bf16[2,448,768]{2,1,0:T(8,128)(2,1)} %bitcast.173), custom_call_target="tpu_custom_call" | custom-call | flops 9865003008 | bytes 9633792 | tf_op jit(solution)/shard_map/attend_back/pallas_call | solution.py:123
  606.1 8.2 multiply_reduce_fusion.4
  624.4 11.2 fusion.11
  667.6 25.2 %attend_back.3 = (bf16[2,448,768]{2,1,0:T(8,128)(2,1)}, bf16[2,448,768]{2,1,0:T(8,128)(2,1)}, bf16[2,448,768]{2,1,0:T(8,128)(2,1)}) custom-call(bf16[2,448,2304]{2,1,0:T(8,128)(2,1)} %bitcast.153, bf16[2,448,2304]{2,1,0:T(8,128)(2,1)} %bitcast.154, bf16[2,448,2304]{2,1,0:T(8,128)(2,1)} %bitcast.155, bf16[2,448,768]{2,1,0:T(8,128)(2,1)} %bitcast.174), custom_call_target="tpu_custom_call" | custom-call | flops 9865003008 | bytes 9633792 | tf_op jit(solution)/shard_map/attend_back/pallas_call | solution.py:123
  842.8 38.3 %collective-permute-done.44 = f32[192,3840]{1,0:T(8,128)} collective-permute-done((f32[192,3840]{1,0:T(8,128)S(1)}, f32[192,3840]{1,0:T(8,128)}, u32[]{:S(2)}, u32[]{:S(2)}) %collective-permute-start.44) | collective-permute-done | bytes 2949152 | tf_op jit(solution)/shard_map/ppermute | solution.py:183
  888.2 11.6 collective-permute-done.52
  899.9 18.7 %collective-permute-done.45 = f32[96,3840]{1,0:T(8,128)S(1)} collective-permute-done((f32[96,3840]{1,0:T(8,128)S(1)}, f32[96,3840]{1,0:T(8,128)S(1)}, u32[]{:S(2)}, u32[]{:S(2)}) %collective-permute-start.45) | collective-permute-done | bytes 1474592 | tf_op jit(solution)/shard_map/ppermute | solution.py:183
  922.1 14.8 %collective-permute-done.46 = f32[48,3840]{1,0:T(8,128)S(1)} collective-permute-done((f32[48,3840]{1,0:T(8,128)}, f32[48,3840]{1,0:T(8,128)S(1)}, u32[]{:S(2)}, u32[]{:S(2)}) %collective-permute-start.46) | collective-permute-done | bytes 737312 | tf_op jit(solution)/shard_map/ppermute | solution.py:183
  937.1 10.4 collective-permute-done.56
  953.7 69.6 %collective-permute-done.62 = f32[192,6144]{1,0:T(8,128)} collective-permute-done((f32[192,6144]{1,0:T(8,128)}, f32[192,6144]{1,0:T(8,128)}, u32[]{:S(2)}, u32[]{:S(2)}) %collective-permute-start.62) | collective-permute-done | bytes 4718624 | tf_op jit(solution)/shard_map/ppermute | solution.py:183
  1030.0 25.3 %collective-permute-done.63 = f32[96,6144]{1,0:T(8,128)S(1)} collective-permute-done((f32[96,6144]{1,0:T(8,128)S(1)}, f32[96,6144]{1,0:T(8,128)S(1)}, u32[]{:S(2)}, u32[]{:S(2)}) %collective-permute-start.63) | collective-permute-done | bytes 2359328 | tf_op jit(solution)/shard_map/ppermute | solution.py:183
  1057.5 37.5 %collective-permute-done.64 = f32[48,6144]{1,0:T(8,128)S(1)} collective-permute-done((f32[48,6144]{1,0:T(8,128)S(1)}, f32[48,6144]{1,0:T(8,128)S(1)}, u32[]{:S(2)}, u32[]{:S(2)}) %collective-permute-start.64) | collective-permute-done | bytes 1179680 | tf_op jit(solution)/shard_map/ppermute | solution.py:183
  1095.4 25.6 %collective-permute-done.65 = f32[24,6144]{1,0:T(8,128)S(1)} collective-permute-done((f32[24,6144]{1,0:T(8,128)S(1)}, f32[24,6144]{1,0:T(8,128)S(1)}, u32[]{:S(2)}, u32[]{:S(2)}) %collective-permute-start.65) | collective-permute-done | bytes 589856 | tf_op jit(solution)/shard_map/ppermute | solution.py:183
  (771 shorter events, 580.1 us)
Async XLA Ops:
  40.8 44.1 %collective-permute-start.8 = (bf16[96,4352]{1,0:T(8,128)(2,1)S(1)}, bf16[96,4352]{1,0:T(8,128)(2,1)S(1)}, u32[]{:S(2)}, u32[]{:S(2)}) collective-permute-start(bf16[96,4352]{1,0:T(8,128)(2,1)S(1)} %pad_maximum_fusion.47), channel_id=1, source_target_pairs={{0,4},{1,5},{2,3},{3,2},{4,0},{5,1},{6,7},{7,6},{8,12},{9,13},{10,... | collective-permute-start | bytes 2506760 | tf_op jit(solution)/shard_map/ppermute | solution.py:183
  68.9 45.9 %collective-permute-start.6 = (bf16[48,9216]{1,0:T(8,128)(2,1)S(1)}, bf16[48,9216]{1,0:T(8,128)(2,1)S(1)}, u32[]{:S(2)}, u32[]{:S(2)}) collective-permute-start(bf16[48,9216]{1,0:T(8,128)(2,1)S(1)} %pad_maximum_fusion.45), channel_id=1, source_target_pairs={{0,8},{1,9},{2,10},{3,11},{4,12},{5,13},{6,14},{7,15},{8,0},{9,1},... | collective-permute-start | bytes 2654216 | tf_op jit(solution)/shard_map/ppermute | solution.py:183
  84.9 41.4 %collective-permute-start.9 = (bf16[96,6144]{1,0:T(8,128)(2,1)S(1)}, bf16[96,6144]{1,0:T(8,128)(2,1)S(1)}, u32[]{:S(2)}, u32[]{:S(2)}) collective-permute-start(bf16[96,6144]{1,0:T(8,128)(2,1)S(1)} %pad_maximum_fusion.41), channel_id=1, source_target_pairs={{0,4},{1,5},{2,3},{3,2},{4,0},{5,1},{6,7},{7,6},{8,12},{9,13},{10,... | collective-permute-start | bytes 3538952 | tf_op jit(solution)/shard_map/ppermute | solution.py:183
  86.6 53.9 %collective-permute-start.12 = (bf16[192,4352]{1,0:T(8,128)(2,1)S(1)}, bf16[192,4352]{1,0:T(8,128)(2,1)S(1)}, u32[]{:S(2)}, u32[]{:S(2)}) collective-permute-start(bf16[192,4352]{1,0:T(8,128)(2,1)S(1)} %pad_maximum_fusion.33), channel_id=1, source_target_pairs={{0,1},{1,0},{2,6},{3,7},{4,5},{5,4},{6,2},{7,3},{8,9},{9,8},{10,14... | collective-permute-start | bytes 5013512 | tf_op jit(solution)/shard_map/ppermute | solution.py:183
  126.3 35.3 %collective-permute-start.10 = (bf16[96,9216]{1,0:T(8,128)(2,1)S(1)}, bf16[96,9216]{1,0:T(8,128)(2,1)S(1)}, u32[]{:S(2)}, u32[]{:S(2)}) collective-permute-start(bf16[96,9216]{1,0:T(8,128)(2,1)S(1)} %pad_maximum_fusion.31), channel_id=1, source_target_pairs={{0,4},{1,5},{2,3},{3,2},{4,0},{5,1},{6,7},{7,6},{8,12},{9,13},{10,... | collective-permute-start | bytes 5308424 | tf_op jit(solution)/shard_map/ppermute | solution.py:183
  140.5 43.9 %collective-permute-start.13 = (bf16[192,6144]{1,0:T(8,128)(2,1)S(1)}, bf16[192,6144]{1,0:T(8,128)(2,1)S(1)}, u32[]{:S(2)}, u32[]{:S(2)}) collective-permute-start(bf16[192,6144]{1,0:T(8,128)(2,1)S(1)} %pad_maximum_fusion.23), channel_id=1, source_target_pairs={{0,1},{1,0},{2,6},{3,7},{4,5},{5,4},{6,2},{7,3},{8,9},{9,8},{10,14... | collective-permute-start | bytes 7077896 | tf_op jit(solution)/shard_map/ppermute | solution.py:183
  143.4 64.0 %collective-permute-start.32 = (bf16[384,4352]{1,0:T(8,128)(2,1)S(1)}, bf16[384,4352]{1,0:T(8,128)(2,1)S(1)}, u32[]{:S(2)}, u32[]{:S(2)}) collective-permute-start(bf16[384,4352]{1,0:T(8,128)(2,1)S(1)} %constant_dynamic-update-slice_fusion.8), channel_id=1, source_target_pairs={{0,2},{1,3},{2,0},{3,1},{4,6},{5,7},{6,4},{7,5},{8,10},{9,11},{10,... | collective-permute-start | bytes 10027016 | tf_op jit(solution)/shard_map/ppermute | solution.py:183
  185.9 97.9 %collective-permute-start.33 = (bf16[384,6144]{1,0:T(8,128)(2,1)}, bf16[384,6144]{1,0:T(8,128)(2,1)}, u32[]{:S(2)}, u32[]{:S(2)}) collective-permute-start(bf16[384,6144]{1,0:T(8,128)(2,1)} %constant_dynamic-update-slice_fusion.13), channel_id=1, source_target_pairs={{0,2},{1,3},{2,0},{3,1},{4,6},{5,7},{6,4},{7,5},{8,10},{9,11},{10,... | collective-permute-start | bytes 14155784 | tf_op jit(solution)/shard_map/ppermute | solution.py:183
  190.8 76.0 %collective-permute-start.14 = (bf16[192,9216]{1,0:T(8,128)(2,1)}, bf16[192,9216]{1,0:T(8,128)(2,1)}, u32[]{:S(2)}, u32[]{:S(2)}) collective-permute-start(bf16[192,9216]{1,0:T(8,128)(2,1)} %pad_maximum_fusion.8), channel_id=1, source_target_pairs={{0,1},{1,0},{2,6},{3,7},{4,5},{5,4},{6,2},{7,3},{8,9},{9,8},{10,14... | collective-permute-start | bytes 10616840 | tf_op jit(solution)/shard_map/ppermute | solution.py:183
  204.5 42.9 %collective-permute-start.24 = (bf16[96,3840]{1,0:T(8,128)(2,1)}, bf16[96,3840]{1,0:T(8,128)(2,1)}, u32[]{:S(2)}, u32[]{:S(2)}) collective-permute-start(bf16[96,3840]{1,0:T(8,128)(2,1)} %pad_maximum_fusion.49), channel_id=1, source_target_pairs={{0,4},{1,5},{2,3},{3,2},{4,0},{5,1},{6,7},{7,6},{8,12},{9,13},{10,... | collective-permute-start | bytes 2211848 | tf_op jit(solution)/shard_map/ppermute | solution.py:183
  270.8 136.5 %collective-permute-start.34 = (bf16[384,9216]{1,0:T(8,128)(2,1)}, bf16[384,9216]{1,0:T(8,128)(2,1)}, u32[]{:S(2)}, u32[]{:S(2)}) collective-permute-start(bf16[384,9216]{1,0:T(8,128)(2,1)} %constant_dynamic-update-slice_fusion.15), channel_id=1, source_target_pairs={{0,2},{1,3},{2,0},{3,1},{4,6},{5,7},{6,4},{7,5},{8,10},{9,11},{10,... | collective-permute-start | bytes 21233672 | tf_op jit(solution)/shard_map/ppermute | solution.py:183
  275.6 31.1 %collective-permute-start.15 = (bf16[192,4352]{1,0:T(8,128)(2,1)S(1)}, bf16[192,4352]{1,0:T(8,128)(2,1)}, u32[]{:S(2)}, u32[]{:S(2)}) collective-permute-start(bf16[192,4352]{1,0:T(8,128)(2,1)S(1)} %pad_maximum_fusion.32), channel_id=1, source_target_pairs={{0,1},{1,0},{2,6},{3,7},{4,5},{5,4},{6,2},{7,3},{8,9},{9,8},{10,14... | collective-permute-start | bytes 5013512 | tf_op jit(solution)/shard_map/ppermute | solution.py:183
  311.9 32.9 %collective-permute-start.16 = (bf16[384,4352]{1,0:T(8,128)(2,1)}, bf16[384,4352]{1,0:T(8,128)(2,1)S(1)}, u32[]{:S(2)}, u32[]{:S(2)}) collective-permute-start(bf16[384,4352]{1,0:T(8,128)(2,1)} %constant_dynamic-update-slice_fusion), channel_id=1, source_target_pairs={{0,2},{1,3},{2,0},{3,1},{4,6},{5,7},{6,4},{7,5},{8,10},{9,11},{10,... | collective-permute-start | bytes 10027016 | tf_op jit(solution)/shard_map/ppermute | solution.py:183
  335.8 57.9 %collective-permute-start.25 = (bf16[192,3840]{1,0:T(8,128)(2,1)}, bf16[192,3840]{1,0:T(8,128)(2,1)}, u32[]{:S(2)}, u32[]{:S(2)}) collective-permute-start(bf16[192,3840]{1,0:T(8,128)(2,1)} %pad_maximum_fusion.38), channel_id=1, source_target_pairs={{0,1},{1,0},{2,6},{3,7},{4,5},{5,4},{6,2},{7,3},{8,9},{9,8},{10,14... | collective-permute-start | bytes 4423688 | tf_op jit(solution)/shard_map/ppermute | solution.py:183
  337.4 147.5 %collective-permute-start.21 = (bf16[384,6144]{1,0:T(8,128)(2,1)}, bf16[384,6144]{1,0:T(8,128)(2,1)}, u32[]{:S(2)}, u32[]{:S(2)}) collective-permute-start(bf16[384,6144]{1,0:T(8,128)(2,1)} %constant_dynamic-update-slice_fusion.2), channel_id=1, source_target_pairs={{0,2},{1,3},{2,0},{3,1},{4,6},{5,7},{6,4},{7,5},{8,10},{9,11},{10,... | collective-permute-start | bytes 14155784 | tf_op jit(solution)/shard_map/ppermute | solution.py:183
  396.4 79.0 %collective-permute-start.26 = (bf16[384,3840]{1,0:T(8,128)(2,1)}, bf16[384,3840]{1,0:T(8,128)(2,1)}, u32[]{:S(2)}, u32[]{:S(2)}) collective-permute-start(bf16[384,3840]{1,0:T(8,128)(2,1)} %constant_dynamic-update-slice_fusion.4), channel_id=1, source_target_pairs={{0,2},{1,3},{2,0},{3,1},{4,6},{5,7},{6,4},{7,5},{8,10},{9,11},{10,... | collective-permute-start | bytes 8847368 | tf_op jit(solution)/shard_map/ppermute | solution.py:183
  399.7 67.4 %collective-permute-start.30 = (bf16[192,6144]{1,0:T(8,128)(2,1)}, bf16[192,6144]{1,0:T(8,128)(2,1)}, u32[]{:S(2)}, u32[]{:S(2)}) collective-permute-start(bf16[192,6144]{1,0:T(8,128)(2,1)} %pad_maximum_fusion.25), channel_id=1, source_target_pairs={{0,1},{1,0},{2,6},{3,7},{4,5},{5,4},{6,2},{7,3},{8,9},{9,8},{10,14... | collective-permute-start | bytes 7077896 | tf_op jit(solution)/shard_map/ppermute | solution.py:183
  470.4 62.0 %collective-permute-start.31 = (bf16[384,6144]{1,0:T(8,128)(2,1)}, bf16[384,6144]{1,0:T(8,128)(2,1)}, u32[]{:S(2)}, u32[]{:S(2)}) collective-permute-start(bf16[384,6144]{1,0:T(8,128)(2,1)} %constant_dynamic-update-slice_fusion.6), channel_id=1, source_target_pairs={{0,2},{1,3},{2,0},{3,1},{4,6},{5,7},{6,4},{7,5},{8,10},{9,11},{10,... | collective-permute-start | bytes 14155784 | tf_op jit(solution)/shard_map/ppermute | solution.py:183
  755.1 58.7 %collective-permute-start.55 = (f32[384,3072]{1,0:T(8,128)}, f32[384,3072]{1,0:T(8,128)}, u32[]{:S(2)}, u32[]{:S(2)}) collective-permute-start(f32[384,3072]{1,0:T(8,128)} %fusion.187), channel_id=1, source_target_pairs={{0,2},{1,3},{2,0},{3,1},{4,6},{5,7},{6,4},{7,5},{8,10},{9,11},{10,... | collective-permute-start | bytes 14155784 | tf_op jit(solution)/shard_map/ppermute | solution.py:183
  755.6 46.4 %collective-permute-start.48 = (f32[384,2304]{1,0:T(8,128)}, f32[384,2304]{1,0:T(8,128)}, u32[]{:S(2)}, u32[]{:S(2)}) collective-permute-start(f32[384,2304]{1,0:T(8,128)} %fusion.199), channel_id=1, source_target_pairs={{0,2},{1,3},{2,0},{3,1},{4,6},{5,7},{6,4},{7,5},{8,10},{9,11},{10,... | collective-permute-start | bytes 10616840 | tf_op jit(solution)/shard_map/ppermute | solution.py:183
  776.0 31.7 %collective-permute-start.42 = (f32[384,2304]{1,0:T(8,128)}, f32[384,2304]{1,0:T(8,128)}, u32[]{:S(2)}, u32[]{:S(2)}) collective-permute-start(f32[384,2304]{1,0:T(8,128)} %fusion.207), channel_id=1, source_target_pairs={{0,2},{1,3},{2,0},{3,1},{4,6},{5,7},{6,4},{7,5},{8,10},{9,11},{10,... | collective-permute-start | bytes 10616840 | tf_op jit(solution)/shard_map/ppermute | solution.py:183
  789.2 30.4 %collective-permute-start.54 = (f32[384,3072]{1,0:T(8,128)}, f32[384,3072]{1,0:T(8,128)}, u32[]{:S(2)}, u32[]{:S(2)}) collective-permute-start(f32[384,3072]{1,0:T(8,128)} %fusion.191), channel_id=1, source_target_pairs={{0,2},{1,3},{2,0},{3,1},{4,6},{5,7},{6,4},{7,5},{8,10},{9,11},{10,... | collective-permute-start | bytes 14155784 | tf_op jit(solution)/shard_map/ppermute | solution.py:183
  802.0 38.6 %collective-permute-start.60 = (f32[384,3072]{1,0:T(8,128)}, f32[384,3072]{1,0:T(8,128)S(1)}, u32[]{:S(2)}, u32[]{:S(2)}) collective-permute-start(f32[384,3072]{1,0:T(8,128)} %fusion.183), channel_id=1, source_target_pairs={{0,2},{1,3},{2,0},{3,1},{4,6},{5,7},{6,4},{7,5},{8,10},{9,11},{10,... | collective-permute-start | bytes 14155784 | tf_op jit(solution)/shard_map/ppermute | solution.py:183
  813.8 67.3 %collective-permute-start.44 = (f32[192,3840]{1,0:T(8,128)S(1)}, f32[192,3840]{1,0:T(8,128)}, u32[]{:S(2)}, u32[]{:S(2)}) collective-permute-start(f32[192,3840]{1,0:T(8,128)S(1)} %pad_maximum_fusion.20), channel_id=1, source_target_pairs={{0,1},{1,0},{2,6},{3,7},{4,5},{5,4},{6,2},{7,3},{8,9},{9,8},{10,14... | collective-permute-start | bytes 8847368 | tf_op jit(solution)/shard_map/ppermute | solution.py:183
  826.8 120.7 %collective-permute-start.56 = (f32[192,6144]{1,0:T(8,128)}, f32[192,6144]{1,0:T(8,128)}, u32[]{:S(2)}, u32[]{:S(2)}) collective-permute-start(f32[192,6144]{1,0:T(8,128)} %pad_maximum_fusion.4), channel_id=1, source_target_pairs={{0,1},{1,0},{2,6},{3,7},{4,5},{5,4},{6,2},{7,3},{8,9},{9,8},{10,14... | collective-permute-start | bytes 14155784 | tf_op jit(solution)/shard_map/ppermute | solution.py:183
  838.9 46.2 %collective-permute-start.51 = (f32[96,3072]{1,0:T(8,128)S(1)}, f32[96,3072]{1,0:T(8,128)S(1)}, u32[]{:S(2)}, u32[]{:S(2)}) collective-permute-start(f32[96,3072]{1,0:T(8,128)S(1)} %get-tuple-element.265), channel_id=1, source_target_pairs={{0,4},{1,5},{2,3},{3,2},{4,0},{5,1},{6,7},{7,6},{8,12},{9,13},{10,... | collective-permute-start | bytes 3538952 | tf_op jit(solution)/shard_map/ppermute | solution.py:183
  883.3 35.3 %collective-permute-start.45 = (f32[96,3840]{1,0:T(8,128)S(1)}, f32[96,3840]{1,0:T(8,128)S(1)}, u32[]{:S(2)}, u32[]{:S(2)}) collective-permute-start(f32[96,3840]{1,0:T(8,128)S(1)} %get-tuple-element.259), channel_id=1, source_target_pairs={{0,4},{1,5},{2,3},{3,2},{4,0},{5,1},{6,7},{7,6},{8,12},{9,13},{10,... | collective-permute-start | bytes 4423688 | tf_op jit(solution)/shard_map/ppermute | solution.py:183
  887.8 135.5 %collective-permute-start.62 = (f32[192,6144]{1,0:T(8,128)}, f32[192,6144]{1,0:T(8,128)}, u32[]{:S(2)}, u32[]{:S(2)}) collective-permute-start(f32[192,6144]{1,0:T(8,128)} %pad_maximum_fusion.5), channel_id=1, source_target_pairs={{0,1},{1,0},{2,6},{3,7},{4,5},{5,4},{6,2},{7,3},{8,9},{9,8},{10,14... | collective-permute-start | bytes 14155784 | tf_op jit(solution)/shard_map/ppermute | solution.py:183
  937.0 91.1 %collective-permute-start.47 = (f32[24,3840]{1,0:T(8,128)S(1)}, f32[24,3840]{1,0:T(8,128)S(1)}, u32[]{:S(2)}, u32[]{:S(2)}) collective-permute-start(f32[24,3840]{1,0:T(8,128)S(1)} %slice_add_fusion.41), channel_id=1, source_target_pairs={{0,16},{1,17},{2,18},{3,19},{4,20},{5,21},{6,22},{7,23},{8,24},{9,... | collective-permute-start | bytes 1105928 | tf_op jit(solution)/shard_map/ppermute | solution.py:183
  951.9 77.7 %collective-permute-start.57 = (f32[96,6144]{1,0:T(8,128)S(1)}, f32[96,6144]{1,0:T(8,128)S(1)}, u32[]{:S(2)}, u32[]{:S(2)}) collective-permute-start(f32[96,6144]{1,0:T(8,128)S(1)} %get-tuple-element.239), channel_id=1, source_target_pairs={{0,4},{1,5},{2,3},{3,2},{4,0},{5,1},{6,7},{7,6},{8,12},{9,13},{10,... | collective-permute-start | bytes 7077896 | tf_op jit(solution)/shard_map/ppermute | solution.py:183
  1055.5 39.5 %collective-permute-start.64 = (f32[48,6144]{1,0:T(8,128)S(1)}, f32[48,6144]{1,0:T(8,128)S(1)}, u32[]{:S(2)}, u32[]{:S(2)}) collective-permute-start(f32[48,6144]{1,0:T(8,128)S(1)} %get-tuple-element.263), channel_id=1, source_target_pairs={{0,8},{1,9},{2,10},{3,11},{4,12},{5,13},{6,14},{7,15},{8,0},{9,1},... | collective-permute-start | bytes 3538952 | tf_op jit(solution)/shard_map/ppermute | solution.py:183
  1057.5 37.8 %collective-permute-start.59 = (f32[24,6144]{1,0:T(8,128)S(1)}, f32[24,6144]{1,0:T(8,128)S(1)}, u32[]{:S(2)}, u32[]{:S(2)}) collective-permute-start(f32[24,6144]{1,0:T(8,128)S(1)} %slice_add_fusion.31), channel_id=1, source_target_pairs={{0,16},{1,17},{2,18},{3,19},{4,20},{5,21},{6,22},{7,23},{8,24},{9,... | collective-permute-start | bytes 1769480 | tf_op jit(solution)/shard_map/ppermute | solution.py:183
  (211 other events, 2356.6 us)

commit v2 on v1

--- a/solution.py
+++ b/solution.py
@@ -212,40 +212,70 @@
     return contract(values, mover, 1, 1).astype(half_type)
 
 
-def gather_chunks(plan, chunks):
-    done = []
-    last = [None] * len(plan.stages)
-    for parts in chunks:
-        value = jnp.concatenate(parts, axis=1)
-        for step, perm in enumerate(plan.stages):
-            if last[step] is not None:
-                value, _ = lax.optimization_barrier((value, last[step]))
-            got = plan.swap(value, perm)
-            last[step] = got
-            value = jnp.concatenate([value, got], axis=0)
-        got = plan.swap(value, plan.core_stage)
-        outs = []
-        start = 0
-        for part in parts:
-            stop = start + part.shape[1]
-            outs.append(jnp.concatenate([value[:, start:stop], got[:, start:stop]], axis=0))
-            start = stop
-        done.append(outs)
-    return done
-
-
-def scatter_chunk(plan, pieces):
-    gots = [plan.swap(far, plan.core_stage) for _, far in pieces]
+class Pump:
+    def __init__(self, plan):
+        self.plan = plan
+        self.jobs = []
+        self.flying = []
+
+    def add(self, steps, done):
+        self.jobs.append([steps, next(steps), done])
+
+    def begin(self):
+        self.flying = [
+            [self.plan.swap(value, perm) for value, perm in sends] for _, sends, _ in self.jobs
+        ]
+
+    def end(self, values=()):
+        flying, values = lax.optimization_barrier((self.flying, values))
+        left = []
+        for (steps, _, done), gots in zip(self.jobs, flying):
+            try:
+                left.append([steps, steps.send(gots), done])
+            except StopIteration as stop:
+                done(stop.value)
+        self.jobs = left
+        self.flying = []
+        return values
+
+    def drain(self):
+        while self.jobs:
+            self.begin()
+            self.end()
+
+
+def gather_steps(plan, parts):
+    value = jnp.concatenate(parts, axis=1)
+    for perm in plan.stages:
+        (got,) = yield [(value, perm)]
+        value = jnp.concatenate([value, got], axis=0)
+    (got,) = yield [(value, plan.core_stage)]
+    outs = []
+    start = 0
+    for part in parts:
+        stop = start + part.shape[1]
+        outs.append(jnp.concatenate([value[:, start:stop], got[:, start:stop]], axis=0))
+        start = stop
+    return outs
+
+
+def scatter_steps(plan, pieces):
+    gots = yield [(far, plan.core_stage) for _, far in pieces]
     quarter = pieces[0][0].shape[0] // 2
     send = jnp.concatenate(
-        [near[quarter:] + got[quarter:] for (near, _), got in zip(pieces, gots)], axis=1
+        [
+            (near[quarter:] + got[quarter:]).astype(half_type)
+            for (near, _), got in zip(pieces, gots)
+        ],
+        axis=1,
     )
     keep = jnp.concatenate(
         [near[:quarter] + got[:quarter] for (near, _), got in zip(pieces, gots)], axis=1
     )
     stages = plan.stages[::-1]
     for step, perm in enumerate(stages):
-        got = plan.swap(send, perm)
+        (got,) = yield [(send, perm)]
+        got = got.astype(full_type)
         if step == len(stages) - 1:
             return keep + got
         half = keep.shape[0] // 2
@@ -263,73 +293,22 @@
     return value[:half], value[half:]
 
 
-def layer_forward(flat_in, seqs, weights, gain_one, gain_two):
-    w_qkv, w_out, w_up, w_down = weights
+def attend_forward(flat_in, seqs, w_qkv, w_out, gain):
     tokens = flat_in.shape[0] // seqs
-    normed_one, unit_one, scale_one = normalize(flat_in, gain_one)
-    projected = contract(normed_one, w_qkv, 1, 0).astype(half_type)
+    normed, unit, scale = normalize(flat_in, gain)
+    projected = contract(normed, w_qkv, 1, 0).astype(half_type)
     projected = projected.reshape(seqs, tokens, projected.shape[1])
     mixed = attend(projected).reshape(flat_in.shape)
     middle = flat_in + contract(mixed, w_out, 1, 0)
-    normed_two, unit_two, scale_two = normalize(middle, gain_two)
-    hidden_up = contract(normed_two, w_up, 1, 0)
+    return middle, (unit, scale, normed, projected, mixed)
+
+
+def mlp_forward(middle, w_up, w_down, gain):
+    normed, unit, scale = normalize(middle, gain)
+    hidden_up = contract(normed, w_up, 1, 0)
     active = gelu_exact(hidden_up).astype(half_type)
     out = middle + contract(active, w_down, 1, 1)
-    saved = (
-        unit_one,
-        scale_one,
-        normed_one,
-        projected,
-        mixed,
-        unit_two,
-        scale_two,
-        normed_two,
-        hidden_up,
-        active,
-    )
-    return out, saved
-
-
-def layer_backward(grad_out, saved, weights, gain_one, gain_two, mover):
-    (
-        unit_one,
-        scale_one,
-        normed_one,
-        projected,
-        mixed,
-        unit_two,
-        scale_two,
-        normed_two,
-        hidden_up,
-        active,
-    ) = saved
-    w_qkv, w_out, w_up, w_down = weights
-    grad_down = grad_out.astype(half_type)
-    grad_active = contract(grad_down, w_down, 1, 0)
-    grad_hidden = (grad_active * gelu_slope(hidden_up)).astype(half_type)
-    mlp_pieces = [halves(normed_two, grad_hidden), halves(grad_down, active)]
-    grad_norm_two = contract(grad_hidden, w_up, 1, 1)
-    grad_middle, grad_gain_two = normalize_back(grad_norm_two, gain_two, unit_two, scale_two)
-    grad_middle = grad_out + grad_middle
-    grad_branch = grad_middle.astype(half_type)
-    out_piece = halves(to_relative(mixed, mover), to_whole(grad_branch, mover))
-    grad_mixed = contract(grad_branch, w_out, 1, 1).astype(half_type)
-    grad_q, grad_k, grad_v = attend_back(
-        projected, grad_mixed.reshape(projected.shape[0], projected.shape[1], -1)
-    )
-    grad_proj = jnp.concatenate([grad_q, grad_k, grad_v], axis=2).reshape(
-        grad_out.shape[0], projected.shape[2]
-    )
-    qkv_piece = halves(normed_one, grad_proj)
-    grad_norm_one = contract(grad_proj, w_qkv, 1, 1)
-    grad_in, grad_gain_one = normalize_back(grad_norm_one, gain_one, unit_one, scale_one)
-    return (
-        grad_middle + grad_in,
-        [qkv_piece, out_piece],
-        mlp_pieces,
-        grad_gain_one,
-        grad_gain_two,
-    )
+    return out, (unit, scale, normed, hidden_up, active)
 
 
 def adam_step(weight, first_mom, second_mom, teacher, gradient):
@@ -408,57 +387,90 @@
         s_attn[1] + [s_head],
         s_mlp[1],
     ]
-    gathered = gather_chunks(plan, chunks)
-    t_first, t_mlp0, t_second, s_first, s_mlp0, s_second, s_mlp1 = gathered
-
     mover = plan.mover(width)
     patch_rel = to_relative(flat_patch, mover)
 
     def both_sides(w_out):
         return contract(mover, to_relative(w_out, mover), 1, 0).astype(half_type)
 
-    def ready(first, mlp0, attn1, mlp1):
-        patch, small, qkv0, out0 = first
-        qkv1, out1 = attn1
+    def spread(table):
+        return jnp.broadcast_to(table[None], (seqs, tokens, width)).reshape(-1, width)
+
+    def small_parts(small):
         vec_table = small[:, tokens:small_cols].astype(full_type).T
         posit = small[:, :tokens].astype(full_type).T
-        layers = [
-            (qkv0, both_sides(out0), mlp0[0], mlp0[1]),
-            (qkv1, both_sides(out1), mlp1[0], mlp1[1]),
-        ]
-        return to_relative(patch, mover), posit, vec_table, layers
-
-    t_embed, t_posit, t_vecs, t_layers = ready(t_first, t_mlp0, t_second[:2], t_second[2:])
-    s_embed, s_posit, s_vecs, s_layers = ready(s_first, s_mlp0, s_second[:2], s_mlp1)
-    head_rel = to_relative(s_second[2], mover)
-
-    def spread(table):
-        return jnp.broadcast_to(table[None], (seqs, tokens, width)).reshape(-1, width)
-
-    state = contract(patch_rel, t_embed, 1, 0) + spread(t_posit)
-    target = None
-    for layer in range(LAYERS):
-        state, _ = layer_forward(
-            state, seqs, t_layers[layer], t_vecs[layer], t_vecs[LAYERS + layer]
-        )
-        if layer >= LAYERS - TOPK:
-            by_seq = state.reshape(seqs, tokens, width)
-            centred = by_seq - jnp.mean(by_seq, axis=1, keepdims=True)
-            variance = jnp.mean(centred * centred, axis=1, keepdims=True)
-            term = centred * lax.rsqrt(variance + in_eps)
-            target = term if target is None else target + term
-    target = (target / TOPK).reshape(-1, width)
-
-    embedded = contract(patch_rel, s_embed, 1, 0)
-    current = (
-        embedded * (1.0 - mask_flat) + mask_flat * s_vecs[2 * LAYERS + 1] + spread(s_posit)
-    )
-    kept = []
-    for layer in range(LAYERS):
-        current, saved = layer_forward(
-            current, seqs, s_layers[layer], s_vecs[layer], s_vecs[LAYERS + layer]
-        )
-        kept.append(saved)
+        return vec_table, spread(posit)
+
+    def target_term(state):
+        by_seq = state.reshape(seqs, tokens, width)
+        centred = by_seq - jnp.mean(by_seq, axis=1, keepdims=True)
+        variance = jnp.mean(centred * centred, axis=1, keepdims=True)
+        return (centred * lax.rsqrt(variance + in_eps)).reshape(-1, width)
+
+    pump = Pump(plan)
+    arrived = []
+    saved_attn = [None] * LAYERS
+    saved_mlp = [None] * LAYERS
+    s_layers = [None] * LAYERS
+
+    def segment_t0(_, chunk):
+        patch, small, w_qkv, w_out = chunk
+        vec_table, posit = small_parts(small)
+        state = contract(patch_rel, to_relative(patch, mover), 1, 0) + posit
+        middle, _ = attend_forward(state, seqs, w_qkv, both_sides(w_out), vec_table[0])
+        return middle, vec_table
+
+    def segment_t1(values, chunk):
+        middle, vec_table = values
+        state, _ = mlp_forward(middle, chunk[0], chunk[1], vec_table[LAYERS])
+        return state, vec_table
+
+    def segment_t2(values, chunk):
+        state, vec_table = values
+        w_qkv, w_out, w_up, w_down = chunk
+        target = target_term(state)
+        middle, _ = attend_forward(state, seqs, w_qkv, both_sides(w_out), vec_table[1])
+        state, _ = mlp_forward(middle, w_up, w_down, vec_table[LAYERS + 1])
+        return (target + target_term(state)) / TOPK
+
+    def segment_s0(target, chunk):
+        patch, small, w_qkv, w_out = chunk
+        vec_table, posit = small_parts(small)
+        embedded = contract(patch_rel, to_relative(patch, mover), 1, 0)
+        current = embedded * (1.0 - mask_flat) + mask_flat * vec_table[2 * LAYERS + 1] + posit
+        w_out = both_sides(w_out)
+        middle, saved = attend_forward(current, seqs, w_qkv, w_out, vec_table[0])
+        return target, middle, vec_table, (w_qkv, w_out), saved
+
+    def segment_s1(values, chunk):
+        target, middle, vec_table, weights, saved = values
+        saved_attn[0] = (weights, saved)
+        current, saved = mlp_forward(middle, chunk[0], chunk[1], vec_table[LAYERS])
+        return target, current, vec_table, tuple(chunk), saved
+
+    def segment_s2(values, chunk):
+        target, current, vec_table, weights, saved = values
+        saved_mlp[0] = (weights, saved)
+        w_qkv, w_out, head = chunk
+        w_out = both_sides(w_out)
+        middle, saved = attend_forward(current, seqs, w_qkv, w_out, vec_table[1])
+        saved_attn[1] = ((w_qkv, w_out), saved)
+        return target, middle, vec_table, to_relative(head, mover)
+
+    segments = [segment_t0, segment_t1, segment_t2, segment_s0, segment_s1, segment_s2]
+    values = ()
+    for tick in range(len(chunks) + len(plan.stages)):
+        if tick < len(chunks):
+            pump.add(gather_steps(plan, chunks[tick]), arrived.append)
+        pump.begin()
+        place = tick - len(plan.stages) - 1
+        if place >= 0:
+            values = segments[place](values, arrived[place])
+        values = pump.end(values)
+    target, middle, s_vecs, head_rel = values
+    current, saved = mlp_forward(middle, arrived[-1][0], arrived[-1][1], s_vecs[LAYERS + 1])
+    saved_mlp[1] = (tuple(arrived[-1]), saved)
+
     final_normed, final_unit, final_scale = normalize(current, s_vecs[2 * LAYERS])
     predicted = contract(final_normed, head_rel, 1, 0)
     differ = predicted - target
@@ -470,44 +482,80 @@
     grad_pred = (mask_flat * jnp.clip(differ / huber_beta, -1.0, 1.0) / total_masked).astype(
         half_type
     )
-    head_piece = halves(final_normed, to_whole(grad_pred, mover))
     grad_flow, grad_gain_final = normalize_back(
         contract(grad_pred, head_rel, 1, 1), s_vecs[2 * LAYERS], final_unit, final_scale
     )
+    head_piece = halves(final_normed, to_whole(grad_pred, mover))
+
     gain_ones = [None] * LAYERS
     gain_twos = [None] * LAYERS
     attn_shards = [None] * LAYERS
     mlp_shards = [None] * LAYERS
-    head_shard = None
+    extra_pieces = [head_piece]
     for layer in reversed(range(LAYERS)):
-        grad_flow, attn_pieces, mlp_pieces, gain_ones[layer], gain_twos[layer] = layer_backward(
-            grad_flow,
-            kept[layer],
-            s_layers[layer],
-            s_vecs[layer],
-            s_vecs[LAYERS + layer],
-            mover,
+        (w_qkv, w_out), (unit_one, scale_one, normed_one, projected, mixed) = saved_attn[layer]
+        (w_up, w_down), (unit_two, scale_two, normed_two, hidden_up, active) = saved_mlp[layer]
+        pump.begin()
+        grad_down = grad_flow.astype(half_type)
+        grad_active = contract(grad_down, w_down, 1, 0)
+        grad_hidden = (grad_active * gelu_slope(hidden_up)).astype(half_type)
+        pieces = [halves(normed_two, grad_hidden), halves(grad_down, active)] + extra_pieces
+        grad_flow, grad_hidden, pieces = pump.end((grad_flow, grad_hidden, pieces))
+        pump.add(
+            scatter_steps(plan, pieces), lambda out, layer=layer: mlp_shards.__setitem__(layer, out)
         )
-        mlp_shards[layer] = scatter_chunk(plan, mlp_pieces)
-        if head_shard is None:
-            summed = scatter_chunk(plan, [head_piece] + attn_pieces)
-            head_shard = summed[:, :width]
-            attn_shards[layer] = summed[:, width:]
-        else:
-            attn_shards[layer] = scatter_chunk(plan, attn_pieces)
+        extra_pieces = []
+        pump.begin()
+        grad_norm_two = contract(grad_hidden, w_up, 1, 1)
+        grad_middle, gain_twos[layer] = normalize_back(
+            grad_norm_two, s_vecs[LAYERS + layer], unit_two, scale_two
+        )
+        grad_middle = grad_flow + grad_middle
+        grad_branch = grad_middle.astype(half_type)
+        grad_mixed = contract(grad_branch, w_out, 1, 1).astype(half_type)
+        out_piece = halves(to_relative(mixed, mover), to_whole(grad_branch, mover))
+        grad_middle, grad_mixed, out_piece = pump.end((grad_middle, grad_mixed, out_piece))
+        pump.begin()
+        grad_proj = attend_back(
+            projected, grad_mixed.reshape(projected.shape[0], projected.shape[1], -1)
+        )
+        grad_proj = pump.end(tuple(grad_proj))
+        pump.begin()
+        grad_proj = jnp.concatenate(grad_proj, axis=2).reshape(
+            grad_flow.shape[0], projected.shape[2]
+        )
+        grad_norm_one = contract(grad_proj, w_qkv, 1, 1)
+        grad_in, gain_ones[layer] = normalize_back(
+            grad_norm_one, s_vecs[layer], unit_one, scale_one
+        )
+        grad_flow = grad_middle + grad_in
+        pieces = [halves(normed_one, grad_proj), out_piece]
+        if layer:
+            grad_flow, pieces = pump.end((grad_flow, pieces))
+            pump.add(
+                scatter_steps(plan, pieces),
+                lambda out, layer=layer: attn_shards.__setitem__(layer, out),
+            )
     grad_maskvec = jnp.sum(grad_flow * mask_flat, axis=0)
     grad_posit = jnp.sum(grad_flow.reshape(seqs, tokens, width), axis=0).T
     grad_embed = to_whole((grad_flow * (1.0 - mask_flat)).astype(half_type), mover)
     patch_piece = halves(patch_rel, grad_embed)
     vec_grads = jnp.stack(gain_ones + gain_twos + [grad_gain_final, grad_maskvec], axis=1)
     small_grads = pad_lanes(jnp.concatenate([grad_posit, vec_grads], axis=1))
-    summed = scatter_chunk(plan, [patch_piece, row_halves(small_grads)])
+    pieces = pump.end(pieces + [patch_piece, row_halves(small_grads)])
+    last = []
+    pump.add(scatter_steps(plan, pieces), last.append)
+    pump.drain()
+    attn_shards[0], patch_shard, small_shard = jnp.split(
+        last[0], [4 * width, 5 * width], axis=1
+    )
+    mlp_shards[-1], head_shard = jnp.split(mlp_shards[-1], [2 * ff_width], axis=1)
     raw = (
-        jnp.concatenate([summed[:, :width], head_shard], axis=1),
+        jnp.concatenate([patch_shard, head_shard], axis=1),
         jnp.concatenate(attn_shards, axis=1),
         jnp.concatenate(mlp_shards, axis=1),
-        summed[:, width : width + tokens],
-        summed[:, width + tokens : width + small_cols],
+        small_shard[:, :tokens],
+        small_shard[:, tokens:small_cols],
     )
     totals = jnp.stack([loss_local] + [jnp.sum(part * part) for part in raw])
     totals = jnp.broadcast_to(totals[:, None], (totals.shape[0], LANES))

time: 1180 us -> 1180 us (level)
  waiting for transfers between devices: 440 us -> 271 us
  local copies, waits for them, and re-layouts: 148 us -> 261 us
  other arithmetic: 130 us -> 201 us
    ppermute x71 -> x67, waiting for transfers between devices: 440 us -> 271 us  [swap(): return lax.ppermute(value, AXES, perm)]
    concatenate x33 -> x32, other arithmetic: 27.7 us -> 62.7 us  [the longest x21 34.3 us: gather_steps(): value = jnp.concatenate([value, got], axis=0)]
    unnamed x365 -> x329, local copies, waits for them, and re-layouts: 47.4 us -> 73.1 us
    optimization_barrier x0 -> x9, local copies, waits for them, and re-layouts: none -> 25 us  [end(): flying, values = lax.optimization_barrier((self.flying, values))]
    add x33 -> x30, other arithmetic: 52.6 us -> 68.6 us  [the longest x11 29.4 us: scatter_steps(): near[:quarter] + got[:quarter]]
    add x3 -> x5, local copies, waits for them, and re-layouts: 0.63 us -> 14.8 us  [the longest x3 8.05 us: scatter_steps(): send = keep[half:] + got[half:]]
    slice x39 -> x38, local copies, waits for them, and re-layouts: 69.5 us -> 77.8 us  [the longest x14 39.4 us: gather_steps(): value[:, start:stop]]
    dot_general x59 -> x58, matrix products: 265 us -> 261 us  [contract(): lax.dot_general(left, right, (((left_dim,), (right_dim,)), ((), ())), pre...]
  transfers between devices with their start and end apart: 71 -> 67, of which waited for: 34 -> 24; matrix products, arithmetic and copies ran while one was open for 30% -> 41% of each run, Pallas kernels for 6% -> 10%
where the time goes in v2:
time: 1180 us; the launch traced here: 1170 us
  waiting for transfers between devices  271 us (23%)
  local copies, waits for them, and re-layouts  261 us (22%)
  matrix products  261 us (22%)
  other arithmetic  201 us (17%)
  Pallas kernels  117 us (10%)
  starting transfers between devices  56.6 us (5%)
    ppermute x67, waiting for transfers between devices, swap(): return lax.ppermute(value, AXES, perm)  271 us
    dot_general x58, matrix products, contract(): lax.dot_general(left, right, (((left_dim,), (right_dim,)), ((), ())), pre...  261 us
    unnamed x329, local copies, waits for them, and re-layouts  73.1 us
    pallas_call x4, Pallas kernels, attend(): pl.pallas_call(attend_kernel, grid=(seqs, blocks), in_specs=qkv_specs(tok...  66.2 us
    ppermute x67, starting transfers between devices, swap(): return lax.ppermute(value, AXES, perm)  56.6 us
    pallas_call x2, Pallas kernels, attend_back(): pl.pallas_call(attend_back_kernel, grid=(seqs, blocks), in_specs=qkv_spec...  50.5 us
    slice x14, local copies, waits for them, and re-layouts, gather_steps(): value[:, start:stop]  39.4 us
    concatenate x21, other arithmetic, gather_steps(): value = jnp.concatenate([value, got], axis=0)  34.3 us
  transfers between devices with their start and end apart: 67, of which 24 were waited for; matrix products, arithmetic and copies ran while one was open for 41% of the time, Pallas kernels for 10%

profile of v2, /device:TPU:0, one launch (start us, length us, event | category | flops | bytes accessed | tf_op | source)
XLA Modules:
  0.0 1174.1 jit_solution(17092272479142298756)
XLA Ops:
  28.6 18.2 %collective-permute-done = bf16[24,4352]{1,0:T(8,128)(2,1)} collective-permute-done((bf16[24,4352]{1,0:T(8,128)(2,1)}, bf16[24,4352]{1,0:T(8,128)(2,1)}, u32[]{:S(2)}, u32[]{:S(2)}) %collective-permute-start) | collective-permute-done | bytes 208928 | tf_op jit(solution)/shard_map/ppermute | solution.py:183
  53.1 28.3 %collective-permute-done.1 = bf16[48,4352]{1,0:T(8,128)(2,1)S(1)} collective-permute-done((bf16[48,4352]{1,0:T(8,128)(2,1)S(1)}, bf16[48,4352]{1,0:T(8,128)(2,1)S(1)}, u32[]{:S(2)}, u32[]{:S(2)}) %collective-permute-start.1) | collective-permute-done | bytes 417824 | tf_op jit(solution)/shard_map/ppermute | solution.py:183
  85.9 14.2 %collective-permute-done.4 = bf16[48,6144]{1,0:T(8,128)(2,1)S(1)} collective-permute-done((bf16[48,6144]{1,0:T(8,128)(2,1)S(1)}, bf16[48,6144]{1,0:T(8,128)(2,1)S(1)}, u32[]{:S(2)}, u32[]{:S(2)}) %collective-permute-start.4) | collective-permute-done | bytes 589856 | tf_op jit(solution)/shard_map/ppermute | solution.py:183
  106.4 19.5 %collective-permute-done.8 = bf16[48,9216]{1,0:T(8,128)(2,1)S(1)} collective-permute-done((bf16[48,9216]{1,0:T(8,128)(2,1)S(1)}, bf16[48,9216]{1,0:T(8,128)(2,1)S(1)}, u32[]{:S(2)}, u32[]{:S(2)}) %collective-permute-start.8) | collective-permute-done | bytes 884768 | tf_op jit(solution)/shard_map/ppermute | solution.py:183
  126.0 6.6 collective-permute-done.7
  154.1 25.7 %collective-permute-done.12 = bf16[96,9216]{1,0:T(8,128)(2,1)S(1)} collective-permute-done((bf16[96,9216]{1,0:T(8,128)(2,1)S(1)}, bf16[96,9216]{1,0:T(8,128)(2,1)S(1)}, u32[]{:S(2)}, u32[]{:S(2)}) %collective-permute-start.12) | collective-permute-done | bytes 1769504 | tf_op jit(solution)/shard_map/ppermute | solution.py:183
  203.8 6.0 fusion.306
  218.7 16.5 %attend.4 = bf16[2,448,768]{2,1,0:T(8,128)(2,1)} custom-call(bf16[2,448,2304]{2,1,0:T(8,128)(2,1)} %bitcast.138, bf16[2,448,2304]{2,1,0:T(8,128)(2,1)} %bitcast.139, bf16[2,448,2304]{2,1,0:T(8,128)(2,1)} %bitcast.140), custom_call_target="tpu_custom_call" | custom-call | flops 4932501504 | bytes 5505024 | tf_op jit(solution)/shard_map/attend/pallas_call | solution.py:102
  277.2 15.6 %fusion.77 = f32[896,768]{0,1:T(8,128)S(1)} fusion(f32[896,768]{0,1:T(8,128)} %copy-done.5, bf16[384,3072]{1,0:T(8,128)(2,1)} %get-tuple-element.486, bf16[384,3072]{1,0:T(8,128)(2,1)} %get-tuple-element.484, bf16[384,3072]{1,0:T(8,128)(2,1)} %get-tuple-element.485, bf16[384,3072]{1,0:T(8,128)(2,1)} %get-tuple-element.483, ...), kind=kOutput, calls=%fused_computation.183 | convolution fusion | flops 8491794432 | bytes 14952448 | tf_op jit(solution)/shard_map/dot_general | solution.py:30
  338.4 16.7 %attend.5 = bf16[2,448,768]{2,1,0:T(8,128)(2,1)} custom-call(bf16[2,448,2304]{2,1,0:T(8,128)(2,1)} %bitcast.141, bf16[2,448,2304]{2,1,0:T(8,128)(2,1)} %bitcast.142, bf16[2,448,2304]{2,1,0:T(8,128)(2,1)} %bitcast.143), custom_call_target="tpu_custom_call" | custom-call | flops 4932501504 | bytes 5505024 | tf_op jit(solution)/shard_map/attend/pallas_call | solution.py:102
  364.5 17.1 %fusion.72 = f32[896,768]{0,1:T(8,128)} fusion(f32[896,768]{0,1:T(8,128)} %copy-done.16, bf16[384,3072]{1,0:T(8,128)(2,1)} %get-tuple-element.468, bf16[384,3072]{1,0:T(8,128)(2,1)} %get-tuple-element.466, bf16[384,3072]{1,0:T(8,128)(2,1)} %get-tuple-element.467, bf16[384,3072]{1,0:T(8,128)(2,1)} %get-tuple-element.465, f32[768]{0:T(1024)S(1)} %get-tuple-element.416, ...), kind=kOutput, calls=%fused_computation.182 | convolution fusion | flops 8491794432 | bytes 14952448 | tf_op jit(solution)/shard_map/dot_general | solution.py:30
  417.7 6.7 add_multiply_fusion
  452.0 6.0 fusion.310
  469.6 16.6 %attend.6 = bf16[2,448,768]{2,1,0:T(8,128)(2,1)} custom-call(bf16[2,448,2304]{2,1,0:T(8,128)(2,1)} %bitcast.126, bf16[2,448,2304]{2,1,0:T(8,128)(2,1)} %bitcast.127, bf16[2,448,2304]{2,1,0:T(8,128)(2,1)} %bitcast.128), custom_call_target="tpu_custom_call" | custom-call | flops 4932501504 | bytes 5505024 | tf_op jit(solution)/shard_map/attend/pallas_call | solution.py:102
  516.3 7.8 multiply_convert_fusion.1
  560.8 8.0 convolution_convert_fusion
  568.8 16.3 %attend.7 = bf16[2,448,768]{2,1,0:T(8,128)(2,1)} custom-call(bf16[2,448,2304]{2,1,0:T(8,128)(2,1)} %bitcast.132, bf16[2,448,2304]{2,1,0:T(8,128)(2,1)} %bitcast.133, bf16[2,448,2304]{2,1,0:T(8,128)(2,1)} %bitcast.134), custom_call_target="tpu_custom_call" | custom-call | flops 4932501504 | bytes 5505024 | tf_op jit(solution)/shard_map/attend/pallas_call | solution.py:102
  605.7 7.9 multiply_convert_fusion
  625.6 11.8 %fusion.5 = bf16[896,3072]{1,0:T(8,128)(2,1)} fusion(f32[896,3072]{1,0:T(8,128)} %get-tuple-element.555, bf16[896,768]{0,1:T(8,128)(2,1)S(1)} %get-tuple-element.441, bf16[384,3072]{1,0:T(8,128)(2,1)S(1)} %get-tuple-element.477, bf16[384,3072]{1,0:T(8,128)(2,1)S(1)} %copy-done.74), kind=kOutput, calls=%fused_computation.7 | convolution fusion | flops 4264820736 | bytes 22609920 | tf_op jit(solution)/shard_map/dot_general | solution.py:30
  642.2 7.2 fusion.203
  664.4 9.2 multiply_reduce_fusion.2
  701.0 25.2 %attend_back.2 = (bf16[2,448,768]{2,1,0:T(8,128)(2,1)}, bf16[2,448,768]{2,1,0:T(8,128)(2,1)}, bf16[2,448,768]{2,1,0:T(8,128)(2,1)}) custom-call(bf16[2,448,2304]{2,1,0:T(8,128)(2,1)} %bitcast.135, bf16[2,448,2304]{2,1,0:T(8,128)(2,1)} %bitcast.136, bf16[2,448,2304]{2,1,0:T(8,128)(2,1)} %bitcast.137, bf16[2,448,768]{2,1,0:T(8,128)(2,1)} %bitcast.147), custom_call_target="tpu_custom_call" | custom-call | flops 9865003008 | bytes 9633792 | tf_op jit(solution)/shard_map/attend_back/pallas_call | solution.py:123
  747.6 16.2 %collective-permute-done.39 = f32[96,6912]{1,0:T(8,128)S(1)} collective-permute-done((f32[96,6912]{1,0:T(8,128)}, f32[96,6912]{1,0:T(8,128)S(1)}, u32[]{:S(2)}, u32[]{:S(2)}) %collective-permute-start.39) | collective-permute-done | bytes 2654240 | tf_op jit(solution)/shard_map/ppermute | solution.py:183
  766.5 10.1 fusion.11
  804.0 9.3 multiply_reduce_fusion.3
  837.6 25.4 %attend_back.3 = (bf16[2,448,768]{2,1,0:T(8,128)(2,1)}, bf16[2,448,768]{2,1,0:T(8,128)(2,1)}, bf16[2,448,768]{2,1,0:T(8,128)(2,1)}) custom-call(bf16[2,448,2304]{2,1,0:T(8,128)(2,1)} %bitcast.129, bf16[2,448,2304]{2,1,0:T(8,128)(2,1)} %bitcast.130, bf16[2,448,2304]{2,1,0:T(8,128)(2,1)} %bitcast.131, bf16[2,448,768]{2,1,0:T(8,128)(2,1)} %bitcast.146), custom_call_target="tpu_custom_call" | custom-call | flops 9865003008 | bytes 9633792 | tf_op jit(solution)/shard_map/attend_back/pallas_call | solution.py:123
  865.8 8.1 collective-permute-done.48
  939.5 25.4 %collective-permute-done.51 = f32[24,3072]{1,0:T(8,128)S(1)} collective-permute-done((f32[24,3072]{1,0:T(8,128)S(1)}, f32[24,3072]{1,0:T(8,128)S(1)}, u32[]{:S(2)}, u32[]{:S(2)}) %collective-permute-start.51) | collective-permute-done | bytes 294944 | tf_op jit(solution)/shard_map/ppermute | solution.py:183
  1001.3 21.8 %collective-permute-done.57 = f32[24,6144]{1,0:T(8,128)S(1)} collective-permute-done((f32[24,6144]{1,0:T(8,128)S(1)}, f32[24,6144]{1,0:T(8,128)S(1)}, u32[]{:S(2)}, u32[]{:S(2)}) %collective-permute-start.57) | collective-permute-done | bytes 589856 | tf_op jit(solution)/shard_map/ppermute | solution.py:183
  1034.9 20.3 %collective-permute-done.59 = f32[96,4352]{1,0:T(8,128)S(1)} collective-permute-done((f32[96,4352]{1,0:T(8,128)}, f32[96,4352]{1,0:T(8,128)S(1)}, u32[]{:S(2)}, u32[]{:S(2)}) %collective-permute-start.59) | collective-permute-done | bytes 1671200 | tf_op jit(solution)/shard_map/ppermute | solution.py:183
  1072.3 15.5 %collective-permute-done.60 = f32[48,4352]{1,0:T(8,128)} collective-permute-done((f32[48,4352]{1,0:T(8,128)}, f32[48,4352]{1,0:T(8,128)}, u32[]{:S(2)}, u32[]{:S(2)}) %collective-permute-start.60) | collective-permute-done | bytes 835616 | tf_op jit(solution)/shard_map/ppermute | solution.py:183
  1103.8 14.1 %collective-permute-done.61 = f32[24,4352]{1,0:T(8,128)} collective-permute-done((f32[24,4352]{1,0:T(8,128)}, f32[24,4352]{1,0:T(8,128)}, u32[]{:S(2)}, u32[]{:S(2)}) %collective-permute-start.61) | collective-permute-done | bytes 417824 | tf_op jit(solution)/shard_map/ppermute | solution.py:183
  (763 shorter events, 693.9 us)
Async XLA Ops:
  5.4 41.4 %collective-permute-start = (bf16[24,4352]{1,0:T(8,128)(2,1)}, bf16[24,4352]{1,0:T(8,128)(2,1)}, u32[]{:S(2)}, u32[]{:S(2)}) collective-permute-start(bf16[24,4352]{1,0:T(8,128)(2,1)} %get-tuple-element.535), channel_id=1, source_target_pairs={{0,16},{1,17},{2,18},{3,19},{4,20},{5,21},{6,22},{7,23},{8,24},{9,... | collective-permute-start | bytes 626696 | tf_op jit(solution)/shard_map/ppermute | solution.py:183
  10.4 42.7 %collective-permute-start.2 = (bf16[24,6144]{1,0:T(8,128)(2,1)}, bf16[24,6144]{1,0:T(8,128)(2,1)S(1)}, u32[]{:S(2)}, u32[]{:S(2)}) collective-permute-start(bf16[24,6144]{1,0:T(8,128)(2,1)} %get-tuple-element.524), channel_id=1, source_target_pairs={{0,16},{1,17},{2,18},{3,19},{4,20},{5,21},{6,22},{7,23},{8,24},{9,... | collective-permute-start | bytes 884744 | tf_op jit(solution)/shard_map/ppermute | solution.py:183
  11.5 74.5 %collective-permute-start.5 = (bf16[24,9216]{1,0:T(8,128)(2,1)}, bf16[24,9216]{1,0:T(8,128)(2,1)S(1)}, u32[]{:S(2)}, u32[]{:S(2)}) collective-permute-start(bf16[24,9216]{1,0:T(8,128)(2,1)} %get-tuple-element.526), channel_id=1, source_target_pairs={{0,16},{1,17},{2,18},{3,19},{4,20},{5,21},{6,22},{7,23},{8,24},{9,... | collective-permute-start | bytes 1327112 | tf_op jit(solution)/shard_map/ppermute | solution.py:183
  17.2 89.2 %collective-permute-start.9 = (bf16[24,4352]{1,0:T(8,128)(2,1)}, bf16[24,4352]{1,0:T(8,128)(2,1)}, u32[]{:S(2)}, u32[]{:S(2)}) collective-permute-start(bf16[24,4352]{1,0:T(8,128)(2,1)} %get-tuple-element.533), channel_id=1, source_target_pairs={{0,16},{1,17},{2,18},{3,19},{4,20},{5,21},{6,22},{7,23},{8,24},{9,... | collective-permute-start | bytes 626696 | tf_op jit(solution)/shard_map/ppermute | solution.py:183
  19.5 127.7 %collective-permute-start.14 = (bf16[24,6144]{1,0:T(8,128)(2,1)S(1)}, bf16[24,6144]{1,0:T(8,128)(2,1)S(1)}, u32[]{:S(2)}, u32[]{:S(2)}) collective-permute-start(bf16[24,6144]{1,0:T(8,128)(2,1)S(1)} %get-tuple-element.521), channel_id=1, source_target_pairs={{0,16},{1,17},{2,18},{3,19},{4,20},{5,21},{6,22},{7,23},{8,24},{9,... | collective-permute-start | bytes 884744 | tf_op jit(solution)/shard_map/ppermute | solution.py:183
  102.0 34.2 %collective-permute-start.6 = (bf16[192,4352]{1,0:T(8,128)(2,1)S(1)}, bf16[192,4352]{1,0:T(8,128)(2,1)S(1)}, u32[]{:S(2)}, u32[]{:S(2)}) collective-permute-start(bf16[192,4352]{1,0:T(8,128)(2,1)S(1)} %pad_maximum_fusion.25), channel_id=1, source_target_pairs={{0,1},{1,0},{2,6},{3,7},{4,5},{5,4},{6,2},{7,3},{8,9},{9,8},{10,14... | collective-permute-start | bytes 5013512 | tf_op jit(solution)/shard_map/ppermute | solution.py:183
  136.3 49.2 %collective-permute-start.10 = (bf16[384,4352]{1,0:T(8,128)(2,1)S(1)}, bf16[384,4352]{1,0:T(8,128)(2,1)S(1)}, u32[]{:S(2)}, u32[]{:S(2)}) collective-permute-start(bf16[384,4352]{1,0:T(8,128)(2,1)S(1)} %constant_dynamic-update-slice_fusion), channel_id=1, source_target_pairs={{0,2},{1,3},{2,0},{3,1},{4,6},{5,7},{6,4},{7,5},{8,10},{9,11},{10,... | collective-permute-start | bytes 10027016 | tf_op jit(solution)/shard_map/ppermute | solution.py:183
  137.6 47.9 %collective-permute-start.11 = (bf16[192,6144]{1,0:T(8,128)(2,1)S(1)}, bf16[192,6144]{1,0:T(8,128)(2,1)S(1)}, u32[]{:S(2)}, u32[]{:S(2)}) collective-permute-start(bf16[192,6144]{1,0:T(8,128)(2,1)S(1)} %pad_maximum_fusion.17), channel_id=1, source_target_pairs={{0,1},{1,0},{2,6},{3,7},{4,5},{5,4},{6,2},{7,3},{8,9},{9,8},{10,14... | collective-permute-start | bytes 7077896 | tf_op jit(solution)/shard_map/ppermute | solution.py:183
  138.3 41.6 %collective-permute-start.12 = (bf16[96,9216]{1,0:T(8,128)(2,1)S(1)}, bf16[96,9216]{1,0:T(8,128)(2,1)S(1)}, u32[]{:S(2)}, u32[]{:S(2)}) collective-permute-start(bf16[96,9216]{1,0:T(8,128)(2,1)S(1)} %pad_maximum_fusion.24), channel_id=1, source_target_pairs={{0,4},{1,5},{2,3},{3,2},{4,0},{5,1},{6,7},{7,6},{8,12},{9,13},{10,... | collective-permute-start | bytes 5308424 | tf_op jit(solution)/shard_map/ppermute | solution.py:183
  147.3 102.6 %collective-permute-start.19 = (bf16[24,3840]{1,0:T(8,128)(2,1)}, bf16[24,3840]{1,0:T(8,128)(2,1)}, u32[]{:S(2)}, u32[]{:S(2)}) collective-permute-start(bf16[24,3840]{1,0:T(8,128)(2,1)} %get-tuple-element.537), channel_id=1, source_target_pairs={{0,16},{1,17},{2,18},{3,19},{4,20},{5,21},{6,22},{7,23},{8,24},{9,... | collective-permute-start | bytes 552968 | tf_op jit(solution)/shard_map/ppermute | solution.py:183
  190.7 63.0 %collective-permute-start.15 = (bf16[384,6144]{1,0:T(8,128)(2,1)}, bf16[384,6144]{1,0:T(8,128)(2,1)}, u32[]{:S(2)}, u32[]{:S(2)}) collective-permute-start(bf16[384,6144]{1,0:T(8,128)(2,1)} %constant_dynamic-update-slice_fusion.5), channel_id=1, source_target_pairs={{0,2},{1,3},{2,0},{3,1},{4,6},{5,7},{6,4},{7,5},{8,10},{9,11},{10,... | collective-permute-start | bytes 14155784 | tf_op jit(solution)/shard_map/ppermute | solution.py:183
  193.5 60.2 %collective-permute-start.16 = (bf16[192,9216]{1,0:T(8,128)(2,1)}, bf16[192,9216]{1,0:T(8,128)(2,1)}, u32[]{:S(2)}, u32[]{:S(2)}) collective-permute-start(bf16[192,9216]{1,0:T(8,128)(2,1)} %pad_maximum_fusion.8), channel_id=1, source_target_pairs={{0,1},{1,0},{2,6},{3,7},{4,5},{5,4},{6,2},{7,3},{8,9},{9,8},{10,14... | collective-permute-start | bytes 10616840 | tf_op jit(solution)/shard_map/ppermute | solution.py:183
  195.9 57.8 %collective-permute-start.17 = (bf16[96,4352]{1,0:T(8,128)(2,1)}, bf16[96,4352]{1,0:T(8,128)(2,1)}, u32[]{:S(2)}, u32[]{:S(2)}) collective-permute-start(bf16[96,4352]{1,0:T(8,128)(2,1)} %pad_maximum_fusion.38), channel_id=1, source_target_pairs={{0,4},{1,5},{2,3},{3,2},{4,0},{5,1},{6,7},{7,6},{8,12},{9,13},{10,... | collective-permute-start | bytes 2506760 | tf_op jit(solution)/shard_map/ppermute | solution.py:183
  198.2 55.5 %collective-permute-start.18 = (bf16[48,6144]{1,0:T(8,128)(2,1)}, bf16[48,6144]{1,0:T(8,128)(2,1)}, u32[]{:S(2)}, u32[]{:S(2)}) collective-permute-start(bf16[48,6144]{1,0:T(8,128)(2,1)} %pad_maximum_fusion.42), channel_id=1, source_target_pairs={{0,8},{1,9},{2,10},{3,11},{4,12},{5,13},{6,14},{7,15},{8,0},{9,1},... | collective-permute-start | bytes 1769480 | tf_op jit(solution)/shard_map/ppermute | solution.py:183
  249.9 53.3 %collective-permute-start.24 = (bf16[24,6144]{1,0:T(8,128)(2,1)S(1)}, bf16[24,6144]{1,0:T(8,128)(2,1)}, u32[]{:S(2)}, u32[]{:S(2)}) collective-permute-start(bf16[24,6144]{1,0:T(8,128)(2,1)S(1)} %get-tuple-element.522), channel_id=1, source_target_pairs={{0,16},{1,17},{2,18},{3,19},{4,20},{5,21},{6,22},{7,23},{8,24},{9,... | collective-permute-start | bytes 884744 | tf_op jit(solution)/shard_map/ppermute | solution.py:183
  257.7 45.5 %collective-permute-start.20 = (bf16[384,9216]{1,0:T(8,128)(2,1)}, bf16[384,9216]{1,0:T(8,128)(2,1)}, u32[]{:S(2)}, u32[]{:S(2)}) collective-permute-start(bf16[384,9216]{1,0:T(8,128)(2,1)} %constant_dynamic-update-slice_fusion.10), channel_id=1, source_target_pairs={{0,2},{1,3},{2,0},{3,1},{4,6},{5,7},{6,4},{7,5},{8,10},{9,11},{10,... | collective-permute-start | bytes 21233672 | tf_op jit(solution)/shard_map/ppermute | solution.py:183
  260.3 42.9 %collective-permute-start.21 = (bf16[192,4352]{1,0:T(8,128)(2,1)}, bf16[192,4352]{1,0:T(8,128)(2,1)}, u32[]{:S(2)}, u32[]{:S(2)}) collective-permute-start(bf16[192,4352]{1,0:T(8,128)(2,1)} %pad_maximum_fusion.26), channel_id=1, source_target_pairs={{0,1},{1,0},{2,6},{3,7},{4,5},{5,4},{6,2},{7,3},{8,9},{9,8},{10,14... | collective-permute-start | bytes 5013512 | tf_op jit(solution)/shard_map/ppermute | solution.py:183
  264.0 39.1 %collective-permute-start.22 = (bf16[96,6144]{1,0:T(8,128)(2,1)}, bf16[96,6144]{1,0:T(8,128)(2,1)}, u32[]{:S(2)}, u32[]{:S(2)}) collective-permute-start(bf16[96,6144]{1,0:T(8,128)(2,1)} %pad_maximum_fusion.32), channel_id=1, source_target_pairs={{0,4},{1,5},{2,3},{3,2},{4,0},{5,1},{6,7},{7,6},{8,12},{9,13},{10,... | collective-permute-start | bytes 3538952 | tf_op jit(solution)/shard_map/ppermute | solution.py:183
  266.3 36.9 %collective-permute-start.23 = (bf16[48,3840]{1,0:T(8,128)(2,1)}, bf16[48,3840]{1,0:T(8,128)(2,1)}, u32[]{:S(2)}, u32[]{:S(2)}) collective-permute-start(bf16[48,3840]{1,0:T(8,128)(2,1)} %pad_maximum_fusion.48), channel_id=1, source_target_pairs={{0,8},{1,9},{2,10},{3,11},{4,12},{5,13},{6,14},{7,15},{8,0},{9,1},... | collective-permute-start | bytes 1105928 | tf_op jit(solution)/shard_map/ppermute | solution.py:183
  318.2 111.3 %collective-permute-start.25 = (bf16[384,4352]{1,0:T(8,128)(2,1)}, bf16[384,4352]{1,0:T(8,128)(2,1)}, u32[]{:S(2)}, u32[]{:S(2)}) collective-permute-start(bf16[384,4352]{1,0:T(8,128)(2,1)} %constant_dynamic-update-slice_fusion.15), channel_id=1, source_target_pairs={{0,2},{1,3},{2,0},{3,1},{4,6},{5,7},{6,4},{7,5},{8,10},{9,11},{10,... | collective-permute-start | bytes 10027016 | tf_op jit(solution)/shard_map/ppermute | solution.py:183
  324.3 105.2 %collective-permute-start.26 = (bf16[192,6144]{1,0:T(8,128)(2,1)}, bf16[192,6144]{1,0:T(8,128)(2,1)}, u32[]{:S(2)}, u32[]{:S(2)}) collective-permute-start(bf16[192,6144]{1,0:T(8,128)(2,1)} %pad_maximum_fusion.18), channel_id=1, source_target_pairs={{0,1},{1,0},{2,6},{3,7},{4,5},{5,4},{6,2},{7,3},{8,9},{9,8},{10,14... | collective-permute-start | bytes 7077896 | tf_op jit(solution)/shard_map/ppermute | solution.py:183
  327.0 102.5 %collective-permute-start.27 = (bf16[96,3840]{1,0:T(8,128)(2,1)}, bf16[96,3840]{1,0:T(8,128)(2,1)}, u32[]{:S(2)}, u32[]{:S(2)}) collective-permute-start(bf16[96,3840]{1,0:T(8,128)(2,1)} %pad_maximum_fusion.40), channel_id=1, source_target_pairs={{0,4},{1,5},{2,3},{3,2},{4,0},{5,1},{6,7},{7,6},{8,12},{9,13},{10,... | collective-permute-start | bytes 2211848 | tf_op jit(solution)/shard_map/ppermute | solution.py:183
  330.3 99.2 %collective-permute-start.28 = (bf16[48,6144]{1,0:T(8,128)(2,1)}, bf16[48,6144]{1,0:T(8,128)(2,1)}, u32[]{:S(2)}, u32[]{:S(2)}) collective-permute-start(bf16[48,6144]{1,0:T(8,128)(2,1)} %pad_maximum_fusion.43), channel_id=1, source_target_pairs={{0,8},{1,9},{2,10},{3,11},{4,12},{5,13},{6,14},{7,15},{8,0},{9,1},... | collective-permute-start | bytes 1769480 | tf_op jit(solution)/shard_map/ppermute | solution.py:183
  439.3 64.4 %collective-permute-start.29 = (bf16[384,6144]{1,0:T(8,128)(2,1)}, bf16[384,6144]{1,0:T(8,128)(2,1)}, u32[]{:S(2)}, u32[]{:S(2)}) collective-permute-start(bf16[384,6144]{1,0:T(8,128)(2,1)} %constant_dynamic-update-slice_fusion.20), channel_id=1, source_target_pairs={{0,2},{1,3},{2,0},{3,1},{4,6},{5,7},{6,4},{7,5},{8,10},{9,11},{10,... | collective-permute-start | bytes 14155784 | tf_op jit(solution)/shard_map/ppermute | solution.py:183
  441.8 61.9 %collective-permute-start.30 = (bf16[192,3840]{1,0:T(8,128)(2,1)}, bf16[192,3840]{1,0:T(8,128)(2,1)}, u32[]{:S(2)}, u32[]{:S(2)}) collective-permute-start(bf16[192,3840]{1,0:T(8,128)(2,1)} %pad_maximum_fusion.29), channel_id=1, source_target_pairs={{0,1},{1,0},{2,6},{3,7},{4,5},{5,4},{6,2},{7,3},{8,9},{9,8},{10,14... | collective-permute-start | bytes 4423688 | tf_op jit(solution)/shard_map/ppermute | solution.py:183
  445.4 58.4 %collective-permute-start.31 = (bf16[96,6144]{1,0:T(8,128)(2,1)}, bf16[96,6144]{1,0:T(8,128)(2,1)}, u32[]{:S(2)}, u32[]{:S(2)}) collective-permute-start(bf16[96,6144]{1,0:T(8,128)(2,1)} %pad_maximum_fusion.33), channel_id=1, source_target_pairs={{0,4},{1,5},{2,3},{3,2},{4,0},{5,1},{6,7},{7,6},{8,12},{9,13},{10,... | collective-permute-start | bytes 3538952 | tf_op jit(solution)/shard_map/ppermute | solution.py:183
  506.3 34.2 %collective-permute-start.32 = (bf16[384,3840]{1,0:T(8,128)(2,1)}, bf16[384,3840]{1,0:T(8,128)(2,1)}, u32[]{:S(2)}, u32[]{:S(2)}) collective-permute-start(bf16[384,3840]{1,0:T(8,128)(2,1)} %constant_dynamic-update-slice_fusion.25), channel_id=1, source_target_pairs={{0,2},{1,3},{2,0},{3,1},{4,6},{5,7},{6,4},{7,5},{8,10},{9,11},{10,... | collective-permute-start | bytes 8847368 | tf_op jit(solution)/shard_map/ppermute | solution.py:183
  543.8 51.0 %collective-permute-start.34 = (bf16[384,6144]{1,0:T(8,128)(2,1)}, bf16[384,6144]{1,0:T(8,128)(2,1)}, u32[]{:S(2)}, u32[]{:S(2)}) collective-permute-start(bf16[384,6144]{1,0:T(8,128)(2,1)} %constant_dynamic-update-slice_fusion.30), channel_id=1, source_target_pairs={{0,2},{1,3},{2,0},{3,1},{4,6},{5,7},{6,4},{7,5},{8,10},{9,11},{10,... | collective-permute-start | bytes 14155784 | tf_op jit(solution)/shard_map/ppermute | solution.py:183
  832.1 41.8 %collective-permute-start.48 = (bf16[192,6144]{1,0:T(8,128)(2,1)}, bf16[192,6144]{1,0:T(8,128)(2,1)}, u32[]{:S(2)}, u32[]{:S(2)}) collective-permute-start(bf16[192,6144]{1,0:T(8,128)(2,1)} %pad_maximum_fusion.20), channel_id=1, source_target_pairs={{0,1},{1,0},{2,6},{3,7},{4,5},{5,4},{6,2},{7,3},{8,9},{9,8},{10,14... | collective-permute-start | bytes 7077896 | tf_op jit(solution)/shard_map/ppermute | solution.py:183
  927.3 44.5 %collective-permute-start.53 = (f32[384,2304]{0,1:T(8,128)}, f32[384,2304]{0,1:T(8,128)}, u32[]{:S(2)}, u32[]{:S(2)}) collective-permute-start(f32[384,2304]{0,1:T(8,128)} %copy.254), channel_id=1, source_target_pairs={{0,2},{1,3},{2,0},{3,1},{4,6},{5,7},{6,4},{7,5},{8,10},{9,11},{10,... | collective-permute-start | bytes 10616840 | tf_op jit(solution)/shard_map/ppermute | solution.py:183
  930.6 41.2 %collective-permute-start.52 = (f32[48,6144]{1,0:T(8,128)}, f32[48,6144]{1,0:T(8,128)}, u32[]{:S(2)}, u32[]{:S(2)}) collective-permute-start(f32[48,6144]{1,0:T(8,128)} %get-tuple-element.471), channel_id=1, source_target_pairs={{0,8},{1,9},{2,10},{3,11},{4,12},{5,13},{6,14},{7,15},{8,0},{9,1},... | collective-permute-start | bytes 3538952 | tf_op jit(solution)/shard_map/ppermute | solution.py:183
  935.2 36.6 %collective-permute-start.54 = (f32[384,768]{0,1:T(8,128)}, f32[384,768]{0,1:T(8,128)}, u32[]{:S(2)}, u32[]{:S(2)}) collective-permute-start(f32[384,768]{0,1:T(8,128)} %copy.255), channel_id=1, source_target_pairs={{0,2},{1,3},{2,0},{3,1},{4,6},{5,7},{6,4},{7,5},{8,10},{9,11},{10,... | collective-permute-start | bytes 3538952 | tf_op jit(solution)/shard_map/ppermute | solution.py:183
  (183 other events, 2222.5 us)

commit v3 on v2

v3 whole, which is shorter than its diff:
```python
import jax
import jax.numpy as jnp
from jax import lax
from jax.experimental import pallas as pl
from jax.experimental.pallas import tpu as pltpu
from jax.sharding import PartitionSpec as P

HDIM = 64
LAYERS = 2
TOPK = 2
LANES = 128
FF_TILE = 512

ln_eps = 1e-05
in_eps = 1e-05
learn_rate = 0.02
first_decay = 0.5
second_decay = 0.5
adam_eps = 1e-08
weight_decay = 0.1
teacher_keep = 0.5
huber_beta = 1.0
score_scale = 0.125
entry_clip = 1e-05
half_type = jnp.bfloat16
full_type = jnp.float32
AXES = ("dp", "seq")


def contract(left, right, left_dim, right_dim):
    return lax.dot_general(
        left,
        right,
        (((left_dim,), (right_dim,)), ((), ())),
        preferred_element_type=full_type,
    )


def head_mask(which, width):
    lane = lax.broadcasted_iota(jnp.int32, (1, width), 1)
    return (lane // HDIM) == which


def attend_kernel(q_ref, k_ref, v_ref, o_ref):
    queries = q_ref[0] * jnp.asarray(score_scale, half_type)
    keys_all = k_ref[0]
    values_all = v_ref[0]
    width = queries.shape[1]
    mixed = None
    for which in range(width // HDIM):
        mask = head_mask(which, width)
        head_q = jnp.where(mask, queries, jnp.zeros_like(queries))
        scores = contract(head_q, keys_all, 1, 1)
        exps = jnp.exp(scores - jnp.max(scores, axis=1, keepdims=True))
        probs = (exps * (1.0 / jnp.sum(exps, axis=1, keepdims=True))).astype(half_type)
        head_out = contract(probs, values_all, 1, 0)
        mixed = head_out if mixed is None else jnp.where(mask, head_out, mixed)
    o_ref[0] = mixed.astype(half_type)


def attend_back_kernel(q_ref, k_ref, v_ref, do_ref, dq_ref, dk_ref, dv_ref):
    queries = q_ref[0] * jnp.asarray(score_scale, half_type)
    keys_all = k_ref[0]
    values_all = v_ref[0]
    grad_out = do_ref[0]
    width = queries.shape[1]
    grad_k = None
    grad_v = None
    grad_q_rows = []
    for which in range(width // HDIM):
        mask = head_mask(which, width)
        head_q = jnp.where(mask, queries, jnp.zeros_like(queries))
        head_do = jnp.where(mask, grad_out, jnp.zeros_like(grad_out))
        scores = contract(keys_all, head_q, 1, 1)
        exps = jnp.exp(scores - jnp.max(scores, axis=0, keepdims=True))
        probs = exps * (1.0 / jnp.sum(exps, axis=0, keepdims=True))
        grad_probs = contract(values_all, head_do, 1, 1)
        prods = probs * grad_probs
        grad_scores = (prods - probs * jnp.sum(prods, axis=0, keepdims=True)).astype(half_type)
        head_dv = contract(probs.astype(half_type), grad_out, 1, 0)
        head_dk = contract(grad_scores, queries, 1, 0)
        head_dq = contract(keys_all, grad_scores, 0, 0)
        grad_q_rows.append(head_dq[which * HDIM : (which + 1) * HDIM])
        grad_v = head_dv if grad_v is None else jnp.where(mask, head_dv, grad_v)
        grad_k = head_dk if grad_k is None else jnp.where(mask, head_dk, grad_k)
    grad_q = jnp.concatenate(grad_q_rows, axis=0).T * score_scale
    dq_ref[0] = grad_q.astype(half_type)
    dk_ref[0] = grad_k.astype(half_type)
    dv_ref[0] = grad_v.astype(half_type)


def qkv_specs(tokens, blocks):
    return [
        pl.BlockSpec((1, tokens, LANES), lambda s, j, off=off: (s, 0, off * blocks + j))
        for off in range(3)
    ]


def attend(projected):
    seqs, tokens, width3 = projected.shape
    width = width3 // 3
    blocks = width // LANES
    return pl.pallas_call(
        attend_kernel,
        grid=(seqs, blocks),
        in_specs=qkv_specs(tokens, blocks),
        out_specs=pl.BlockSpec((1, tokens, LANES), lambda s, j: (s, 0, j)),
        out_shape=jax.ShapeDtypeStruct((seqs, tokens, width), half_type),
        cost_estimate=pl.CostEstimate(
            flops=16 * seqs * tokens * tokens * width,
            transcendentals=seqs * tokens * tokens * width // HDIM,
            bytes_accessed=8 * seqs * tokens * width,
        ),
        name="attend",
    )(projected, projected, projected)


def attend_back(projected, grad_mixed):
    seqs, tokens, width3 = projected.shape
    width = width3 // 3
    blocks = width // LANES
    block = pl.BlockSpec((1, tokens, LANES), lambda s, j: (s, 0, j))
    shape = jax.ShapeDtypeStruct((seqs, tokens, width), half_type)
    return pl.pallas_call(
        attend_back_kernel,
        grid=(seqs, blocks),
        in_specs=qkv_specs(tokens, blocks) + [block],
        out_specs=[block, block, block],
        out_shape=[shape, shape, shape],
        cost_estimate=pl.CostEstimate(
            flops=32 * seqs * tokens * tokens * width,
            transcendentals=seqs * tokens * tokens * width // HDIM,
            bytes_accessed=14 * seqs * tokens * width,
        ),
        name="attend_back",
    )(projected, projected, projected, grad_mixed)


def normal_cdf(values):
    return 0.5 + 0.5 * lax.erf(values * (0.5**0.5))


def whole_block(shape):
    zeros = (0,) * len(shape)
    return pl.BlockSpec(shape, lambda *_: zeros)


def stacked(own_ref, got_ref):
    return jnp.concatenate([own_ref[...], got_ref[...]], axis=0)


def unit_of(values):
    centre = values - jnp.mean(values, axis=1, keepdims=True)
    inv_scale = lax.rsqrt(jnp.mean(centre * centre, axis=1, keepdims=True) + ln_eps)
    return centre * inv_scale, inv_scale


def norm_back(grad_out, gain, values):
    unit, inv_scale = unit_of(values)
    grad_unit = grad_out * gain
    inner_mean = jnp.mean(grad_unit, axis=1, keepdims=True)
    along_mean = jnp.mean(grad_unit * unit, axis=1, keepdims=True)
    grad_in = (grad_unit - inner_mean - unit * along_mean) * inv_scale
    return grad_in, jnp.sum(grad_out * unit, axis=0, keepdims=True)


def half(values):
    return values.astype(half_type)


def shape_of(shape, kind):
    return jax.ShapeDtypeStruct(shape, kind)


def cost(flops, moved):
    return pl.CostEstimate(flops=flops, transcendentals=0, bytes_accessed=moved)


class Weight:
    def __init__(self, own, got, start, cols):
        self.own, self.got, self.start, self.cols = own, got, start, cols

    def specs(self, width, index=lambda j: j):
        base = self.start // width
        spec = pl.BlockSpec(
            (self.own.shape[0], width), lambda j, base=base: (0, base + index(j))
        )
        return [spec, spec]

    def refs(self):
        return [self.own, self.got]


def embed(patches, mask, mover, weight, small, keep_patches):
    rows, width = patches.shape
    tokens = rows // 2
    masked = mask is not None

    def kernel(*refs):
        x_ref, mover_ref, own_ref, got_ref, sown_ref, sgot_ref = refs[:6]
        refs = refs[6:]
        if masked:
            mask_ref, refs = refs[0], refs[1:]
        h_ref, table_ref = refs[:2]
        x_rel = half(contract(x_ref[...], mover_ref[...], 1, 0))
        if keep_patches:
            refs[2][...] = x_rel
        w_rel = half(contract(stacked(own_ref, got_ref), mover_ref[...], 1, 0))
        small_t = stacked(sown_ref, sgot_ref).astype(full_type).T
        posit = small_t[:tokens]
        table = small_t[tokens : tokens + 8]
        table_ref[...] = table
        states = contract(x_rel, w_rel, 1, 0)
        for seq in range(rows // tokens):
            part = slice(seq * tokens, (seq + 1) * tokens)
            state = states[part]
            if masked:
                flag = mask_ref[part, :]
                state = state * (1.0 - flag) + flag * table[2 * LAYERS + 1 : 2 * LAYERS + 2]
            h_ref[part, :] = state + posit

    outs = [shape_of((rows, width), full_type), shape_of((8, width), full_type)]
    if keep_patches:
        outs.append(shape_of((rows, width), half_type))
    args = [patches, mover] + weight.refs() + list(small) + ([mask] if masked else [])
    specs = [whole_block(patches.shape), whole_block(mover.shape)] + weight.specs(width)
    specs += [whole_block(part.shape) for part in small]
    if masked:
        specs.append(whole_block(mask.shape))
    return pl.pallas_call(
        kernel,
        grid=(1,),
        in_specs=specs,
        out_specs=[whole_block(out.shape) for out in outs],
        out_shape=outs,
        cost_estimate=cost(6 * rows * width * width, 12 * rows * width),
        name="embed",
    )(*args)


def norm_project(states, table, row, weight, keep):
    rows, width = states.shape
    steps = weight.cols // width

    def kernel(h_ref, table_ref, own_ref, got_ref, out_ref, a_ref):
        @pl.when(pl.program_id(0) == 0)
        def _():
            unit, _ = unit_of(h_ref[...])
            a_ref[...] = half(unit * table_ref[row : row + 1, :])

        out_ref[...] = half(contract(a_ref[...], stacked(own_ref, got_ref), 1, 0))

    outs = [shape_of((rows, weight.cols), half_type)]
    out_specs = [pl.BlockSpec((rows, width), lambda j: (0, j))]
    scratch = []
    if keep:
        outs.append(shape_of((rows, width), half_type))
        out_specs.append(whole_block((rows, width)))
    else:
        scratch.append(pltpu.VMEM((rows, width), half_type))
    return pl.pallas_call(
        kernel,
        grid=(steps,),
        in_specs=[whole_block(states.shape), whole_block(table.shape)] + weight.specs(width),
        out_specs=out_specs,
        out_shape=outs,
        scratch_shapes=scratch,
        cost_estimate=cost(2 * rows * width * weight.cols, 12 * rows * width),
        name="norm_project",
    )(states, table, *weight.refs())


def mix_out(mixed, states, mover, table, row, weight, keep):
    rows, width = states.shape
    tile = rows // 2

    def kernel(o_ref, h_ref, mover_ref, table_ref, own_ref, got_ref, m_ref, b_ref, *rest):
        if keep:
            rel_ref, w_ref = rest
        else:
            (w_ref,) = rest

        @pl.when(pl.program_id(0) == 0)
        def _():
            w_ref[...] = half(contract(stacked(own_ref, got_ref), mover_ref[...], 1, 0))

        mixed_rel = half(contract(o_ref[...], mover_ref[...], 1, 0))
        if keep:
            rel_ref[...] = mixed_rel
        middle = h_ref[...] + contract(mixed_rel, w_ref[...], 1, 0)
        m_ref[...] = middle
        unit, _ = unit_of(middle)
        b_ref[...] = half(unit * table_ref[row : row + 1, :])

    part = pl.BlockSpec((tile, width), lambda j: (j, 0))
    outs = [shape_of((rows, width), full_type), shape_of((rows, width), half_type)]
    out_specs = [part, part]
    scratch = []
    if keep:
        outs += [shape_of((rows, width), half_type), shape_of((width, width), half_type)]
        out_specs += [part, whole_block((width, width))]
    else:
        scratch.append(pltpu.VMEM((width, width), half_type))
    return pl.pallas_call(
        kernel,
        grid=(2,),
        in_specs=[part, part, whole_block(mover.shape), whole_block(table.shape)]
        + weight.specs(width, lambda j: 0),
        out_specs=out_specs,
        out_shape=outs,
        scratch_shapes=scratch,
        cost_estimate=cost(6 * rows * width * width, 14 * rows * width),
        name="mix_out",
    )(mixed, states, mover, table, *weight.refs())


def feed_forward(normed, middle, w_up, w_down, keep):
    rows, width = middle.shape
    tile = FF_TILE
    steps = w_up.cols // tile

    def kernel(b_ref, m_ref, uown_ref, ugot_ref, down_ref, dgot_ref, out_ref, *rest):
        step = pl.program_id(0)
        hidden = contract(b_ref[...], stacked(uown_ref, ugot_ref), 1, 0)
        cdf = normal_cdf(hidden)
        active = half(hidden * cdf)
        if keep:
            rest[0][...] = active
            rest[1][...] = cdf + hidden * (
                jnp.exp(-0.5 * hidden * hidden) * ((0.5 / jnp.pi) ** 0.5)
            )
        part = contract(active, stacked(down_ref, dgot_ref), 1, 1)

        @pl.when(step == 0)
        def _():
            out_ref[...] = m_ref[...] + part

        @pl.when(step > 0)
        def _():
            out_ref[...] += part

    outs = [shape_of((rows, width), full_type)]
    out_specs = [whole_block((rows, width))]
    if keep:
        outs += [shape_of((rows, w_up.cols), half_type), shape_of((rows, w_up.cols), full_type)]
        out_specs += [pl.BlockSpec((rows, tile), lambda j: (0, j))] * 2
    return pl.pallas_call(
        kernel,
        grid=(steps,),
        in_specs=[whole_block(normed.shape), whole_block(middle.shape)]
        + w_up.specs(tile)
        + w_down.specs(tile),
        out_specs=out_specs,
        out_shape=outs,
        cost_estimate=cost(4 * rows * width * w_up.cols, 12 * rows * width + 16 * width * w_up.cols),
        name="feed_forward",
    )(normed, middle, *w_up.refs(), *w_down.refs())


def make_target(first, second, seqs):
    rows, width = first.shape
    tokens = rows // seqs
    cols = width // 2

    def kernel(one_ref, two_ref, out_ref):
        total = None
        for ref in (one_ref, two_ref):
            values = ref[...]
            centre = values - jnp.mean(values, axis=0, keepdims=True)
            variance = jnp.mean(centre * centre, axis=0, keepdims=True)
            term = centre * lax.rsqrt(variance + in_eps)
            total = term if total is None else total + term
        out_ref[...] = total * (1.0 / TOPK)

    block = pl.BlockSpec((tokens, cols), lambda s, j: (s, j))
    return pl.pallas_call(
        kernel,
        grid=(seqs, 2),
        in_specs=[block, block],
        out_specs=block,
        out_shape=shape_of((rows, width), full_type),
        cost_estimate=cost(20 * rows * width, 12 * rows * width),
        name="make_target",
    )(first, second)


def head_step(states, table, mover, weight, target, mask, total_masked):
    rows, width = states.shape
    tile = rows // 2
    final_row = 2 * LAYERS

    def kernel(
        h_ref, table_ref, mover_ref, own_ref, got_ref, t_ref, mask_ref,
        flow_ref, f_ref, pred_ref, gain_ref, loss_ref, w_ref,
    ):
        step = pl.program_id(0)

        @pl.when(step == 0)
        def _():
            w_ref[...] = half(contract(stacked(own_ref, got_ref), mover_ref[...], 1, 0))
            gain_ref[...] = jnp.zeros_like(gain_ref)
            loss_ref[...] = jnp.zeros_like(loss_ref)

        states_now = h_ref[...]
        gain = table_ref[final_row : final_row + 1, :]
        unit, _ = unit_of(states_now)
        final_normed = half(unit * gain)
        f_ref[...] = final_normed
        flag = mask_ref[...]
        differ = contract(final_normed, w_ref[...], 1, 0) - t_ref[...]
        magnitude = jnp.abs(differ)
        terms = jnp.where(
            magnitude < huber_beta,
            0.5 * differ * differ / huber_beta,
            magnitude - 0.5 * huber_beta,
        )
        loss_ref[...] += jnp.sum(terms * flag, axis=0, keepdims=True)
        grad_pred = half(flag * jnp.clip(differ / huber_beta, -1.0, 1.0) / total_masked)
        pred_ref[...] = half(contract(grad_pred, mover_ref[...], 1, 1))
        grad_in, grad_gain = norm_back(contract(grad_pred, w_ref[...], 1, 1), gain, states_now)
        flow_ref[...] = grad_in
        gain_ref[...] += grad_gain

    part = pl.BlockSpec((tile, width), lambda j: (j, 0))
    row = whole_block((1, width))
    return pl.pallas_call(
        kernel,
        grid=(2,),
        in_specs=[part, whole_block(table.shape), whole_block(mover.shape)]
        + weight.specs(width, lambda j: 0)
        + [part, pl.BlockSpec((tile, 1), lambda j: (j, 0))],
        out_specs=[part, part, part, row, row],
        out_shape=[
            shape_of((rows, width), full_type),
            shape_of((rows, width), half_type),
            shape_of((rows, width), half_type),
            shape_of((1, width), full_type),
            shape_of((1, width), full_type),
        ],
        scratch_shapes=[pltpu.VMEM((width, width), half_type)],
        cost_estimate=cost(8 * rows * width * width, 16 * rows * width),
        name="head_step",
    )(states, table, mover, *weight.refs(), target, mask)


def feed_back(flow, slope, middle, table, row, w_up, w_down):
    rows, width = flow.shape
    tile = FF_TILE
    steps = w_up.cols // tile

    def kernel(
        flow_ref, slope_ref, m_ref, table_ref, uown_ref, ugot_ref, down_ref, dgot_ref,
        du_ref, dy_ref, dm_ref, dz_ref, gain_ref, acc_ref,
    ):
        step = pl.program_id(0)

        @pl.when(step == 0)
        def _():
            dy_ref[...] = half(flow_ref[...])

        grad_active = contract(dy_ref[...], stacked(down_ref, dgot_ref), 1, 0)
        grad_hidden = half(grad_active * slope_ref[...])
        du_ref[...] = grad_hidden
        part = contract(grad_hidden, stacked(uown_ref, ugot_ref), 1, 1)

        @pl.when(step == 0)
        def _():
            acc_ref[...] = part

        @pl.when(step > 0)
        def _():
            acc_ref[...] += part

        @pl.when(step == steps - 1)
        def _():
            grad_in, grad_gain = norm_back(
                acc_ref[...], table_ref[row : row + 1, :], m_ref[...]
            )
            grad_middle = flow_ref[...] + grad_in
            dm_ref[...] = grad_middle
            dz_ref[...] = half(grad_middle)
            gain_ref[...] = grad_gain

    full = whole_block((rows, width))
    column = pl.BlockSpec((rows, tile), lambda j: (0, j))
    return pl.pallas_call(
        kernel,
        grid=(steps,),
        in_specs=[full, column, full, whole_block(table.shape)]
        + w_up.specs(tile)
        + w_down.specs(tile),
        out_specs=[column, full, full, full, whole_block((1, width))],
        out_shape=[
            shape_of((rows, w_up.cols), half_type),
            shape_of((rows, width), half_type),
            shape_of((rows, width), full_type),
            shape_of((rows, width), half_type),
            shape_of((1, width), full_type),
        ],
        scratch_shapes=[pltpu.VMEM((rows, width), full_type)],
        cost_estimate=cost(4 * rows * width * w_up.cols, 40 * rows * width + 8 * width * w_up.cols),
        name="feed_back",
    )(flow, slope, middle, table, *w_up.refs(), *w_down.refs())


def mix_back(grad_branch, w_rel, mover):
    rows, width = grad_branch.shape
    tile = rows // 2

    def kernel(dz_ref, w_ref, mover_ref, do_ref, nat_ref):
        branch = dz_ref[...]
        grad_rel = half(contract(branch, w_ref[...], 1, 1))
        do_ref[...] = half(contract(grad_rel, mover_ref[...], 1, 1))
        nat_ref[...] = half(contract(branch, mover_ref[...], 1, 1))

    part = pl.BlockSpec((tile, width), lambda j: (j, 0))
    square = whole_block((width, width))
    return pl.pallas_call(
        kernel,
        grid=(2,),
        in_specs=[part, square, square],
        out_specs=[part, part],
        out_shape=[shape_of((rows, width), half_type)] * 2,
        cost_estimate=cost(6 * rows * width * width, 10 * rows * width),
        name="mix_back",
    )(grad_branch, w_rel, mover)


def project_back(grads, grad_middle, states, table, row, weight, mover, mask):
    rows, width = states.shape
    tile = rows // 2
    count = len(grads)
    first = mask is not None

    def kernel(*refs):
        grad_refs, refs = refs[:count], refs[count:]
        w_refs, refs = refs[: 2 * count], refs[2 * count :]
        dm_ref, h_ref, table_ref = refs[:3]
        refs = refs[3:]
        if first:
            mover_ref, mask_ref = refs[:2]
            refs = refs[2:]
        dh_ref, gain_ref = refs[:2]
        step = pl.program_id(0)

        @pl.when(step == 0)
        def _():
            for ref in (gain_ref,) + ((refs[3],) if first else ()):
                ref[...] = jnp.zeros_like(ref)

        total = None
        for place in range(count):
            part = contract(
                grad_refs[place][...], stacked(w_refs[2 * place], w_refs[2 * place + 1]), 1, 1
            )
            total = part if total is None else total + part
        grad_in, grad_gain = norm_back(total, table_ref[row : row + 1, :], h_ref[...])
        flow = dm_ref[...] + grad_in
        dh_ref[...] = flow
        gain_ref[...] += grad_gain
        if first:
            flag = mask_ref[...]
            refs[2][...] = half(contract(half(flow * (1.0 - flag)), mover_ref[...], 1, 1))
            refs[3][...] += jnp.sum(flow * flag, axis=0, keepdims=True)

    part = pl.BlockSpec((tile, width), lambda j: (j, 0))
    vector = whole_block((1, width))
    specs = [part] * count
    args = list(grads)
    for place in range(count):
        specs += weight.specs(width, lambda j, place=place: place)
        args += weight.refs()
    specs += [part, part, whole_block(table.shape)]
    args += [grad_middle, states, table]
    outs = [shape_of((rows, width), full_type), shape_of((1, width), full_type)]
    out_specs = [part, vector]
    if first:
        specs += [whole_block(mover.shape), pl.BlockSpec((tile, 1), lambda j: (j, 0))]
        args += [mover, mask]
        outs += [shape_of((rows, width), half_type), shape_of((1, width), full_type)]
        out_specs += [part, vector]
    return pl.pallas_call(
        kernel,
        grid=(2,),
        in_specs=specs,
        out_specs=out_specs,
        out_shape=outs,
        cost_estimate=cost(2 * rows * width * weight.cols, 22 * rows * width),
        name="project_back",
    )(*args)


def weight_grads(pairs):
    rows, width = pairs[0][0].shape
    plan = []
    start = 0
    for place, (_, rights) in enumerate(pairs):
        first = start
        for right in rights:
            tiles = right.shape[1] // width
            plan.append((place, start, tiles, start == first))
            start += tiles
    total = start
    near_rows = width // 2

    def kernel(*refs):
        left_refs, refs = refs[: len(pairs)], refs[len(pairs) :]
        right_refs, refs = refs[: len(plan)], refs[len(plan) :]
        near_ref, far_ref, turned_ref = refs
        step = pl.program_id(0)
        for (place, begin, tiles, fresh), right_ref in zip(plan, right_refs):
            if fresh:

                @pl.when(step == begin)
                def _(place=place):
                    turned_ref[...] = left_refs[place][...].T

            @pl.when((step >= begin) & (step < begin + tiles))
            def _(right_ref=right_ref):
                out = contract(turned_ref[...], right_ref[...], 1, 0)
                near_ref[...] = out[:near_rows]
                far_ref[...] = out[near_rows:]

    specs = [whole_block((rows, width)) for _ in pairs]
    args = [left for left, _ in pairs]
    for (_, rights) in pairs:
        args += list(rights)
    for _, begin, tiles, _ in plan:
        specs.append(
            pl.BlockSpec(
                (rows, width),
                lambda j, begin=begin, tiles=tiles: (0, jnp.clip(j - begin, 0, tiles - 1)),
            )
        )
    block = pl.BlockSpec((near_rows, width), lambda j: (0, j))
    shape = shape_of((near_rows, total * width), full_type)
    return tuple(
        pl.pallas_call(
            kernel,
            grid=(total,),
            in_specs=specs,
            out_specs=[block, block],
            out_shape=[shape, shape],
            scratch_shapes=[pltpu.VMEM((width, rows), half_type)],
            cost_estimate=cost(
                2 * rows * width * width * total, width * total * (4 * width + 2 * rows)
            ),
            name="weight_grads",
        )(*args)
    )


def small_grads(flow, vectors, seqs):
    rows, width = flow.shape
    tokens = rows // seqs
    cols = tokens + 8
    cols += -cols % LANES

    def kernel(flow_ref, *refs):
        vector_refs, (near_ref, far_ref) = refs[:-2], refs[-2:]
        posit = flow_ref[:tokens]
        for seq in range(1, seqs):
            posit = posit + flow_ref[seq * tokens : (seq + 1) * tokens]
        fill = jnp.zeros((cols - tokens - len(vector_refs), width), full_type)
        table = jnp.concatenate([posit] + [ref[...] for ref in vector_refs] + [fill], axis=0).T
        near_ref[...] = table[: width // 2]
        far_ref[...] = table[width // 2 :]

    shape = shape_of((width // 2, cols), full_type)
    return tuple(
        pl.pallas_call(
            kernel,
            grid=(1,),
            in_specs=[whole_block(flow.shape)] + [whole_block((1, width)) for _ in vectors],
            out_specs=[whole_block(shape.shape)] * 2,
            out_shape=[shape, shape],
            cost_estimate=cost(2 * rows * width, 8 * rows * width),
            name="small_grads",
        )(flow, *vectors)
    )


class Plan:
    def __init__(self):
        self.seq_size = lax.axis_size("seq")
        self.count = lax.axis_size("dp") * self.seq_size
        self.bits = self.count.bit_length() - 1
        self.early = list(range(self.bits - 1, 2, -1))

        def flips(pick):
            return [(i, i ^ (1 << pick((i >> 1) & 1))) for i in range(self.count)]

        self.stages = [flips(lambda core, b=b: b) for b in self.early]
        self.stages.append(flips(lambda core: 0 if core else 2))
        self.stages.append(flips(lambda core: 2 if core else 0))
        self.core_stage = flips(lambda core: 1)
        self.index = lax.axis_index("dp") * self.seq_size + lax.axis_index("seq")

    def swap(self, value, perm):
        return lax.ppermute(value, AXES, perm)

    def row_table(self, width):
        rows = width // self.count
        place = lax.broadcasted_iota(jnp.int32, (1, width), 1)
        spot = place // rows
        early_count = len(self.early)
        other = (spot >> (self.bits - 1)) & 1
        holder_core = ((self.index >> 1) & 1) ^ other
        block = self.index ^ (other << 1)
        for step, bit in enumerate(self.early):
            block = block ^ (((spot >> step) & 1) << bit)
        first = (spot >> early_count) & 1
        second = (spot >> (early_count + 1)) & 1
        block = block ^ jnp.where(holder_core == 0, first << 2, first)
        block = block ^ jnp.where(holder_core == 0, second, second << 2)
        return block * rows + place % rows

    def mover(self, width):
        table = self.row_table(width)
        whole = lax.broadcasted_iota(jnp.int32, (width, width), 0)
        return (whole == table).astype(half_type)


class Pump:
    def __init__(self, plan):
        self.plan = plan
        self.jobs = []
        self.flying = []

    def add(self, steps, done):
        self.jobs.append([steps, next(steps), done])

    def begin(self):
        self.flying = [
            [self.plan.swap(value, perm) for value, perm in sends] for _, sends, _ in self.jobs
        ]

    def end(self, values=()):
        flying, values = lax.optimization_barrier((self.flying, values))
        left = []
        for (steps, _, done), gots in zip(self.jobs, flying):
            try:
                left.append([steps, steps.send(gots), done])
            except StopIteration as stop:
                done(stop.value)
        self.jobs = left
        self.flying = []
        return values

    def drain(self):
        while self.jobs:
            self.begin()
            self.end()


def gather_steps(plan, value):
    for perm in plan.stages:
        (got,) = yield [(value, perm)]
        value = jnp.concatenate([value, got], axis=0)
    return value


def scatter_steps(plan, pieces):
    gots = yield [(far, plan.core_stage) for _, far in pieces]
    quarter = pieces[0][0].shape[0] // 2
    sums = [
        (half(near[quarter:] + got[quarter:]), near[:quarter] + got[:quarter])
        for (near, _), got in zip(pieces, gots)
    ]
    send = jnp.concatenate([part for part, _ in sums], axis=1)
    keep = jnp.concatenate([part for _, part in sums], axis=1)
    stages = plan.stages[::-1]
    for step, perm in enumerate(stages):
        (got,) = yield [(send, perm)]
        got = got.astype(full_type)
        if step == len(stages) - 1:
            return keep + got
        middle = keep.shape[0] // 2
        send = keep[middle:] + got[middle:]
        keep = keep[:middle] + got[:middle]


def adam_step(weight, first_mom, second_mom, teacher, gradient):
    first_new = first_decay * first_mom + (1.0 - first_decay) * gradient
    second_new = second_decay * second_mom + (1.0 - second_decay) * gradient * gradient
    weight_new = weight - learn_rate * (
        first_new / (jnp.sqrt(second_new) + adam_eps) + weight_decay * weight
    )
    teacher_new = teacher_keep * teacher + (1.0 - teacher_keep) * weight_new
    return (weight_new, first_new, second_new, teacher_new)


def pad_lanes(value):
    extra = -value.shape[1] % LANES
    return jnp.pad(value, ((0, 0), (0, extra)))


def local(
    patches,
    masked_at,
    edge_w,
    attn_w,
    mlp_w,
    posit_w,
    vecs_w,
    edge_m,
    attn_m,
    mlp_m,
    posit_m,
    vecs_m,
    edge_v,
    attn_v,
    mlp_v,
    posit_v,
    vecs_v,
    edge_t,
    attn_t,
    mlp_t,
    posit_t,
    vecs_t,
):
    seqs, tokens, width = patches.shape
    plan = Plan()
    total_masked = seqs * plan.count * tokens // 2
    ff_width = mlp_w.shape[1] // (2 * LAYERS)
    small_cols = tokens + vecs_w.shape[1]
    flat_patch = patches.reshape(-1, width)
    mask_flat = masked_at.astype(full_type).reshape(-1, 1)
    mover = plan.mover(width)

    def shards(edge, attn, mlp, posit, vecs):
        small = pad_lanes(jnp.concatenate([posit, vecs], axis=1))
        return [edge[:, :width], edge[:, width:], small] + [
            [
                part[:, layer * part.shape[1] // LAYERS : (layer + 1) * part.shape[1] // LAYERS]
                for part in (attn, mlp)
            ]
            for layer in range(LAYERS)
        ]

    def joined(parts):
        return jnp.concatenate([half(part) for part in parts], axis=1)

    t_patch, _, t_small, t_one, t_two = shards(edge_t, attn_t, mlp_t, posit_t, vecs_t)
    s_patch, s_head, s_small, s_one, s_two = shards(edge_w, attn_w, mlp_w, posit_w, vecs_w)
    waiting = [
        joined([t_patch, t_one[0], t_small]),
        joined([t_one[1]]),
        joined(t_two),
        joined([s_patch, s_one[0], s_small]),
        joined([s_one[1]]),
        joined([s_two[0], s_head]),
        joined([s_two[1]]),
    ]

    def attn_weights(own, got, start):
        return Weight(own, got, start, 3 * width), Weight(own, got, start + 3 * width, width)

    def mlp_weights(own, got, start):
        return Weight(own, got, start, ff_width), Weight(own, got, start + ff_width, ff_width)

    def small_of(own, got):
        start = own.shape[1] - t_small.shape[1]
        return own[:, start:], got[:, start:]

    def attend_forward(states, table, layer, w_qkv, w_out, keep):
        outs = norm_project(states, table, layer, w_qkv, keep)
        projected = outs[0].reshape(seqs, tokens, w_qkv.cols)
        mixed = attend(projected).reshape(-1, width)
        results = mix_out(mixed, states, mover, table, LAYERS + layer, w_out, keep)
        if keep:
            return results[0], results[1], (states, outs[1], projected) + tuple(results[2:])
        return results[0], results[1], ()

    saved_attn = [None] * LAYERS
    saved_mlp = [None] * LAYERS

    def segment_t0(_, own, got):
        patch = Weight(own, got, 0, width)
        states, table, patch_rel = embed(
            flat_patch, None, mover, patch, small_of(own, got), True
        )
        middle, normed, _ = attend_forward(
            states, table, 0, *attn_weights(own, got, width), False
        )
        return middle, normed, table, patch_rel

    def segment_t1(values, own, got):
        middle, normed, table, patch_rel = values
        (states,) = feed_forward(normed, middle, *mlp_weights(own, got, 0), False)
        return states, table, patch_rel

    def segment_t2(values, own, got):
        first, table, patch_rel = values
        middle, normed, _ = attend_forward(first, table, 1, *attn_weights(own, got, 0), False)
        (second,) = feed_forward(normed, middle, *mlp_weights(own, got, 4 * width), False)
        return make_target(first, second, seqs), patch_rel

    def segment_s0(values, own, got):
        target, patch_rel = values
        patch = Weight(own, got, 0, width)
        states, table = embed(flat_patch, mask_flat, mover, patch, small_of(own, got), False)
        weights = attn_weights(own, got, width)
        middle, normed, saved = attend_forward(states, table, 0, *weights, True)
        saved_attn[0] = (weights[0], saved)
        return target, patch_rel, table, middle, normed

    def segment_s1(values, own, got):
        target, patch_rel, table, middle, normed = values
        weights = mlp_weights(own, got, 0)
        states, active, slope = feed_forward(normed, middle, *weights, True)
        saved_mlp[0] = (weights, middle, normed, active, slope)
        return target, patch_rel, table, states

    def segment_s2(values, own, got):
        target, patch_rel, table, states = values
        weights = attn_weights(own, got, 0)
        middle, normed, saved = attend_forward(states, table, 1, *weights, True)
        saved_attn[1] = (weights[0], saved)
        return target, patch_rel, table, middle, normed, own, got

    segments = [segment_t0, segment_t1, segment_t2, segment_s0, segment_s1, segment_s2]
    pump = Pump(plan)
    arrived = []
    values = ()
    total_chunks = len(waiting)
    for tick in range(total_chunks + len(plan.stages)):
        if waiting:
            pump.add(gather_steps(plan, waiting[0]), arrived.append)
            waiting = waiting[1:]
        pump.begin()
        place = tick - len(plan.stages)
        if 0 <= place < len(segments):
            own = arrived[place]
            values = segments[place](values, own, plan.swap(own, plan.core_stage))
        values, waiting = pump.end((values, waiting))
    target, patch_rel, table, middle, normed, head_own, head_got = values
    own = arrived[-1]
    weights = mlp_weights(own, plan.swap(own, plan.core_stage), 0)
    states, active, slope = feed_forward(normed, middle, *weights, True)
    saved_mlp[1] = (weights, middle, normed, active, slope)
    flow, final_normed, grad_pred, grad_gain_final, loss_row = head_step(
        states,
        table,
        mover,
        Weight(head_own, head_got, 4 * width, width),
        target,
        mask_flat,
        total_masked,
    )
    loss_local = jnp.sum(loss_row) / total_masked

    gain_ones = [None] * LAYERS
    gain_twos = [None] * LAYERS
    attn_shards = [None] * LAYERS
    mlp_shards = [None] * LAYERS
    extra_pairs = [(final_normed, [grad_pred])]
    for layer in reversed(range(LAYERS)):
        w_qkv, (states, normed_one, projected, mixed_rel, w_out_rel) = saved_attn[layer]
        (w_up, w_down), middle, normed_two, active, slope = saved_mlp[layer]
        grad_hidden, grad_down, grad_middle, grad_branch, gain_twos[layer] = feed_back(
            flow, slope, middle, table, LAYERS + layer, w_up, w_down
        )
        piece = weight_grads([(normed_two, [grad_hidden]), (grad_down, [active])])
        piece, grad_middle, grad_branch = pump.end((piece, grad_middle, grad_branch))
        pump.add(
            scatter_steps(plan, [piece]),
            lambda out, layer=layer: mlp_shards.__setitem__(layer, out),
        )
        pump.begin()
        grad_mixed, branch_whole = mix_back(grad_branch, w_out_rel, mover)
        grad_proj = attend_back(projected, grad_mixed.reshape(seqs, tokens, width))
        grad_proj, branch_whole = pump.end((tuple(grad_proj), branch_whole))
        grad_proj = [part.reshape(-1, width) for part in grad_proj]
        pump.begin()
        results = project_back(
            grad_proj,
            grad_middle,
            states,
            table,
            layer,
            w_qkv,
            mover,
            None if layer else mask_flat,
        )
        flow, gain_ones[layer] = results[:2]
        if layer == 0:
            grad_embed, grad_maskvec = results[2:]
            extra_pairs = [(patch_rel, [grad_embed])]
        pieces = [
            weight_grads([(normed_one, grad_proj), (mixed_rel, [branch_whole])] + extra_pairs)
        ]
        if layer == 0:
            vectors = gain_ones + gain_twos + [grad_gain_final, grad_maskvec]
            pieces.append(small_grads(flow, vectors, seqs))
        pieces, flow = pump.end((pieces, flow))
        pump.add(
            scatter_steps(plan, pieces),
            lambda out, layer=layer: attn_shards.__setitem__(layer, out),
        )
        if layer:
            pump.begin()
    pump.drain()
    last, first = attn_shards
    raw = (
        jnp.concatenate([last[:, 4 * width : 5 * width], first[:, 4 * width :]], axis=1),
        jnp.concatenate([last[:, : 4 * width], first[:, : 4 * width]], axis=1),
        jnp.concatenate(mlp_shards, axis=1),
        last[:, 5 * width : 5 * width + tokens],
        last[:, 5 * width + tokens : 5 * width + small_cols],
    )
    totals = jnp.stack([loss_local] + [jnp.sum(part * part) for part in raw])
    totals = jnp.broadcast_to(totals[:, None], (totals.shape[0], LANES))
    for perm in [plan.core_stage] + plan.stages:
        totals = totals + plan.swap(totals, perm)
    total_loss = totals[0, 0]
    clipped = []
    for group, part in enumerate(raw):
        limit = entry_clip * jnp.sqrt(jnp.float32(part.size * plan.count))
        norm_value = jnp.sqrt(totals[group + 1, 0])
        clipped.append(part * (limit / jnp.maximum(norm_value, limit)))
    edge_new = adam_step(edge_w, edge_m, edge_v, edge_t, clipped[0])
    attn_new = adam_step(attn_w, attn_m, attn_v, attn_t, clipped[1])
    mlp_new = adam_step(mlp_w, mlp_m, mlp_v, mlp_t, clipped[2])
    posit_new = adam_step(posit_w, posit_m, posit_v, posit_t, clipped[3])
    vecs_new = adam_step(vecs_w, vecs_m, vecs_v, vecs_t, clipped[4])
    news = (edge_new, attn_new, mlp_new, posit_new, vecs_new)
    return (total_loss,) + tuple(group[part] for part in range(4) for group in news)


def solution(mesh):
    rows = P(AXES, None)
    in_specs = (P(AXES, None, None),) + (rows,) * 21
    out_specs = (P(),) + (rows,) * 20
    return jax.shard_map(local, mesh=mesh, in_specs=in_specs, out_specs=out_specs, check_vma=False)
```

time: 1180 us -> 929 us (0.79)
  Pallas kernels: 117 us -> 430 us
  matrix products: 261 us -> 0 us
  local copies, waits for them, and re-layouts: 261 us -> 73.4 us
  other arithmetic: 201 us -> 113 us
  waiting for transfers between devices: 271 us -> 240 us
    pallas_call x0 -> x27, Pallas kernels: none -> 314 us  [the longest x4 70.9 us: feed_forward(): pl.pallas_call(kernel, grid=(steps,), in_specs=[whole_block(normed.shape)...]
    dot_general x58 -> x0, matrix products: 261 us -> none  [contract(): lax.dot_general(left, right, (((left_dim,), (right_dim,)), ((), ())), pre...]
    slice x43 -> x13, local copies, waits for them, and re-layouts: 80.6 us -> 9.21 us  [the longest x4 3.96 us: small_of(): return (own[:, start:], got[:, start:])]
    unnamed x329 -> x185, local copies, waits for them, and re-layouts: 73.1 us -> 41 us
    ppermute x67 -> x61, waiting for transfers between devices: 271 us -> 240 us  [swap(): return lax.ppermute(value, AXES, perm)]
    concatenate x11 -> x4, other arithmetic: 28.4 us -> 2.07 us  [the longest x1 1.3 us: scatter_steps(): send = jnp.concatenate([part for part, _ in sums], axis=1)]
    optimization_barrier x9 -> x0, local copies, waits for them, and re-layouts: 25 us -> none  [end(): flying, values = lax.optimization_barrier((self.flying, values))]
    reduce_sum x20 -> x1, other arithmetic: 22.2 us -> 0.61 us  [local(): loss_local = jnp.sum(loss_row) / total_masked]
  transfers between devices with their start and end apart: 67 -> 61, of which waited for: 24 -> 27; matrix products, arithmetic and copies ran while one was open for 41% -> 12% of each run, Pallas kernels for 10% -> 39%
where the time goes in v3:
time: 929 us; the launch traced here: 920 us
  Pallas kernels  430 us (46%)
  waiting for transfers between devices  240 us (26%)
  other arithmetic  113 us (12%)
  local copies, waits for them, and re-layouts  73.4 us (8%)
  starting transfers between devices  57.4 us (6%)
    ppermute x61, waiting for transfers between devices, swap(): return lax.ppermute(value, AXES, perm)  240 us
    pallas_call x4, Pallas kernels, feed_forward(): pl.pallas_call(kernel, grid=(steps,), in_specs=[whole_block(normed.shape)...  70.9 us
    pallas_call x4, Pallas kernels, weight_grads(): pl.pallas_call(kernel, grid=(total,), in_specs=specs, out_specs=[block, b...  66.1 us
    pallas_call x4, Pallas kernels, attend(): pl.pallas_call(attend_kernel, grid=(seqs, blocks), in_specs=qkv_specs(tok...  65.9 us
    ppermute x61, starting transfers between devices, swap(): return lax.ppermute(value, AXES, perm)  57.4 us
    pallas_call x2, Pallas kernels, attend_back(): pl.pallas_call(attend_back_kernel, grid=(seqs, blocks), in_specs=qkv_spec...  50.4 us
    pallas_call x2, Pallas kernels, feed_back(): pl.pallas_call(kernel, grid=(steps,), in_specs=[full, column, full, whole...  42.5 us
    unnamed x185, local copies, waits for them, and re-layouts  41 us
  transfers between devices with their start and end apart: 61, of which 27 were waited for; matrix products, arithmetic and copies ran while one was open for 12% of the time, Pallas kernels for 39%

profile of v3, /device:TPU:0, one launch (start us, length us, event | category | flops | bytes accessed | tf_op | source)
XLA Modules:
  0.0 920.3 jit_solution(14214533373273540571)
XLA Ops:
  25.9 11.2 %collective-permute-done.2 = bf16[24,6144]{1,0:T(8,128)(2,1)S(1)} collective-permute-done((bf16[24,6144]{1,0:T(8,128)(2,1)S(1)}, bf16[24,6144]{1,0:T(8,128)(2,1)S(1)}, u32[]{:S(2)}, u32[]{:S(2)}) %collective-permute-start.2) | collective-permute-done | bytes 294944 | tf_op jit(solution)/shard_map/ppermute | solution.py:700
  47.5 13.9 %collective-permute-done.5 = bf16[24,9216]{1,0:T(8,128)(2,1)S(1)} collective-permute-done((bf16[24,9216]{1,0:T(8,128)(2,1)S(1)}, bf16[24,9216]{1,0:T(8,128)(2,1)S(1)}, u32[]{:S(2)}, u32[]{:S(2)}) %collective-permute-start.5) | collective-permute-done | bytes 442400 | tf_op jit(solution)/shard_map/ppermute | solution.py:700
  73.8 18.7 %collective-permute-done.9 = bf16[24,4352]{1,0:T(8,128)(2,1)S(1)} collective-permute-done((bf16[24,4352]{1,0:T(8,128)(2,1)S(1)}, bf16[24,4352]{1,0:T(8,128)(2,1)S(1)}, u32[]{:S(2)}, u32[]{:S(2)}) %collective-permute-start.9) | collective-permute-done | bytes 208928 | tf_op jit(solution)/shard_map/ppermute | solution.py:700
  120.4 8.5 norm_project.4
  128.9 16.3 %attend.4 = bf16[2,448,768]{2,1,0:T(8,128)(2,1)} custom-call(bf16[2,448,2304]{2,1,0:T(8,128)(2,1)} %bitcast.31, bf16[2,448,2304]{2,1,0:T(8,128)(2,1)} %bitcast.32, bf16[2,448,2304]{2,1,0:T(8,128)(2,1)} %bitcast.33), custom_call_target="tpu_custom_call" | custom-call | flops 4932501504 | bytes 5505024 | tf_op jit(solution)/shard_map/attend/pallas_call | solution.py:103
  172.7 16.6 %feed_forward.4.h_ref.one_ref = f32[896,768]{1,0:T(8,128)} custom-call(bf16[896,768]{1,0:T(8,128)(2,1)} %get-tuple-element.249.b_ref, f32[896,768]{1,0:T(8,128)} %get-tuple-element.250.m_ref, bf16[384,6144]{1,0:T(8,128)(2,1)} %constant_dynamic-update-slice_fusion.5.uown_ref.down_ref, bf16[384,6144]{1,0:T(8,128)(2,1)} %collective-permute-done.19.ugot_ref.dgot_ref, ...), custom_call_target="tpu_custom_call" | custom-call | flops 8455716864 | bytes 46006272 | tf_op jit(solution)/shard_map/feed_forward/pallas_call | solution.py:347
  189.3 21.9 %collective-permute-done.15 = bf16[192,9216]{1,0:T(8,128)(2,1)} collective-permute-done((bf16[192,9216]{1,0:T(8,128)(2,1)}, bf16[192,9216]{1,0:T(8,128)(2,1)}, u32[]{:S(2)}, u32[]{:S(2)}) %collective-permute-start.15) | collective-permute-done | bytes 3538976 | tf_op jit(solution)/shard_map/ppermute | solution.py:700
  240.1 16.7 %attend.5 = bf16[2,448,768]{2,1,0:T(8,128)(2,1)} custom-call(bf16[2,448,2304]{2,1,0:T(8,128)(2,1)} %bitcast.34, bf16[2,448,2304]{2,1,0:T(8,128)(2,1)} %bitcast.35, bf16[2,448,2304]{2,1,0:T(8,128)(2,1)} %bitcast.36), custom_call_target="tpu_custom_call" | custom-call | flops 4932501504 | bytes 5505024 | tf_op jit(solution)/shard_map/attend/pallas_call | solution.py:103
  264.6 16.5 %feed_forward.5.two_ref = f32[896,768]{1,0:T(8,128)} custom-call(bf16[896,768]{1,0:T(8,128)(2,1)} %get-tuple-element.262.b_ref, f32[896,768]{1,0:T(8,128)} %get-tuple-element.263.m_ref, bf16[384,9216]{1,0:T(8,128)(2,1)} %constant_dynamic-update-slice_fusion.10.own_ref.uown_ref.down_ref, bf16[384,9216]{1,0:T(8,128)(2,1)} %collective-permute-done.24.got_ref.ugot_ref.dgot_ref, ...), custom_call_target="tpu_custom_call" | custom-call | flops 8455716864 | bytes 46006272 | tf_op jit(solution)/shard_map/feed_forward/pallas_call | solution.py:347
  311.5 8.4 norm_project.6
  319.8 16.5 %attend.6 = bf16[2,448,768]{2,1,0:T(8,128)(2,1)} custom-call(bf16[2,448,2304]{2,1,0:T(8,128)(2,1)} %bitcast.54, bf16[2,448,2304]{2,1,0:T(8,128)(2,1)} %bitcast.55, bf16[2,448,2304]{2,1,0:T(8,128)(2,1)} %bitcast.56), custom_call_target="tpu_custom_call" | custom-call | flops 4932501504 | bytes 5505024 | tf_op jit(solution)/shard_map/attend/pallas_call | solution.py:103
  358.1 19.0 %feed_forward.6 = (f32[896,768]{1,0:T(8,128)}, bf16[896,3072]{1,0:T(8,128)(2,1)}, f32[896,3072]{1,0:T(8,128)}) custom-call(bf16[896,768]{1,0:T(8,128)(2,1)} %get-tuple-element.281.b_ref.refs_0_, f32[896,768]{1,0:T(8,128)} %get-tuple-element.282.m_ref, bf16[384,6144]{1,0:T(8,128)(2,1)} %constant_dynamic-update-slice_fusion.20.uown_ref.down_ref, ...), custom_call_target="tpu_custom_call" | custom-call | flops 8455716864 | bytes 46006272 | tf_op jit(solution)/shard_map/feed_forward/pallas_call | solution.py:347
  406.2 16.3 %attend.7 = bf16[2,448,768]{2,1,0:T(8,128)(2,1)} custom-call(bf16[2,448,2304]{2,1,0:T(8,128)(2,1)} %bitcast.60, bf16[2,448,2304]{2,1,0:T(8,128)(2,1)} %bitcast.61, bf16[2,448,2304]{2,1,0:T(8,128)(2,1)} %bitcast.62), custom_call_target="tpu_custom_call" | custom-call | flops 4932501504 | bytes 5505024 | tf_op jit(solution)/shard_map/attend/pallas_call | solution.py:103
  442.3 18.8 %feed_forward.7 = (f32[896,768]{1,0:T(8,128)}, bf16[896,3072]{1,0:T(8,128)(2,1)}, f32[896,3072]{1,0:T(8,128)}) custom-call(bf16[896,768]{1,0:T(8,128)(2,1)} %get-tuple-element.301.b_ref.refs_0_, f32[896,768]{1,0:T(8,128)} %get-tuple-element.302.m_ref, bf16[384,6144]{1,0:T(8,128)(2,1)} %constant_dynamic-update-slice_fusion.30.uown_ref.down_ref, ...), custom_call_target="tpu_custom_call" | custom-call | flops 8455716864 | bytes 46006272 | tf_op jit(solution)/shard_map/feed_forward/pallas_call | solution.py:347
  461.1 10.4 %head_step.1 = (f32[896,768]{1,0:T(8,128)}, bf16[896,768]{1,0:T(8,128)(2,1)}, bf16[896,768]{1,0:T(8,128)(2,1)}, f32[1,768]{1,0:T(1,128)}, f32[1,768]{1,0:T(1,128)}) custom-call(f32[896,768]{1,0:T(8,128)} %get-tuple-element.304.h_ref, f32[8,768]{1,0:T(8,128)} %get-tuple-element.305.table_ref.refs_11_, bf16[768,768]{1,0:T(8,128)(2,1)} %fusion.refs_1_.mover_ref.refs_12_, ...), custom_call_target="tpu_custom_call" | custom-call | flops 4227858432 | bytes 11010048 | tf_op jit(solution)/shard_map/head_step/pallas_call | solution.py:426
  471.5 21.2 %feed_back.2 = (bf16[896,3072]{1,0:T(8,128)(2,1)}, bf16[896,768]{1,0:T(8,128)(2,1)}, f32[896,768]{1,0:T(8,128)}, bf16[896,768]{1,0:T(8,128)(2,1)}, f32[1,768]{1,0:T(1,128)}) custom-call(f32[896,768]{1,0:T(8,128)} %get-tuple-element.310.flow_ref, f32[896,3072]{1,0:T(8,128)} %get-tuple-element.311.slope_ref, f32[896,768]{1,0:T(8,128)} %get-tuple-element.302.m_ref, ...), custom_call_target="tpu_custom_call" | custom-call | flops 8455716864 | bytes 46399488 | tf_op jit(solution)/shard_map/feed_back/pallas_call | solution.py:486
  492.7 18.8 %weight_grads.4 = (f32[384,6144]{1,0:T(8,128)}, f32[384,6144]{1,0:T(8,128)}) custom-call(bf16[896,768]{1,0:T(8,128)(2,1)} %get-tuple-element.301.b_ref.refs_0_, bf16[896,768]{1,0:T(8,128)(2,1)} %get-tuple-element.312.refs_1_, bf16[896,3072]{1,0:T(8,128)(2,1)} %get-tuple-element.313.refs_2_, bf16[896,3072]{1,0:T(8,128)(2,1)} %get-tuple-element.314.refs_3_), custom_call_target="tpu_custom_call" | custom-call | flops 8455716864 | bytes 29884416 | tf_op jit(solution)/shard_map/weight_grads/pallas_call | solution.py:638
  518.0 25.2 %attend_back.2 = (bf16[2,448,768]{2,1,0:T(8,128)(2,1)}, bf16[2,448,768]{2,1,0:T(8,128)(2,1)}, bf16[2,448,768]{2,1,0:T(8,128)(2,1)}) custom-call(bf16[2,448,2304]{2,1,0:T(8,128)(2,1)} %bitcast.63, bf16[2,448,2304]{2,1,0:T(8,128)(2,1)} %bitcast.64, bf16[2,448,2304]{2,1,0:T(8,128)(2,1)} %bitcast.65, bf16[2,448,768]{2,1,0:T(8,128)(2,1)} %bitcast.66), custom_call_target="tpu_custom_call" | custom-call | flops 9865003008 | bytes 9633792 | tf_op jit(solution)/shard_map/attend_back/pallas_call | solution.py:124
  543.2 9.3 %slice_add_fusion.1 = (f32[192,6144]{1,0:T(8,128)}, bf16[192,6144]{1,0:T(8,128)(2,1)S(1)}) fusion(f32[384,6144]{1,0:T(8,128)} %collective-permute-done.35, f32[384,6144]{1,0:T(8,128)} %get-tuple-element.319), kind=kLoop, calls=%fused_computation.3 | loop fusion | flops 3538944 | bytes 25952256 | tf_op jit(solution)/shard_map/add | solution.py:767
  554.3 9.6 %project_back.2 = (f32[896,768]{1,0:T(8,128)}, f32[1,768]{1,0:T(1,128)}) custom-call(bf16[896,768]{1,0:T(8,128)(2,1)} %bitcast.45, bf16[896,768]{1,0:T(8,128)(2,1)} %bitcast.47, bf16[896,768]{1,0:T(8,128)(2,1)} %bitcast.49, bf16[384,3840]{1,0:T(8,128)(2,1)} %copy-done.2, bf16[384,3840]{1,0:T(8,128)(2,1)} %collective-permute-done.33.got_ref.refs_4_.refs_6_.refs_8_, ...), custom_call_target="tpu_custom_call" | custom-call | flops 3170893824 | bytes 15138816 | tf_op jit(solution)/shard_map/project_back/pallas_call | solution.py:582
  563.9 14.4 %weight_grads.5 = (f32[384,3840]{1,0:T(8,128)}, f32[384,3840]{1,0:T(8,128)}) custom-call(bf16[896,768]{1,0:T(8,128)(2,1)} %get-tuple-element.329.refs_0_, bf16[896,768]{1,0:T(8,128)(2,1)} %get-tuple-element.330.refs_1_, bf16[896,768]{1,0:T(8,128)(2,1)} %get-tuple-element.331.refs_2_, bf16[896,768]{1,0:T(8,128)(2,1)} %bitcast.46, bf16[896,768]{1,0:T(8,128)(2,1)} %bitcast.48, ...), custom_call_target="tpu_custom_call" | custom-call | flops 5284823040 | bytes 18677760 | tf_op jit(solution)/shard_map/weight_grads/pallas_call | solution.py:638
  589.1 21.3 %feed_back.3 = (bf16[896,3072]{1,0:T(8,128)(2,1)}, bf16[896,768]{1,0:T(8,128)(2,1)}, f32[896,768]{1,0:T(8,128)}, bf16[896,768]{1,0:T(8,128)(2,1)}, f32[1,768]{1,0:T(1,128)}) custom-call(f32[896,768]{1,0:T(8,128)} %get-tuple-element.343.flow_ref, f32[896,3072]{1,0:T(8,128)} %get-tuple-element.344.slope_ref, f32[896,768]{1,0:T(8,128)} %get-tuple-element.282.m_ref, ...), custom_call_target="tpu_custom_call" | custom-call | flops 8455716864 | bytes 46399488 | tf_op jit(solution)/shard_map/feed_back/pallas_call | solution.py:486
  610.4 18.5 %weight_grads.6 = (f32[384,6144]{1,0:T(8,128)}, f32[384,6144]{1,0:T(8,128)}) custom-call(bf16[896,768]{1,0:T(8,128)(2,1)} %get-tuple-element.281.b_ref.refs_0_, bf16[896,768]{1,0:T(8,128)(2,1)} %get-tuple-element.345.refs_1_, bf16[896,3072]{1,0:T(8,128)(2,1)} %get-tuple-element.346.refs_2_, bf16[896,3072]{1,0:T(8,128)(2,1)} %get-tuple-element.347.refs_3_), custom_call_target="tpu_custom_call" | custom-call | flops 8455716864 | bytes 29884416 | tf_op jit(solution)/shard_map/weight_grads/pallas_call | solution.py:638
  647.1 25.2 %attend_back.3 = (bf16[2,448,768]{2,1,0:T(8,128)(2,1)}, bf16[2,448,768]{2,1,0:T(8,128)(2,1)}, bf16[2,448,768]{2,1,0:T(8,128)(2,1)}) custom-call(bf16[2,448,2304]{2,1,0:T(8,128)(2,1)} %bitcast.57, bf16[2,448,2304]{2,1,0:T(8,128)(2,1)} %bitcast.58, bf16[2,448,2304]{2,1,0:T(8,128)(2,1)} %bitcast.59, bf16[2,448,768]{2,1,0:T(8,128)(2,1)} %bitcast.67), custom_call_target="tpu_custom_call" | custom-call | flops 9865003008 | bytes 9633792 | tf_op jit(solution)/shard_map/attend_back/pallas_call | solution.py:124
  673.8 10.2 %slice_add_fusion = (f32[192,6144]{1,0:T(8,128)}, bf16[192,6144]{1,0:T(8,128)(2,1)}) fusion(f32[384,6144]{1,0:T(8,128)} %collective-permute-done.41, f32[384,6144]{1,0:T(8,128)} %get-tuple-element.365), kind=kLoop, calls=%fused_computation | loop fusion | flops 3538944 | bytes 25952256 | tf_op jit(solution)/shard_map/add | solution.py:767
  689.4 13.1 %project_back.3 = (f32[896,768]{1,0:T(8,128)}, f32[1,768]{1,0:T(1,128)}, bf16[896,768]{1,0:T(8,128)(2,1)}, f32[1,768]{1,0:T(1,128)}) custom-call(bf16[896,768]{1,0:T(8,128)(2,1)} %bitcast.37, bf16[896,768]{1,0:T(8,128)(2,1)} %bitcast.39, bf16[896,768]{1,0:T(8,128)(2,1)} %bitcast.41, bf16[384,4352]{1,0:T(8,128)(2,1)} %copy-done, bf16[384,4352]{1,0:T(8,128)(2,1)} %copy-done.1, ...), custom_call_target="tpu_custom_call" | custom-call | flops 3170893824 | bytes 15138816 | tf_op jit(solution)/shard_map/project_back/pallas_call | solution.py:582
  705.9 14.4 %weight_grads.7 = (f32[384,3840]{1,0:T(8,128)}, f32[384,3840]{1,0:T(8,128)}) custom-call(bf16[896,768]{1,0:T(8,128)(2,1)} %get-tuple-element.367.refs_0_, bf16[896,768]{1,0:T(8,128)(2,1)} %get-tuple-element.368.refs_1_, bf16[896,768]{1,0:T(8,128)(2,1)} %get-tuple-element.369.refs_2_, bf16[896,768]{1,0:T(8,128)(2,1)} %bitcast.38, bf16[896,768]{1,0:T(8,128)(2,1)} %bitcast.40, ...), custom_call_target="tpu_custom_call" | custom-call | flops 5284823040 | bytes 18677760 | tf_op jit(solution)/shard_map/weight_grads/pallas_call | solution.py:638
  736.7 18.6 %collective-permute-done.45 = f32[48,3840]{1,0:T(8,128)S(1)} collective-permute-done((f32[48,3840]{1,0:T(8,128)S(1)}, f32[48,3840]{1,0:T(8,128)S(1)}, u32[]{:S(2)}, u32[]{:S(2)}) %collective-permute-start.45) | collective-permute-done | bytes 737312 | tf_op jit(solution)/shard_map/ppermute | solution.py:700
  773.2 28.8 %collective-permute-done.49 = f32[24,3840]{1,0:T(8,128)} collective-permute-done((f32[24,3840]{1,0:T(8,128)}, f32[24,3840]{1,0:T(8,128)}, u32[]{:S(2)}, u32[]{:S(2)}) %collective-permute-start.49) | collective-permute-done | bytes 368672 | tf_op jit(solution)/shard_map/ppermute | solution.py:700
  810.8 24.7 %collective-permute-done.52 = f32[24,6144]{1,0:T(8,128)S(1)} collective-permute-done((f32[24,6144]{1,0:T(8,128)S(1)}, f32[24,6144]{1,0:T(8,128)S(1)}, u32[]{:S(2)}, u32[]{:S(2)}) %collective-permute-start.52) | collective-permute-done | bytes 589856 | tf_op jit(solution)/shard_map/ppermute | solution.py:700
  838.0 18.0 %collective-permute-done.54 = f32[48,4352]{1,0:T(8,128)S(1)} collective-permute-done((f32[48,4352]{1,0:T(8,128)S(1)}, f32[48,4352]{1,0:T(8,128)S(1)}, u32[]{:S(2)}, u32[]{:S(2)}) %collective-permute-start.54) | collective-permute-done | bytes 835616 | tf_op jit(solution)/shard_map/ppermute | solution.py:700
  858.4 17.9 %collective-permute-done.55 = f32[24,4352]{1,0:T(8,128)S(1)} collective-permute-done((f32[24,4352]{1,0:T(8,128)S(1)}, f32[24,4352]{1,0:T(8,128)S(1)}, u32[]{:S(2)}, u32[]{:S(2)}) %collective-permute-start.55) | collective-permute-done | bytes 417824 | tf_op jit(solution)/shard_map/ppermute | solution.py:700
  (416 shorter events, 374.8 us)
Async XLA Ops:
  68.9 32.7 %collective-permute-start.6 = (bf16[192,4352]{1,0:T(8,128)(2,1)S(1)}, bf16[192,4352]{1,0:T(8,128)(2,1)S(1)}, u32[]{:S(2)}, u32[]{:S(2)}) collective-permute-start(bf16[192,4352]{1,0:T(8,128)(2,1)S(1)} %pad_maximum_fusion.6), channel_id=1, source_target_pairs={{0,1},{1,0},{2,6},{3,7},{4,5},{5,4},{6,2},{7,3},{8,9},{9,8},{10,14... | collective-permute-start | bytes 5013512 | tf_op jit(solution)/shard_map/ppermute | solution.py:700
  69.6 29.0 %collective-permute-start.7 = (bf16[96,6144]{1,0:T(8,128)(2,1)S(1)}, bf16[96,6144]{1,0:T(8,128)(2,1)S(1)}, u32[]{:S(2)}, u32[]{:S(2)}) collective-permute-start(bf16[96,6144]{1,0:T(8,128)(2,1)S(1)} %pad_maximum_fusion.10), channel_id=1, source_target_pairs={{0,4},{1,5},{2,3},{3,2},{4,0},{5,1},{6,7},{7,6},{8,12},{9,13},{10,... | collective-permute-start | bytes 3538952 | tf_op jit(solution)/shard_map/ppermute | solution.py:700
  104.5 48.5 %collective-permute-start.10 = (bf16[192,6144]{1,0:T(8,128)(2,1)}, bf16[192,6144]{1,0:T(8,128)(2,1)}, u32[]{:S(2)}, u32[]{:S(2)}) collective-permute-start(bf16[192,6144]{1,0:T(8,128)(2,1)} %pad_maximum_fusion.1), channel_id=1, source_target_pairs={{0,1},{1,0},{2,6},{3,7},{4,5},{5,4},{6,2},{7,3},{8,9},{9,8},{10,14... | collective-permute-start | bytes 7077896 | tf_op jit(solution)/shard_map/ppermute | solution.py:700
  106.1 46.8 %collective-permute-start.11 = (bf16[96,9216]{1,0:T(8,128)(2,1)}, bf16[96,9216]{1,0:T(8,128)(2,1)}, u32[]{:S(2)}, u32[]{:S(2)}) collective-permute-start(bf16[96,9216]{1,0:T(8,128)(2,1)} %pad_maximum_fusion.4), channel_id=1, source_target_pairs={{0,4},{1,5},{2,3},{3,2},{4,0},{5,1},{6,7},{7,6},{8,12},{9,13},{10,... | collective-permute-start | bytes 5308424 | tf_op jit(solution)/shard_map/ppermute | solution.py:700
  107.2 45.7 %collective-permute-start.12 = (bf16[48,4352]{1,0:T(8,128)(2,1)}, bf16[48,4352]{1,0:T(8,128)(2,1)}, u32[]{:S(2)}, u32[]{:S(2)}) collective-permute-start(bf16[48,4352]{1,0:T(8,128)(2,1)} %pad_maximum_fusion.24), channel_id=1, source_target_pairs={{0,8},{1,9},{2,10},{3,11},{4,12},{5,13},{6,14},{7,15},{8,0},{9,1},... | collective-permute-start | bytes 1253384 | tf_op jit(solution)/shard_map/ppermute | solution.py:700
  107.2 45.7 %collective-permute-start.13 = (bf16[24,6144]{1,0:T(8,128)(2,1)}, bf16[24,6144]{1,0:T(8,128)(2,1)}, u32[]{:S(2)}, u32[]{:S(2)}) collective-permute-start(bf16[24,6144]{1,0:T(8,128)(2,1)} %get-tuple-element.236), channel_id=1, source_target_pairs={{0,16},{1,17},{2,18},{3,19},{4,20},{5,21},{6,22},{7,23},{8,24},{9,... | collective-permute-start | bytes 884744 | tf_op jit(solution)/shard_map/ppermute | solution.py:700
  160.4 50.8 %collective-permute-start.15 = (bf16[192,9216]{1,0:T(8,128)(2,1)}, bf16[192,9216]{1,0:T(8,128)(2,1)}, u32[]{:S(2)}, u32[]{:S(2)}) collective-permute-start(bf16[192,9216]{1,0:T(8,128)(2,1)} %pad_maximum_fusion), channel_id=1, source_target_pairs={{0,1},{1,0},{2,6},{3,7},{4,5},{5,4},{6,2},{7,3},{8,9},{9,8},{10,14... | collective-permute-start | bytes 10616840 | tf_op jit(solution)/shard_map/ppermute | solution.py:700
  222.7 63.7 %collective-permute-start.20 = (bf16[192,4352]{1,0:T(8,128)(2,1)}, bf16[192,4352]{1,0:T(8,128)(2,1)}, u32[]{:S(2)}, u32[]{:S(2)}) collective-permute-start(bf16[192,4352]{1,0:T(8,128)(2,1)} %pad_maximum_fusion.7), channel_id=1, source_target_pairs={{0,1},{1,0},{2,6},{3,7},{4,5},{5,4},{6,2},{7,3},{8,9},{9,8},{10,14... | collective-permute-start | bytes 5013512 | tf_op jit(solution)/shard_map/ppermute | solution.py:700
  226.6 59.8 %collective-permute-start.21 = (bf16[96,6144]{1,0:T(8,128)(2,1)}, bf16[96,6144]{1,0:T(8,128)(2,1)}, u32[]{:S(2)}, u32[]{:S(2)}) collective-permute-start(bf16[96,6144]{1,0:T(8,128)(2,1)} %pad_maximum_fusion.11), channel_id=1, source_target_pairs={{0,4},{1,5},{2,3},{3,2},{4,0},{5,1},{6,7},{7,6},{8,12},{9,13},{10,... | collective-permute-start | bytes 3538952 | tf_op jit(solution)/shard_map/ppermute | solution.py:700
  229.1 57.3 %collective-permute-start.22 = (bf16[48,3840]{1,0:T(8,128)(2,1)}, bf16[48,3840]{1,0:T(8,128)(2,1)}, u32[]{:S(2)}, u32[]{:S(2)}) collective-permute-start(bf16[48,3840]{1,0:T(8,128)(2,1)} %pad_maximum_fusion.25), channel_id=1, source_target_pairs={{0,8},{1,9},{2,10},{3,11},{4,12},{5,13},{6,14},{7,15},{8,0},{9,1},... | collective-permute-start | bytes 1105928 | tf_op jit(solution)/shard_map/ppermute | solution.py:700
  229.1 57.3 %collective-permute-start.23 = (bf16[24,6144]{1,0:T(8,128)(2,1)}, bf16[24,6144]{1,0:T(8,128)(2,1)}, u32[]{:S(2)}, u32[]{:S(2)}) collective-permute-start(bf16[24,6144]{1,0:T(8,128)(2,1)} %get-tuple-element.255), channel_id=1, source_target_pairs={{0,16},{1,17},{2,18},{3,19},{4,20},{5,21},{6,22},{7,23},{8,24},{9,... | collective-permute-start | bytes 884744 | tf_op jit(solution)/shard_map/ppermute | solution.py:700
  294.9 49.4 %collective-permute-start.25 = (bf16[192,6144]{1,0:T(8,128)(2,1)}, bf16[192,6144]{1,0:T(8,128)(2,1)}, u32[]{:S(2)}, u32[]{:S(2)}) collective-permute-start(bf16[192,6144]{1,0:T(8,128)(2,1)} %pad_maximum_fusion.2), channel_id=1, source_target_pairs={{0,1},{1,0},{2,6},{3,7},{4,5},{5,4},{6,2},{7,3},{8,9},{9,8},{10,14... | collective-permute-start | bytes 7077896 | tf_op jit(solution)/shard_map/ppermute | solution.py:700
  297.1 47.2 %collective-permute-start.26 = (bf16[96,3840]{1,0:T(8,128)(2,1)}, bf16[96,3840]{1,0:T(8,128)(2,1)}, u32[]{:S(2)}, u32[]{:S(2)}) collective-permute-start(bf16[96,3840]{1,0:T(8,128)(2,1)} %pad_maximum_fusion.17), channel_id=1, source_target_pairs={{0,4},{1,5},{2,3},{3,2},{4,0},{5,1},{6,7},{7,6},{8,12},{9,13},{10,... | collective-permute-start | bytes 2211848 | tf_op jit(solution)/shard_map/ppermute | solution.py:700
  299.3 45.0 %collective-permute-start.27 = (bf16[48,6144]{1,0:T(8,128)(2,1)}, bf16[48,6144]{1,0:T(8,128)(2,1)}, u32[]{:S(2)}, u32[]{:S(2)}) collective-permute-start(bf16[48,6144]{1,0:T(8,128)(2,1)} %pad_maximum_fusion.20), channel_id=1, source_target_pairs={{0,8},{1,9},{2,10},{3,11},{4,12},{5,13},{6,14},{7,15},{8,0},{9,1},... | collective-permute-start | bytes 1769480 | tf_op jit(solution)/shard_map/ppermute | solution.py:700
  351.2 32.1 %collective-permute-start.29 = (bf16[192,3840]{1,0:T(8,128)(2,1)}, bf16[192,3840]{1,0:T(8,128)(2,1)}, u32[]{:S(2)}, u32[]{:S(2)}) collective-permute-start(bf16[192,3840]{1,0:T(8,128)(2,1)} %pad_maximum_fusion.9), channel_id=1, source_target_pairs={{0,1},{1,0},{2,6},{3,7},{4,5},{5,4},{6,2},{7,3},{8,9},{9,8},{10,14... | collective-permute-start | bytes 4423688 | tf_op jit(solution)/shard_map/ppermute | solution.py:700
  391.8 38.9 %collective-permute-start.32 = (bf16[192,6144]{1,0:T(8,128)(2,1)}, bf16[192,6144]{1,0:T(8,128)(2,1)}, u32[]{:S(2)}, u32[]{:S(2)}) collective-permute-start(bf16[192,6144]{1,0:T(8,128)(2,1)} %pad_maximum_fusion.3), channel_id=1, source_target_pairs={{0,1},{1,0},{2,6},{3,7},{4,5},{5,4},{6,2},{7,3},{8,9},{9,8},{10,14... | collective-permute-start | bytes 7077896 | tf_op jit(solution)/shard_map/ppermute | solution.py:700
  511.5 31.7 %collective-permute-start.35 = (f32[384,6144]{1,0:T(8,128)}, f32[384,6144]{1,0:T(8,128)}, u32[]{:S(2)}, u32[]{:S(2)}) collective-permute-start(f32[384,6144]{1,0:T(8,128)} %get-tuple-element.320), channel_id=1, source_target_pairs={{0,2},{1,3},{2,0},{3,1},{4,6},{5,7},{6,4},{7,5},{8,10},{9,11},{10,... | collective-permute-start | bytes 28311560 | tf_op jit(solution)/shard_map/ppermute | solution.py:700
  552.5 28.9 %collective-permute-start.36 = (bf16[192,6144]{1,0:T(8,128)(2,1)S(1)}, bf16[192,6144]{1,0:T(8,128)(2,1)}, u32[]{:S(2)}, u32[]{:S(2)}) collective-permute-start(bf16[192,6144]{1,0:T(8,128)(2,1)S(1)} %get-tuple-element.489), channel_id=1, source_target_pairs={{0,1},{1,0},{2,6},{3,7},{4,5},{5,4},{6,2},{7,3},{8,9},{9,8},{10,14... | collective-permute-start | bytes 7077896 | tf_op jit(solution)/shard_map/ppermute | solution.py:700
  581.5 47.5 %collective-permute-start.38 = (f32[384,3840]{1,0:T(8,128)}, f32[384,3840]{1,0:T(8,128)}, u32[]{:S(2)}, u32[]{:S(2)}) collective-permute-start(f32[384,3840]{1,0:T(8,128)} %get-tuple-element.342), channel_id=1, source_target_pairs={{0,2},{1,3},{2,0},{3,1},{4,6},{5,7},{6,4},{7,5},{8,10},{9,11},{10,... | collective-permute-start | bytes 17694728 | tf_op jit(solution)/shard_map/ppermute | solution.py:700
  587.3 41.7 %collective-permute-start.37 = (f32[96,6144]{1,0:T(8,128)}, f32[96,6144]{1,0:T(8,128)S(1)}, u32[]{:S(2)}, u32[]{:S(2)}) collective-permute-start(f32[96,6144]{1,0:T(8,128)} %get-tuple-element.496), channel_id=1, source_target_pairs={{0,4},{1,5},{2,3},{3,2},{4,0},{5,1},{6,7},{7,6},{8,12},{9,13},{10,... | collective-permute-start | bytes 7077896 | tf_op jit(solution)/shard_map/ppermute | solution.py:700
  630.4 41.9 %collective-permute-start.41 = (f32[384,6144]{1,0:T(8,128)}, f32[384,6144]{1,0:T(8,128)}, u32[]{:S(2)}, u32[]{:S(2)}) collective-permute-start(f32[384,6144]{1,0:T(8,128)} %get-tuple-element.355), channel_id=1, source_target_pairs={{0,2},{1,3},{2,0},{3,1},{4,6},{5,7},{6,4},{7,5},{8,10},{9,11},{10,... | collective-permute-start | bytes 28311560 | tf_op jit(solution)/shard_map/ppermute | solution.py:700
  636.7 35.5 %collective-permute-start.40 = (bf16[192,3840]{1,0:T(8,128)(2,1)}, bf16[192,3840]{1,0:T(8,128)(2,1)}, u32[]{:S(2)}, u32[]{:S(2)}) collective-permute-start(bf16[192,3840]{1,0:T(8,128)(2,1)} %get-tuple-element.493), channel_id=1, source_target_pairs={{0,1},{1,0},{2,6},{3,7},{4,5},{5,4},{6,2},{7,3},{8,9},{9,8},{10,14... | collective-permute-start | bytes 4423688 | tf_op jit(solution)/shard_map/ppermute | solution.py:700
  638.7 33.5 %collective-permute-start.39 = (f32[48,6144]{1,0:T(8,128)}, f32[48,6144]{1,0:T(8,128)}, u32[]{:S(2)}, u32[]{:S(2)}) collective-permute-start(f32[48,6144]{1,0:T(8,128)} %get-tuple-element.505), channel_id=1, source_target_pairs={{0,8},{1,9},{2,10},{3,11},{4,12},{5,13},{6,14},{7,15},{8,0},{9,1},... | collective-permute-start | bytes 3538952 | tf_op jit(solution)/shard_map/ppermute | solution.py:700
  684.0 45.0 %collective-permute-start.44 = (bf16[192,6144]{1,0:T(8,128)(2,1)}, bf16[192,6144]{1,0:T(8,128)(2,1)}, u32[]{:S(2)}, u32[]{:S(2)}) collective-permute-start(bf16[192,6144]{1,0:T(8,128)(2,1)} %get-tuple-element.487), channel_id=1, source_target_pairs={{0,1},{1,0},{2,6},{3,7},{4,5},{5,4},{6,2},{7,3},{8,9},{9,8},{10,14... | collective-permute-start | bytes 7077896 | tf_op jit(solution)/shard_map/ppermute | solution.py:700
  687.7 35.4 %collective-permute-start.43 = (f32[96,3840]{1,0:T(8,128)}, f32[96,3840]{1,0:T(8,128)S(1)}, u32[]{:S(2)}, u32[]{:S(2)}) collective-permute-start(f32[96,3840]{1,0:T(8,128)} %get-tuple-element.500), channel_id=1, source_target_pairs={{0,4},{1,5},{2,3},{3,2},{4,0},{5,1},{6,7},{7,6},{8,12},{9,13},{10,... | collective-permute-start | bytes 4423688 | tf_op jit(solution)/shard_map/ppermute | solution.py:700
  689.0 31.3 %collective-permute-start.42 = (f32[24,6144]{1,0:T(8,128)S(1)}, f32[24,6144]{1,0:T(8,128)S(1)}, u32[]{:S(2)}, u32[]{:S(2)}) collective-permute-start(f32[24,6144]{1,0:T(8,128)S(1)} %slice_add_fusion.22), channel_id=1, source_target_pairs={{0,16},{1,17},{2,18},{3,19},{4,20},{5,21},{6,22},{7,23},{8,24},{9,... | collective-permute-start | bytes 1769480 | tf_op jit(solution)/shard_map/ppermute | solution.py:700
  728.9 34.4 %collective-permute-start.47 = (f32[384,3840]{1,0:T(8,128)}, f32[384,3840]{1,0:T(8,128)S(1)}, u32[]{:S(2)}, u32[]{:S(2)}) collective-permute-start(f32[384,3840]{1,0:T(8,128)} %get-tuple-element.390), channel_id=1, source_target_pairs={{0,2},{1,3},{2,0},{3,1},{4,6},{5,7},{6,4},{7,5},{8,10},{9,11},{10,... | collective-permute-start | bytes 17694728 | tf_op jit(solution)/shard_map/ppermute | solution.py:700
  734.4 28.9 %collective-permute-start.46 = (f32[96,6144]{1,0:T(8,128)S(1)}, f32[96,6144]{1,0:T(8,128)S(1)}, u32[]{:S(2)}, u32[]{:S(2)}) collective-permute-start(f32[96,6144]{1,0:T(8,128)S(1)} %get-tuple-element.495), channel_id=1, source_target_pairs={{0,4},{1,5},{2,3},{3,2},{4,0},{5,1},{6,7},{7,6},{8,12},{9,13},{10,... | collective-permute-start | bytes 7077896 | tf_op jit(solution)/shard_map/ppermute | solution.py:700
  765.5 38.8 %collective-permute-start.51 = (bf16[192,4352]{1,0:T(8,128)(2,1)}, bf16[192,4352]{1,0:T(8,128)(2,1)}, u32[]{:S(2)}, u32[]{:S(2)}) collective-permute-start(bf16[192,4352]{1,0:T(8,128)(2,1)} %pad_maximum_fusion.8), channel_id=1, source_target_pairs={{0,1},{1,0},{2,6},{3,7},{4,5},{5,4},{6,2},{7,3},{8,9},{9,8},{10,14... | collective-permute-start | bytes 5013512 | tf_op jit(solution)/shard_map/ppermute | solution.py:700
  768.9 35.4 %collective-permute-start.50 = (f32[48,6144]{1,0:T(8,128)}, f32[48,6144]{1,0:T(8,128)}, u32[]{:S(2)}, u32[]{:S(2)}) collective-permute-start(f32[48,6144]{1,0:T(8,128)} %get-tuple-element.503), channel_id=1, source_target_pairs={{0,8},{1,9},{2,10},{3,11},{4,12},{5,13},{6,14},{7,15},{8,0},{9,1},... | collective-permute-start | bytes 3538952 | tf_op jit(solution)/shard_map/ppermute | solution.py:700
  769.7 32.4 %collective-permute-start.49 = (f32[24,3840]{1,0:T(8,128)}, f32[24,3840]{1,0:T(8,128)}, u32[]{:S(2)}, u32[]{:S(2)}) collective-permute-start(f32[24,3840]{1,0:T(8,128)} %slice_add_fusion.27), channel_id=1, source_target_pairs={{0,16},{1,17},{2,18},{3,19},{4,20},{5,21},{6,22},{7,23},{8,24},{9,... | collective-permute-start | bytes 1105928 | tf_op jit(solution)/shard_map/ppermute | solution.py:700
  806.4 29.1 %collective-permute-start.53 = (f32[96,4352]{1,0:T(8,128)S(1)}, f32[96,4352]{1,0:T(8,128)S(1)}, u32[]{:S(2)}, u32[]{:S(2)}) collective-permute-start(f32[96,4352]{1,0:T(8,128)S(1)} %get-tuple-element.498), channel_id=1, source_target_pairs={{0,4},{1,5},{2,3},{3,2},{4,0},{5,1},{6,7},{7,6},{8,12},{9,13},{10,... | collective-permute-start | bytes 5013512 | tf_op jit(solution)/shard_map/ppermute | solution.py:700
  (104 other events, 1281.8 us)

commit v4 on v3

--- a/solution.py
+++ b/solution.py
@@ -10,6 +10,7 @@
 TOPK = 2
 LANES = 128
 FF_TILE = 512
+NARROW_STAGES = 1
 
 ln_eps = 1e-05
 in_eps = 1e-05
@@ -111,6 +112,7 @@
             transcendentals=seqs * tokens * tokens * width // HDIM,
             bytes_accessed=8 * seqs * tokens * width,
         ),
+        compiler_params=grant(8),
         name="attend",
     )(projected, projected, projected)
 
@@ -132,6 +134,7 @@
             transcendentals=seqs * tokens * tokens * width // HDIM,
             bytes_accessed=14 * seqs * tokens * width,
         ),
+        compiler_params=grant(12),
         name="attend_back",
     )(projected, projected, projected, grad_mixed)
 
@@ -142,11 +145,15 @@
 
 def whole_block(shape):
     zeros = (0,) * len(shape)
-    return pl.BlockSpec(shape, lambda *_: zeros)
-
-
-def stacked(own_ref, got_ref):
-    return jnp.concatenate([own_ref[...], got_ref[...]], axis=0)
+    return pl.BlockSpec(shape, lambda *_: zeros, pipeline_mode=pl.Buffered(1))
+
+
+def grant(mib):
+    return pltpu.CompilerParams(vmem_limit_bytes=mib << 20)
+
+
+def stacked(*refs):
+    return jnp.concatenate([ref[...] for ref in refs], axis=0)
 
 
 def unit_of(values):
@@ -177,18 +184,18 @@
 
 
 class Weight:
-    def __init__(self, own, got, start, cols):
-        self.own, self.got, self.start, self.cols = own, got, start, cols
+    def __init__(self, blocks, start, cols):
+        self.blocks, self.start, self.cols = list(blocks), start, cols
 
     def specs(self, width, index=lambda j: j):
         base = self.start // width
         spec = pl.BlockSpec(
-            (self.own.shape[0], width), lambda j, base=base: (0, base + index(j))
+            (self.blocks[0].shape[0], width), lambda j, base=base: (0, base + index(j))
         )
-        return [spec, spec]
+        return [spec] * len(self.blocks)
 
     def refs(self):
-        return [self.own, self.got]
+        return self.blocks
 
 
 def embed(patches, mask, mover, weight, small, keep_patches):
@@ -197,16 +204,16 @@
     masked = mask is not None
 
     def kernel(*refs):
-        x_ref, mover_ref, own_ref, got_ref, sown_ref, sgot_ref = refs[:6]
-        refs = refs[6:]
+        x_ref, mover_ref = refs[:2]
+        w_refs, small_refs, refs = refs[2:6], refs[6:10], refs[10:]
         if masked:
             mask_ref, refs = refs[0], refs[1:]
         h_ref, table_ref = refs[:2]
         x_rel = half(contract(x_ref[...], mover_ref[...], 1, 0))
         if keep_patches:
             refs[2][...] = x_rel
-        w_rel = half(contract(stacked(own_ref, got_ref), mover_ref[...], 1, 0))
-        small_t = stacked(sown_ref, sgot_ref).astype(full_type).T
+        w_rel = half(contract(stacked(*w_refs), mover_ref[...], 1, 0))
+        small_t = stacked(*small_refs).astype(full_type).T
         posit = small_t[:tokens]
         table = small_t[tokens : tokens + 8]
         table_ref[...] = table
@@ -234,6 +241,7 @@
         out_specs=[whole_block(out.shape) for out in outs],
         out_shape=outs,
         cost_estimate=cost(6 * rows * width * width, 12 * rows * width),
+        compiler_params=grant(28),
         name="embed",
     )(*args)
 
@@ -242,13 +250,13 @@
     rows, width = states.shape
     steps = weight.cols // width
 
-    def kernel(h_ref, table_ref, own_ref, got_ref, out_ref, a_ref):
+    def kernel(h_ref, table_ref, own_ref, own2_ref, got_ref, got2_ref, out_ref, a_ref):
         @pl.when(pl.program_id(0) == 0)
         def _():
             unit, _ = unit_of(h_ref[...])
             a_ref[...] = half(unit * table_ref[row : row + 1, :])
 
-        out_ref[...] = half(contract(a_ref[...], stacked(own_ref, got_ref), 1, 0))
+        out_ref[...] = half(contract(a_ref[...], stacked(own_ref, own2_ref, got_ref, got2_ref), 1, 0))
 
     outs = [shape_of((rows, weight.cols), half_type)]
     out_specs = [pl.BlockSpec((rows, width), lambda j: (0, j))]
@@ -266,6 +274,7 @@
         out_shape=outs,
         scratch_shapes=scratch,
         cost_estimate=cost(2 * rows * width * weight.cols, 12 * rows * width),
+        compiler_params=grant(24),
         name="norm_project",
     )(states, table, *weight.refs())
 
@@ -274,7 +283,7 @@
     rows, width = states.shape
     tile = rows // 2
 
-    def kernel(o_ref, h_ref, mover_ref, table_ref, own_ref, got_ref, m_ref, b_ref, *rest):
+    def kernel(o_ref, h_ref, mover_ref, table_ref, own_ref, own2_ref, got_ref, got2_ref, m_ref, b_ref, *rest):
         if keep:
             rel_ref, w_ref = rest
         else:
@@ -282,7 +291,7 @@
 
         @pl.when(pl.program_id(0) == 0)
         def _():
-            w_ref[...] = half(contract(stacked(own_ref, got_ref), mover_ref[...], 1, 0))
+            w_ref[...] = half(contract(stacked(own_ref, own2_ref, got_ref, got2_ref), mover_ref[...], 1, 0))
 
         mixed_rel = half(contract(o_ref[...], mover_ref[...], 1, 0))
         if keep:
@@ -310,6 +319,7 @@
         out_shape=outs,
         scratch_shapes=scratch,
         cost_estimate=cost(6 * rows * width * width, 14 * rows * width),
+        compiler_params=grant(24),
         name="mix_out",
     )(mixed, states, mover, table, *weight.refs())
 
@@ -319,9 +329,9 @@
     tile = FF_TILE
     steps = w_up.cols // tile
 
-    def kernel(b_ref, m_ref, uown_ref, ugot_ref, down_ref, dgot_ref, out_ref, *rest):
+    def kernel(b_ref, m_ref, uown_ref, uown2_ref, ugot_ref, ugot2_ref, down_ref, down2_ref, dgot_ref, dgot2_ref, out_ref, *rest):
         step = pl.program_id(0)
-        hidden = contract(b_ref[...], stacked(uown_ref, ugot_ref), 1, 0)
+        hidden = contract(b_ref[...], stacked(uown_ref, uown2_ref, ugot_ref, ugot2_ref), 1, 0)
         cdf = normal_cdf(hidden)
         active = half(hidden * cdf)
         if keep:
@@ -329,7 +339,7 @@
             rest[1][...] = cdf + hidden * (
                 jnp.exp(-0.5 * hidden * hidden) * ((0.5 / jnp.pi) ** 0.5)
             )
-        part = contract(active, stacked(down_ref, dgot_ref), 1, 1)
+        part = contract(active, stacked(down_ref, down2_ref, dgot_ref, dgot2_ref), 1, 1)
 
         @pl.when(step == 0)
         def _():
@@ -353,6 +363,7 @@
         out_specs=out_specs,
         out_shape=outs,
         cost_estimate=cost(4 * rows * width * w_up.cols, 12 * rows * width + 16 * width * w_up.cols),
+        compiler_params=grant(30),
         name="feed_forward",
     )(normed, middle, *w_up.refs(), *w_down.refs())
 
@@ -380,6 +391,7 @@
         out_specs=block,
         out_shape=shape_of((rows, width), full_type),
         cost_estimate=cost(20 * rows * width, 12 * rows * width),
+        compiler_params=grant(16),
         name="make_target",
     )(first, second)
 
@@ -390,14 +402,14 @@
     final_row = 2 * LAYERS
 
     def kernel(
-        h_ref, table_ref, mover_ref, own_ref, got_ref, t_ref, mask_ref,
+        h_ref, table_ref, mover_ref, own_ref, own2_ref, got_ref, got2_ref, t_ref, mask_ref,
         flow_ref, f_ref, pred_ref, gain_ref, loss_ref, w_ref,
     ):
         step = pl.program_id(0)
 
         @pl.when(step == 0)
         def _():
-            w_ref[...] = half(contract(stacked(own_ref, got_ref), mover_ref[...], 1, 0))
+            w_ref[...] = half(contract(stacked(own_ref, own2_ref, got_ref, got2_ref), mover_ref[...], 1, 0))
             gain_ref[...] = jnp.zeros_like(gain_ref)
             loss_ref[...] = jnp.zeros_like(loss_ref)
 
@@ -439,6 +451,7 @@
         ],
         scratch_shapes=[pltpu.VMEM((width, width), half_type)],
         cost_estimate=cost(8 * rows * width * width, 16 * rows * width),
+        compiler_params=grant(30),
         name="head_step",
     )(states, table, mover, *weight.refs(), target, mask)
 
@@ -449,7 +462,7 @@
     steps = w_up.cols // tile
 
     def kernel(
-        flow_ref, slope_ref, m_ref, table_ref, uown_ref, ugot_ref, down_ref, dgot_ref,
+        flow_ref, slope_ref, m_ref, table_ref, uown_ref, uown2_ref, ugot_ref, ugot2_ref, down_ref, down2_ref, dgot_ref, dgot2_ref,
         du_ref, dy_ref, dm_ref, dz_ref, gain_ref, acc_ref,
     ):
         step = pl.program_id(0)
@@ -458,10 +471,10 @@
         def _():
             dy_ref[...] = half(flow_ref[...])
 
-        grad_active = contract(dy_ref[...], stacked(down_ref, dgot_ref), 1, 0)
+        grad_active = contract(dy_ref[...], stacked(down_ref, down2_ref, dgot_ref, dgot2_ref), 1, 0)
         grad_hidden = half(grad_active * slope_ref[...])
         du_ref[...] = grad_hidden
-        part = contract(grad_hidden, stacked(uown_ref, ugot_ref), 1, 1)
+        part = contract(grad_hidden, stacked(uown_ref, uown2_ref, ugot_ref, ugot2_ref), 1, 1)
 
         @pl.when(step == 0)
         def _():
@@ -499,6 +512,7 @@
         ],
         scratch_shapes=[pltpu.VMEM((rows, width), full_type)],
         cost_estimate=cost(4 * rows * width * w_up.cols, 40 * rows * width + 8 * width * w_up.cols),
+        compiler_params=grant(32),
         name="feed_back",
     )(flow, slope, middle, table, *w_up.refs(), *w_down.refs())
 
@@ -522,6 +536,7 @@
         out_specs=[part, part],
         out_shape=[shape_of((rows, width), half_type)] * 2,
         cost_estimate=cost(6 * rows * width * width, 10 * rows * width),
+        compiler_params=grant(16),
         name="mix_back",
     )(grad_branch, w_rel, mover)
 
@@ -534,7 +549,7 @@
 
     def kernel(*refs):
         grad_refs, refs = refs[:count], refs[count:]
-        w_refs, refs = refs[: 2 * count], refs[2 * count :]
+        w_refs, refs = refs[: 4 * count], refs[4 * count :]
         dm_ref, h_ref, table_ref = refs[:3]
         refs = refs[3:]
         if first:
@@ -551,7 +566,7 @@
         total = None
         for place in range(count):
             part = contract(
-                grad_refs[place][...], stacked(w_refs[2 * place], w_refs[2 * place + 1]), 1, 1
+                grad_refs[place][...], stacked(*w_refs[4 * place : 4 * place + 4]), 1, 1
             )
             total = part if total is None else total + part
         grad_in, grad_gain = norm_back(total, table_ref[row : row + 1, :], h_ref[...])
@@ -586,6 +601,7 @@
         out_specs=out_specs,
         out_shape=outs,
         cost_estimate=cost(2 * rows * width * weight.cols, 22 * rows * width),
+        compiler_params=grant(30),
         name="project_back",
     )(*args)
 
@@ -619,7 +635,7 @@
             def _(right_ref=right_ref):
                 out = contract(turned_ref[...], right_ref[...], 1, 0)
                 near_ref[...] = out[:near_rows]
-                far_ref[...] = out[near_rows:]
+                far_ref[...] = half(out[near_rows:])
 
     specs = [whole_block((rows, width)) for _ in pairs]
     args = [left for left, _ in pairs]
@@ -633,19 +649,20 @@
             )
         )
     block = pl.BlockSpec((near_rows, width), lambda j: (0, j))
-    shape = shape_of((near_rows, total * width), full_type)
+    shapes = [shape_of((near_rows, total * width), kind) for kind in (full_type, half_type)]
     return tuple(
         pl.pallas_call(
             kernel,
             grid=(total,),
             in_specs=specs,
             out_specs=[block, block],
-            out_shape=[shape, shape],
+            out_shape=shapes,
             scratch_shapes=[pltpu.VMEM((width, rows), half_type)],
             cost_estimate=cost(
                 2 * rows * width * width * total, width * total * (4 * width + 2 * rows)
             ),
-            name="weight_grads",
+            compiler_params=grant(30),
+        name="weight_grads",
         )(*args)
     )
 
@@ -664,18 +681,19 @@
         fill = jnp.zeros((cols - tokens - len(vector_refs), width), full_type)
         table = jnp.concatenate([posit] + [ref[...] for ref in vector_refs] + [fill], axis=0).T
         near_ref[...] = table[: width // 2]
-        far_ref[...] = table[width // 2 :]
-
-    shape = shape_of((width // 2, cols), full_type)
+        far_ref[...] = half(table[width // 2 :])
+
+    shapes = [shape_of((width // 2, cols), kind) for kind in (full_type, half_type)]
     return tuple(
         pl.pallas_call(
             kernel,
             grid=(1,),
             in_specs=[whole_block(flow.shape)] + [whole_block((1, width)) for _ in vectors],
-            out_specs=[whole_block(shape.shape)] * 2,
-            out_shape=[shape, shape],
+            out_specs=[whole_block(shape.shape) for shape in shapes],
+            out_shape=shapes,
             cost_estimate=cost(2 * rows * width, 8 * rows * width),
-            name="small_grads",
+            compiler_params=grant(16),
+        name="small_grads",
         )(flow, *vectors)
     )
 
@@ -754,10 +772,11 @@
 
 
 def gather_steps(plan, value):
-    for perm in plan.stages:
+    for perm in plan.stages[:-1]:
         (got,) = yield [(value, perm)]
         value = jnp.concatenate([value, got], axis=0)
-    return value
+    (got,) = yield [(value, plan.stages[-1])]
+    return value, got
 
 
 def scatter_steps(plan, pieces):
@@ -772,11 +791,12 @@
     stages = plan.stages[::-1]
     for step, perm in enumerate(stages):
         (got,) = yield [(send, perm)]
-        got = got.astype(full_type)
         if step == len(stages) - 1:
             return keep + got
         middle = keep.shape[0] // 2
         send = keep[middle:] + got[middle:]
+        if step < NARROW_STAGES:
+            send = half(send)
         keep = keep[:middle] + got[:middle]
 
 
@@ -853,15 +873,18 @@
         joined([s_two[1]]),
     ]
 
-    def attn_weights(own, got, start):
-        return Weight(own, got, start, 3 * width), Weight(own, got, start + 3 * width, width)
-
-    def mlp_weights(own, got, start):
-        return Weight(own, got, start, ff_width), Weight(own, got, start + ff_width, ff_width)
-
-    def small_of(own, got):
-        start = own.shape[1] - t_small.shape[1]
-        return own[:, start:], got[:, start:]
+    def attn_weights(blocks, start):
+        return Weight(blocks, start, 3 * width), Weight(blocks, start + 3 * width, width)
+
+    def mlp_weights(blocks, start):
+        return Weight(blocks, start, ff_width), Weight(blocks, start + ff_width, ff_width)
+
+    def small_of(blocks):
+        start = blocks[0].shape[1] - t_small.shape[1]
+        return [block[:, start:] for block in blocks]
+
+    def with_sibling(blocks):
+        return list(blocks) + [plan.swap(block, plan.core_stage) for block in blocks]
 
     def attend_forward(states, table, layer, w_qkv, w_out, keep):
         outs = norm_project(states, table, layer, w_qkv, keep)
@@ -875,49 +898,49 @@
     saved_attn = [None] * LAYERS
     saved_mlp = [None] * LAYERS
 
-    def segment_t0(_, own, got):
-        patch = Weight(own, got, 0, width)
+    def segment_t0(_, blocks):
+        patch = Weight(blocks, 0, width)
         states, table, patch_rel = embed(
-            flat_patch, None, mover, patch, small_of(own, got), True
+            flat_patch, None, mover, patch, small_of(blocks), True
         )
         middle, normed, _ = attend_forward(
-            states, table, 0, *attn_weights(own, got, width), False
+            states, table, 0, *attn_weights(blocks, width), False
         )
         return middle, normed, table, patch_rel
 
-    def segment_t1(values, own, got):
+    def segment_t1(values, blocks):
         middle, normed, table, patch_rel = values
-        (states,) = feed_forward(normed, middle, *mlp_weights(own, got, 0), False)
+        (states,) = feed_forward(normed, middle, *mlp_weights(blocks, 0), False)
         return states, table, patch_rel
 
-    def segment_t2(values, own, got):
+    def segment_t2(values, blocks):
         first, table, patch_rel = values
-        middle, normed, _ = attend_forward(first, table, 1, *attn_weights(own, got, 0), False)
-        (second,) = feed_forward(normed, middle, *mlp_weights(own, got, 4 * width), False)
+        middle, normed, _ = attend_forward(first, table, 1, *attn_weights(blocks, 0), False)
+        (second,) = feed_forward(normed, middle, *mlp_weights(blocks, 4 * width), False)
         return make_target(first, second, seqs), patch_rel
 
-    def segment_s0(values, own, got):
+    def segment_s0(values, blocks):
         target, patch_rel = values
-        patch = Weight(own, got, 0, width)
-        states, table = embed(flat_patch, mask_flat, mover, patch, small_of(own, got), False)
-        weights = attn_weights(own, got, width)
+        patch = Weight(blocks, 0, width)
+        states, table = embed(flat_patch, mask_flat, mover, patch, small_of(blocks), False)
+        weights = attn_weights(blocks, width)
         middle, normed, saved = attend_forward(states, table, 0, *weights, True)
         saved_attn[0] = (weights[0], saved)
         return target, patch_rel, table, middle, normed
 
-    def segment_s1(values, own, got):
+    def segment_s1(values, blocks):
         target, patch_rel, table, middle, normed = values
-        weights = mlp_weights(own, got, 0)
+        weights = mlp_weights(blocks, 0)
         states, active, slope = feed_forward(normed, middle, *weights, True)
         saved_mlp[0] = (weights, middle, normed, active, slope)
         return target, patch_rel, table, states
 
-    def segment_s2(values, own, got):
+    def segment_s2(values, blocks):
         target, patch_rel, table, states = values
-        weights = attn_weights(own, got, 0)
+        weights = attn_weights(blocks, 0)
         middle, normed, saved = attend_forward(states, table, 1, *weights, True)
         saved_attn[1] = (weights[0], saved)
-        return target, patch_rel, table, middle, normed, own, got
+        return target, patch_rel, table, middle, normed, blocks
 
     segments = [segment_t0, segment_t1, segment_t2, segment_s0, segment_s1, segment_s2]
     pump = Pump(plan)
@@ -931,19 +954,17 @@
         pump.begin()
         place = tick - len(plan.stages)
         if 0 <= place < len(segments):
-            own = arrived[place]
-            values = segments[place](values, own, plan.swap(own, plan.core_stage))
+            values = segments[place](values, with_sibling(arrived[place]))
         values, waiting = pump.end((values, waiting))
-    target, patch_rel, table, middle, normed, head_own, head_got = values
-    own = arrived[-1]
-    weights = mlp_weights(own, plan.swap(own, plan.core_stage), 0)
+    target, patch_rel, table, middle, normed, head_blocks = values
+    weights = mlp_weights(with_sibling(arrived[-1]), 0)
     states, active, slope = feed_forward(normed, middle, *weights, True)
     saved_mlp[1] = (weights, middle, normed, active, slope)
     flow, final_normed, grad_pred, grad_gain_final, loss_row = head_step(
         states,
         table,
         mover,
-        Weight(head_own, head_got, 4 * width, width),
+        Weight(head_blocks, 4 * width, width),
         target,
         mask_flat,
         total_masked,
@@ -952,8 +973,8 @@
 
     gain_ones = [None] * LAYERS
     gain_twos = [None] * LAYERS
-    attn_shards = [None] * LAYERS
-    mlp_shards = [None] * LAYERS
+    qkv_shards = [None] * LAYERS
+    other_shards = [None] * LAYERS
     extra_pairs = [(final_normed, [grad_pred])]
     for layer in reversed(range(LAYERS)):
         w_qkv, (states, normed_one, projected, mixed_rel, w_out_rel) = saved_attn[layer]
@@ -961,16 +982,33 @@
         grad_hidden, grad_down, grad_middle, grad_branch, gain_twos[layer] = feed_back(
             flow, slope, middle, table, LAYERS + layer, w_up, w_down
         )
-        piece = weight_grads([(normed_two, [grad_hidden]), (grad_down, [active])])
-        piece, grad_middle, grad_branch = pump.end((piece, grad_middle, grad_branch))
+        if layer < LAYERS - 1:
+            grad_hidden, grad_down, grad_middle, grad_branch, pieces = pump.end(
+                (grad_hidden, grad_down, grad_middle, grad_branch, pieces)
+            )
+            pump.add(
+                scatter_steps(plan, pieces),
+                lambda out, layer=layer: qkv_shards.__setitem__(layer + 1, out),
+            )
+            pump.begin()
+        grad_mixed, branch_whole = mix_back(grad_branch, w_out_rel, mover)
+        piece = weight_grads(
+            [
+                (normed_two, [grad_hidden]),
+                (grad_down, [active]),
+                (mixed_rel, [branch_whole]),
+            ]
+            + extra_pairs
+        )
+        extra_pairs = []
+        piece, grad_middle, grad_mixed = pump.end((piece, grad_middle, grad_mixed))
         pump.add(
             scatter_steps(plan, [piece]),
-            lambda out, layer=layer: mlp_shards.__setitem__(layer, out),
+            lambda out, layer=layer: other_shards.__setitem__(layer, out),
         )
         pump.begin()
-        grad_mixed, branch_whole = mix_back(grad_branch, w_out_rel, mover)
         grad_proj = attend_back(projected, grad_mixed.reshape(seqs, tokens, width))
-        grad_proj, branch_whole = pump.end((tuple(grad_proj), branch_whole))
+        grad_proj = pump.end(tuple(grad_proj))
         grad_proj = [part.reshape(-1, width) for part in grad_proj]
         pump.begin()
         results = project_back(
@@ -987,27 +1025,26 @@
         if layer == 0:
             grad_embed, grad_maskvec = results[2:]
             extra_pairs = [(patch_rel, [grad_embed])]
-        pieces = [
-            weight_grads([(normed_one, grad_proj), (mixed_rel, [branch_whole])] + extra_pairs)
-        ]
-        if layer == 0:
-            vectors = gain_ones + gain_twos + [grad_gain_final, grad_maskvec]
-            pieces.append(small_grads(flow, vectors, seqs))
-        pieces, flow = pump.end((pieces, flow))
-        pump.add(
-            scatter_steps(plan, pieces),
-            lambda out, layer=layer: attn_shards.__setitem__(layer, out),
-        )
-        if layer:
-            pump.begin()
+        pieces = [weight_grads([(normed_one, grad_proj)] + extra_pairs)]
+        extra_pairs = []
+    vectors = gain_ones + gain_twos + [grad_gain_final, grad_maskvec]
+    pieces.append(small_grads(flow, vectors, seqs))
+    pieces = pump.end(pieces)
+    pump.add(scatter_steps(plan, pieces), lambda out: qkv_shards.__setitem__(0, out))
     pump.drain()
-    last, first = attn_shards
+    last, qkv_one = qkv_shards
+    other_zero, other_one = other_shards
+    start = 2 * ff_width
+    stop = start + width
     raw = (
-        jnp.concatenate([last[:, 4 * width : 5 * width], first[:, 4 * width :]], axis=1),
-        jnp.concatenate([last[:, : 4 * width], first[:, : 4 * width]], axis=1),
-        jnp.concatenate(mlp_shards, axis=1),
-        last[:, 5 * width : 5 * width + tokens],
-        last[:, 5 * width + tokens : 5 * width + small_cols],
+        jnp.concatenate([last[:, 3 * width : 4 * width], other_one[:, stop:]], axis=1),
+        jnp.concatenate(
+            [last[:, : 3 * width], other_zero[:, start:stop], qkv_one, other_one[:, start:stop]],
+            axis=1,
+        ),
+        jnp.concatenate([other_zero[:, :start], other_one[:, :start]], axis=1),
+        last[:, 4 * width : 4 * width + tokens],
+        last[:, 4 * width + tokens : 4 * width + small_cols],
     )
     totals = jnp.stack([loss_local] + [jnp.sum(part * part) for part in raw])
     totals = jnp.broadcast_to(totals[:, None], (totals.shape[0], LANES))
@@ -1023,7 +1060,9 @@
     attn_new = adam_step(attn_w, attn_m, attn_v, attn_t, clipped[1])
     mlp_new = adam_step(mlp_w, mlp_m, mlp_v, mlp_t, clipped[2])
     posit_new = adam_step(posit_w, posit_m, posit_v, posit_t, clipped[3])
-    vecs_new = adam_step(vecs_w, vecs_m, vecs_v, vecs_t, clipped[4])
+    vecs_new = [
+        part.T for part in adam_step(vecs_w.T, vecs_m.T, vecs_v.T, vecs_t.T, clipped[4].T)
+    ]
     news = (edge_new, attn_new, mlp_new, posit_new, vecs_new)
     return (total_loss,) + tuple(group[part] for part in range(4) for group in news)
 

time: 929 us -> 844 us (0.909)
  Pallas kernels: 430 us -> 333 us
  local copies, waits for them, and re-layouts: 73.4 us -> 125 us
  other arithmetic: 113 us -> 71.8 us
  starting transfers between devices: 57.4 us -> 79.4 us
  waiting for transfers between devices: 240 us -> 220 us
    unnamed x185 -> x326, local copies, waits for them, and re-layouts: 41 us -> 115 us
    ppermute x61 -> x68, starting transfers between devices: 57.4 us -> 79.4 us  [swap(): return lax.ppermute(value, AXES, perm)]
    concatenate x21 -> x15, other arithmetic: 32.5 us -> 11.2 us  [gather_steps(): value = jnp.concatenate([value, got], axis=0)]
    ppermute x61 -> x68, waiting for transfers between devices: 240 us -> 220 us  [swap(): return lax.ppermute(value, AXES, perm)]
    pallas_call x4, Pallas kernels: 66.1 us -> 46.7 us  [weight_grads(): pl.pallas_call(kernel, grid=(total,), in_specs=specs, out_specs=[block, b...]
    add x5 -> x2, other arithmetic: 26.7 us -> 9.5 us  [scatter_steps(): near[:quarter] + got[:quarter]]
    concatenate x7 -> x6, local copies, waits for them, and re-layouts: 17.3 us -> 3.91 us  [gather_steps(): value = jnp.concatenate([value, got], axis=0)]
    convert_element_type x4 -> x5, other arithmetic: 7.75 us -> 20 us  [half(): return values.astype(half_type)]
  transfers between devices with their start and end apart: 61 -> 68, of which waited for: 27 -> 30; matrix products, arithmetic and copies ran while one was open for 12% -> 5% of each run, Pallas kernels for 39% -> 32%
where the time goes in v4:
time: 844 us; the launch traced here: 837 us
  Pallas kernels  333 us (39%)
  waiting for transfers between devices  220 us (26%)
  local copies, waits for them, and re-layouts  125 us (15%)
  starting transfers between devices  79.4 us (9%)
  other arithmetic  71.8 us (9%)
    ppermute x68, waiting for transfers between devices, swap(): return lax.ppermute(value, AXES, perm)  220 us
    unnamed x326, local copies, waits for them, and re-layouts  115 us
    ppermute x68, starting transfers between devices, swap(): return lax.ppermute(value, AXES, perm)  79.4 us
    pallas_call x4, Pallas kernels, attend(): pl.pallas_call(attend_kernel, grid=(seqs, blocks), in_specs=qkv_specs(tok...  61.8 us
    pallas_call x4, Pallas kernels, feed_forward(): pl.pallas_call(kernel, grid=(steps,), in_specs=[whole_block(normed.shape)...  58.8 us
    pallas_call x2, Pallas kernels, attend_back(): pl.pallas_call(attend_back_kernel, grid=(seqs, blocks), in_specs=qkv_spec...  50.2 us
    pallas_call x4, Pallas kernels, weight_grads(): pl.pallas_call(kernel, grid=(total,), in_specs=specs, out_specs=[block, b...  46.7 us
    pallas_call x2, Pallas kernels, feed_back(): pl.pallas_call(kernel, grid=(steps,), in_specs=[full, column, full, whole...  35.3 us
  transfers between devices with their start and end apart: 68, of which 30 were waited for; matrix products, arithmetic and copies ran while one was open for 5% of the time, Pallas kernels for 32%

profile of v4, /device:TPU:0, one launch (start us, length us, event | category | flops | bytes accessed | tf_op | source)
XLA Modules:
  0.0 836.8 jit_solution(3466754132386620687)
XLA Ops:
  25.0 12.0 %collective-permute-done.2 = bf16[24,6144]{1,0:T(8,128)(2,1)S(1)} collective-permute-done((bf16[24,6144]{1,0:T(8,128)(2,1)S(1)}, bf16[24,6144]{1,0:T(8,128)(2,1)S(1)}, u32[]{:S(2)}, u32[]{:S(2)}) %collective-permute-start.2) | collective-permute-done | bytes 294944 | tf_op jit(solution)/shard_map/ppermute | solution.py:718
  45.6 14.0 %collective-permute-done.5 = bf16[24,9216]{1,0:T(8,128)(2,1)S(1)} collective-permute-done((bf16[24,9216]{1,0:T(8,128)(2,1)S(1)}, bf16[24,9216]{1,0:T(8,128)(2,1)S(1)}, u32[]{:S(2)}, u32[]{:S(2)}) %collective-permute-start.5) | collective-permute-done | bytes 442400 | tf_op jit(solution)/shard_map/ppermute | solution.py:718
  73.8 17.7 %collective-permute-done.9 = bf16[24,4352]{1,0:T(8,128)(2,1)S(1)} collective-permute-done((bf16[24,4352]{1,0:T(8,128)(2,1)S(1)}, bf16[24,4352]{1,0:T(8,128)(2,1)S(1)}, u32[]{:S(2)}, u32[]{:S(2)}) %collective-permute-start.9) | collective-permute-done | bytes 208928 | tf_op jit(solution)/shard_map/ppermute | solution.py:718
  112.9 6.0 norm_project.4
  118.8 15.4 %attend.4 = bf16[2,448,768]{2,1,0:T(8,128)(2,1)S(1)} custom-call(bf16[2,448,2304]{2,1,0:T(8,128)(2,1)S(1)} %bitcast.29, bf16[2,448,2304]{2,1,0:T(8,128)(2,1)S(1)} %bitcast.30, bf16[2,448,2304]{2,1,0:T(8,128)(2,1)S(1)} %bitcast.31), custom_call_target="tpu_custom_call" | custom-call | flops 4932501504 | bytes 5505024 | tf_op jit(solution)/shard_map/attend/pallas_call | solution.py:104
  169.2 13.9 %feed_forward.4.h_ref.one_ref = f32[896,768]{1,0:T(8,128)S(1)} custom-call(bf16[896,768]{1,0:T(8,128)(2,1)S(1)} %copy-done.77, f32[896,768]{1,0:T(8,128)S(1)} %copy-done.62, bf16[192,6144]{1,0:T(8,128)(2,1)S(1)} %copy-done.58, bf16[192,6144]{1,0:T(8,128)(2,1)S(1)} %copy-done.64, bf16[192,6144]{1,0:T(8,128)(2,1)} %collective-permute-done.20.ugot_ref.dgot_ref, ...), custom_call_target="tpu_custom_call" | custom-call | flops 8455716864 | bytes 46006272 | tf_op jit(solution)/shard_map/feed_forward/pallas_call | solution.py:357
  183.1 14.7 %collective-permute-done.16.own2_ref.uown2_ref.down2_ref = bf16[192,9216]{1,0:T(8,128)(2,1)S(1)} collective-permute-done((bf16[192,9216]{1,0:T(8,128)(2,1)S(1)}, bf16[192,9216]{1,0:T(8,128)(2,1)S(1)}, u32[]{:S(2)}, u32[]{:S(2)}) %collective-permute-start.16) | collective-permute-done | bytes 3538976 | tf_op jit(solution)/shard_map/ppermute | solution.py:718
  218.4 15.5 %attend.5 = bf16[2,448,768]{2,1,0:T(8,128)(2,1)S(1)} custom-call(bf16[2,448,2304]{2,1,0:T(8,128)(2,1)S(1)} %bitcast.32, bf16[2,448,2304]{2,1,0:T(8,128)(2,1)S(1)} %bitcast.33, bf16[2,448,2304]{2,1,0:T(8,128)(2,1)S(1)} %bitcast.34), custom_call_target="tpu_custom_call" | custom-call | flops 4932501504 | bytes 5505024 | tf_op jit(solution)/shard_map/attend/pallas_call | solution.py:104
  238.6 12.9 %feed_forward.5.two_ref = f32[896,768]{1,0:T(8,128)S(1)} custom-call(bf16[896,768]{1,0:T(8,128)(2,1)S(1)} %get-tuple-element.267.b_ref, f32[896,768]{1,0:T(8,128)S(1)} %get-tuple-element.268.m_ref, bf16[192,9216]{1,0:T(8,128)(2,1)S(1)} %constant_dynamic-update-slice_fusion.4.own_ref.uown_ref.down_ref, ...), custom_call_target="tpu_custom_call" | custom-call | flops 8455716864 | bytes 46006272 | tf_op jit(solution)/shard_map/feed_forward/pallas_call | solution.py:357
  270.6 15.6 %attend.6 = bf16[2,448,768]{2,1,0:T(8,128)(2,1)S(1)} custom-call(bf16[2,448,2304]{2,1,0:T(8,128)(2,1)S(1)} %bitcast.52, bf16[2,448,2304]{2,1,0:T(8,128)(2,1)S(1)} %bitcast.53, bf16[2,448,2304]{2,1,0:T(8,128)(2,1)S(1)} %bitcast.54), custom_call_target="tpu_custom_call" | custom-call | flops 4932501504 | bytes 5505024 | tf_op jit(solution)/shard_map/attend/pallas_call | solution.py:104
  307.7 15.6 %feed_forward.6 = (f32[896,768]{1,0:T(8,128)S(1)}, bf16[896,3072]{1,0:T(8,128)(2,1)S(1)}, f32[896,3072]{1,0:T(8,128)}) custom-call(bf16[896,768]{1,0:T(8,128)(2,1)S(1)} %copy-done.72, f32[896,768]{1,0:T(8,128)S(1)} %get-tuple-element.287.m_ref, bf16[192,6144]{1,0:T(8,128)(2,1)S(1)} %copy-done.16, bf16[192,6144]{1,0:T(8,128)(2,1)S(1)} %copy-done.19, ...), custom_call_target="tpu_custom_call" | custom-call | flops 8455716864 | bytes 46006272 | tf_op jit(solution)/shard_map/feed_forward/pallas_call | solution.py:357
  332.3 6.1 norm_project.7
  338.4 15.4 %attend.7 = bf16[2,448,768]{2,1,0:T(8,128)(2,1)S(1)} custom-call(bf16[2,448,2304]{2,1,0:T(8,128)(2,1)S(1)} %bitcast.58, bf16[2,448,2304]{2,1,0:T(8,128)(2,1)S(1)} %bitcast.59, bf16[2,448,2304]{2,1,0:T(8,128)(2,1)S(1)} %bitcast.60), custom_call_target="tpu_custom_call" | custom-call | flops 4932501504 | bytes 5505024 | tf_op jit(solution)/shard_map/attend/pallas_call | solution.py:104
  376.2 16.3 %feed_forward.7 = (f32[896,768]{1,0:T(8,128)S(1)}, bf16[896,3072]{1,0:T(8,128)(2,1)S(1)}, f32[896,3072]{1,0:T(8,128)}) custom-call(bf16[896,768]{1,0:T(8,128)(2,1)S(1)} %get-tuple-element.308.b_ref.refs_0_, f32[896,768]{1,0:T(8,128)S(1)} %copy-done.49, bf16[192,6144]{1,0:T(8,128)(2,1)} %constant_dynamic-update-slice_fusion.20.uown_ref.down_ref, ...), custom_call_target="tpu_custom_call" | custom-call | flops 8455716864 | bytes 46006272 | tf_op jit(solution)/shard_map/feed_forward/pallas_call | solution.py:357
  402.5 7.4 head_step.1
  422.2 17.5 %feed_back.2 = (bf16[896,3072]{1,0:T(8,128)(2,1)}, bf16[896,768]{1,0:T(8,128)(2,1)S(1)}, f32[896,768]{1,0:T(8,128)S(1)}, bf16[896,768]{1,0:T(8,128)(2,1)S(1)}, f32[1,768]{1,0:T(1,128)S(1)}) custom-call(f32[896,768]{1,0:T(8,128)S(1)} %copy-done.54, f32[896,3072]{1,0:T(8,128)} %get-tuple-element.320.slope_ref, f32[896,768]{1,0:T(8,128)S(1)} %copy-done.50, ...), custom_call_target="tpu_custom_call" | custom-call | flops 8455716864 | bytes 46399488 | tf_op jit(solution)/shard_map/feed_back/pallas_call | solution.py:499
  453.1 18.2 %weight_grads.4 = (f32[384,7680]{1,0:T(8,128)}, bf16[384,7680]{1,0:T(8,128)(2,1)}) custom-call(bf16[896,768]{1,0:T(8,128)(2,1)S(1)} %copy-done.89, bf16[896,768]{1,0:T(8,128)(2,1)S(1)} %copy-done.79, bf16[896,768]{1,0:T(8,128)(2,1)S(1)} %copy-done.91, bf16[896,768]{1,0:T(8,128)(2,1)S(1)} %copy-done.101, bf16[896,3072]{1,0:T(8,128)(2,1)S(1)} %copy-done.60, ...), custom_call_target="tpu_custom_call" | custom-call | flops 10569646080 | bytes 37355520 | tf_op jit(solution)/shard_map/weight_grads/pallas_call | solution.py:654
  473.7 25.1 %attend_back.2 = (bf16[2,448,768]{2,1,0:T(8,128)(2,1)S(1)}, bf16[2,448,768]{2,1,0:T(8,128)(2,1)S(1)}, bf16[2,448,768]{2,1,0:T(8,128)(2,1)S(1)}) custom-call(bf16[2,448,2304]{2,1,0:T(8,128)(2,1)S(1)} %bitcast.61, bf16[2,448,2304]{2,1,0:T(8,128)(2,1)S(1)} %bitcast.62, bf16[2,448,2304]{2,1,0:T(8,128)(2,1)S(1)} %bitcast.63, bf16[2,448,768]{2,1,0:T(8,128)(2,1)S(1)} %bitcast.65), custom_call_target="tpu_custom_call" | custom-call | flops 9865003008 | bytes 9633792 | tf_op jit(solution)/shard_map/attend_back/pallas_call | solution.py:126
  501.3 10.4 %add_convert_fusion = (bf16[192,7680]{1,0:T(8,128)(2,1)}, f32[192,7680]{1,0:T(8,128)}) fusion(f32[384,7680]{1,0:T(8,128)} %get-tuple-element.334, bf16[384,7680]{1,0:T(8,128)(2,1)} %copy-done.114), kind=kLoop, calls=%fused_computation | loop fusion | flops 7372800 | bytes 26542080 | tf_op jit(solution)/shard_map/convert_element_type | solution.py:175
  540.6 17.8 %feed_back.3 = (bf16[896,3072]{1,0:T(8,128)(2,1)}, bf16[896,768]{1,0:T(8,128)(2,1)S(1)}, f32[896,768]{1,0:T(8,128)S(1)}, bf16[896,768]{1,0:T(8,128)(2,1)S(1)}, f32[1,768]{1,0:T(1,128)S(1)}) custom-call(f32[896,768]{1,0:T(8,128)S(1)} %copy-done.52, f32[896,3072]{1,0:T(8,128)} %get-tuple-element.346.slope_ref, f32[896,768]{1,0:T(8,128)S(1)} %copy-done.41, ...), custom_call_target="tpu_custom_call" | custom-call | flops 8455716864 | bytes 46399488 | tf_op jit(solution)/shard_map/feed_back/pallas_call | solution.py:499
  558.6 7.1 fusion
  572.4 16.3 %weight_grads.6 = (f32[384,6912]{1,0:T(8,128)}, bf16[384,6912]{1,0:T(8,128)(2,1)S(1)}) custom-call(bf16[896,768]{1,0:T(8,128)(2,1)S(1)} %copy-done.73, bf16[896,768]{1,0:T(8,128)(2,1)S(1)} %get-tuple-element.356.refs_1_, bf16[896,768]{1,0:T(8,128)(2,1)S(1)} %copy-done.75, bf16[896,3072]{1,0:T(8,128)(2,1)S(1)} %copy-done.59, ...), custom_call_target="tpu_custom_call" | custom-call | flops 9512681472 | bytes 33619968 | tf_op jit(solution)/shard_map/weight_grads/pallas_call | solution.py:654
  597.5 25.1 %attend_back.3 = (bf16[2,448,768]{2,1,0:T(8,128)(2,1)S(1)}, bf16[2,448,768]{2,1,0:T(8,128)(2,1)S(1)}, bf16[2,448,768]{2,1,0:T(8,128)(2,1)S(1)}) custom-call(bf16[2,448,2304]{2,1,0:T(8,128)(2,1)S(1)} %bitcast.55, bf16[2,448,2304]{2,1,0:T(8,128)(2,1)S(1)} %bitcast.56, bf16[2,448,2304]{2,1,0:T(8,128)(2,1)S(1)} %bitcast.57, bf16[2,448,768]{2,1,0:T(8,128)(2,1)S(1)} %bitcast.64), custom_call_target="tpu_custom_call" | custom-call | flops 9865003008 | bytes 9633792 | tf_op jit(solution)/shard_map/attend_back/pallas_call | solution.py:126
  627.5 6.8 convert_add_fusion.1
  639.7 8.4 %project_back.3 = (f32[896,768]{1,0:T(8,128)S(1)}, f32[1,768]{1,0:T(1,128)S(1)}, bf16[896,768]{1,0:T(8,128)(2,1)S(1)}, f32[1,768]{1,0:T(1,128)S(1)}) custom-call(bf16[896,768]{1,0:T(8,128)(2,1)S(1)} %bitcast.35, bf16[896,768]{1,0:T(8,128)(2,1)S(1)} %bitcast.37, bf16[896,768]{1,0:T(8,128)(2,1)S(1)} %bitcast.39, ...), custom_call_target="tpu_custom_call" | custom-call | flops 3170893824 | bytes 15138816 | tf_op jit(solution)/shard_map/project_back/pallas_call | solution.py:597
  649.8 7.2 weight_grads.7
  657.1 14.5 %collective-permute-done.49 = f32[24,7680]{1,0:T(8,128)S(1)} collective-permute-done((f32[24,7680]{1,0:T(8,128)}, f32[24,7680]{1,0:T(8,128)S(1)}, u32[]{:S(2)}, u32[]{:S(2)}) %collective-permute-start.49) | collective-permute-done | bytes 737312 | tf_op jit(solution)/shard_map/ppermute | solution.py:718
  678.7 8.7 %collective-permute-done.52 = f32[48,2304]{1,0:T(8,128)S(1)} collective-permute-done((f32[48,2304]{1,0:T(8,128)S(1)}, f32[48,2304]{1,0:T(8,128)S(1)}, u32[]{:S(2)}, u32[]{:S(2)}) %collective-permute-start.52) | collective-permute-done | bytes 442400 | tf_op jit(solution)/shard_map/ppermute | solution.py:718
  701.6 29.8 %collective-permute-done.56 = f32[24,2304]{1,0:T(8,128)} collective-permute-done((f32[24,2304]{1,0:T(8,128)}, f32[24,2304]{1,0:T(8,128)}, u32[]{:S(2)}, u32[]{:S(2)}) %collective-permute-start.56) | collective-permute-done | bytes 221216 | tf_op jit(solution)/shard_map/ppermute | solution.py:718
  738.7 25.3 %collective-permute-done.59 = f32[24,6912]{1,0:T(8,128)S(1)} collective-permute-done((f32[24,6912]{1,0:T(8,128)S(1)}, f32[24,6912]{1,0:T(8,128)S(1)}, u32[]{:S(2)}, u32[]{:S(2)}) %collective-permute-start.59) | collective-permute-done | bytes 663584 | tf_op jit(solution)/shard_map/ppermute | solution.py:718
  766.0 14.9 %collective-permute-done.61 = f32[48,3584]{1,0:T(8,128)S(1)} collective-permute-done((f32[48,3584]{1,0:T(8,128)S(1)}, f32[48,3584]{1,0:T(8,128)S(1)}, u32[]{:S(2)}, u32[]{:S(2)}) %collective-permute-start.61) | collective-permute-done | bytes 688160 | tf_op jit(solution)/shard_map/ppermute | solution.py:718
  783.6 14.2 %collective-permute-done.62 = f32[24,3584]{1,0:T(8,128)S(1)} collective-permute-done((f32[24,3584]{1,0:T(8,128)S(1)}, f32[24,3584]{1,0:T(8,128)S(1)}, u32[]{:S(2)}, u32[]{:S(2)}) %collective-permute-start.62) | collective-permute-done | bytes 344096 | tf_op jit(solution)/shard_map/ppermute | solution.py:718
  (566 shorter events, 364.3 us)
Async XLA Ops:
  65.0 34.2 %collective-permute-start.6 = (bf16[192,4352]{1,0:T(8,128)(2,1)S(1)}, bf16[192,4352]{1,0:T(8,128)(2,1)S(1)}, u32[]{:S(2)}, u32[]{:S(2)}) collective-permute-start(bf16[192,4352]{1,0:T(8,128)(2,1)S(1)} %pad_maximum_fusion.1.refs_2_.own_ref), channel_id=1, source_target_pairs={{0,1},{1,0},{2,6},{3,7},{4,5},{5,4},{6,2},{7,3},{8,9},{9,8},{10,14... | collective-permute-start | bytes 5013512 | tf_op jit(solution)/shard_map/ppermute | solution.py:718
  65.6 36.7 %collective-permute-start.14 = (bf16[192,4352]{1,0:T(8,128)(2,1)S(1)}, bf16[192,4352]{1,0:T(8,128)(2,1)S(1)}, u32[]{:S(2)}, u32[]{:S(2)}) collective-permute-start(bf16[192,4352]{1,0:T(8,128)(2,1)S(1)} %pad_maximum_fusion.1.refs_2_.own_ref), channel_id=1, source_target_pairs={{0,2},{1,3},{2,0},{3,1},{4,6},{5,7},{6,4},{7,5},{8,10},{9,11},{10,... | collective-permute-start | bytes 5013512 | tf_op jit(solution)/shard_map/ppermute | solution.py:718
  99.3 47.9 %collective-permute-start.10 = (bf16[192,6144]{1,0:T(8,128)(2,1)S(1)}, bf16[192,6144]{1,0:T(8,128)(2,1)S(1)}, u32[]{:S(2)}, u32[]{:S(2)}) collective-permute-start(bf16[192,6144]{1,0:T(8,128)(2,1)S(1)} %constant_dynamic-update-slice_fusion.uown_ref.down_ref), channel_id=1, source_target_pairs={{0,1},{1,0},{2,6},{3,7},{4,5},{5,4},{6,2},{7,3},{8,9},{9,8},{10,14... | collective-permute-start | bytes 7077896 | tf_op jit(solution)/shard_map/ppermute | solution.py:718
  99.9 56.9 %collective-permute-start.20 = (bf16[192,6144]{1,0:T(8,128)(2,1)S(1)}, bf16[192,6144]{1,0:T(8,128)(2,1)}, u32[]{:S(2)}, u32[]{:S(2)}) collective-permute-start(bf16[192,6144]{1,0:T(8,128)(2,1)S(1)} %constant_dynamic-update-slice_fusion.uown_ref.down_ref), channel_id=1, source_target_pairs={{0,2},{1,3},{2,0},{3,1},{4,6},{5,7},{6,4},{7,5},{8,10},{9,11},{10,... | collective-permute-start | bytes 7077896 | tf_op jit(solution)/shard_map/ppermute | solution.py:718
  101.3 41.6 %collective-permute-start.11 = (bf16[96,9216]{1,0:T(8,128)(2,1)S(1)}, bf16[96,9216]{1,0:T(8,128)(2,1)S(1)}, u32[]{:S(2)}, u32[]{:S(2)}) collective-permute-start(bf16[96,9216]{1,0:T(8,128)(2,1)S(1)} %pad_maximum_fusion), channel_id=1, source_target_pairs={{0,4},{1,5},{2,3},{3,2},{4,0},{5,1},{6,7},{7,6},{8,12},{9,13},{10,... | collective-permute-start | bytes 5308424 | tf_op jit(solution)/shard_map/ppermute | solution.py:718
  102.3 37.7 %collective-permute-start.13 = (bf16[24,6144]{1,0:T(8,128)(2,1)S(1)}, bf16[24,6144]{1,0:T(8,128)(2,1)S(1)}, u32[]{:S(2)}, u32[]{:S(2)}) collective-permute-start(bf16[24,6144]{1,0:T(8,128)(2,1)S(1)} %get-tuple-element.241), channel_id=1, source_target_pairs={{0,16},{1,17},{2,18},{3,19},{4,20},{5,21},{6,22},{7,23},{8,24},{9,... | collective-permute-start | bytes 884744 | tf_op jit(solution)/shard_map/ppermute | solution.py:718
  107.1 32.9 %collective-permute-start.12 = (bf16[48,4352]{1,0:T(8,128)(2,1)}, bf16[48,4352]{1,0:T(8,128)(2,1)S(1)}, u32[]{:S(2)}, u32[]{:S(2)}) collective-permute-start(bf16[48,4352]{1,0:T(8,128)(2,1)} %pad_maximum_fusion.18), channel_id=1, source_target_pairs={{0,8},{1,9},{2,10},{3,11},{4,12},{5,13},{6,14},{7,15},{8,0},{9,1},... | collective-permute-start | bytes 1253384 | tf_op jit(solution)/shard_map/ppermute | solution.py:718
  147.3 50.5 %collective-permute-start.16 = (bf16[192,9216]{1,0:T(8,128)(2,1)S(1)}, bf16[192,9216]{1,0:T(8,128)(2,1)S(1)}, u32[]{:S(2)}, u32[]{:S(2)}) collective-permute-start(bf16[192,9216]{1,0:T(8,128)(2,1)S(1)} %constant_dynamic-update-slice_fusion.4.own_ref.uown_ref.down_ref), channel_id=1, source_target_pairs={{0,1},{1,0},{2,6},{3,7},{4,5},{5,4},{6,2},{7,3},{8,9},{9,8},{10,14... | collective-permute-start | bytes 10616840 | tf_op jit(solution)/shard_map/ppermute | solution.py:718
  148.9 34.3 %collective-permute-start.17 = (bf16[96,4352]{1,0:T(8,128)(2,1)}, bf16[96,4352]{1,0:T(8,128)(2,1)}, u32[]{:S(2)}, u32[]{:S(2)}) collective-permute-start(bf16[96,4352]{1,0:T(8,128)(2,1)} %pad_maximum_fusion.10), channel_id=1, source_target_pairs={{0,4},{1,5},{2,3},{3,2},{4,0},{5,1},{6,7},{7,6},{8,12},{9,13},{10,... | collective-permute-start | bytes 2506760 | tf_op jit(solution)/shard_map/ppermute | solution.py:718
  150.4 32.7 %collective-permute-start.19 = (bf16[24,3840]{1,0:T(8,128)(2,1)}, bf16[24,3840]{1,0:T(8,128)(2,1)S(1)}, u32[]{:S(2)}, u32[]{:S(2)}) collective-permute-start(bf16[24,3840]{1,0:T(8,128)(2,1)} %pad_maximum_fusion.22), channel_id=1, source_target_pairs={{0,16},{1,17},{2,18},{3,19},{4,20},{5,21},{6,22},{7,23},{8,24},{9,... | collective-permute-start | bytes 552968 | tf_op jit(solution)/shard_map/ppermute | solution.py:718
  156.8 54.1 %collective-permute-start.26 = (bf16[192,9216]{1,0:T(8,128)(2,1)S(1)}, bf16[192,9216]{1,0:T(8,128)(2,1)S(1)}, u32[]{:S(2)}, u32[]{:S(2)}) collective-permute-start(bf16[192,9216]{1,0:T(8,128)(2,1)S(1)} %constant_dynamic-update-slice_fusion.4.own_ref.uown_ref.down_ref), channel_id=1, source_target_pairs={{0,2},{1,3},{2,0},{3,1},{4,6},{5,7},{6,4},{7,5},{8,10},{9,11},{10,... | collective-permute-start | bytes 10616840 | tf_op jit(solution)/shard_map/ppermute | solution.py:718
  199.0 56.2 %collective-permute-start.22 = (bf16[192,4352]{1,0:T(8,128)(2,1)S(1)}, bf16[192,4352]{1,0:T(8,128)(2,1)S(1)}, u32[]{:S(2)}, u32[]{:S(2)}) collective-permute-start(bf16[192,4352]{1,0:T(8,128)(2,1)S(1)} %constant_dynamic-update-slice_fusion.8.refs_2_.own_ref.refs_3_.refs_7_.refs_11_), channel_id=1, source_target_pairs={{0,1},{1,0},{2,6},{3,7},{4,5},{5,4},{6,2},{7,3},{8,9},{9,8},{10,14... | collective-permute-start | bytes 5013512 | tf_op jit(solution)/shard_map/ppermute | solution.py:718
  200.9 54.3 %collective-permute-start.25 = (bf16[24,6144]{1,0:T(8,128)(2,1)S(1)}, bf16[24,6144]{1,0:T(8,128)(2,1)S(1)}, u32[]{:S(2)}, u32[]{:S(2)}) collective-permute-start(bf16[24,6144]{1,0:T(8,128)(2,1)S(1)} %get-tuple-element.260), channel_id=1, source_target_pairs={{0,16},{1,17},{2,18},{3,19},{4,20},{5,21},{6,22},{7,23},{8,24},{9,... | collective-permute-start | bytes 884744 | tf_op jit(solution)/shard_map/ppermute | solution.py:718
  209.1 46.1 %collective-permute-start.23 = (bf16[96,6144]{1,0:T(8,128)(2,1)}, bf16[96,6144]{1,0:T(8,128)(2,1)S(1)}, u32[]{:S(2)}, u32[]{:S(2)}) collective-permute-start(bf16[96,6144]{1,0:T(8,128)(2,1)} %pad_maximum_fusion.5), channel_id=1, source_target_pairs={{0,4},{1,5},{2,3},{3,2},{4,0},{5,1},{6,7},{7,6},{8,12},{9,13},{10,... | collective-permute-start | bytes 3538952 | tf_op jit(solution)/shard_map/ppermute | solution.py:718
  210.9 44.3 %collective-permute-start.24 = (bf16[48,3840]{1,0:T(8,128)(2,1)}, bf16[48,3840]{1,0:T(8,128)(2,1)S(1)}, u32[]{:S(2)}, u32[]{:S(2)}) collective-permute-start(bf16[48,3840]{1,0:T(8,128)(2,1)} %pad_maximum_fusion.19), channel_id=1, source_target_pairs={{0,8},{1,9},{2,10},{3,11},{4,12},{5,13},{6,14},{7,15},{8,0},{9,1},... | collective-permute-start | bytes 1105928 | tf_op jit(solution)/shard_map/ppermute | solution.py:718
  255.5 38.6 %collective-permute-start.28 = (bf16[192,6144]{1,0:T(8,128)(2,1)S(1)}, bf16[192,6144]{1,0:T(8,128)(2,1)S(1)}, u32[]{:S(2)}, u32[]{:S(2)}) collective-permute-start(bf16[192,6144]{1,0:T(8,128)(2,1)S(1)} %constant_dynamic-update-slice_fusion.12.uown_ref.down_ref), channel_id=1, source_target_pairs={{0,1},{1,0},{2,6},{3,7},{4,5},{5,4},{6,2},{7,3},{8,9},{9,8},{10,14... | collective-permute-start | bytes 7077896 | tf_op jit(solution)/shard_map/ppermute | solution.py:718
  256.8 43.0 %collective-permute-start.35 = (bf16[192,6144]{1,0:T(8,128)(2,1)S(1)}, bf16[192,6144]{1,0:T(8,128)(2,1)S(1)}, u32[]{:S(2)}, u32[]{:S(2)}) collective-permute-start(bf16[192,6144]{1,0:T(8,128)(2,1)S(1)} %constant_dynamic-update-slice_fusion.12.uown_ref.down_ref), channel_id=1, source_target_pairs={{0,2},{1,3},{2,0},{3,1},{4,6},{5,7},{6,4},{7,5},{8,10},{9,11},{10,... | collective-permute-start | bytes 7077896 | tf_op jit(solution)/shard_map/ppermute | solution.py:718
  258.6 35.5 %collective-permute-start.29 = (bf16[96,3840]{1,0:T(8,128)(2,1)S(1)}, bf16[96,3840]{1,0:T(8,128)(2,1)S(1)}, u32[]{:S(2)}, u32[]{:S(2)}) collective-permute-start(bf16[96,3840]{1,0:T(8,128)(2,1)S(1)} %pad_maximum_fusion.11), channel_id=1, source_target_pairs={{0,4},{1,5},{2,3},{3,2},{4,0},{5,1},{6,7},{7,6},{8,12},{9,13},{10,... | collective-permute-start | bytes 2211848 | tf_op jit(solution)/shard_map/ppermute | solution.py:718
  260.2 33.8 %collective-permute-start.30 = (bf16[48,6144]{1,0:T(8,128)(2,1)S(1)}, bf16[48,6144]{1,0:T(8,128)(2,1)S(1)}, u32[]{:S(2)}, u32[]{:S(2)}) collective-permute-start(bf16[48,6144]{1,0:T(8,128)(2,1)S(1)} %pad_maximum_fusion.14), channel_id=1, source_target_pairs={{0,8},{1,9},{2,10},{3,11},{4,12},{5,13},{6,14},{7,15},{8,0},{9,1},... | collective-permute-start | bytes 1769480 | tf_op jit(solution)/shard_map/ppermute | solution.py:718
  295.2 32.1 %collective-permute-start.33 = (bf16[192,3840]{1,0:T(8,128)(2,1)S(1)}, bf16[192,3840]{1,0:T(8,128)(2,1)S(1)}, u32[]{:S(2)}, u32[]{:S(2)}) collective-permute-start(bf16[192,3840]{1,0:T(8,128)(2,1)S(1)} %constant_dynamic-update-slice_fusion.16.own_ref.refs_3_.refs_7_.refs_11_), channel_id=1, source_target_pairs={{0,1},{1,0},{2,6},{3,7},{4,5},{5,4},{6,2},{7,3},{8,9},{9,8},{10,14... | collective-permute-start | bytes 4423688 | tf_op jit(solution)/shard_map/ppermute | solution.py:718
  295.8 34.6 %collective-permute-start.38 = (bf16[192,3840]{1,0:T(8,128)(2,1)S(1)}, bf16[192,3840]{1,0:T(8,128)(2,1)}, u32[]{:S(2)}, u32[]{:S(2)}) collective-permute-start(bf16[192,3840]{1,0:T(8,128)(2,1)S(1)} %constant_dynamic-update-slice_fusion.16.own_ref.refs_3_.refs_7_.refs_11_), channel_id=1, source_target_pairs={{0,2},{1,3},{2,0},{3,1},{4,6},{5,7},{6,4},{7,5},{8,10},{9,11},{10,... | collective-permute-start | bytes 4423688 | tf_op jit(solution)/shard_map/ppermute | solution.py:718
  329.7 33.8 %collective-permute-start.37 = (bf16[192,6144]{1,0:T(8,128)(2,1)}, bf16[192,6144]{1,0:T(8,128)(2,1)S(1)}, u32[]{:S(2)}, u32[]{:S(2)}) collective-permute-start(bf16[192,6144]{1,0:T(8,128)(2,1)} %constant_dynamic-update-slice_fusion.20.uown_ref.down_ref), channel_id=1, source_target_pairs={{0,1},{1,0},{2,6},{3,7},{4,5},{5,4},{6,2},{7,3},{8,9},{9,8},{10,14... | collective-permute-start | bytes 7077896 | tf_op jit(solution)/shard_map/ppermute | solution.py:718
  330.2 35.0 %collective-permute-start.40 = (bf16[192,6144]{1,0:T(8,128)(2,1)}, bf16[192,6144]{1,0:T(8,128)(2,1)S(1)}, u32[]{:S(2)}, u32[]{:S(2)}) collective-permute-start(bf16[192,6144]{1,0:T(8,128)(2,1)} %constant_dynamic-update-slice_fusion.20.uown_ref.down_ref), channel_id=1, source_target_pairs={{0,2},{1,3},{2,0},{3,1},{4,6},{5,7},{6,4},{7,5},{8,10},{9,11},{10,... | collective-permute-start | bytes 7077896 | tf_op jit(solution)/shard_map/ppermute | solution.py:718
  511.7 46.8 %collective-permute-start.43 = (bf16[192,7680]{1,0:T(8,128)(2,1)}, bf16[192,7680]{1,0:T(8,128)(2,1)}, u32[]{:S(2)}, u32[]{:S(2)}) collective-permute-start(bf16[192,7680]{1,0:T(8,128)(2,1)} %get-tuple-element.495), channel_id=1, source_target_pairs={{0,1},{1,0},{2,6},{3,7},{4,5},{5,4},{6,2},{7,3},{8,9},{9,8},{10,14... | collective-permute-start | bytes 8847368 | tf_op jit(solution)/shard_map/ppermute | solution.py:718
  588.7 37.7 %collective-permute-start.48 = (bf16[384,6912]{1,0:T(8,128)(2,1)S(1)}, bf16[384,6912]{1,0:T(8,128)(2,1)S(1)}, u32[]{:S(2)}, u32[]{:S(2)}) collective-permute-start(bf16[384,6912]{1,0:T(8,128)(2,1)S(1)} %get-tuple-element.370), channel_id=1, source_target_pairs={{0,2},{1,3},{2,0},{3,1},{4,6},{5,7},{6,4},{7,5},{8,10},{9,11},{10,... | collective-permute-start | bytes 15925256 | tf_op jit(solution)/shard_map/ppermute | solution.py:718
  591.4 35.0 %collective-permute-start.46 = (f32[48,7680]{1,0:T(8,128)S(1)}, f32[48,7680]{1,0:T(8,128)S(1)}, u32[]{:S(2)}, u32[]{:S(2)}) collective-permute-start(f32[48,7680]{1,0:T(8,128)S(1)} %get-tuple-element.507), channel_id=1, source_target_pairs={{0,8},{1,9},{2,10},{3,11},{4,12},{5,13},{6,14},{7,15},{8,0},{9,1},... | collective-permute-start | bytes 4423688 | tf_op jit(solution)/shard_map/ppermute | solution.py:718
  634.3 37.4 %collective-permute-start.51 = (bf16[192,6912]{1,0:T(8,128)(2,1)}, bf16[192,6912]{1,0:T(8,128)(2,1)}, u32[]{:S(2)}, u32[]{:S(2)}) collective-permute-start(bf16[192,6912]{1,0:T(8,128)(2,1)} %get-tuple-element.498), channel_id=1, source_target_pairs={{0,1},{1,0},{2,6},{3,7},{4,5},{5,4},{6,2},{7,3},{8,9},{9,8},{10,14... | collective-permute-start | bytes 7962632 | tf_op jit(solution)/shard_map/ppermute | solution.py:718
  636.6 35.1 %collective-permute-start.49 = (f32[24,7680]{1,0:T(8,128)}, f32[24,7680]{1,0:T(8,128)S(1)}, u32[]{:S(2)}, u32[]{:S(2)}) collective-permute-start(f32[24,7680]{1,0:T(8,128)} %slice_add_fusion.11), channel_id=1, source_target_pairs={{0,16},{1,17},{2,18},{3,19},{4,20},{5,21},{6,22},{7,23},{8,24},{9,... | collective-permute-start | bytes 2211848 | tf_op jit(solution)/shard_map/ppermute | solution.py:718
  693.9 38.1 %collective-permute-start.58 = (bf16[192,3584]{1,0:T(8,128)(2,1)}, bf16[192,3584]{1,0:T(8,128)(2,1)}, u32[]{:S(2)}, u32[]{:S(2)}) collective-permute-start(bf16[192,3584]{1,0:T(8,128)(2,1)} %pad_maximum_fusion.3), channel_id=1, source_target_pairs={{0,1},{1,0},{2,6},{3,7},{4,5},{5,4},{6,2},{7,3},{8,9},{9,8},{10,14... | collective-permute-start | bytes 4128776 | tf_op jit(solution)/shard_map/ppermute | solution.py:718
  696.4 35.6 %collective-permute-start.57 = (f32[48,6912]{1,0:T(8,128)}, f32[48,6912]{1,0:T(8,128)}, u32[]{:S(2)}, u32[]{:S(2)}) collective-permute-start(f32[48,6912]{1,0:T(8,128)} %get-tuple-element.512), channel_id=1, source_target_pairs={{0,8},{1,9},{2,10},{3,11},{4,12},{5,13},{6,14},{7,15},{8,0},{9,1},... | collective-permute-start | bytes 3981320 | tf_op jit(solution)/shard_map/ppermute | solution.py:718
  698.9 32.4 %collective-permute-start.56 = (f32[24,2304]{1,0:T(8,128)}, f32[24,2304]{1,0:T(8,128)}, u32[]{:S(2)}, u32[]{:S(2)}) collective-permute-start(f32[24,2304]{1,0:T(8,128)} %slice_add_fusion.21), channel_id=1, source_target_pairs={{0,16},{1,17},{2,18},{3,19},{4,20},{5,21},{6,22},{7,23},{8,24},{9,... | collective-permute-start | bytes 663560 | tf_op jit(solution)/shard_map/ppermute | solution.py:718
  733.4 30.6 %collective-permute-start.59 = (f32[24,6912]{1,0:T(8,128)S(1)}, f32[24,6912]{1,0:T(8,128)S(1)}, u32[]{:S(2)}, u32[]{:S(2)}) collective-permute-start(f32[24,6912]{1,0:T(8,128)S(1)} %slice_add_fusion.15), channel_id=1, source_target_pairs={{0,16},{1,17},{2,18},{3,19},{4,20},{5,21},{6,22},{7,23},{8,24},{9,... | collective-permute-start | bytes 1990664 | tf_op jit(solution)/shard_map/ppermute | solution.py:718
  (186 other events, 1486.5 us)

commit v5 on v4

--- a/solution.py
+++ b/solution.py
@@ -11,6 +11,7 @@
 LANES = 128
 FF_TILE = 512
 NARROW_STAGES = 1
+FAST_LANE = True
 
 ln_eps = 1e-05
 in_eps = 1e-05
@@ -117,26 +118,35 @@
     )(projected, projected, projected)
 
 
-def attend_back(projected, grad_mixed):
+def attend_back(projected, grad_mixed, seq, into=()):
     seqs, tokens, width3 = projected.shape
     width = width3 // 3
     blocks = width // LANES
-    block = pl.BlockSpec((1, tokens, LANES), lambda s, j: (s, 0, j))
+    block = pl.BlockSpec((1, tokens, LANES), lambda j: (seq, 0, j))
+    specs = [
+        pl.BlockSpec((1, tokens, LANES), lambda j, off=off: (seq, 0, off * blocks + j))
+        for off in range(3)
+    ]
+
+    def kernel(q_ref, k_ref, v_ref, do_ref, *refs):
+        attend_back_kernel(q_ref, k_ref, v_ref, do_ref, *refs[-3:])
+
     shape = jax.ShapeDtypeStruct((seqs, tokens, width), half_type)
     return pl.pallas_call(
-        attend_back_kernel,
-        grid=(seqs, blocks),
-        in_specs=qkv_specs(tokens, blocks) + [block],
+        kernel,
+        grid=(blocks,),
+        in_specs=specs + [block] + [pl.BlockSpec(memory_space=pl.ANY)] * len(into),
         out_specs=[block, block, block],
         out_shape=[shape, shape, shape],
+        input_output_aliases={4 + place: place for place in range(len(into))},
         cost_estimate=pl.CostEstimate(
-            flops=32 * seqs * tokens * tokens * width,
-            transcendentals=seqs * tokens * tokens * width // HDIM,
-            bytes_accessed=14 * seqs * tokens * width,
+            flops=32 * tokens * tokens * width,
+            transcendentals=tokens * tokens * width // HDIM,
+            bytes_accessed=14 * tokens * width,
         ),
         compiler_params=grant(12),
         name="attend_back",
-    )(projected, projected, projected, grad_mixed)
+    )(projected, projected, projected, grad_mixed, *into)
 
 
 def normal_cdf(values):
@@ -179,6 +189,10 @@
     return jax.ShapeDtypeStruct(shape, kind)
 
 
+def kept_shape(shape, kind):
+    return pltpu.HBM(shape, kind)
+
+
 def cost(flops, moved):
     return pl.CostEstimate(flops=flops, transcendentals=0, bytes_accessed=moved)
 
@@ -195,7 +209,7 @@
         return [spec] * len(self.blocks)
 
     def refs(self):
-        return self.blocks
+        return [pltpu.with_memory_space_constraint(block, pltpu.HBM) for block in self.blocks]
 
 
 def embed(patches, mask, mover, weight, small, keep_patches):
@@ -262,7 +276,7 @@
     out_specs = [pl.BlockSpec((rows, width), lambda j: (0, j))]
     scratch = []
     if keep:
-        outs.append(shape_of((rows, width), half_type))
+        outs.append(kept_shape((rows, width), half_type))
         out_specs.append(whole_block((rows, width)))
     else:
         scratch.append(pltpu.VMEM((rows, width), half_type))
@@ -306,7 +320,7 @@
     out_specs = [part, part]
     scratch = []
     if keep:
-        outs += [shape_of((rows, width), half_type), shape_of((width, width), half_type)]
+        outs += [kept_shape((rows, width), half_type), kept_shape((width, width), half_type)]
         out_specs += [part, whole_block((width, width))]
     else:
         scratch.append(pltpu.VMEM((width, width), half_type))
@@ -352,7 +366,7 @@
     outs = [shape_of((rows, width), full_type)]
     out_specs = [whole_block((rows, width))]
     if keep:
-        outs += [shape_of((rows, w_up.cols), half_type), shape_of((rows, w_up.cols), full_type)]
+        outs += [kept_shape((rows, w_up.cols), half_type), kept_shape((rows, w_up.cols), full_type)]
         out_specs += [pl.BlockSpec((rows, tile), lambda j: (0, j))] * 2
     return pl.pallas_call(
         kernel,
@@ -766,17 +780,13 @@
         return values
 
     def drain(self):
-        while self.jobs:
-            self.begin()
-            self.end()
-
-
-def gather_steps(plan, value):
-    for perm in plan.stages[:-1]:
-        (got,) = yield [(value, perm)]
-        value = jnp.concatenate([value, got], axis=0)
-    (got,) = yield [(value, plan.stages[-1])]
-    return value, got
+        for steps, sends, done in self.jobs:
+            try:
+                while True:
+                    sends = steps.send([self.plan.swap(value, perm) for value, perm in sends])
+            except StopIteration as stop:
+                done(stop.value)
+        self.jobs = []
 
 
 def scatter_steps(plan, pieces):
@@ -808,6 +818,85 @@
     )
     teacher_new = teacher_keep * teacher + (1.0 - teacher_keep) * weight_new
     return (weight_new, first_new, second_new, teacher_new)
+
+
+def norm_totals(last, attn_one, mlp_zero, mlp_one, loss_row, width, tokens):
+    stop = mlp_zero.shape[1]
+
+    def kernel(last_ref, attn_ref, zero_ref, one_ref, loss_ref, out_ref):
+        def square(value):
+            return jnp.sum(value * value)
+
+        small = last_ref[:, 5 * width :]
+        lane = lax.broadcasted_iota(jnp.int32, small.shape, 1)
+        posit = jnp.where(lane < tokens, small, 0.0)
+        vecs = jnp.where(lane >= tokens, small, 0.0)
+        parts = [
+            jnp.sum(loss_ref[...]),
+            square(last_ref[:, 4 * width : 5 * width]) + square(one_ref[:, stop:]),
+            square(last_ref[:, : 4 * width]) + square(attn_ref[...]),
+            square(zero_ref[...]) + square(one_ref[:, :stop]),
+            square(posit),
+            square(vecs),
+        ]
+        row = lax.broadcasted_iota(jnp.int32, (8, LANES), 0)
+        out = jnp.zeros((8, LANES), full_type)
+        for place, part in enumerate(parts):
+            out = jnp.where(row == place, part, out)
+        out_ref[...] = out
+
+    args = (last, attn_one, mlp_zero, mlp_one, loss_row)
+    return pl.pallas_call(
+        kernel,
+        grid=(1,),
+        in_specs=[whole_block(arg.shape) for arg in args],
+        out_specs=whole_block((8, LANES)),
+        out_shape=shape_of((8, LANES), full_type),
+        compiler_params=grant(16),
+        name="norm_totals",
+    )(*args)
+
+
+def update(totals, last, attn_one, mlp_zero, mlp_one, groups, sizes, width, tokens):
+    stop = mlp_zero.shape[1]
+
+    def kernel(total_ref, last_ref, attn_ref, zero_ref, one_ref, *refs):
+        ins, outs = refs[:20], refs[20:]
+
+        def step(group, gradient, cols=slice(None)):
+            limit = entry_clip * sizes[group] ** 0.5
+            norm_value = jnp.sqrt(total_ref[group + 1 : group + 2, 0:1])
+            gradient = gradient * (limit / jnp.maximum(norm_value, limit))
+            weight, first, second, teacher = (
+                ref[:, cols] for ref in ins[4 * group : 4 * group + 4]
+            )
+            news = adam_step(weight, first, second, teacher, gradient)
+            for ref, new in zip(outs[4 * group : 4 * group + 4], news):
+                ref[:, cols] = new
+
+        step(0, last_ref[:, 4 * width : 5 * width], slice(0, width))
+        step(0, one_ref[:, stop:], slice(width, 2 * width))
+        step(1, last_ref[:, : 4 * width], slice(0, 4 * width))
+        step(1, attn_ref[...], slice(4 * width, 8 * width))
+        step(2, zero_ref[...], slice(0, stop))
+        step(2, one_ref[:, :stop], slice(stop, 2 * stop))
+        step(3, last_ref[:, 5 * width : 5 * width + tokens])
+        start = tokens // LANES * LANES
+        turned = last_ref[:, 5 * width + start : 5 * width + start + LANES].T
+        count = ins[16].shape[0]
+        step(4, turned[tokens - start : tokens - start + count])
+
+    args = [totals, last, attn_one, mlp_zero, mlp_one] + [part for group in groups for part in group]
+    outs = [shape_of(part.shape, full_type) for group in groups for part in group]
+    return pl.pallas_call(
+        kernel,
+        grid=(1,),
+        in_specs=[whole_block(arg.shape) for arg in args],
+        out_specs=[whole_block(out.shape) for out in outs],
+        out_shape=outs,
+        compiler_params=grant(40),
+        name="update",
+    )(*args)
 
 
 def pad_lanes(value):
@@ -863,15 +952,17 @@
 
     t_patch, _, t_small, t_one, t_two = shards(edge_t, attn_t, mlp_t, posit_t, vecs_t)
     s_patch, s_head, s_small, s_one, s_two = shards(edge_w, attn_w, mlp_w, posit_w, vecs_w)
-    waiting = [
-        joined([t_patch, t_one[0], t_small]),
-        joined([t_one[1]]),
-        joined(t_two),
-        joined([s_patch, s_one[0], s_small]),
-        joined([s_one[1]]),
-        joined([s_two[0], s_head]),
-        joined([s_two[1]]),
+    chunks = [
+        [t_patch, t_one[0], t_small],
+        [t_one[1]],
+        t_two,
+        [s_patch, s_one[0], s_small],
+        [s_one[1]],
+        [s_two[0], s_head],
+        [s_two[1]],
     ]
+    groups = [[0], [1], [2, 3], [4, 5, 6]]
+    group_start = [0, 1, 2, 4]
 
     def attn_weights(blocks, start):
         return Weight(blocks, start, 3 * width), Weight(blocks, start + 3 * width, width)
@@ -883,11 +974,12 @@
         start = blocks[0].shape[1] - t_small.shape[1]
         return [block[:, start:] for block in blocks]
 
-    def with_sibling(blocks):
-        return list(blocks) + [plan.swap(block, plan.core_stage) for block in blocks]
-
-    def attend_forward(states, table, layer, w_qkv, w_out, keep):
-        outs = norm_project(states, table, layer, w_qkv, keep)
+    def finish(blocks):
+        return list(blocks) + [plan.swap(blocks[1], plan.core_stage)]
+
+    def attend_forward(states, table, layer, w_qkv, w_out, keep, outs=None):
+        if outs is None:
+            outs = norm_project(states, table, layer, w_qkv, keep)
         projected = outs[0].reshape(seqs, tokens, w_qkv.cols)
         mixed = attend(projected).reshape(-1, width)
         results = mix_out(mixed, states, mover, table, LAYERS + layer, w_out, keep)
@@ -903,9 +995,13 @@
         states, table, patch_rel = embed(
             flat_patch, None, mover, patch, small_of(blocks), True
         )
-        middle, normed, _ = attend_forward(
-            states, table, 0, *attn_weights(blocks, width), False
-        )
+        weights = attn_weights(blocks, width)
+        return states, table, patch_rel, norm_project(states, table, 0, weights[0], False)
+
+    def segment_t0_rest(values, blocks):
+        states, table, patch_rel, outs = values
+        weights = attn_weights(blocks, width)
+        middle, normed, _ = attend_forward(states, table, 0, *weights, False, outs)
         return middle, normed, table, patch_rel
 
     def segment_t1(values, blocks):
@@ -942,22 +1038,59 @@
         saved_attn[1] = (weights[0], saved)
         return target, patch_rel, table, middle, normed, blocks
 
-    segments = [segment_t0, segment_t1, segment_t2, segment_s0, segment_s1, segment_s2]
+    segments = [segment_t0_rest, segment_t1, segment_t2, segment_s0, segment_s1, segment_s2]
+    early = len(plan.early)
+    group_values = [joined([part for c in group for part in chunks[c]]) for group in groups]
+    own = [None] * len(chunks)
+    blocks = [None] * len(chunks)
+    values = ()
+    for tick in range(len(chunks) + early + 1):
+        sends = {}
+        for group, start in enumerate(group_start):
+            if 0 <= tick - start < early:
+                sends["early", group] = (group_values[group], plan.stages[tick - start])
+        for chunk in range(len(chunks)):
+            if tick == chunk + early:
+                sends["first", chunk] = (own[chunk], plan.stages[early])
+            if tick == chunk + early + 1:
+                sends["second", chunk] = (own[chunk], plan.stages[early + 1])
+                sends["core", chunk] = (own[chunk], plan.core_stage)
+        gots = {key: plan.swap(value, perm) for key, (value, perm) in sends.items()}
+        place = tick - early - 2
+        if 0 <= place < len(segments):
+            values = segments[place](values, finish(blocks[place]))
+        if tick == early + 1:
+            first_blocks = (own[0], gots["second", 0], gots["core", 0])
+            values = segment_t0(values, finish(first_blocks))
+        apart = {key: got for key, got in gots.items() if FAST_LANE and key[1] == 0 and tick}
+        gots = {key: got for key, got in gots.items() if key not in apart}
+        later = [g for g in range(len(groups)) if group_start[g] > tick]
+        idle = [c for c in range(1, len(chunks)) if own[c] is not None and c + early > tick]
+        gots, values, held, held_own, _ = lax.optimization_barrier(
+            (gots, values, [group_values[g] for g in later], [own[c] for c in idle], apart)
+        )
+        for g, value in zip(later, held):
+            group_values[g] = value
+        for c, value in zip(idle, held_own):
+            own[c] = value
+        gots.update(apart)
+        for (kind, index), got in gots.items():
+            if kind == "early":
+                group_values[index] = jnp.concatenate([group_values[index], got], axis=0)
+                if tick - group_start[index] == early - 1:
+                    start = 0
+                    for chunk in groups[index]:
+                        stop = start + sum(part.shape[1] for part in chunks[chunk])
+                        own[chunk] = group_values[index][:, start:stop]
+                        start = stop
+            elif kind == "first":
+                own[index] = jnp.concatenate([own[index], got], axis=0)
+        for chunk in range(len(chunks)):
+            if ("second", chunk) in gots:
+                blocks[chunk] = (own[chunk], gots["second", chunk], gots["core", chunk])
     pump = Pump(plan)
-    arrived = []
-    values = ()
-    total_chunks = len(waiting)
-    for tick in range(total_chunks + len(plan.stages)):
-        if waiting:
-            pump.add(gather_steps(plan, waiting[0]), arrived.append)
-            waiting = waiting[1:]
-        pump.begin()
-        place = tick - len(plan.stages)
-        if 0 <= place < len(segments):
-            values = segments[place](values, with_sibling(arrived[place]))
-        values, waiting = pump.end((values, waiting))
     target, patch_rel, table, middle, normed, head_blocks = values
-    weights = mlp_weights(with_sibling(arrived[-1]), 0)
+    weights = mlp_weights(finish(blocks[-1]), 0)
     states, active, slope = feed_forward(normed, middle, *weights, True)
     saved_mlp[1] = (weights, middle, normed, active, slope)
     flow, final_normed, grad_pred, grad_gain_final, loss_row = head_step(
@@ -969,12 +1102,11 @@
         mask_flat,
         total_masked,
     )
-    loss_local = jnp.sum(loss_row) / total_masked
 
     gain_ones = [None] * LAYERS
     gain_twos = [None] * LAYERS
-    qkv_shards = [None] * LAYERS
-    other_shards = [None] * LAYERS
+    attn_shards = [None] * LAYERS
+    mlp_shards = [None] * LAYERS
     extra_pairs = [(final_normed, [grad_pred])]
     for layer in reversed(range(LAYERS)):
         w_qkv, (states, normed_one, projected, mixed_rel, w_out_rel) = saved_attn[layer]
@@ -982,35 +1114,30 @@
         grad_hidden, grad_down, grad_middle, grad_branch, gain_twos[layer] = feed_back(
             flow, slope, middle, table, LAYERS + layer, w_up, w_down
         )
-        if layer < LAYERS - 1:
-            grad_hidden, grad_down, grad_middle, grad_branch, pieces = pump.end(
-                (grad_hidden, grad_down, grad_middle, grad_branch, pieces)
-            )
-            pump.add(
-                scatter_steps(plan, pieces),
-                lambda out, layer=layer: qkv_shards.__setitem__(layer + 1, out),
-            )
-            pump.begin()
-        grad_mixed, branch_whole = mix_back(grad_branch, w_out_rel, mover)
         piece = weight_grads(
-            [
-                (normed_two, [grad_hidden]),
-                (grad_down, [active]),
-                (mixed_rel, [branch_whole]),
-            ]
-            + extra_pairs
+            [(normed_two, [grad_hidden]), (grad_down, [active])] + extra_pairs
         )
         extra_pairs = []
-        piece, grad_middle, grad_mixed = pump.end((piece, grad_middle, grad_mixed))
+        piece, grad_middle, grad_branch = pump.end((piece, grad_middle, grad_branch))
         pump.add(
             scatter_steps(plan, [piece]),
-            lambda out, layer=layer: other_shards.__setitem__(layer, out),
+            lambda out, layer=layer: mlp_shards.__setitem__(layer, out),
         )
         pump.begin()
-        grad_proj = attend_back(projected, grad_mixed.reshape(seqs, tokens, width))
-        grad_proj = pump.end(tuple(grad_proj))
+        grad_mixed, branch_whole = mix_back(grad_branch, w_out_rel, mover)
+        grad_mixed = grad_mixed.reshape(seqs, tokens, width)
+        grad_proj = ()
+        for seq in range(seqs):
+            if seq == seqs - 1:
+                grad_proj, grad_mixed, branch_whole = pump.end(
+                    (grad_proj, grad_mixed, branch_whole)
+                )
+                pump.begin()
+            grad_proj = attend_back(projected, grad_mixed, seq, tuple(grad_proj))
+        if layer == 0:
+            grad_proj = pump.end(tuple(grad_proj))
+            pump.begin()
         grad_proj = [part.reshape(-1, width) for part in grad_proj]
-        pump.begin()
         results = project_back(
             grad_proj,
             grad_middle,
@@ -1025,46 +1152,39 @@
         if layer == 0:
             grad_embed, grad_maskvec = results[2:]
             extra_pairs = [(patch_rel, [grad_embed])]
-        pieces = [weight_grads([(normed_one, grad_proj)] + extra_pairs)]
+        pieces = [
+            weight_grads([(normed_one, grad_proj), (mixed_rel, [branch_whole])] + extra_pairs)
+        ]
         extra_pairs = []
-    vectors = gain_ones + gain_twos + [grad_gain_final, grad_maskvec]
-    pieces.append(small_grads(flow, vectors, seqs))
-    pieces = pump.end(pieces)
-    pump.add(scatter_steps(plan, pieces), lambda out: qkv_shards.__setitem__(0, out))
+        if layer == 0:
+            vectors = gain_ones + gain_twos + [grad_gain_final, grad_maskvec]
+            pieces.append(small_grads(flow, vectors, seqs))
+        pieces, flow = pump.end((pieces, flow))
+        pump.add(
+            scatter_steps(plan, pieces),
+            lambda out, layer=layer: attn_shards.__setitem__(layer, out),
+        )
+        if layer:
+            pump.begin()
     pump.drain()
-    last, qkv_one = qkv_shards
-    other_zero, other_one = other_shards
-    start = 2 * ff_width
-    stop = start + width
-    raw = (
-        jnp.concatenate([last[:, 3 * width : 4 * width], other_one[:, stop:]], axis=1),
-        jnp.concatenate(
-            [last[:, : 3 * width], other_zero[:, start:stop], qkv_one, other_one[:, start:stop]],
-            axis=1,
-        ),
-        jnp.concatenate([other_zero[:, :start], other_one[:, :start]], axis=1),
-        last[:, 4 * width : 4 * width + tokens],
-        last[:, 4 * width + tokens : 4 * width + small_cols],
-    )
-    totals = jnp.stack([loss_local] + [jnp.sum(part * part) for part in raw])
-    totals = jnp.broadcast_to(totals[:, None], (totals.shape[0], LANES))
+    last, attn_one = attn_shards
+    pieces = (last, attn_one, mlp_shards[0], mlp_shards[1])
+    totals = norm_totals(*pieces, loss_row, width, tokens)
     for perm in [plan.core_stage] + plan.stages:
         totals = totals + plan.swap(totals, perm)
-    total_loss = totals[0, 0]
-    clipped = []
-    for group, part in enumerate(raw):
-        limit = entry_clip * jnp.sqrt(jnp.float32(part.size * plan.count))
-        norm_value = jnp.sqrt(totals[group + 1, 0])
-        clipped.append(part * (limit / jnp.maximum(norm_value, limit)))
-    edge_new = adam_step(edge_w, edge_m, edge_v, edge_t, clipped[0])
-    attn_new = adam_step(attn_w, attn_m, attn_v, attn_t, clipped[1])
-    mlp_new = adam_step(mlp_w, mlp_m, mlp_v, mlp_t, clipped[2])
-    posit_new = adam_step(posit_w, posit_m, posit_v, posit_t, clipped[3])
-    vecs_new = [
-        part.T for part in adam_step(vecs_w.T, vecs_m.T, vecs_v.T, vecs_t.T, clipped[4].T)
+    groups = [
+        (edge_w, edge_m, edge_v, edge_t),
+        (attn_w, attn_m, attn_v, attn_t),
+        (mlp_w, mlp_m, mlp_v, mlp_t),
+        (posit_w, posit_m, posit_v, posit_t),
+        (vecs_w.T, vecs_m.T, vecs_v.T, vecs_t.T),
     ]
-    news = (edge_new, attn_new, mlp_new, posit_new, vecs_new)
-    return (total_loss,) + tuple(group[part] for part in range(4) for group in news)
+    sizes = [group[0].size * plan.count for group in groups]
+    news = update(totals, *pieces, groups, sizes, width, tokens)
+    news = [
+        [news[4 * group + part] for group in range(4)] + [news[16 + part].T] for part in range(4)
+    ]
+    return (totals[0, 0] / total_masked,) + tuple(new for part in news for new in part)
 
 
 def solution(mesh):

time: 844 us -> 785 us (0.930)
  local copies, waits for them, and re-layouts: 125 us -> 53.9 us
  waiting for transfers between devices: 220 us -> 268 us
  other arithmetic: 71.8 us -> 40.9 us
  Pallas kernels: 333 us -> 354 us
  starting transfers between devices: 79.4 us -> 58.5 us
    unnamed x326 -> x214, local copies, waits for them, and re-layouts: 115 us -> 45.4 us
    ppermute x68 -> x62, waiting for transfers between devices: 220 us -> 268 us  [swap(): return lax.ppermute(value, AXES, perm)]
    ppermute x68 -> x62, starting transfers between devices: 79.4 us -> 58.5 us  [swap(): return lax.ppermute(value, AXES, perm)]
    convert_element_type x5, other arithmetic: 20 us -> 4.48 us  [half(): return values.astype(half_type)]
    concatenate x15 -> x9, other arithmetic: 11.2 us -> 2.6 us  [the longest x3 2.16 us: local(): own[index] = jnp.concatenate([own[index], got], axis=0)]
    pallas_call x2 -> x6, Pallas kernels: 50.2 us -> 54.6 us  [the longest x4 49.6 us: attend_back(): pl.pallas_call(kernel, grid=(blocks,), in_specs=specs + [block] + [pl.Blo...]
  transfers between devices with their start and end apart: 68 -> 62, of which waited for: 30 -> 36; matrix products, arithmetic and copies ran while one was open for 5% -> 4% of each run, Pallas kernels for 32% -> 37%
where the time goes in v5:
time: 785 us; the launch traced here: 780 us
  Pallas kernels  354 us (45%)
  waiting for transfers between devices  268 us (34%)
  starting transfers between devices  58.5 us (7%)
  local copies, waits for them, and re-layouts  53.9 us (7%)
  other arithmetic  40.9 us (5%)
    ppermute x62, waiting for transfers between devices, swap(): return lax.ppermute(value, AXES, perm)  268 us
    pallas_call x4, Pallas kernels, attend(): pl.pallas_call(attend_kernel, grid=(seqs, blocks), in_specs=qkv_specs(tok...  62 us
    pallas_call x4, Pallas kernels, feed_forward(): pl.pallas_call(kernel, grid=(steps,), in_specs=[whole_block(normed.shape)...  61.2 us
    ppermute x62, starting transfers between devices, swap(): return lax.ppermute(value, AXES, perm)  58.5 us
    pallas_call x4, Pallas kernels, attend_back(): pl.pallas_call(kernel, grid=(blocks,), in_specs=specs + [block] + [pl.Blo...  49.6 us
    pallas_call x4, Pallas kernels, weight_grads(): pl.pallas_call(kernel, grid=(total,), in_specs=specs, out_specs=[block, b...  48.4 us
    unnamed x214, local copies, waits for them, and re-layouts  45.4 us
    pallas_call x2, Pallas kernels, feed_back(): pl.pallas_call(kernel, grid=(steps,), in_specs=[full, column, full, whole...  33.7 us
  transfers between devices with their start and end apart: 62, of which 36 were waited for; matrix products, arithmetic and copies ran while one was open for 4% of the time, Pallas kernels for 37%

profile of v5, /device:TPU:0, one launch (start us, length us, event | category | flops | bytes accessed | tf_op | source)
XLA Modules:
  0.0 779.7 jit_solution(16846449477866830881)
XLA Ops:
  22.5 11.3 %collective-permute-done.1 = bf16[24,6144]{1,0:T(8,128)(2,1)S(1)} collective-permute-done((bf16[24,6144]{1,0:T(8,128)(2,1)S(1)}, bf16[24,6144]{1,0:T(8,128)(2,1)S(1)}, u32[]{:S(2)}, u32[]{:S(2)}) %collective-permute-start.1) | collective-permute-done | bytes 294944 | tf_op jit(solution)/shard_map/ppermute | solution.py:732
  42.2 9.1 %collective-permute-done.5 = bf16[96,4352]{1,0:T(8,128)(2,1)S(1)} collective-permute-done((bf16[96,4352]{1,0:T(8,128)(2,1)S(1)}, bf16[96,4352]{1,0:T(8,128)(2,1)S(1)}, u32[]{:S(2)}, u32[]{:S(2)}) %collective-permute-start.5) | collective-permute-done | bytes 835616 | tf_op jit(solution)/shard_map/ppermute | solution.py:732
  53.1 14.8 %collective-permute-done.3 = bf16[48,6144]{1,0:T(8,128)(2,1)S(1)} collective-permute-done((bf16[48,6144]{1,0:T(8,128)(2,1)S(1)}, bf16[48,6144]{1,0:T(8,128)(2,1)S(1)}, u32[]{:S(2)}, u32[]{:S(2)}) %collective-permute-start.3) | collective-permute-done | bytes 589856 | tf_op jit(solution)/shard_map/ppermute | solution.py:732
  104.0 15.4 %attend.4 = bf16[2,448,768]{2,1,0:T(8,128)(2,1)S(1)} custom-call(bf16[2,448,2304]{2,1,0:T(8,128)(2,1)S(1)} %bitcast.26, bf16[2,448,2304]{2,1,0:T(8,128)(2,1)S(1)} %bitcast.27, bf16[2,448,2304]{2,1,0:T(8,128)(2,1)S(1)} %bitcast.28), custom_call_target="tpu_custom_call" | custom-call | flops 4932501504 | bytes 5505024 | tf_op jit(solution)/shard_map/attend/pallas_call | solution.py:105
  125.1 11.7 %collective-permute-done.12 = bf16[24,16128]{1,0:T(8,128)(2,1)S(1)} collective-permute-done((bf16[24,16128]{1,0:T(8,128)(2,1)S(1)}, bf16[24,16128]{1,0:T(8,128)(2,1)S(1)}, u32[]{:S(2)}, u32[]{:S(2)}) %collective-permute-start.12) | collective-permute-done | bytes 774176 | tf_op jit(solution)/shard_map/ppermute | solution.py:732
  160.6 13.8 %feed_forward.4.h_ref.one_ref = f32[896,768]{1,0:T(8,128)S(1)} custom-call(bf16[896,768]{1,0:T(8,128)(2,1)S(1)} %get-tuple-element.247.b_ref, f32[896,768]{1,0:T(8,128)S(1)} %get-tuple-element.248.m_ref, bf16[192,6144]{1,0:T(8,128)(2,1)} %copy-done.95, bf16[192,6144]{1,0:T(8,128)(2,1)} %copy-done.97, bf16[192,6144]{1,0:T(8,128)(2,1)} %copy-done.99, ...), custom_call_target="tpu_custom_call" | custom-call | flops 8455716864 | bytes 46006272 | tf_op jit(solution)/shard_map/feed_forward/pallas_call | solution.py:371
  174.4 12.4 %collective-permute-done.16 = bf16[48,16128]{1,0:T(8,128)(2,1)S(1)} collective-permute-done((bf16[48,16128]{1,0:T(8,128)(2,1)S(1)}, bf16[48,16128]{1,0:T(8,128)(2,1)S(1)}, u32[]{:S(2)}, u32[]{:S(2)}) %collective-permute-start.16) | collective-permute-done | bytes 1548320 | tf_op jit(solution)/shard_map/ppermute | solution.py:732
  186.8 12.2 %collective-permute-done.18.own2_ref.uown2_ref.down2_ref = bf16[192,9216]{1,0:T(8,128)(2,1)S(1)} collective-permute-done((bf16[192,9216]{1,0:T(8,128)(2,1)S(1)}, bf16[192,9216]{1,0:T(8,128)(2,1)S(1)}, u32[]{:S(2)}, u32[]{:S(2)}) %collective-permute-start.18) | collective-permute-done | bytes 3538976 | tf_op jit(solution)/shard_map/ppermute | solution.py:732
  213.1 15.8 %attend.5 = bf16[2,448,768]{2,1,0:T(8,128)(2,1)S(1)} custom-call(bf16[2,448,2304]{2,1,0:T(8,128)(2,1)S(1)} %bitcast.29, bf16[2,448,2304]{2,1,0:T(8,128)(2,1)S(1)} %bitcast.30, bf16[2,448,2304]{2,1,0:T(8,128)(2,1)S(1)} %bitcast.31), custom_call_target="tpu_custom_call" | custom-call | flops 4932501504 | bytes 5505024 | tf_op jit(solution)/shard_map/attend/pallas_call | solution.py:105
  234.6 13.7 %feed_forward.5.two_ref = f32[896,768]{1,0:T(8,128)S(1)} custom-call(bf16[896,768]{1,0:T(8,128)(2,1)S(1)} %get-tuple-element.259.b_ref, f32[896,768]{1,0:T(8,128)S(1)} %get-tuple-element.260.m_ref, bf16[192,9216]{1,0:T(8,128)(2,1)} %copy-done.65, bf16[192,9216]{1,0:T(8,128)(2,1)} %copy-done.66, bf16[192,9216]{1,0:T(8,128)(2,1)} %copy-done.67, ...), custom_call_target="tpu_custom_call" | custom-call | flops 8455716864 | bytes 46006272 | tf_op jit(solution)/shard_map/feed_forward/pallas_call | solution.py:371
  273.3 15.5 %attend.6 = bf16[2,448,768]{2,1,0:T(8,128)(2,1)S(1)} custom-call(bf16[2,448,2304]{2,1,0:T(8,128)(2,1)S(1)} %bitcast.53, bf16[2,448,2304]{2,1,0:T(8,128)(2,1)S(1)} %bitcast.54, bf16[2,448,2304]{2,1,0:T(8,128)(2,1)S(1)} %bitcast.55), custom_call_target="tpu_custom_call" | custom-call | flops 4932501504 | bytes 5505024 | tf_op jit(solution)/shard_map/attend/pallas_call | solution.py:105
  301.5 16.8 %feed_forward.6 = (f32[896,768]{1,0:T(8,128)S(1)}, bf16[896,3072]{1,0:T(8,128)(2,1)}, f32[896,3072]{1,0:T(8,128)}) custom-call(bf16[896,768]{1,0:T(8,128)(2,1)S(1)} %get-tuple-element.279.b_ref.refs_0_, f32[896,768]{1,0:T(8,128)S(1)} %get-tuple-element.280.m_ref, bf16[192,6144]{1,0:T(8,128)(2,1)} %pad_maximum_fusion.1.uown_ref.down_ref, ...), custom_call_target="tpu_custom_call" | custom-call | flops 8455716864 | bytes 46006272 | tf_op jit(solution)/shard_map/feed_forward/pallas_call | solution.py:371
  339.3 15.4 %attend.7 = bf16[2,448,768]{2,1,0:T(8,128)(2,1)S(1)} custom-call(bf16[2,448,2304]{2,1,0:T(8,128)(2,1)S(1)} %bitcast.62, bf16[2,448,2304]{2,1,0:T(8,128)(2,1)S(1)} %bitcast.63, bf16[2,448,2304]{2,1,0:T(8,128)(2,1)S(1)} %bitcast.64), custom_call_target="tpu_custom_call" | custom-call | flops 4932501504 | bytes 5505024 | tf_op jit(solution)/shard_map/attend/pallas_call | solution.py:105
  367.2 17.0 %feed_forward.7 = (f32[896,768]{1,0:T(8,128)S(1)}, bf16[896,3072]{1,0:T(8,128)(2,1)}, f32[896,3072]{1,0:T(8,128)}) custom-call(bf16[896,768]{1,0:T(8,128)(2,1)S(1)} %get-tuple-element.294.b_ref.refs_0_, f32[896,768]{1,0:T(8,128)S(1)} %get-tuple-element.295.m_ref, bf16[192,6144]{1,0:T(8,128)(2,1)} %copy-done.72, bf16[192,6144]{1,0:T(8,128)(2,1)} %copy-done.78, ...), custom_call_target="tpu_custom_call" | custom-call | flops 8455716864 | bytes 46006272 | tf_op jit(solution)/shard_map/feed_forward/pallas_call | solution.py:371
  392.9 16.9 %feed_back.2 = (bf16[896,3072]{1,0:T(8,128)(2,1)S(1)}, bf16[896,768]{1,0:T(8,128)(2,1)S(1)}, f32[896,768]{1,0:T(8,128)S(1)}, bf16[896,768]{1,0:T(8,128)(2,1)S(1)}, f32[1,768]{1,0:T(1,128)S(1)}) custom-call(f32[896,768]{1,0:T(8,128)S(1)} %get-tuple-element.305.flow_ref, f32[896,3072]{1,0:T(8,128)} %get-tuple-element.306.slope_ref, ...), custom_call_target="tpu_custom_call" | custom-call | flops 8455716864 | bytes 46399488 | tf_op jit(solution)/shard_map/feed_back/pallas_call | solution.py:513
  422.4 16.8 %weight_grads.4 = (f32[384,6912]{1,0:T(8,128)}, bf16[384,6912]{1,0:T(8,128)(2,1)S(1)}) custom-call(bf16[896,768]{1,0:T(8,128)(2,1)S(1)} %copy-done.51, bf16[896,768]{1,0:T(8,128)(2,1)S(1)} %copy-done.43, bf16[896,768]{1,0:T(8,128)(2,1)S(1)} %copy-done.57, bf16[896,3072]{1,0:T(8,128)(2,1)S(1)} %copy-done.34, bf16[896,3072]{1,0:T(8,128)(2,1)S(1)} %copy-done.60, ...), custom_call_target="tpu_custom_call" | custom-call | flops 9512681472 | bytes 33619968 | tf_op jit(solution)/shard_map/weight_grads/pallas_call | solution.py:668
  443.0 12.4 %attend_back.4 = (bf16[2,448,768]{2,1,0:T(8,128)(2,1)S(1)}, bf16[2,448,768]{2,1,0:T(8,128)(2,1)S(1)}, bf16[2,448,768]{2,1,0:T(8,128)(2,1)S(1)}) custom-call(bf16[2,448,2304]{2,1,0:T(8,128)(2,1)S(1)} %bitcast.65, bf16[2,448,2304]{2,1,0:T(8,128)(2,1)S(1)} %bitcast.66, bf16[2,448,2304]{2,1,0:T(8,128)(2,1)S(1)} %bitcast.67, bf16[2,448,768]{2,1,0:T(8,128)(2,1)S(1)} %bitcast.73), custom_call_target="tpu_custom_call" | custom-call | flops 4932501504 | bytes 4816896 | tf_op jit(solution)/shard_map/attend_back/pallas_call | solution.py:135
  457.9 8.4 %convert_add_fusion = (f32[192,6912]{1,0:T(8,128)}, bf16[192,6912]{1,0:T(8,128)(2,1)S(1)}) fusion(f32[384,6912]{1,0:T(8,128)} %get-tuple-element.316, bf16[384,6912]{1,0:T(8,128)(2,1)} %copy-done.84), kind=kLoop, calls=%fused_computation | loop fusion | flops 6635520 | bytes 23887872 | tf_op jit(solution)/shard_map/add | solution.py:796
  467.6 12.4 %attend_back.5 = (bf16[2,448,768]{2,1,0:T(8,128)(2,1)S(1)}, bf16[2,448,768]{2,1,0:T(8,128)(2,1)S(1)}, bf16[2,448,768]{2,1,0:T(8,128)(2,1)S(1)}) custom-call(bf16[2,448,2304]{2,1,0:T(8,128)(2,1)S(1)} %bitcast.68, bf16[2,448,2304]{2,1,0:T(8,128)(2,1)S(1)} %bitcast.69, ...), custom_call_target="tpu_custom_call", output_to_operand_aliasing={{0}: (4, {}), {1}: (5, {}), {2}: (6, {})} | custom-call | flops 4932501504 | bytes 4816896 | tf_op jit(solution)/shard_map/attend_back/pallas_call | solution.py:135
  486.7 7.9 %weight_grads.5 = (f32[384,3072]{1,0:T(8,128)S(1)}, bf16[384,3072]{1,0:T(8,128)(2,1)}) custom-call(bf16[896,768]{1,0:T(8,128)(2,1)S(1)} %copy-done.58, bf16[896,768]{1,0:T(8,128)(2,1)S(1)} %copy-done.49, bf16[896,768]{1,0:T(8,128)(2,1)S(1)} %bitcast.41, bf16[896,768]{1,0:T(8,128)(2,1)S(1)} %bitcast.43, bf16[896,768]{1,0:T(8,128)(2,1)S(1)} %bitcast.45, ...), custom_call_target="tpu_custom_call" | custom-call | flops 4227858432 | bytes 14942208 | tf_op jit(solution)/shard_map/weight_grads/pallas_call | solution.py:668
  507.1 16.8 %feed_back.3 = (bf16[896,3072]{1,0:T(8,128)(2,1)S(1)}, bf16[896,768]{1,0:T(8,128)(2,1)S(1)}, f32[896,768]{1,0:T(8,128)S(1)}, bf16[896,768]{1,0:T(8,128)(2,1)S(1)}, f32[1,768]{1,0:T(1,128)S(1)}) custom-call(f32[896,768]{1,0:T(8,128)S(1)} %copy-done.9, f32[896,3072]{1,0:T(8,128)} %get-tuple-element.344.slope_ref, f32[896,768]{1,0:T(8,128)S(1)} %copy-done.7, ...), custom_call_target="tpu_custom_call" | custom-call | flops 8455716864 | bytes 46399488 | tf_op jit(solution)/shard_map/feed_back/pallas_call | solution.py:513
  529.1 14.6 %weight_grads.6 = (f32[384,6144]{1,0:T(8,128)}, bf16[384,6144]{1,0:T(8,128)(2,1)S(1)}) custom-call(bf16[896,768]{1,0:T(8,128)(2,1)S(1)} %copy-done.39, bf16[896,768]{1,0:T(8,128)(2,1)S(1)} %get-tuple-element.345.refs_1_, bf16[896,3072]{1,0:T(8,128)(2,1)S(1)} %get-tuple-element.346.refs_2_, bf16[896,3072]{1,0:T(8,128)(2,1)S(1)} %copy-done.59), custom_call_target="tpu_custom_call" | custom-call | flops 8455716864 | bytes 29884416 | tf_op jit(solution)/shard_map/weight_grads/pallas_call | solution.py:668
  556.4 12.4 %attend_back.6 = (bf16[2,448,768]{2,1,0:T(8,128)(2,1)S(1)}, bf16[2,448,768]{2,1,0:T(8,128)(2,1)S(1)}, bf16[2,448,768]{2,1,0:T(8,128)(2,1)S(1)}) custom-call(bf16[2,448,2304]{2,1,0:T(8,128)(2,1)S(1)} %bitcast.56, bf16[2,448,2304]{2,1,0:T(8,128)(2,1)S(1)} %bitcast.57, bf16[2,448,2304]{2,1,0:T(8,128)(2,1)S(1)} %bitcast.58, bf16[2,448,768]{2,1,0:T(8,128)(2,1)S(1)} %bitcast.71), custom_call_target="tpu_custom_call" | custom-call | flops 4932501504 | bytes 4816896 | tf_op jit(solution)/shard_map/attend_back/pallas_call | solution.py:135
  568.9 8.2 %collective-permute-done.40 = f32[48,6912]{1,0:T(8,128)} collective-permute-done((f32[48,6912]{1,0:T(8,128)S(1)}, f32[48,6912]{1,0:T(8,128)}, u32[]{:S(2)}, u32[]{:S(2)}) %collective-permute-start.40) | collective-permute-done | bytes 1327136 | tf_op jit(solution)/shard_map/ppermute | solution.py:732
  591.4 12.4 %attend_back.7 = (bf16[2,448,768]{2,1,0:T(8,128)(2,1)S(1)}, bf16[2,448,768]{2,1,0:T(8,128)(2,1)S(1)}, bf16[2,448,768]{2,1,0:T(8,128)(2,1)S(1)}) custom-call(bf16[2,448,2304]{2,1,0:T(8,128)(2,1)S(1)} %bitcast.59, bf16[2,448,2304]{2,1,0:T(8,128)(2,1)S(1)} %bitcast.60, ...), custom_call_target="tpu_custom_call", output_to_operand_aliasing={{0}: (4, {}), {1}: (5, {}), {2}: (6, {})} | custom-call | flops 4932501504 | bytes 4816896 | tf_op jit(solution)/shard_map/attend_back/pallas_call | solution.py:135
  606.4 11.1 %collective-permute-done.43 = f32[24,6912]{1,0:T(8,128)S(1)} collective-permute-done((f32[24,6912]{1,0:T(8,128)S(1)}, f32[24,6912]{1,0:T(8,128)S(1)}, u32[]{:S(2)}, u32[]{:S(2)}) %collective-permute-start.43) | collective-permute-done | bytes 663584 | tf_op jit(solution)/shard_map/ppermute | solution.py:732
  624.6 10.1 %project_back.3 = (f32[896,768]{1,0:T(8,128)S(1)}, f32[1,768]{1,0:T(1,128)S(1)}, bf16[896,768]{1,0:T(8,128)(2,1)S(1)}, f32[1,768]{1,0:T(1,128)S(1)}) custom-call(bf16[896,768]{1,0:T(8,128)(2,1)S(1)} %bitcast.32, bf16[896,768]{1,0:T(8,128)(2,1)S(1)} %bitcast.34, bf16[896,768]{1,0:T(8,128)(2,1)S(1)} %bitcast.36, ...), custom_call_target="tpu_custom_call" | custom-call | flops 3170893824 | bytes 15138816 | tf_op jit(solution)/shard_map/project_back/pallas_call | solution.py:611
  636.4 9.2 %weight_grads.7 = (f32[384,3840]{1,0:T(8,128)S(1)}, bf16[384,3840]{1,0:T(8,128)(2,1)S(1)}) custom-call(bf16[896,768]{1,0:T(8,128)(2,1)S(1)} %copy-done.55, bf16[896,768]{1,0:T(8,128)(2,1)S(1)} %copy-done.37, bf16[896,768]{1,0:T(8,128)(2,1)S(1)} %copy-done.54, bf16[896,768]{1,0:T(8,128)(2,1)S(1)} %bitcast.33, bf16[896,768]{1,0:T(8,128)(2,1)S(1)} %bitcast.35, ...), custom_call_target="tpu_custom_call" | custom-call | flops 5284823040 | bytes 18677760 | tf_op jit(solution)/shard_map/weight_grads/pallas_call | solution.py:668
  659.2 14.8 %collective-permute-done.50 = bf16[192,4352]{1,0:T(8,128)(2,1)S(1)} collective-permute-done((bf16[192,4352]{1,0:T(8,128)(2,1)S(1)}, bf16[192,4352]{1,0:T(8,128)(2,1)S(1)}, u32[]{:S(2)}, u32[]{:S(2)}) %collective-permute-start.50) | collective-permute-done | bytes 1671200 | tf_op jit(solution)/shard_map/ppermute | solution.py:732
  687.7 25.0 %collective-permute-done.55 = f32[48,6144]{1,0:T(8,128)S(1)} collective-permute-done((f32[48,6144]{1,0:T(8,128)S(1)}, f32[48,6144]{1,0:T(8,128)S(1)}, u32[]{:S(2)}, u32[]{:S(2)}) %collective-permute-start.55) | collective-permute-done | bytes 1179680 | tf_op jit(solution)/shard_map/ppermute | solution.py:732
  713.4 21.3 %collective-permute-done.52 = f32[48,4352]{1,0:T(8,128)S(1)} collective-permute-done((f32[48,4352]{1,0:T(8,128)S(1)}, f32[48,4352]{1,0:T(8,128)S(1)}, u32[]{:S(2)}, u32[]{:S(2)}) %collective-permute-start.52) | collective-permute-done | bytes 835616 | tf_op jit(solution)/shard_map/ppermute | solution.py:732
  735.1 20.0 %collective-permute-done.53 = f32[24,4352]{1,0:T(8,128)S(1)} collective-permute-done((f32[24,4352]{1,0:T(8,128)S(1)}, f32[24,4352]{1,0:T(8,128)S(1)}, u32[]{:S(2)}, u32[]{:S(2)}) %collective-permute-start.53) | collective-permute-done | bytes 417824 | tf_op jit(solution)/shard_map/ppermute | solution.py:732
  (421 shorter events, 330.0 us)
Async XLA Ops:
  36.6 31.2 %collective-permute-start.4 = (bf16[24,13568]{1,0:T(8,128)(2,1)S(1)}, bf16[24,13568]{1,0:T(8,128)(2,1)S(1)}, u32[]{:S(2)}, u32[]{:S(2)}) collective-permute-start(bf16[24,13568]{1,0:T(8,128)(2,1)S(1)} %constant_dynamic-update-slice_fusion), channel_id=1, source_target_pairs={{0,16},{1,17},{2,18},{3,19},{4,20},{5,21},{6,22},{7,23},{8,24},{9,... | collective-permute-start | bytes 1953800 | tf_op jit(solution)/shard_map/ppermute | solution.py:732
  40.3 27.5 %collective-permute-start.3 = (bf16[48,6144]{1,0:T(8,128)(2,1)S(1)}, bf16[48,6144]{1,0:T(8,128)(2,1)S(1)}, u32[]{:S(2)}, u32[]{:S(2)}) collective-permute-start(bf16[48,6144]{1,0:T(8,128)(2,1)S(1)} %pad_maximum_fusion.10), channel_id=1, source_target_pairs={{0,8},{1,9},{2,10},{3,11},{4,12},{5,13},{6,14},{7,15},{8,0},{9,1},... | collective-permute-start | bytes 1769480 | tf_op jit(solution)/shard_map/ppermute | solution.py:732
  51.4 25.4 %collective-permute-start.9 = (bf16[192,4352]{1,0:T(8,128)(2,1)S(1)}, bf16[192,4352]{1,0:T(8,128)(2,1)S(1)}, u32[]{:S(2)}, u32[]{:S(2)}) collective-permute-start(bf16[192,4352]{1,0:T(8,128)(2,1)S(1)} %pad_maximum_fusion.3.refs_2_.own_ref), channel_id=1, source_target_pairs={{0,2},{1,3},{2,0},{3,1},{4,6},{5,7},{6,4},{7,5},{8,10},{9,11},{10,... | collective-permute-start | bytes 5013512 | tf_op jit(solution)/shard_map/ppermute | solution.py:732
  51.5 25.1 %collective-permute-start.8 = (bf16[192,4352]{1,0:T(8,128)(2,1)S(1)}, bf16[192,4352]{1,0:T(8,128)(2,1)S(1)}, u32[]{:S(2)}, u32[]{:S(2)}) collective-permute-start(bf16[192,4352]{1,0:T(8,128)(2,1)S(1)} %pad_maximum_fusion.3.refs_2_.own_ref), channel_id=1, source_target_pairs={{0,1},{1,0},{2,6},{3,7},{4,5},{5,4},{6,2},{7,3},{8,9},{9,8},{10,14... | collective-permute-start | bytes 5013512 | tf_op jit(solution)/shard_map/ppermute | solution.py:732
  69.4 28.8 %collective-permute-start.6 = (bf16[48,13568]{1,0:T(8,128)(2,1)S(1)}, bf16[48,13568]{1,0:T(8,128)(2,1)S(1)}, u32[]{:S(2)}, u32[]{:S(2)}) collective-permute-start(bf16[48,13568]{1,0:T(8,128)(2,1)S(1)} %pad_maximum_fusion.6), channel_id=1, source_target_pairs={{0,8},{1,9},{2,10},{3,11},{4,12},{5,13},{6,14},{7,15},{8,0},{9,1},... | collective-permute-start | bytes 3907592 | tf_op jit(solution)/shard_map/ppermute | solution.py:732
  98.3 47.9 %collective-permute-start.14 = (bf16[192,6144]{1,0:T(8,128)(2,1)S(1)}, bf16[192,6144]{1,0:T(8,128)(2,1)S(1)}, u32[]{:S(2)}, u32[]{:S(2)}) collective-permute-start(bf16[192,6144]{1,0:T(8,128)(2,1)S(1)} %constant_dynamic-update-slice_fusion.2.uown_ref.down_ref), channel_id=1, source_target_pairs={{0,1},{1,0},{2,6},{3,7},{4,5},{5,4},{6,2},{7,3},{8,9},{9,8},{10,14... | collective-permute-start | bytes 7077896 | tf_op jit(solution)/shard_map/ppermute | solution.py:732
  99.4 46.7 %collective-permute-start.11 = (bf16[192,6144]{1,0:T(8,128)(2,1)S(1)}, bf16[192,6144]{1,0:T(8,128)(2,1)S(1)}, u32[]{:S(2)}, u32[]{:S(2)}) collective-permute-start(bf16[192,6144]{1,0:T(8,128)(2,1)S(1)} %constant_dynamic-update-slice_fusion.2.uown_ref.down_ref), channel_id=1, source_target_pairs={{0,2},{1,3},{2,0},{3,1},{4,6},{5,7},{6,4},{7,5},{8,10},{9,11},{10,... | collective-permute-start | bytes 7077896 | tf_op jit(solution)/shard_map/ppermute | solution.py:732
  99.4 37.4 %collective-permute-start.12 = (bf16[24,16128]{1,0:T(8,128)(2,1)S(1)}, bf16[24,16128]{1,0:T(8,128)(2,1)S(1)}, u32[]{:S(2)}, u32[]{:S(2)}) collective-permute-start(bf16[24,16128]{1,0:T(8,128)(2,1)S(1)} %pad_maximum_fusion.9), channel_id=1, source_target_pairs={{0,16},{1,17},{2,18},{3,19},{4,20},{5,21},{6,22},{7,23},{8,24},{9,... | collective-permute-start | bytes 2322440 | tf_op jit(solution)/shard_map/ppermute | solution.py:732
  103.0 40.6 %collective-permute-start.13 = (bf16[96,9216]{1,0:T(8,128)(2,1)S(1)}, bf16[96,9216]{1,0:T(8,128)(2,1)S(1)}, u32[]{:S(2)}, u32[]{:S(2)}) collective-permute-start(bf16[96,9216]{1,0:T(8,128)(2,1)S(1)} %slice.398), channel_id=1, source_target_pairs={{0,4},{1,5},{2,3},{3,2},{4,0},{5,1},{6,7},{7,6},{8,12},{9,13},{10,... | collective-permute-start | bytes 5308424 | tf_op jit(solution)/shard_map/ppermute | solution.py:732
  148.5 50.5 %collective-permute-start.18 = (bf16[192,9216]{1,0:T(8,128)(2,1)S(1)}, bf16[192,9216]{1,0:T(8,128)(2,1)S(1)}, u32[]{:S(2)}, u32[]{:S(2)}) collective-permute-start(bf16[192,9216]{1,0:T(8,128)(2,1)S(1)} %pad_maximum_fusion.own_ref.uown_ref.down_ref), channel_id=1, source_target_pairs={{0,1},{1,0},{2,6},{3,7},{4,5},{5,4},{6,2},{7,3},{8,9},{9,8},{10,14... | collective-permute-start | bytes 10616840 | tf_op jit(solution)/shard_map/ppermute | solution.py:732
  149.6 49.4 %collective-permute-start.15 = (bf16[192,9216]{1,0:T(8,128)(2,1)S(1)}, bf16[192,9216]{1,0:T(8,128)(2,1)S(1)}, u32[]{:S(2)}, u32[]{:S(2)}) collective-permute-start(bf16[192,9216]{1,0:T(8,128)(2,1)S(1)} %pad_maximum_fusion.own_ref.uown_ref.down_ref), channel_id=1, source_target_pairs={{0,2},{1,3},{2,0},{3,1},{4,6},{5,7},{6,4},{7,5},{8,10},{9,11},{10,... | collective-permute-start | bytes 10616840 | tf_op jit(solution)/shard_map/ppermute | solution.py:732
  150.8 36.0 %collective-permute-start.16 = (bf16[48,16128]{1,0:T(8,128)(2,1)S(1)}, bf16[48,16128]{1,0:T(8,128)(2,1)S(1)}, u32[]{:S(2)}, u32[]{:S(2)}) collective-permute-start(bf16[48,16128]{1,0:T(8,128)(2,1)S(1)} %pad_maximum_fusion.5), channel_id=1, source_target_pairs={{0,8},{1,9},{2,10},{3,11},{4,12},{5,13},{6,14},{7,15},{8,0},{9,1},... | collective-permute-start | bytes 4644872 | tf_op jit(solution)/shard_map/ppermute | solution.py:732
  200.2 51.8 %collective-permute-start.22 = (bf16[192,4352]{1,0:T(8,128)(2,1)}, bf16[192,4352]{1,0:T(8,128)(2,1)}, u32[]{:S(2)}, u32[]{:S(2)}) collective-permute-start(bf16[192,4352]{1,0:T(8,128)(2,1)} %constant_dynamic-update-slice_fusion.12.refs_2_.own_ref.refs_3_.refs_7_.refs_11_), channel_id=1, source_target_pairs={{0,1},{1,0},{2,6},{3,7},{4,5},{5,4},{6,2},{7,3},{8,9},{9,8},{10,14... | collective-permute-start | bytes 5013512 | tf_op jit(solution)/shard_map/ppermute | solution.py:732
  201.2 50.7 %collective-permute-start.20 = (bf16[192,4352]{1,0:T(8,128)(2,1)}, bf16[192,4352]{1,0:T(8,128)(2,1)S(1)}, u32[]{:S(2)}, u32[]{:S(2)}) collective-permute-start(bf16[192,4352]{1,0:T(8,128)(2,1)} %constant_dynamic-update-slice_fusion.12.refs_2_.own_ref.refs_3_.refs_7_.refs_11_), channel_id=1, source_target_pairs={{0,2},{1,3},{2,0},{3,1},{4,6},{5,7},{6,4},{7,5},{8,10},{9,11},{10,... | collective-permute-start | bytes 5013512 | tf_op jit(solution)/shard_map/ppermute | solution.py:732
  203.0 49.0 %collective-permute-start.21 = (bf16[96,6144]{1,0:T(8,128)(2,1)S(1)}, bf16[96,6144]{1,0:T(8,128)(2,1)S(1)}, u32[]{:S(2)}, u32[]{:S(2)}) collective-permute-start(bf16[96,6144]{1,0:T(8,128)(2,1)S(1)} %get-tuple-element.444), channel_id=1, source_target_pairs={{0,4},{1,5},{2,3},{3,2},{4,0},{5,1},{6,7},{7,6},{8,12},{9,13},{10,... | collective-permute-start | bytes 3538952 | tf_op jit(solution)/shard_map/ppermute | solution.py:732
  254.0 41.3 %collective-permute-start.26 = (bf16[192,6144]{1,0:T(8,128)(2,1)}, bf16[192,6144]{1,0:T(8,128)(2,1)}, u32[]{:S(2)}, u32[]{:S(2)}) collective-permute-start(bf16[192,6144]{1,0:T(8,128)(2,1)} %pad_maximum_fusion.1.uown_ref.down_ref), channel_id=1, source_target_pairs={{0,1},{1,0},{2,6},{3,7},{4,5},{5,4},{6,2},{7,3},{8,9},{9,8},{10,14... | collective-permute-start | bytes 7077896 | tf_op jit(solution)/shard_map/ppermute | solution.py:732
  255.1 40.3 %collective-permute-start.24 = (bf16[192,6144]{1,0:T(8,128)(2,1)}, bf16[192,6144]{1,0:T(8,128)(2,1)}, u32[]{:S(2)}, u32[]{:S(2)}) collective-permute-start(bf16[192,6144]{1,0:T(8,128)(2,1)} %pad_maximum_fusion.1.uown_ref.down_ref), channel_id=1, source_target_pairs={{0,2},{1,3},{2,0},{3,1},{4,6},{5,7},{6,4},{7,5},{8,10},{9,11},{10,... | collective-permute-start | bytes 7077896 | tf_op jit(solution)/shard_map/ppermute | solution.py:732
  258.6 36.8 %collective-permute-start.25 = (bf16[96,3840]{1,0:T(8,128)(2,1)}, bf16[96,3840]{1,0:T(8,128)(2,1)S(1)}, u32[]{:S(2)}, u32[]{:S(2)}) collective-permute-start(bf16[96,3840]{1,0:T(8,128)(2,1)} %slice.401), channel_id=1, source_target_pairs={{0,4},{1,5},{2,3},{3,2},{4,0},{5,1},{6,7},{7,6},{8,12},{9,13},{10,... | collective-permute-start | bytes 2211848 | tf_op jit(solution)/shard_map/ppermute | solution.py:732
  295.7 32.1 %collective-permute-start.30 = (bf16[192,3840]{1,0:T(8,128)(2,1)S(1)}, bf16[192,3840]{1,0:T(8,128)(2,1)S(1)}, u32[]{:S(2)}, u32[]{:S(2)}) collective-permute-start(bf16[192,3840]{1,0:T(8,128)(2,1)S(1)} %constant_dynamic-update-slice_fusion.14.own_ref.refs_3_.refs_7_.refs_11_), channel_id=1, source_target_pairs={{0,1},{1,0},{2,6},{3,7},{4,5},{5,4},{6,2},{7,3},{8,9},{9,8},{10,14... | collective-permute-start | bytes 4423688 | tf_op jit(solution)/shard_map/ppermute | solution.py:732
  297.1 30.7 %collective-permute-start.28 = (bf16[192,3840]{1,0:T(8,128)(2,1)S(1)}, bf16[192,3840]{1,0:T(8,128)(2,1)S(1)}, u32[]{:S(2)}, u32[]{:S(2)}) collective-permute-start(bf16[192,3840]{1,0:T(8,128)(2,1)S(1)} %constant_dynamic-update-slice_fusion.14.own_ref.refs_3_.refs_7_.refs_11_), channel_id=1, source_target_pairs={{0,2},{1,3},{2,0},{3,1},{4,6},{5,7},{6,4},{7,5},{8,10},{9,11},{10,... | collective-permute-start | bytes 4423688 | tf_op jit(solution)/shard_map/ppermute | solution.py:732
  297.1 28.9 %collective-permute-start.29 = (bf16[96,6144]{1,0:T(8,128)(2,1)S(1)}, bf16[96,6144]{1,0:T(8,128)(2,1)S(1)}, u32[]{:S(2)}, u32[]{:S(2)}) collective-permute-start(bf16[96,6144]{1,0:T(8,128)(2,1)S(1)} %get-tuple-element.274), channel_id=1, source_target_pairs={{0,4},{1,5},{2,3},{3,2},{4,0},{5,1},{6,7},{7,6},{8,12},{9,13},{10,... | collective-permute-start | bytes 3538952 | tf_op jit(solution)/shard_map/ppermute | solution.py:732
  327.9 33.2 %collective-permute-start.33 = (bf16[192,6144]{1,0:T(8,128)(2,1)S(1)}, bf16[192,6144]{1,0:T(8,128)(2,1)S(1)}, u32[]{:S(2)}, u32[]{:S(2)}) collective-permute-start(bf16[192,6144]{1,0:T(8,128)(2,1)S(1)} %constant_dynamic-update-slice_fusion.16.uown_ref.down_ref), channel_id=1, source_target_pairs={{0,1},{1,0},{2,6},{3,7},{4,5},{5,4},{6,2},{7,3},{8,9},{9,8},{10,14... | collective-permute-start | bytes 7077896 | tf_op jit(solution)/shard_map/ppermute | solution.py:732
  329.3 31.8 %collective-permute-start.32 = (bf16[192,6144]{1,0:T(8,128)(2,1)S(1)}, bf16[192,6144]{1,0:T(8,128)(2,1)S(1)}, u32[]{:S(2)}, u32[]{:S(2)}) collective-permute-start(bf16[192,6144]{1,0:T(8,128)(2,1)S(1)} %constant_dynamic-update-slice_fusion.16.uown_ref.down_ref), channel_id=1, source_target_pairs={{0,2},{1,3},{2,0},{3,1},{4,6},{5,7},{6,4},{7,5},{8,10},{9,11},{10,... | collective-permute-start | bytes 7077896 | tf_op jit(solution)/shard_map/ppermute | solution.py:732
  466.3 32.0 %collective-permute-start.37 = (bf16[192,6912]{1,0:T(8,128)(2,1)S(1)}, bf16[192,6912]{1,0:T(8,128)(2,1)S(1)}, u32[]{:S(2)}, u32[]{:S(2)}) collective-permute-start(bf16[192,6912]{1,0:T(8,128)(2,1)S(1)} %get-tuple-element.424), channel_id=1, source_target_pairs={{0,1},{1,0},{2,6},{3,7},{4,5},{5,4},{6,2},{7,3},{8,9},{9,8},{10,14... | collective-permute-start | bytes 7962632 | tf_op jit(solution)/shard_map/ppermute | solution.py:732
  498.3 45.4 %collective-permute-start.39 = (bf16[384,3072]{1,0:T(8,128)(2,1)}, bf16[384,3072]{1,0:T(8,128)(2,1)}, u32[]{:S(2)}, u32[]{:S(2)}) collective-permute-start(bf16[384,3072]{1,0:T(8,128)(2,1)} %get-tuple-element.342), channel_id=1, source_target_pairs={{0,2},{1,3},{2,0},{3,1},{4,6},{5,7},{6,4},{7,5},{8,10},{9,11},{10,... | collective-permute-start | bytes 7077896 | tf_op jit(solution)/shard_map/ppermute | solution.py:732
  505.5 38.1 %collective-permute-start.38 = (bf16[96,6912]{1,0:T(8,128)(2,1)}, bf16[96,6912]{1,0:T(8,128)(2,1)S(1)}, u32[]{:S(2)}, u32[]{:S(2)}) collective-permute-start(bf16[96,6912]{1,0:T(8,128)(2,1)} %get-tuple-element.430), channel_id=1, source_target_pairs={{0,4},{1,5},{2,3},{3,2},{4,0},{5,1},{6,7},{7,6},{8,12},{9,13},{10,... | collective-permute-start | bytes 3981320 | tf_op jit(solution)/shard_map/ppermute | solution.py:732
  543.7 33.4 %collective-permute-start.42 = (bf16[384,6144]{1,0:T(8,128)(2,1)S(1)}, bf16[384,6144]{1,0:T(8,128)(2,1)S(1)}, u32[]{:S(2)}, u32[]{:S(2)}) collective-permute-start(bf16[384,6144]{1,0:T(8,128)(2,1)S(1)} %get-tuple-element.354), channel_id=1, source_target_pairs={{0,2},{1,3},{2,0},{3,1},{4,6},{5,7},{6,4},{7,5},{8,10},{9,11},{10,... | collective-permute-start | bytes 14155784 | tf_op jit(solution)/shard_map/ppermute | solution.py:732
  546.3 30.7 %collective-permute-start.40 = (f32[48,6912]{1,0:T(8,128)S(1)}, f32[48,6912]{1,0:T(8,128)}, u32[]{:S(2)}, u32[]{:S(2)}) collective-permute-start(f32[48,6912]{1,0:T(8,128)S(1)} %get-tuple-element.438), channel_id=1, source_target_pairs={{0,8},{1,9},{2,10},{3,11},{4,12},{5,13},{6,14},{7,15},{8,0},{9,1},... | collective-permute-start | bytes 3981320 | tf_op jit(solution)/shard_map/ppermute | solution.py:732
  584.8 35.2 %collective-permute-start.45 = (bf16[192,6144]{1,0:T(8,128)(2,1)S(1)}, bf16[192,6144]{1,0:T(8,128)(2,1)S(1)}, u32[]{:S(2)}, u32[]{:S(2)}) collective-permute-start(bf16[192,6144]{1,0:T(8,128)(2,1)S(1)} %get-tuple-element.426), channel_id=1, source_target_pairs={{0,1},{1,0},{2,6},{3,7},{4,5},{5,4},{6,2},{7,3},{8,9},{9,8},{10,14... | collective-permute-start | bytes 7077896 | tf_op jit(solution)/shard_map/ppermute | solution.py:732
  586.6 30.8 %collective-permute-start.43 = (f32[24,6912]{1,0:T(8,128)S(1)}, f32[24,6912]{1,0:T(8,128)S(1)}, u32[]{:S(2)}, u32[]{:S(2)}) collective-permute-start(f32[24,6912]{1,0:T(8,128)S(1)} %slice_add_fusion.13), channel_id=1, source_target_pairs={{0,16},{1,17},{2,18},{3,19},{4,20},{5,21},{6,22},{7,23},{8,24},{9,... | collective-permute-start | bytes 1990664 | tf_op jit(solution)/shard_map/ppermute | solution.py:732
  677.4 35.3 %collective-permute-start.55 = (f32[48,6144]{1,0:T(8,128)S(1)}, f32[48,6144]{1,0:T(8,128)S(1)}, u32[]{:S(2)}, u32[]{:S(2)}) collective-permute-start(f32[48,6144]{1,0:T(8,128)S(1)} %get-tuple-element.440), channel_id=1, source_target_pairs={{0,8},{1,9},{2,10},{3,11},{4,12},{5,13},{6,14},{7,15},{8,0},{9,1},... | collective-permute-start | bytes 3538952 | tf_op jit(solution)/shard_map/ppermute | solution.py:732
  687.1 47.6 %collective-permute-start.52 = (f32[48,4352]{1,0:T(8,128)S(1)}, f32[48,4352]{1,0:T(8,128)S(1)}, u32[]{:S(2)}, u32[]{:S(2)}) collective-permute-start(f32[48,4352]{1,0:T(8,128)S(1)} %get-tuple-element.446), channel_id=1, source_target_pairs={{0,8},{1,9},{2,10},{3,11},{4,12},{5,13},{6,14},{7,15},{8,0},{9,1},... | collective-permute-start | bytes 2506760 | tf_op jit(solution)/shard_map/ppermute | solution.py:732
  (131 other events, 1991.1 us)

commit v6 on v5

--- a/solution.py
+++ b/solution.py
@@ -10,7 +10,8 @@
 TOPK = 2
 LANES = 128
 FF_TILE = 512
-NARROW_STAGES = 1
+ROW_TILE = 64
+PAIRS = 2
 FAST_LANE = True
 
 ln_eps = 1e-05
@@ -43,77 +44,95 @@
     return (lane // HDIM) == which
 
 
-def attend_kernel(q_ref, k_ref, v_ref, o_ref):
-    queries = q_ref[0] * jnp.asarray(score_scale, half_type)
-    keys_all = k_ref[0]
-    values_all = v_ref[0]
-    width = queries.shape[1]
-    mixed = None
-    for which in range(width // HDIM):
-        mask = head_mask(which, width)
-        head_q = jnp.where(mask, queries, jnp.zeros_like(queries))
-        scores = contract(head_q, keys_all, 1, 1)
-        exps = jnp.exp(scores - jnp.max(scores, axis=1, keepdims=True))
-        probs = (exps * (1.0 / jnp.sum(exps, axis=1, keepdims=True))).astype(half_type)
-        head_out = contract(probs, values_all, 1, 0)
-        mixed = head_out if mixed is None else jnp.where(mask, head_out, mixed)
-    o_ref[0] = mixed.astype(half_type)
-
-
-def attend_back_kernel(q_ref, k_ref, v_ref, do_ref, dq_ref, dk_ref, dv_ref):
-    queries = q_ref[0] * jnp.asarray(score_scale, half_type)
-    keys_all = k_ref[0]
-    values_all = v_ref[0]
-    grad_out = do_ref[0]
-    width = queries.shape[1]
-    grad_k = None
-    grad_v = None
-    grad_q_rows = []
-    for which in range(width // HDIM):
-        mask = head_mask(which, width)
-        head_q = jnp.where(mask, queries, jnp.zeros_like(queries))
-        head_do = jnp.where(mask, grad_out, jnp.zeros_like(grad_out))
-        scores = contract(keys_all, head_q, 1, 1)
-        exps = jnp.exp(scores - jnp.max(scores, axis=0, keepdims=True))
-        probs = exps * (1.0 / jnp.sum(exps, axis=0, keepdims=True))
-        grad_probs = contract(values_all, head_do, 1, 1)
-        prods = probs * grad_probs
-        grad_scores = (prods - probs * jnp.sum(prods, axis=0, keepdims=True)).astype(half_type)
-        head_dv = contract(probs.astype(half_type), grad_out, 1, 0)
-        head_dk = contract(grad_scores, queries, 1, 0)
-        head_dq = contract(keys_all, grad_scores, 0, 0)
-        grad_q_rows.append(head_dq[which * HDIM : (which + 1) * HDIM])
-        grad_v = head_dv if grad_v is None else jnp.where(mask, head_dv, grad_v)
-        grad_k = head_dk if grad_k is None else jnp.where(mask, head_dk, grad_k)
-    grad_q = jnp.concatenate(grad_q_rows, axis=0).T * score_scale
-    dq_ref[0] = grad_q.astype(half_type)
-    dk_ref[0] = grad_k.astype(half_type)
-    dv_ref[0] = grad_v.astype(half_type)
-
-
-def qkv_specs(tokens, blocks):
-    return [
-        pl.BlockSpec((1, tokens, LANES), lambda s, j, off=off: (s, 0, off * blocks + j))
-        for off in range(3)
-    ]
+def head_part(values, which):
+    return jnp.where(head_mask(which, LANES), values, jnp.zeros_like(values))
+
+
+def softmax_rows(scores):
+    exps = jnp.exp(scores - jnp.max(scores, axis=1, keepdims=True))
+    return exps * (1.0 / jnp.sum(exps, axis=1, keepdims=True))
+
+
+def attend_kernel(q_ref, k_ref, v_ref, o_ref, score_ref, prob_ref):
+    tokens = q_ref.shape[1]
+    heads = LANES // HDIM
+    for start in range(0, q_ref.shape[2], LANES):
+        cols = slice(start, start + LANES)
+        queries = q_ref[0, :, cols] * jnp.asarray(score_scale, half_type)
+        for which in range(heads):
+            score_ref[which] = contract(head_part(queries, which), k_ref[0, :, cols], 1, 1)
+        for which in range(heads):
+            for row in range(0, tokens, ROW_TILE):
+                rows = slice(row, row + ROW_TILE)
+                prob_ref[which, rows] = softmax_rows(score_ref[which, rows]).astype(half_type)
+        mixed = None
+        for which in range(heads):
+            out = contract(prob_ref[which], v_ref[0, :, cols], 1, 0)
+            mixed = out if mixed is None else jnp.where(head_mask(which, LANES), out, mixed)
+        o_ref[0, :, cols] = mixed.astype(half_type)
+
+
+def attend_back_kernel(q_ref, k_ref, v_ref, do_ref, dq_ref, dk_ref, dv_ref, *scratch):
+    score_ref, grad_ref, prob_ref, back_ref = scratch
+    tokens = q_ref.shape[1]
+    heads = LANES // HDIM
+    for start in range(0, q_ref.shape[2], LANES):
+        cols = slice(start, start + LANES)
+        queries = q_ref[0, :, cols] * jnp.asarray(score_scale, half_type)
+        keys_now = k_ref[0, :, cols]
+        grad_out = do_ref[0, :, cols]
+        for which in range(heads):
+            score_ref[which] = contract(head_part(queries, which), keys_now, 1, 1)
+            grad_ref[which] = contract(head_part(grad_out, which), v_ref[0, :, cols], 1, 1)
+        for which in range(heads):
+            for row in range(0, tokens, ROW_TILE):
+                rows = slice(row, row + ROW_TILE)
+                probs = softmax_rows(score_ref[which, rows])
+                prob_ref[which, rows] = probs.astype(half_type)
+                prods = probs * grad_ref[which, rows]
+                back_ref[which, rows] = (
+                    prods - probs * jnp.sum(prods, axis=1, keepdims=True)
+                ).astype(half_type)
+        turned_k = []
+        turned_v = []
+        grad_q = None
+        for which in range(heads):
+            part = slice(which * HDIM, (which + 1) * HDIM)
+            turned_v.append(contract(grad_out, prob_ref[which], 0, 0)[part])
+            turned_k.append(contract(queries, back_ref[which], 0, 0)[part])
+            out = contract(back_ref[which], keys_now, 1, 0)
+            grad_q = out if grad_q is None else jnp.where(head_mask(which, LANES), out, grad_q)
+        dq_ref[0, :, cols] = (grad_q * score_scale).astype(half_type)
+        dk_ref[0, :, cols] = jnp.concatenate(turned_k, axis=0).T.astype(half_type)
+        dv_ref[0, :, cols] = jnp.concatenate(turned_v, axis=0).T.astype(half_type)
 
 
 def attend(projected):
     seqs, tokens, width3 = projected.shape
     width = width3 // 3
-    blocks = width // LANES
+    wide = PAIRS * LANES
+    blocks = width // wide
+    specs = [
+        pl.BlockSpec((1, tokens, wide), lambda s, j, off=off: (s, 0, off * blocks + j))
+        for off in range(3)
+    ]
+    heads = LANES // HDIM
     return pl.pallas_call(
         attend_kernel,
         grid=(seqs, blocks),
-        in_specs=qkv_specs(tokens, blocks),
-        out_specs=pl.BlockSpec((1, tokens, LANES), lambda s, j: (s, 0, j)),
+        in_specs=specs,
+        out_specs=pl.BlockSpec((1, tokens, wide), lambda s, j: (s, 0, j)),
         out_shape=jax.ShapeDtypeStruct((seqs, tokens, width), half_type),
+        scratch_shapes=[
+            pltpu.VMEM((heads, tokens, tokens), full_type),
+            pltpu.VMEM((heads, tokens, tokens), half_type),
+        ],
         cost_estimate=pl.CostEstimate(
             flops=16 * seqs * tokens * tokens * width,
             transcendentals=seqs * tokens * tokens * width // HDIM,
             bytes_accessed=8 * seqs * tokens * width,
         ),
-        compiler_params=grant(8),
+        compiler_params=grant(16),
         name="attend",
     )(projected, projected, projected)
 
@@ -121,30 +140,37 @@
 def attend_back(projected, grad_mixed, seq, into=()):
     seqs, tokens, width3 = projected.shape
     width = width3 // 3
-    blocks = width // LANES
-    block = pl.BlockSpec((1, tokens, LANES), lambda j: (seq, 0, j))
+    wide = PAIRS * LANES
+    blocks = width // wide
+    block = pl.BlockSpec((1, tokens, wide), lambda j: (seq, 0, j))
     specs = [
-        pl.BlockSpec((1, tokens, LANES), lambda j, off=off: (seq, 0, off * blocks + j))
+        pl.BlockSpec((1, tokens, wide), lambda j, off=off: (seq, 0, off * blocks + j))
         for off in range(3)
     ]
+    heads = LANES // HDIM
+    skip = len(into)
 
     def kernel(q_ref, k_ref, v_ref, do_ref, *refs):
-        attend_back_kernel(q_ref, k_ref, v_ref, do_ref, *refs[-3:])
-
-    shape = jax.ShapeDtypeStruct((seqs, tokens, width), half_type)
+        attend_back_kernel(q_ref, k_ref, v_ref, do_ref, *refs[skip:])
+
+    shape = kept_shape((seqs, tokens, width), half_type)
     return pl.pallas_call(
         kernel,
         grid=(blocks,),
-        in_specs=specs + [block] + [pl.BlockSpec(memory_space=pl.ANY)] * len(into),
+        in_specs=specs + [block] + [pl.BlockSpec(memory_space=pl.ANY)] * skip,
         out_specs=[block, block, block],
         out_shape=[shape, shape, shape],
-        input_output_aliases={4 + place: place for place in range(len(into))},
+        input_output_aliases={4 + place: place for place in range(skip)},
+        scratch_shapes=[
+            pltpu.VMEM((heads, tokens, tokens), kind)
+            for kind in (full_type, full_type, half_type, half_type)
+        ],
         cost_estimate=pl.CostEstimate(
             flops=32 * tokens * tokens * width,
             transcendentals=tokens * tokens * width // HDIM,
             bytes_accessed=14 * tokens * width,
         ),
-        compiler_params=grant(12),
+        compiler_params=grant(20),
         name="attend_back",
     )(projected, projected, projected, grad_mixed, *into)
 
@@ -197,6 +223,10 @@
     return pl.CostEstimate(flops=flops, transcendentals=0, bytes_accessed=moved)
 
 
+def in_hbm(value):
+    return pltpu.with_memory_space_constraint(value, pltpu.HBM)
+
+
 class Weight:
     def __init__(self, blocks, start, cols):
         self.blocks, self.start, self.cols = list(blocks), start, cols
@@ -209,7 +239,7 @@
         return [spec] * len(self.blocks)
 
     def refs(self):
-        return [pltpu.with_memory_space_constraint(block, pltpu.HBM) for block in self.blocks]
+        return [in_hbm(block) for block in self.blocks]
 
 
 def embed(patches, mask, mover, weight, small, keep_patches):
@@ -242,7 +272,7 @@
 
     outs = [shape_of((rows, width), full_type), shape_of((8, width), full_type)]
     if keep_patches:
-        outs.append(shape_of((rows, width), half_type))
+        outs.append(kept_shape((rows, width), half_type))
     args = [patches, mover] + weight.refs() + list(small) + ([mask] if masked else [])
     specs = [whole_block(patches.shape), whole_block(mover.shape)] + weight.specs(width)
     specs += [whole_block(part.shape) for part in small]
@@ -458,8 +488,8 @@
         out_specs=[part, part, part, row, row],
         out_shape=[
             shape_of((rows, width), full_type),
-            shape_of((rows, width), half_type),
-            shape_of((rows, width), half_type),
+            kept_shape((rows, width), half_type),
+            kept_shape((rows, width), half_type),
             shape_of((1, width), full_type),
             shape_of((1, width), full_type),
         ],
@@ -518,8 +548,8 @@
         + w_down.specs(tile),
         out_specs=[column, full, full, full, whole_block((1, width))],
         out_shape=[
-            shape_of((rows, w_up.cols), half_type),
-            shape_of((rows, width), half_type),
+            kept_shape((rows, w_up.cols), half_type),
+            kept_shape((rows, width), half_type),
             shape_of((rows, width), full_type),
             shape_of((rows, width), half_type),
             shape_of((1, width), full_type),
@@ -548,7 +578,7 @@
         grid=(2,),
         in_specs=[part, square, square],
         out_specs=[part, part],
-        out_shape=[shape_of((rows, width), half_type)] * 2,
+        out_shape=[shape_of((rows, width), half_type), kept_shape((rows, width), half_type)],
         cost_estimate=cost(6 * rows * width * width, 10 * rows * width),
         compiler_params=grant(16),
         name="mix_back",
@@ -606,7 +636,7 @@
     if first:
         specs += [whole_block(mover.shape), pl.BlockSpec((tile, 1), lambda j: (j, 0))]
         args += [mover, mask]
-        outs += [shape_of((rows, width), half_type), shape_of((1, width), full_type)]
+        outs += [kept_shape((rows, width), half_type), shape_of((1, width), full_type)]
         out_specs += [part, vector]
     return pl.pallas_call(
         kernel,
@@ -677,7 +707,7 @@
             ),
             compiler_params=grant(30),
         name="weight_grads",
-        )(*args)
+        )(*[in_hbm(arg) for arg in args])
     )
 
 
@@ -757,39 +787,55 @@
     def __init__(self, plan):
         self.plan = plan
         self.jobs = []
-        self.flying = []
-
-    def add(self, steps, done):
-        self.jobs.append([steps, next(steps), done])
+
+    def add(self, steps, done, ticks=()):
+        self.jobs.append(
+            {"steps": steps, "sends": next(steps), "done": done, "stage": 0, "ticks": dict(ticks)}
+        )
+
+    def start(self, job):
+        job["gots"] = [self.plan.swap(value, perm) for value, perm in job["sends"]]
+        job["left"] = job["ticks"].get(job["stage"], 1)
+
+    def advance(self, job, gots):
+        job["stage"] += 1
+        job["gots"] = None
+        try:
+            job["sends"] = job["steps"].send(gots)
+            return True
+        except StopIteration as stop:
+            job["done"](stop.value)
+            return False
 
     def begin(self):
-        self.flying = [
-            [self.plan.swap(value, perm) for value, perm in sends] for _, sends, _ in self.jobs
-        ]
+        for job in self.jobs:
+            if job.get("gots") is None:
+                self.start(job)
 
     def end(self, values=()):
-        flying, values = lax.optimization_barrier((self.flying, values))
-        left = []
-        for (steps, _, done), gots in zip(self.jobs, flying):
-            try:
-                left.append([steps, steps.send(gots), done])
-            except StopIteration as stop:
-                done(stop.value)
-        self.jobs = left
-        self.flying = []
+        due = []
+        for job in self.jobs:
+            job["left"] -= 1
+            if job["left"] == 0:
+                due.append(job)
+        flying, values = lax.optimization_barrier(([job["gots"] for job in due], values))
+        over = [job for job, gots in zip(due, flying) if not self.advance(job, gots)]
+        self.jobs = [job for job in self.jobs if job not in over]
         return values
 
     def drain(self):
-        for steps, sends, done in self.jobs:
-            try:
-                while True:
-                    sends = steps.send([self.plan.swap(value, perm) for value, perm in sends])
-            except StopIteration as stop:
-                done(stop.value)
-        self.jobs = []
-
-
-def scatter_steps(plan, pieces):
+        newest = self.jobs[-1]
+        while self.jobs:
+            self.begin()
+            if self.jobs[-1] is newest:
+                if self.advance(newest, newest["gots"]):
+                    self.start(newest)
+                else:
+                    self.jobs.pop()
+            self.end()
+
+
+def scatter_steps(plan, pieces, narrow):
     gots = yield [(far, plan.core_stage) for _, far in pieces]
     quarter = pieces[0][0].shape[0] // 2
     sums = [
@@ -805,7 +851,7 @@
             return keep + got
         middle = keep.shape[0] // 2
         send = keep[middle:] + got[middle:]
-        if step < NARROW_STAGES:
+        if step < narrow - 1:
             send = half(send)
         keep = keep[:middle] + got[:middle]
 
@@ -820,22 +866,22 @@
     return (weight_new, first_new, second_new, teacher_new)
 
 
-def norm_totals(last, attn_one, mlp_zero, mlp_one, loss_row, width, tokens):
-    stop = mlp_zero.shape[1]
-
-    def kernel(last_ref, attn_ref, zero_ref, one_ref, loss_ref, out_ref):
+def norm_totals(edge, attn_zero, attn_one, mlp_zero, mlp_one, loss_row, width, tokens):
+    stop = 4 * width
+
+    def kernel(edge_ref, first_ref, second_ref, zero_ref, one_ref, loss_ref, out_ref):
         def square(value):
             return jnp.sum(value * value)
 
-        small = last_ref[:, 5 * width :]
+        small = edge_ref[:, width:]
         lane = lax.broadcasted_iota(jnp.int32, small.shape, 1)
         posit = jnp.where(lane < tokens, small, 0.0)
         vecs = jnp.where(lane >= tokens, small, 0.0)
         parts = [
             jnp.sum(loss_ref[...]),
-            square(last_ref[:, 4 * width : 5 * width]) + square(one_ref[:, stop:]),
-            square(last_ref[:, : 4 * width]) + square(attn_ref[...]),
-            square(zero_ref[...]) + square(one_ref[:, :stop]),
+            square(edge_ref[:, :width]) + square(second_ref[:, stop:]),
+            square(first_ref[...]) + square(second_ref[:, :stop]),
+            square(zero_ref[...]) + square(one_ref[...]),
             square(posit),
             square(vecs),
         ]
@@ -845,7 +891,7 @@
             out = jnp.where(row == place, part, out)
         out_ref[...] = out
 
-    args = (last, attn_one, mlp_zero, mlp_one, loss_row)
+    args = (edge, attn_zero, attn_one, mlp_zero, mlp_one, loss_row)
     return pl.pallas_call(
         kernel,
         grid=(1,),
@@ -857,10 +903,10 @@
     )(*args)
 
 
-def update(totals, last, attn_one, mlp_zero, mlp_one, groups, sizes, width, tokens):
+def update(totals, edge, attn_zero, attn_one, mlp_zero, mlp_one, groups, sizes, width, tokens):
     stop = mlp_zero.shape[1]
 
-    def kernel(total_ref, last_ref, attn_ref, zero_ref, one_ref, *refs):
+    def kernel(total_ref, edge_ref, first_ref, second_ref, zero_ref, one_ref, *refs):
         ins, outs = refs[:20], refs[20:]
 
         def step(group, gradient, cols=slice(None)):
@@ -874,19 +920,19 @@
             for ref, new in zip(outs[4 * group : 4 * group + 4], news):
                 ref[:, cols] = new
 
-        step(0, last_ref[:, 4 * width : 5 * width], slice(0, width))
-        step(0, one_ref[:, stop:], slice(width, 2 * width))
-        step(1, last_ref[:, : 4 * width], slice(0, 4 * width))
-        step(1, attn_ref[...], slice(4 * width, 8 * width))
+        step(0, edge_ref[:, :width], slice(0, width))
+        step(0, second_ref[:, 4 * width :], slice(width, 2 * width))
+        step(1, first_ref[...], slice(0, 4 * width))
+        step(1, second_ref[:, : 4 * width], slice(4 * width, 8 * width))
         step(2, zero_ref[...], slice(0, stop))
-        step(2, one_ref[:, :stop], slice(stop, 2 * stop))
-        step(3, last_ref[:, 5 * width : 5 * width + tokens])
+        step(2, one_ref[...], slice(stop, 2 * stop))
+        step(3, edge_ref[:, width : width + tokens])
         start = tokens // LANES * LANES
-        turned = last_ref[:, 5 * width + start : 5 * width + start + LANES].T
+        turned = edge_ref[:, width + start : width + start + LANES].T
         count = ins[16].shape[0]
         step(4, turned[tokens - start : tokens - start + count])
 
-    args = [totals, last, attn_one, mlp_zero, mlp_one] + [part for group in groups for part in group]
+    args = [totals, edge, attn_zero, attn_one, mlp_zero, mlp_one] + [part for group in groups for part in group]
     outs = [shape_of(part.shape, full_type) for group in groups for part in group]
     return pl.pallas_call(
         kernel,
@@ -961,8 +1007,8 @@
         [s_two[0], s_head],
         [s_two[1]],
     ]
-    groups = [[0], [1], [2, 3], [4, 5, 6]]
-    group_start = [0, 1, 2, 4]
+    groups = [[0], [1], [2], [3], [4, 5, 6]]
+    group_start = [0, 1, 2, 3, 4]
 
     def attn_weights(blocks, start):
         return Weight(blocks, start, 3 * width), Weight(blocks, start + 3 * width, width)
@@ -1105,39 +1151,46 @@
 
     gain_ones = [None] * LAYERS
     gain_twos = [None] * LAYERS
-    attn_shards = [None] * LAYERS
-    mlp_shards = [None] * LAYERS
-    extra_pairs = [(final_normed, [grad_pred])]
+    shards = {}
+    last_stage = len(plan.stages)
+
+    def send_off(name, pieces, narrow, ticks=()):
+        pump.add(
+            scatter_steps(plan, pieces, narrow), lambda out: shards.__setitem__(name, out), ticks
+        )
+
     for layer in reversed(range(LAYERS)):
         w_qkv, (states, normed_one, projected, mixed_rel, w_out_rel) = saved_attn[layer]
         (w_up, w_down), middle, normed_two, active, slope = saved_mlp[layer]
+        pump.begin()
         grad_hidden, grad_down, grad_middle, grad_branch, gain_twos[layer] = feed_back(
             flow, slope, middle, table, LAYERS + layer, w_up, w_down
         )
-        piece = weight_grads(
-            [(normed_two, [grad_hidden]), (grad_down, [active])] + extra_pairs
+        grad_hidden, grad_down, grad_middle, grad_branch = pump.end(
+            (grad_hidden, grad_down, grad_middle, grad_branch)
         )
-        extra_pairs = []
-        piece, grad_middle, grad_branch = pump.end((piece, grad_middle, grad_branch))
-        pump.add(
-            scatter_steps(plan, [piece]),
-            lambda out, layer=layer: mlp_shards.__setitem__(layer, out),
+        pump.begin()
+        piece = weight_grads([(normed_two, [grad_hidden]), (grad_down, [active])])
+        piece, grad_branch = pump.end((piece, grad_branch))
+        send_off(
+            ("mlp", layer), [piece], 3, {1: 2, last_stage: 2} if layer else {last_stage: 2}
         )
         pump.begin()
         grad_mixed, branch_whole = mix_back(grad_branch, w_out_rel, mover)
         grad_mixed = grad_mixed.reshape(seqs, tokens, width)
         grad_proj = ()
-        for seq in range(seqs):
-            if seq == seqs - 1:
-                grad_proj, grad_mixed, branch_whole = pump.end(
-                    (grad_proj, grad_mixed, branch_whole)
-                )
-                pump.begin()
+        for seq in range(seqs - 1):
             grad_proj = attend_back(projected, grad_mixed, seq, tuple(grad_proj))
+        grad_proj, grad_mixed, branch_whole = pump.end((grad_proj, grad_mixed, branch_whole))
+        pump.begin()
+        grad_proj = attend_back(projected, grad_mixed, seqs - 1, tuple(grad_proj))
+        grad_proj = [part.reshape(-1, width) for part in grad_proj]
+        pairs = [(normed_one, grad_proj), (mixed_rel, [branch_whole])]
         if layer == 0:
-            grad_proj = pump.end(tuple(grad_proj))
+            piece = weight_grads(pairs)
+            piece, grad_proj = pump.end((piece, grad_proj))
+            send_off(("attn", 0), [piece], 3)
             pump.begin()
-        grad_proj = [part.reshape(-1, width) for part in grad_proj]
         results = project_back(
             grad_proj,
             grad_middle,
@@ -1149,26 +1202,28 @@
             None if layer else mask_flat,
         )
         flow, gain_ones[layer] = results[:2]
-        if layer == 0:
-            grad_embed, grad_maskvec = results[2:]
-            extra_pairs = [(patch_rel, [grad_embed])]
-        pieces = [
-            weight_grads([(normed_one, grad_proj), (mixed_rel, [branch_whole])] + extra_pairs)
-        ]
-        extra_pairs = []
-        if layer == 0:
-            vectors = gain_ones + gain_twos + [grad_gain_final, grad_maskvec]
-            pieces.append(small_grads(flow, vectors, seqs))
-        pieces, flow = pump.end((pieces, flow))
-        pump.add(
-            scatter_steps(plan, pieces),
-            lambda out, layer=layer: attn_shards.__setitem__(layer, out),
-        )
         if layer:
+            flow, grad_proj = pump.end((flow, grad_proj))
+            pairs = [(normed_one, grad_proj), (mixed_rel, [branch_whole])]
+            pairs.append((final_normed, [grad_pred]))
             pump.begin()
+            piece = weight_grads(pairs)
+            piece, flow = pump.end((piece, flow))
+            send_off(("attn", layer), [piece], 2)
+    grad_embed, grad_maskvec = results[2:]
+    vectors = gain_ones + gain_twos + [grad_gain_final, grad_maskvec]
+    pieces = pump.end(
+        [weight_grads([(patch_rel, [grad_embed])]), small_grads(flow, vectors, seqs)]
+    )
+    send_off("edge", pieces, 2)
     pump.drain()
-    last, attn_one = attn_shards
-    pieces = (last, attn_one, mlp_shards[0], mlp_shards[1])
+    pieces = (
+        shards["edge"],
+        shards["attn", 0],
+        shards["attn", 1],
+        shards["mlp", 0],
+        shards["mlp", 1],
+    )
     totals = norm_totals(*pieces, loss_row, width, tokens)
     for perm in [plan.core_stage] + plan.stages:
         totals = totals + plan.swap(totals, perm)

time: 785 us -> 714 us (0.910)
  waiting for transfers between devices: 268 us -> 214 us
  local copies, waits for them, and re-layouts: 53.9 us -> 43.2 us
  other arithmetic: 40.9 us -> 31.8 us
  starting transfers between devices: 58.5 us -> 67.6 us
    ppermute x62 -> x69, waiting for transfers between devices: 268 us -> 214 us  [swap(): return lax.ppermute(value, AXES, perm)]
    pallas_call x4, Pallas kernels: 62 us -> 45.5 us  [attend(): pl.pallas_call(attend_kernel, grid=(seqs, blocks), in_specs=specs, out_sp...]
    pallas_call x4 -> x5, Pallas kernels: 48.4 us -> 59.8 us  [weight_grads(): pl.pallas_call(kernel, grid=(total,), in_specs=specs, out_specs=[block, b...]
    unnamed x214 -> x195, local copies, waits for them, and re-layouts: 45.4 us -> 35.4 us
    ppermute x62 -> x69, starting transfers between devices: 58.5 us -> 67.6 us  [swap(): return lax.ppermute(value, AXES, perm)]
    pallas_call x4, Pallas kernels: 49.6 us -> 41.3 us  [attend_back(): pl.pallas_call(kernel, grid=(blocks,), in_specs=specs + [block] + [pl.Blo...]
  transfers between devices with their start and end apart: 62 -> 69, of which waited for: 36 -> 35; matrix products, arithmetic and copies ran while one was open for 4% -> 3% of each run, Pallas kernels for 37% -> 40%
where the time goes in v6:
time: 714 us; the launch traced here: 708 us
  Pallas kernels  347 us (49%)
  waiting for transfers between devices  214 us (30%)
  starting transfers between devices  67.6 us (9%)
  local copies, waits for them, and re-layouts  43.2 us (6%)
  other arithmetic  31.8 us (4%)
    ppermute x69, waiting for transfers between devices, swap(): return lax.ppermute(value, AXES, perm)  214 us
    ppermute x69, starting transfers between devices, swap(): return lax.ppermute(value, AXES, perm)  67.6 us
    pallas_call x4, Pallas kernels, feed_forward(): pl.pallas_call(kernel, grid=(steps,), in_specs=[whole_block(normed.shape)...  61.8 us
    pallas_call x5, Pallas kernels, weight_grads(): pl.pallas_call(kernel, grid=(total,), in_specs=specs, out_specs=[block, b...  59.8 us
    pallas_call x4, Pallas kernels, attend(): pl.pallas_call(attend_kernel, grid=(seqs, blocks), in_specs=specs, out_sp...  45.5 us
    pallas_call x4, Pallas kernels, attend_back(): pl.pallas_call(kernel, grid=(blocks,), in_specs=specs + [block] + [pl.Blo...  41.3 us
    pallas_call x2, Pallas kernels, feed_back(): pl.pallas_call(kernel, grid=(steps,), in_specs=[full, column, full, whole...  36 us
    unnamed x195, local copies, waits for them, and re-layouts  35.4 us
  transfers between devices with their start and end apart: 69, of which 35 were waited for; matrix products, arithmetic and copies ran while one was open for 3% of the time, Pallas kernels for 40%

profile of v6, /device:TPU:0, one launch (start us, length us, event | category | flops | bytes accessed | tf_op | source)
XLA Modules:
  0.0 708.2 jit_solution(3203433847864884764)
XLA Ops:
  11.5 7.6 %collective-permute-done = bf16[24,4352]{1,0:T(8,128)(2,1)S(1)} collective-permute-done((bf16[24,4352]{1,0:T(8,128)(2,1)}, bf16[24,4352]{1,0:T(8,128)(2,1)S(1)}, u32[]{:S(2)}, u32[]{:S(2)}) %collective-permute-start) | collective-permute-done | bytes 208928 | tf_op jit(solution)/shard_map/ppermute | solution.py:762
  23.4 11.3 %collective-permute-done.1 = bf16[24,6144]{1,0:T(8,128)(2,1)S(1)} collective-permute-done((bf16[24,6144]{1,0:T(8,128)(2,1)S(1)}, bf16[24,6144]{1,0:T(8,128)(2,1)S(1)}, u32[]{:S(2)}, u32[]{:S(2)}) %collective-permute-start.1) | collective-permute-done | bytes 294944 | tf_op jit(solution)/shard_map/ppermute | solution.py:762
  43.0 9.1 %collective-permute-done.5 = bf16[96,4352]{1,0:T(8,128)(2,1)S(1)} collective-permute-done((bf16[96,4352]{1,0:T(8,128)(2,1)S(1)}, bf16[96,4352]{1,0:T(8,128)(2,1)S(1)}, u32[]{:S(2)}, u32[]{:S(2)}) %collective-permute-start.5) | collective-permute-done | bytes 835616 | tf_op jit(solution)/shard_map/ppermute | solution.py:762
  68.4 12.6 %collective-permute-done.9.refs_3_.own2_ref = bf16[192,4352]{1,0:T(8,128)(2,1)S(1)} collective-permute-done((bf16[192,4352]{1,0:T(8,128)(2,1)S(1)}, bf16[192,4352]{1,0:T(8,128)(2,1)S(1)}, u32[]{:S(2)}, u32[]{:S(2)}) %collective-permute-start.9) | collective-permute-done | bytes 1671200 | tf_op jit(solution)/shard_map/ppermute | solution.py:762
  103.4 11.2 %attend.4 = bf16[2,448,768]{2,1,0:T(8,128)(2,1)S(1)} custom-call(bf16[2,448,2304]{2,1,0:T(8,128)(2,1)S(1)} %bitcast.32, bf16[2,448,2304]{2,1,0:T(8,128)(2,1)S(1)} %bitcast.33, bf16[2,448,2304]{2,1,0:T(8,128)(2,1)S(1)} %bitcast.34), custom_call_target="tpu_custom_call" | custom-call | flops 4932501504 | bytes 5505024 | tf_op jit(solution)/shard_map/attend/pallas_call | solution.py:120
  125.6 10.7 %collective-permute-done.14 = bf16[24,16128]{1,0:T(8,128)(2,1)S(1)} collective-permute-done((bf16[24,16128]{1,0:T(8,128)(2,1)S(1)}, bf16[24,16128]{1,0:T(8,128)(2,1)S(1)}, u32[]{:S(2)}, u32[]{:S(2)}) %collective-permute-start.14) | collective-permute-done | bytes 774176 | tf_op jit(solution)/shard_map/ppermute | solution.py:762
  158.1 14.2 %feed_forward.4.h_ref.one_ref = f32[896,768]{1,0:T(8,128)S(1)} custom-call(bf16[896,768]{1,0:T(8,128)(2,1)S(1)} %get-tuple-element.278.b_ref, f32[896,768]{1,0:T(8,128)S(1)} %get-tuple-element.279.m_ref, bf16[192,6144]{1,0:T(8,128)(2,1)} %copy-done.77, bf16[192,6144]{1,0:T(8,128)(2,1)} %copy-done.79, bf16[192,6144]{1,0:T(8,128)(2,1)} %copy-done.80, ...), custom_call_target="tpu_custom_call" | custom-call | flops 8455716864 | bytes 46006272 | tf_op jit(solution)/shard_map/feed_forward/pallas_call | solution.py:401
  172.4 12.5 %collective-permute-done.18 = bf16[48,16128]{1,0:T(8,128)(2,1)S(1)} collective-permute-done((bf16[48,16128]{1,0:T(8,128)(2,1)S(1)}, bf16[48,16128]{1,0:T(8,128)(2,1)S(1)}, u32[]{:S(2)}, u32[]{:S(2)}) %collective-permute-start.18) | collective-permute-done | bytes 1548320 | tf_op jit(solution)/shard_map/ppermute | solution.py:762
  184.9 10.6 %collective-permute-done.20.own2_ref.uown2_ref.down2_ref = bf16[192,9216]{1,0:T(8,128)(2,1)S(1)} collective-permute-done((bf16[192,9216]{1,0:T(8,128)(2,1)S(1)}, bf16[192,9216]{1,0:T(8,128)(2,1)S(1)}, u32[]{:S(2)}, u32[]{:S(2)}) %collective-permute-start.20) | collective-permute-done | bytes 3538976 | tf_op jit(solution)/shard_map/ppermute | solution.py:762
  209.6 11.4 %attend.5 = bf16[2,448,768]{2,1,0:T(8,128)(2,1)S(1)} custom-call(bf16[2,448,2304]{2,1,0:T(8,128)(2,1)S(1)} %bitcast.35, bf16[2,448,2304]{2,1,0:T(8,128)(2,1)S(1)} %bitcast.36, bf16[2,448,2304]{2,1,0:T(8,128)(2,1)S(1)} %bitcast.37), custom_call_target="tpu_custom_call" | custom-call | flops 4932501504 | bytes 5505024 | tf_op jit(solution)/shard_map/attend/pallas_call | solution.py:120
  226.8 14.2 %feed_forward.5.two_ref = f32[896,768]{1,0:T(8,128)S(1)} custom-call(bf16[896,768]{1,0:T(8,128)(2,1)S(1)} %get-tuple-element.290.b_ref, f32[896,768]{1,0:T(8,128)S(1)} %get-tuple-element.291.m_ref, bf16[192,9216]{1,0:T(8,128)(2,1)} %copy-done.52, bf16[192,9216]{1,0:T(8,128)(2,1)} %copy-done.53, bf16[192,9216]{1,0:T(8,128)(2,1)} %copy-done.54, ...), custom_call_target="tpu_custom_call" | custom-call | flops 8455716864 | bytes 46006272 | tf_op jit(solution)/shard_map/feed_forward/pallas_call | solution.py:401
  266.2 11.6 %attend.6 = bf16[2,448,768]{2,1,0:T(8,128)(2,1)S(1)} custom-call(bf16[2,448,2304]{2,1,0:T(8,128)(2,1)S(1)} %bitcast.59, bf16[2,448,2304]{2,1,0:T(8,128)(2,1)S(1)} %bitcast.60, bf16[2,448,2304]{2,1,0:T(8,128)(2,1)S(1)} %bitcast.61), custom_call_target="tpu_custom_call" | custom-call | flops 4932501504 | bytes 5505024 | tf_op jit(solution)/shard_map/attend/pallas_call | solution.py:120
  290.6 16.7 %feed_forward.6 = (f32[896,768]{1,0:T(8,128)S(1)}, bf16[896,3072]{1,0:T(8,128)(2,1)}, f32[896,3072]{1,0:T(8,128)}) custom-call(bf16[896,768]{1,0:T(8,128)(2,1)S(1)} %get-tuple-element.310.b_ref.refs_0_, f32[896,768]{1,0:T(8,128)S(1)} %get-tuple-element.311.m_ref, bf16[192,6144]{1,0:T(8,128)(2,1)} %pad_maximum_fusion.uown_ref.down_ref, ...), custom_call_target="tpu_custom_call" | custom-call | flops 8455716864 | bytes 46006272 | tf_op jit(solution)/shard_map/feed_forward/pallas_call | solution.py:401
  307.3 8.1 %collective-permute-done.31 = bf16[96,6144]{1,0:T(8,128)(2,1)S(1)} collective-permute-done((bf16[96,6144]{1,0:T(8,128)(2,1)S(1)}, bf16[96,6144]{1,0:T(8,128)(2,1)S(1)}, u32[]{:S(2)}, u32[]{:S(2)}) %collective-permute-start.31) | collective-permute-done | bytes 1179680 | tf_op jit(solution)/shard_map/ppermute | solution.py:762
  328.3 11.2 %attend.7 = bf16[2,448,768]{2,1,0:T(8,128)(2,1)S(1)} custom-call(bf16[2,448,2304]{2,1,0:T(8,128)(2,1)S(1)} %bitcast.68, bf16[2,448,2304]{2,1,0:T(8,128)(2,1)S(1)} %bitcast.69, bf16[2,448,2304]{2,1,0:T(8,128)(2,1)S(1)} %bitcast.70), custom_call_target="tpu_custom_call" | custom-call | flops 4932501504 | bytes 5505024 | tf_op jit(solution)/shard_map/attend/pallas_call | solution.py:120
  352.3 16.7 %feed_forward.7 = (f32[896,768]{1,0:T(8,128)S(1)}, bf16[896,3072]{1,0:T(8,128)(2,1)}, f32[896,3072]{1,0:T(8,128)}) custom-call(bf16[896,768]{1,0:T(8,128)(2,1)S(1)} %get-tuple-element.325.b_ref.refs_0_, f32[896,768]{1,0:T(8,128)S(1)} %get-tuple-element.326.m_ref, bf16[192,6144]{1,0:T(8,128)(2,1)} %copy-done.60, bf16[192,6144]{1,0:T(8,128)(2,1)} %copy-done.66, ...), custom_call_target="tpu_custom_call" | custom-call | flops 8455716864 | bytes 46006272 | tf_op jit(solution)/shard_map/feed_forward/pallas_call | solution.py:401
  369.1 7.8 %head_step.1 = (f32[896,768]{1,0:T(8,128)S(1)}, bf16[896,768]{1,0:T(8,128)(2,1)}, bf16[896,768]{1,0:T(8,128)(2,1)}, f32[1,768]{1,0:T(1,128)S(1)}, f32[1,768]{1,0:T(1,128)S(1)}) custom-call(f32[896,768]{1,0:T(8,128)S(1)} %get-tuple-element.329.h_ref, f32[8,768]{1,0:T(8,128)S(1)} %get-tuple-element.330.table_ref.refs_17_, ...), custom_call_target="tpu_custom_call" | custom-call | flops 4227858432 | bytes 11010048 | tf_op jit(solution)/shard_map/head_step/pallas_call | solution.py:482
  382.8 18.1 %feed_back.2 = (bf16[896,3072]{1,0:T(8,128)(2,1)}, bf16[896,768]{1,0:T(8,128)(2,1)}, f32[896,768]{1,0:T(8,128)S(1)}, bf16[896,768]{1,0:T(8,128)(2,1)S(1)}, f32[1,768]{1,0:T(1,128)S(1)}) custom-call(f32[896,768]{1,0:T(8,128)S(1)} %get-tuple-element.336.flow_ref, f32[896,3072]{1,0:T(8,128)S(1)} %copy-done, f32[896,768]{1,0:T(8,128)S(1)} %copy-done.12, ...), custom_call_target="tpu_custom_call" | custom-call | flops 8455716864 | bytes 46399488 | tf_op jit(solution)/shard_map/feed_back/pallas_call | solution.py:543
  400.9 16.0 %weight_grads.5 = (f32[384,6144]{1,0:T(8,128)S(1)}, bf16[384,6144]{1,0:T(8,128)(2,1)S(1)}) custom-call(bf16[896,768]{1,0:T(8,128)(2,1)} %copy-done.50, bf16[896,768]{1,0:T(8,128)(2,1)} %get-tuple-element.342.refs_1_, bf16[896,3072]{1,0:T(8,128)(2,1)} %get-tuple-element.343.refs_2_, bf16[896,3072]{1,0:T(8,128)(2,1)} %get-tuple-element.344.refs_3_), custom_call_target="tpu_custom_call" | custom-call | flops 8455716864 | bytes 29884416 | tf_op jit(solution)/shard_map/weight_grads/pallas_call | solution.py:698
  422.4 10.3 %attend_back.4 = (bf16[2,448,768]{2,1,0:T(8,128)(2,1)}, bf16[2,448,768]{2,1,0:T(8,128)(2,1)}, bf16[2,448,768]{2,1,0:T(8,128)(2,1)}) custom-call(bf16[2,448,2304]{2,1,0:T(8,128)(2,1)S(1)} %bitcast.71, bf16[2,448,2304]{2,1,0:T(8,128)(2,1)S(1)} %bitcast.72, bf16[2,448,2304]{2,1,0:T(8,128)(2,1)S(1)} %bitcast.73, bf16[2,448,768]{2,1,0:T(8,128)(2,1)S(1)} %bitcast.79), custom_call_target="tpu_custom_call" | custom-call | flops 4932501504 | bytes 4816896 | tf_op jit(solution)/shard_map/attend_back/pallas_call | solution.py:157
  441.5 10.3 %attend_back.5 = (bf16[2,448,768]{2,1,0:T(8,128)(2,1)}, bf16[2,448,768]{2,1,0:T(8,128)(2,1)}, bf16[2,448,768]{2,1,0:T(8,128)(2,1)}) custom-call(bf16[2,448,2304]{2,1,0:T(8,128)(2,1)S(1)} %bitcast.74, bf16[2,448,2304]{2,1,0:T(8,128)(2,1)S(1)} %bitcast.75, ...), custom_call_target="tpu_custom_call", output_to_operand_aliasing={{0}: (4, {}), {1}: (5, {}), {2}: (6, {})} | custom-call | flops 4932501504 | bytes 4816896 | tf_op jit(solution)/shard_map/attend_back/pallas_call | solution.py:157
  462.9 14.0 %weight_grads.6 = (f32[384,3840]{1,0:T(8,128)S(1)}, bf16[384,3840]{1,0:T(8,128)(2,1)}) custom-call(bf16[896,768]{1,0:T(8,128)(2,1)} %get-tuple-element.358.refs_0_, bf16[896,768]{1,0:T(8,128)(2,1)} %get-tuple-element.359.refs_1_, bf16[896,768]{1,0:T(8,128)(2,1)} %get-tuple-element.360.refs_2_, bf16[896,768]{1,0:T(8,128)(2,1)} %bitcast.46, ...), custom_call_target="tpu_custom_call" | custom-call | flops 5284823040 | bytes 18677760 | tf_op jit(solution)/shard_map/weight_grads/pallas_call | solution.py:698
  484.5 18.0 %feed_back.3 = (bf16[896,3072]{1,0:T(8,128)(2,1)}, bf16[896,768]{1,0:T(8,128)(2,1)}, f32[896,768]{1,0:T(8,128)S(1)}, bf16[896,768]{1,0:T(8,128)(2,1)S(1)}, f32[1,768]{1,0:T(1,128)S(1)}) custom-call(f32[896,768]{1,0:T(8,128)S(1)} %get-tuple-element.381.flow_ref, f32[896,3072]{1,0:T(8,128)S(1)} %bitcast.27, f32[896,768]{1,0:T(8,128)S(1)} %copy-done.10, ...), custom_call_target="tpu_custom_call" | custom-call | flops 8455716864 | bytes 46399488 | tf_op jit(solution)/shard_map/feed_back/pallas_call | solution.py:543
  512.4 16.0 %weight_grads.7 = (f32[384,6144]{1,0:T(8,128)S(1)}, bf16[384,6144]{1,0:T(8,128)(2,1)S(1)}) custom-call(bf16[896,768]{1,0:T(8,128)(2,1)} %copy-done.44, bf16[896,768]{1,0:T(8,128)(2,1)} %get-tuple-element.389.refs_1_, bf16[896,3072]{1,0:T(8,128)(2,1)} %get-tuple-element.390.refs_2_, bf16[896,3072]{1,0:T(8,128)(2,1)} %get-tuple-element.391.refs_3_), custom_call_target="tpu_custom_call" | custom-call | flops 8455716864 | bytes 29884416 | tf_op jit(solution)/shard_map/weight_grads/pallas_call | solution.py:698
  537.8 10.5 %attend_back.6 = (bf16[2,448,768]{2,1,0:T(8,128)(2,1)}, bf16[2,448,768]{2,1,0:T(8,128)(2,1)}, bf16[2,448,768]{2,1,0:T(8,128)(2,1)}) custom-call(bf16[2,448,2304]{2,1,0:T(8,128)(2,1)S(1)} %bitcast.62, bf16[2,448,2304]{2,1,0:T(8,128)(2,1)S(1)} %bitcast.63, bf16[2,448,2304]{2,1,0:T(8,128)(2,1)S(1)} %bitcast.64, bf16[2,448,768]{2,1,0:T(8,128)(2,1)S(1)} %bitcast.77), custom_call_target="tpu_custom_call" | custom-call | flops 4932501504 | bytes 4816896 | tf_op jit(solution)/shard_map/attend_back/pallas_call | solution.py:157
  556.0 10.2 %attend_back.7 = (bf16[2,448,768]{2,1,0:T(8,128)(2,1)}, bf16[2,448,768]{2,1,0:T(8,128)(2,1)}, bf16[2,448,768]{2,1,0:T(8,128)(2,1)}) custom-call(bf16[2,448,2304]{2,1,0:T(8,128)(2,1)S(1)} %bitcast.65, bf16[2,448,2304]{2,1,0:T(8,128)(2,1)S(1)} %bitcast.66, ...), custom_call_target="tpu_custom_call", output_to_operand_aliasing={{0}: (4, {}), {1}: (5, {}), {2}: (6, {})} | custom-call | flops 4932501504 | bytes 4816896 | tf_op jit(solution)/shard_map/attend_back/pallas_call | solution.py:157
  566.2 10.7 %weight_grads.8 = (f32[384,3072]{1,0:T(8,128)S(1)}, bf16[384,3072]{1,0:T(8,128)(2,1)S(1)}) custom-call(bf16[896,768]{1,0:T(8,128)(2,1)} %get-tuple-element.408.refs_0_, bf16[896,768]{1,0:T(8,128)(2,1)} %get-tuple-element.409.refs_1_, bf16[896,768]{1,0:T(8,128)(2,1)} %bitcast.38, bf16[896,768]{1,0:T(8,128)(2,1)} %bitcast.40, bf16[896,768]{1,0:T(8,128)(2,1)} %bitcast.42, ...), custom_call_target="tpu_custom_call" | custom-call | flops 4227858432 | bytes 14942208 | tf_op jit(solution)/shard_map/weight_grads/pallas_call | solution.py:698
  591.5 10.7 %project_back.3 = (f32[896,768]{1,0:T(8,128)S(1)}, f32[1,768]{1,0:T(1,128)S(1)}, bf16[896,768]{1,0:T(8,128)(2,1)}, f32[1,768]{1,0:T(1,128)S(1)}) custom-call(bf16[896,768]{1,0:T(8,128)(2,1)S(1)} %bitcast.39, bf16[896,768]{1,0:T(8,128)(2,1)S(1)} %bitcast.41, bf16[896,768]{1,0:T(8,128)(2,1)S(1)} %bitcast.43, bf16[192,4352]{1,0:T(8,128)(2,1)} %copy-done.56, ...), custom_call_target="tpu_custom_call" | custom-call | flops 3170893824 | bytes 15138816 | tf_op jit(solution)/shard_map/project_back/pallas_call | solution.py:641
  611.7 10.8 %collective-permute-done.54 = bf16[48,6144]{1,0:T(8,128)(2,1)S(1)} collective-permute-done((bf16[48,6144]{1,0:T(8,128)(2,1)S(1)}, bf16[48,6144]{1,0:T(8,128)(2,1)S(1)}, u32[]{:S(2)}, u32[]{:S(2)}) %collective-permute-start.54) | collective-permute-done | bytes 589856 | tf_op jit(solution)/shard_map/ppermute | solution.py:762
  622.6 7.2 %collective-permute-done.56 = bf16[192,1280]{1,0:T(8,128)(2,1)S(1)} collective-permute-done((bf16[192,1280]{1,0:T(8,128)(2,1)S(1)}, bf16[192,1280]{1,0:T(8,128)(2,1)S(1)}, u32[]{:S(2)}, u32[]{:S(2)}) %collective-permute-start.56) | collective-permute-done | bytes 491552 | tf_op jit(solution)/shard_map/ppermute | solution.py:762
  650.8 19.3 %collective-permute-done.60 = f32[24,1280]{1,0:T(8,128)S(1)} collective-permute-done((f32[24,1280]{1,0:T(8,128)S(1)}, f32[24,1280]{1,0:T(8,128)S(1)}, u32[]{:S(2)}, u32[]{:S(2)}) %collective-permute-start.60) | collective-permute-done | bytes 122912 | tf_op jit(solution)/shard_map/ppermute | solution.py:762
  670.5 13.1 %collective-permute-done.63 = f32[24,3072]{1,0:T(8,128)S(1)} collective-permute-done((f32[24,3072]{1,0:T(8,128)S(1)}, f32[24,3072]{1,0:T(8,128)S(1)}, u32[]{:S(2)}, u32[]{:S(2)}) %collective-permute-start.63) | collective-permute-done | bytes 294944 | tf_op jit(solution)/shard_map/ppermute | solution.py:762
  (429 shorter events, 311.1 us)
Async XLA Ops:
  52.2 28.9 %collective-permute-start.10 = (bf16[192,4352]{1,0:T(8,128)(2,1)S(1)}, bf16[192,4352]{1,0:T(8,128)(2,1)S(1)}, u32[]{:S(2)}, u32[]{:S(2)}) collective-permute-start(bf16[192,4352]{1,0:T(8,128)(2,1)S(1)} %pad_maximum_fusion.2.refs_2_.own_ref), channel_id=1, source_target_pairs={{0,2},{1,3},{2,0},{3,1},{4,6},{5,7},{6,4},{7,5},{8,10},{9,11},{10,... | collective-permute-start | bytes 5013512 | tf_op jit(solution)/shard_map/ppermute | solution.py:762
  52.3 28.7 %collective-permute-start.9 = (bf16[192,4352]{1,0:T(8,128)(2,1)S(1)}, bf16[192,4352]{1,0:T(8,128)(2,1)S(1)}, u32[]{:S(2)}, u32[]{:S(2)}) collective-permute-start(bf16[192,4352]{1,0:T(8,128)(2,1)S(1)} %pad_maximum_fusion.2.refs_2_.own_ref), channel_id=1, source_target_pairs={{0,1},{1,0},{2,6},{3,7},{4,5},{5,4},{6,2},{7,3},{8,9},{9,8},{10,14... | collective-permute-start | bytes 5013512 | tf_op jit(solution)/shard_map/ppermute | solution.py:762
  64.2 32.3 %collective-permute-start.7 = (bf16[24,4352]{1,0:T(8,128)(2,1)S(1)}, bf16[24,4352]{1,0:T(8,128)(2,1)S(1)}, u32[]{:S(2)}, u32[]{:S(2)}) collective-permute-start(bf16[24,4352]{1,0:T(8,128)(2,1)S(1)} %pad_maximum_fusion.16), channel_id=1, source_target_pairs={{0,16},{1,17},{2,18},{3,19},{4,20},{5,21},{6,22},{7,23},{8,24},{9,... | collective-permute-start | bytes 626696 | tf_op jit(solution)/shard_map/ppermute | solution.py:762
  64.3 32.2 %collective-permute-start.6 = (bf16[48,9216]{1,0:T(8,128)(2,1)S(1)}, bf16[48,9216]{1,0:T(8,128)(2,1)S(1)}, u32[]{:S(2)}, u32[]{:S(2)}) collective-permute-start(bf16[48,9216]{1,0:T(8,128)(2,1)S(1)} %pad_maximum_fusion.5), channel_id=1, source_target_pairs={{0,8},{1,9},{2,10},{3,11},{4,12},{5,13},{6,14},{7,15},{8,0},{9,1},... | collective-permute-start | bytes 2654216 | tf_op jit(solution)/shard_map/ppermute | solution.py:762
  66.8 29.7 %collective-permute-start.8 = (bf16[96,6144]{1,0:T(8,128)(2,1)S(1)}, bf16[96,6144]{1,0:T(8,128)(2,1)S(1)}, u32[]{:S(2)}, u32[]{:S(2)}) collective-permute-start(bf16[96,6144]{1,0:T(8,128)(2,1)S(1)} %pad_maximum_fusion.4), channel_id=1, source_target_pairs={{0,4},{1,5},{2,3},{3,2},{4,0},{5,1},{6,7},{7,6},{8,12},{9,13},{10,... | collective-permute-start | bytes 3538952 | tf_op jit(solution)/shard_map/ppermute | solution.py:762
  96.6 48.3 %collective-permute-start.16 = (bf16[192,6144]{1,0:T(8,128)(2,1)S(1)}, bf16[192,6144]{1,0:T(8,128)(2,1)S(1)}, u32[]{:S(2)}, u32[]{:S(2)}) collective-permute-start(bf16[192,6144]{1,0:T(8,128)(2,1)S(1)} %constant_dynamic-update-slice_fusion.uown_ref.down_ref), channel_id=1, source_target_pairs={{0,1},{1,0},{2,6},{3,7},{4,5},{5,4},{6,2},{7,3},{8,9},{9,8},{10,14... | collective-permute-start | bytes 7077896 | tf_op jit(solution)/shard_map/ppermute | solution.py:762
  99.1 45.8 %collective-permute-start.12 = (bf16[192,6144]{1,0:T(8,128)(2,1)S(1)}, bf16[192,6144]{1,0:T(8,128)(2,1)S(1)}, u32[]{:S(2)}, u32[]{:S(2)}) collective-permute-start(bf16[192,6144]{1,0:T(8,128)(2,1)S(1)} %constant_dynamic-update-slice_fusion.uown_ref.down_ref), channel_id=1, source_target_pairs={{0,2},{1,3},{2,0},{3,1},{4,6},{5,7},{6,4},{7,5},{8,10},{9,11},{10,... | collective-permute-start | bytes 7077896 | tf_op jit(solution)/shard_map/ppermute | solution.py:762
  99.1 37.2 %collective-permute-start.14 = (bf16[24,16128]{1,0:T(8,128)(2,1)S(1)}, bf16[24,16128]{1,0:T(8,128)(2,1)S(1)}, u32[]{:S(2)}, u32[]{:S(2)}) collective-permute-start(bf16[24,16128]{1,0:T(8,128)(2,1)S(1)} %pad_maximum_fusion.8), channel_id=1, source_target_pairs={{0,16},{1,17},{2,18},{3,19},{4,20},{5,21},{6,22},{7,23},{8,24},{9,... | collective-permute-start | bytes 2322440 | tf_op jit(solution)/shard_map/ppermute | solution.py:762
  99.4 41.6 %collective-permute-start.15 = (bf16[96,9216]{1,0:T(8,128)(2,1)S(1)}, bf16[96,9216]{1,0:T(8,128)(2,1)S(1)}, u32[]{:S(2)}, u32[]{:S(2)}) collective-permute-start(bf16[96,9216]{1,0:T(8,128)(2,1)S(1)} %pad_maximum_fusion.1), channel_id=1, source_target_pairs={{0,4},{1,5},{2,3},{3,2},{4,0},{5,1},{6,7},{7,6},{8,12},{9,13},{10,... | collective-permute-start | bytes 5308424 | tf_op jit(solution)/shard_map/ppermute | solution.py:762
  100.7 25.0 %collective-permute-start.13 = (bf16[48,4352]{1,0:T(8,128)(2,1)S(1)}, bf16[48,4352]{1,0:T(8,128)(2,1)S(1)}, u32[]{:S(2)}, u32[]{:S(2)}) collective-permute-start(bf16[48,4352]{1,0:T(8,128)(2,1)S(1)} %pad_maximum_fusion.14), channel_id=1, source_target_pairs={{0,8},{1,9},{2,10},{3,11},{4,12},{5,13},{6,14},{7,15},{8,0},{9,1},... | collective-permute-start | bytes 1253384 | tf_op jit(solution)/shard_map/ppermute | solution.py:762
  145.1 50.5 %collective-permute-start.20 = (bf16[192,9216]{1,0:T(8,128)(2,1)S(1)}, bf16[192,9216]{1,0:T(8,128)(2,1)S(1)}, u32[]{:S(2)}, u32[]{:S(2)}) collective-permute-start(bf16[192,9216]{1,0:T(8,128)(2,1)S(1)} %constant_dynamic-update-slice_fusion.4.own_ref.uown_ref.down_ref), channel_id=1, source_target_pairs={{0,1},{1,0},{2,6},{3,7},{4,5},{5,4},{6,2},{7,3},{8,9},{9,8},{10,14... | collective-permute-start | bytes 10616840 | tf_op jit(solution)/shard_map/ppermute | solution.py:762
  147.1 48.4 %collective-permute-start.17 = (bf16[192,9216]{1,0:T(8,128)(2,1)S(1)}, bf16[192,9216]{1,0:T(8,128)(2,1)S(1)}, u32[]{:S(2)}, u32[]{:S(2)}) collective-permute-start(bf16[192,9216]{1,0:T(8,128)(2,1)S(1)} %constant_dynamic-update-slice_fusion.4.own_ref.uown_ref.down_ref), channel_id=1, source_target_pairs={{0,2},{1,3},{2,0},{3,1},{4,6},{5,7},{6,4},{7,5},{8,10},{9,11},{10,... | collective-permute-start | bytes 10616840 | tf_op jit(solution)/shard_map/ppermute | solution.py:762
  147.2 25.2 %collective-permute-start.19 = (bf16[96,4352]{1,0:T(8,128)(2,1)S(1)}, bf16[96,4352]{1,0:T(8,128)(2,1)S(1)}, u32[]{:S(2)}, u32[]{:S(2)}) collective-permute-start(bf16[96,4352]{1,0:T(8,128)(2,1)S(1)} %pad_maximum_fusion.7), channel_id=1, source_target_pairs={{0,4},{1,5},{2,3},{3,2},{4,0},{5,1},{6,7},{7,6},{8,12},{9,13},{10,... | collective-permute-start | bytes 2506760 | tf_op jit(solution)/shard_map/ppermute | solution.py:762
  147.8 37.1 %collective-permute-start.18 = (bf16[48,16128]{1,0:T(8,128)(2,1)S(1)}, bf16[48,16128]{1,0:T(8,128)(2,1)S(1)}, u32[]{:S(2)}, u32[]{:S(2)}) collective-permute-start(bf16[48,16128]{1,0:T(8,128)(2,1)S(1)} %pad_maximum_fusion.3), channel_id=1, source_target_pairs={{0,8},{1,9},{2,10},{3,11},{4,12},{5,13},{6,14},{7,15},{8,0},{9,1},... | collective-permute-start | bytes 4644872 | tf_op jit(solution)/shard_map/ppermute | solution.py:762
  195.7 48.9 %collective-permute-start.24 = (bf16[192,4352]{1,0:T(8,128)(2,1)S(1)}, bf16[192,4352]{1,0:T(8,128)(2,1)}, u32[]{:S(2)}, u32[]{:S(2)}) collective-permute-start(bf16[192,4352]{1,0:T(8,128)(2,1)S(1)} %constant_dynamic-update-slice_fusion.11.refs_2_.own_ref.refs_3_.refs_7_.refs_11_), channel_id=1, source_target_pairs={{0,1},{1,0},{2,6},{3,7},{4,5},{5,4},{6,2},{7,3},{8,9},{9,8},{10,14... | collective-permute-start | bytes 5013512 | tf_op jit(solution)/shard_map/ppermute | solution.py:762
  197.8 46.9 %collective-permute-start.22 = (bf16[192,4352]{1,0:T(8,128)(2,1)S(1)}, bf16[192,4352]{1,0:T(8,128)(2,1)S(1)}, u32[]{:S(2)}, u32[]{:S(2)}) collective-permute-start(bf16[192,4352]{1,0:T(8,128)(2,1)S(1)} %constant_dynamic-update-slice_fusion.11.refs_2_.own_ref.refs_3_.refs_7_.refs_11_), channel_id=1, source_target_pairs={{0,2},{1,3},{2,0},{3,1},{4,6},{5,7},{6,4},{7,5},{8,10},{9,11},{10,... | collective-permute-start | bytes 5013512 | tf_op jit(solution)/shard_map/ppermute | solution.py:762
  199.4 45.2 %collective-permute-start.23 = (bf16[96,6144]{1,0:T(8,128)(2,1)S(1)}, bf16[96,6144]{1,0:T(8,128)(2,1)S(1)}, u32[]{:S(2)}, u32[]{:S(2)}) collective-permute-start(bf16[96,6144]{1,0:T(8,128)(2,1)S(1)} %get-tuple-element.498), channel_id=1, source_target_pairs={{0,4},{1,5},{2,3},{3,2},{4,0},{5,1},{6,7},{7,6},{8,12},{9,13},{10,... | collective-permute-start | bytes 3538952 | tf_op jit(solution)/shard_map/ppermute | solution.py:762
  246.6 37.8 %collective-permute-start.28 = (bf16[192,6144]{1,0:T(8,128)(2,1)}, bf16[192,6144]{1,0:T(8,128)(2,1)}, u32[]{:S(2)}, u32[]{:S(2)}) collective-permute-start(bf16[192,6144]{1,0:T(8,128)(2,1)} %pad_maximum_fusion.uown_ref.down_ref), channel_id=1, source_target_pairs={{0,1},{1,0},{2,6},{3,7},{4,5},{5,4},{6,2},{7,3},{8,9},{9,8},{10,14... | collective-permute-start | bytes 7077896 | tf_op jit(solution)/shard_map/ppermute | solution.py:762
  248.6 35.8 %collective-permute-start.26 = (bf16[192,6144]{1,0:T(8,128)(2,1)}, bf16[192,6144]{1,0:T(8,128)(2,1)}, u32[]{:S(2)}, u32[]{:S(2)}) collective-permute-start(bf16[192,6144]{1,0:T(8,128)(2,1)} %pad_maximum_fusion.uown_ref.down_ref), channel_id=1, source_target_pairs={{0,2},{1,3},{2,0},{3,1},{4,6},{5,7},{6,4},{7,5},{8,10},{9,11},{10,... | collective-permute-start | bytes 7077896 | tf_op jit(solution)/shard_map/ppermute | solution.py:762
  251.7 32.6 %collective-permute-start.27 = (bf16[96,3840]{1,0:T(8,128)(2,1)}, bf16[96,3840]{1,0:T(8,128)(2,1)S(1)}, u32[]{:S(2)}, u32[]{:S(2)}) collective-permute-start(bf16[96,3840]{1,0:T(8,128)(2,1)} %slice.455), channel_id=1, source_target_pairs={{0,4},{1,5},{2,3},{3,2},{4,0},{5,1},{6,7},{7,6},{8,12},{9,13},{10,... | collective-permute-start | bytes 2211848 | tf_op jit(solution)/shard_map/ppermute | solution.py:762
  284.7 32.1 %collective-permute-start.32 = (bf16[192,3840]{1,0:T(8,128)(2,1)S(1)}, bf16[192,3840]{1,0:T(8,128)(2,1)S(1)}, u32[]{:S(2)}, u32[]{:S(2)}) collective-permute-start(bf16[192,3840]{1,0:T(8,128)(2,1)S(1)} %constant_dynamic-update-slice_fusion.15.own_ref.refs_3_.refs_7_.refs_11_), channel_id=1, source_target_pairs={{0,1},{1,0},{2,6},{3,7},{4,5},{5,4},{6,2},{7,3},{8,9},{9,8},{10,14... | collective-permute-start | bytes 4423688 | tf_op jit(solution)/shard_map/ppermute | solution.py:762
  286.5 30.3 %collective-permute-start.30 = (bf16[192,3840]{1,0:T(8,128)(2,1)S(1)}, bf16[192,3840]{1,0:T(8,128)(2,1)S(1)}, u32[]{:S(2)}, u32[]{:S(2)}) collective-permute-start(bf16[192,3840]{1,0:T(8,128)(2,1)S(1)} %constant_dynamic-update-slice_fusion.15.own_ref.refs_3_.refs_7_.refs_11_), channel_id=1, source_target_pairs={{0,2},{1,3},{2,0},{3,1},{4,6},{5,7},{6,4},{7,5},{8,10},{9,11},{10,... | collective-permute-start | bytes 4423688 | tf_op jit(solution)/shard_map/ppermute | solution.py:762
  286.5 28.9 %collective-permute-start.31 = (bf16[96,6144]{1,0:T(8,128)(2,1)S(1)}, bf16[96,6144]{1,0:T(8,128)(2,1)S(1)}, u32[]{:S(2)}, u32[]{:S(2)}) collective-permute-start(bf16[96,6144]{1,0:T(8,128)(2,1)S(1)} %get-tuple-element.305), channel_id=1, source_target_pairs={{0,4},{1,5},{2,3},{3,2},{4,0},{5,1},{6,7},{7,6},{8,12},{9,13},{10,... | collective-permute-start | bytes 3538952 | tf_op jit(solution)/shard_map/ppermute | solution.py:762
  316.9 29.3 %collective-permute-start.35 = (bf16[192,6144]{1,0:T(8,128)(2,1)S(1)}, bf16[192,6144]{1,0:T(8,128)(2,1)S(1)}, u32[]{:S(2)}, u32[]{:S(2)}) collective-permute-start(bf16[192,6144]{1,0:T(8,128)(2,1)S(1)} %constant_dynamic-update-slice_fusion.17.uown_ref.down_ref), channel_id=1, source_target_pairs={{0,1},{1,0},{2,6},{3,7},{4,5},{5,4},{6,2},{7,3},{8,9},{9,8},{10,14... | collective-permute-start | bytes 7077896 | tf_op jit(solution)/shard_map/ppermute | solution.py:762
  318.6 27.7 %collective-permute-start.34 = (bf16[192,6144]{1,0:T(8,128)(2,1)S(1)}, bf16[192,6144]{1,0:T(8,128)(2,1)S(1)}, u32[]{:S(2)}, u32[]{:S(2)}) collective-permute-start(bf16[192,6144]{1,0:T(8,128)(2,1)S(1)} %constant_dynamic-update-slice_fusion.17.uown_ref.down_ref), channel_id=1, source_target_pairs={{0,2},{1,3},{2,0},{3,1},{4,6},{5,7},{6,4},{7,5},{8,10},{9,11},{10,... | collective-permute-start | bytes 7077896 | tf_op jit(solution)/shard_map/ppermute | solution.py:762
  439.9 37.0 %collective-permute-start.39 = (bf16[192,6144]{1,0:T(8,128)(2,1)}, bf16[192,6144]{1,0:T(8,128)(2,1)S(1)}, u32[]{:S(2)}, u32[]{:S(2)}) collective-permute-start(bf16[192,6144]{1,0:T(8,128)(2,1)} %get-tuple-element.480), channel_id=1, source_target_pairs={{0,1},{1,0},{2,6},{3,7},{4,5},{5,4},{6,2},{7,3},{8,9},{9,8},{10,14... | collective-permute-start | bytes 7077896 | tf_op jit(solution)/shard_map/ppermute | solution.py:762
  476.9 25.6 %collective-permute-start.41 = (bf16[384,3840]{1,0:T(8,128)(2,1)}, bf16[384,3840]{1,0:T(8,128)(2,1)}, u32[]{:S(2)}, u32[]{:S(2)}) collective-permute-start(bf16[384,3840]{1,0:T(8,128)(2,1)} %get-tuple-element.380), channel_id=1, source_target_pairs={{0,2},{1,3},{2,0},{3,1},{4,6},{5,7},{6,4},{7,5},{8,10},{9,11},{10,... | collective-permute-start | bytes 8847368 | tf_op jit(solution)/shard_map/ppermute | solution.py:762
  507.9 24.0 %collective-permute-start.43 = (bf16[192,3840]{1,0:T(8,128)(2,1)}, bf16[192,3840]{1,0:T(8,128)(2,1)S(1)}, u32[]{:S(2)}, u32[]{:S(2)}) collective-permute-start(bf16[192,3840]{1,0:T(8,128)(2,1)} %get-tuple-element.481), channel_id=1, source_target_pairs={{0,1},{1,0},{2,6},{3,7},{4,5},{5,4},{6,2},{7,3},{8,9},{9,8},{10,14... | collective-permute-start | bytes 4423688 | tf_op jit(solution)/shard_map/ppermute | solution.py:762
  554.3 32.6 %collective-permute-start.48 = (bf16[192,6144]{1,0:T(8,128)(2,1)}, bf16[192,6144]{1,0:T(8,128)(2,1)S(1)}, u32[]{:S(2)}, u32[]{:S(2)}) collective-permute-start(bf16[192,6144]{1,0:T(8,128)(2,1)} %get-tuple-element.478), channel_id=1, source_target_pairs={{0,1},{1,0},{2,6},{3,7},{4,5},{5,4},{6,2},{7,3},{8,9},{9,8},{10,14... | collective-permute-start | bytes 7077896 | tf_op jit(solution)/shard_map/ppermute | solution.py:762
  555.6 28.4 %collective-permute-start.46 = (f32[24,6144]{1,0:T(8,128)S(1)}, f32[24,6144]{1,0:T(8,128)S(1)}, u32[]{:S(2)}, u32[]{:S(2)}) collective-permute-start(f32[24,6144]{1,0:T(8,128)S(1)} %slice_add_fusion.19), channel_id=1, source_target_pairs={{0,16},{1,17},{2,18},{3,19},{4,20},{5,21},{6,22},{7,23},{8,24},{9,... | collective-permute-start | bytes 1769480 | tf_op jit(solution)/shard_map/ppermute | solution.py:762
  555.8 31.0 %collective-permute-start.47 = (f32[48,3840]{1,0:T(8,128)S(1)}, f32[48,3840]{1,0:T(8,128)S(1)}, u32[]{:S(2)}, u32[]{:S(2)}) collective-permute-start(f32[48,3840]{1,0:T(8,128)S(1)} %get-tuple-element.499), channel_id=1, source_target_pairs={{0,8},{1,9},{2,10},{3,11},{4,12},{5,13},{6,14},{7,15},{8,0},{9,1},... | collective-permute-start | bytes 2211848 | tf_op jit(solution)/shard_map/ppermute | solution.py:762
  637.9 32.2 %collective-permute-start.61 = (f32[24,6144]{1,0:T(8,128)S(1)}, f32[24,6144]{1,0:T(8,128)S(1)}, u32[]{:S(2)}, u32[]{:S(2)}) collective-permute-start(f32[24,6144]{1,0:T(8,128)S(1)} %slice_add_fusion.17), channel_id=1, source_target_pairs={{0,16},{1,17},{2,18},{3,19},{4,20},{5,21},{6,22},{7,23},{8,24},{9,... | collective-permute-start | bytes 1769480 | tf_op jit(solution)/shard_map/ppermute | solution.py:762
  (128 other events, 1736.8 us)

commit v7 on v6

--- a/solution.py
+++ b/solution.py
@@ -10,6 +10,7 @@
 TOPK = 2
 LANES = 128
 FF_TILE = 512
+SMALL_TILE = 256
 ROW_TILE = 64
 PAIRS = 2
 FAST_LANE = True
@@ -239,17 +240,18 @@
         return [spec] * len(self.blocks)
 
     def refs(self):
-        return [in_hbm(block) for block in self.blocks]
+        return [in_hbm(block) for block in self.blocks[:-1]] + self.blocks[-1:]
 
 
 def embed(patches, mask, mover, weight, small, keep_patches):
     rows, width = patches.shape
     tokens = rows // 2
     masked = mask is not None
+    pieces = small.cols // SMALL_TILE
 
     def kernel(*refs):
         x_ref, mover_ref = refs[:2]
-        w_refs, small_refs, refs = refs[2:6], refs[6:10], refs[10:]
+        w_refs, small_refs, refs = refs[2:6], refs[6 : 6 + 4 * pieces], refs[6 + 4 * pieces :]
         if masked:
             mask_ref, refs = refs[0], refs[1:]
         h_ref, table_ref = refs[:2]
@@ -257,7 +259,8 @@
         if keep_patches:
             refs[2][...] = x_rel
         w_rel = half(contract(stacked(*w_refs), mover_ref[...], 1, 0))
-        small_t = stacked(*small_refs).astype(full_type).T
+        small_parts = [stacked(*small_refs[4 * k : 4 * k + 4]) for k in range(pieces)]
+        small_t = jnp.concatenate(small_parts, axis=1).astype(full_type).T
         posit = small_t[:tokens]
         table = small_t[tokens : tokens + 8]
         table_ref[...] = table
@@ -273,9 +276,10 @@
     outs = [shape_of((rows, width), full_type), shape_of((8, width), full_type)]
     if keep_patches:
         outs.append(kept_shape((rows, width), half_type))
-    args = [patches, mover] + weight.refs() + list(small) + ([mask] if masked else [])
+    args = [patches, mover] + weight.refs() + small.refs() * pieces + ([mask] if masked else [])
     specs = [whole_block(patches.shape), whole_block(mover.shape)] + weight.specs(width)
-    specs += [whole_block(part.shape) for part in small]
+    for k in range(pieces):
+        specs += small.specs(SMALL_TILE, lambda j, k=k: k)
     if masked:
         specs.append(whole_block(mask.shape))
     return pl.pallas_call(
@@ -558,7 +562,7 @@
         cost_estimate=cost(4 * rows * width * w_up.cols, 40 * rows * width + 8 * width * w_up.cols),
         compiler_params=grant(32),
         name="feed_back",
-    )(flow, slope, middle, table, *w_up.refs(), *w_down.refs())
+    )(flow, in_hbm(slope), middle, table, *w_up.refs(), *w_down.refs())
 
 
 def mix_back(grad_branch, w_rel, mover):
@@ -625,7 +629,7 @@
     part = pl.BlockSpec((tile, width), lambda j: (j, 0))
     vector = whole_block((1, width))
     specs = [part] * count
-    args = list(grads)
+    args = [in_hbm(grad) for grad in grads]
     for place in range(count):
         specs += weight.specs(width, lambda j, place=place: place)
         args += weight.refs()
@@ -693,7 +697,10 @@
             )
         )
     block = pl.BlockSpec((near_rows, width), lambda j: (0, j))
-    shapes = [shape_of((near_rows, total * width), kind) for kind in (full_type, half_type)]
+    shapes = [
+        kept_shape((near_rows, total * width), full_type),
+        shape_of((near_rows, total * width), half_type),
+    ]
     return tuple(
         pl.pallas_call(
             kernel,
@@ -1017,8 +1024,7 @@
         return Weight(blocks, start, ff_width), Weight(blocks, start + ff_width, ff_width)
 
     def small_of(blocks):
-        start = blocks[0].shape[1] - t_small.shape[1]
-        return [block[:, start:] for block in blocks]
+        return Weight(blocks, 5 * width, t_small.shape[1])
 
     def finish(blocks):
         return list(blocks) + [plan.swap(blocks[1], plan.core_stage)]

time: 714 us -> 695 us (0.973)
  local copies, waits for them, and re-layouts: 43.2 us -> 20.1 us
    unnamed x195 -> x161, local copies, waits for them, and re-layouts: 35.4 us -> 15.1 us
  transfers between devices with their start and end apart: 69 -> 69, of which waited for: 35 -> 36; matrix products, arithmetic and copies ran while one was open for 3% -> 2% of each run, Pallas kernels for 40% -> 41%
where the time goes in v7:
time: 695 us; the launch traced here: 689 us
  Pallas kernels  350 us (50%)
  waiting for transfers between devices  219 us (32%)
  starting transfers between devices  68.1 us (10%)
  other arithmetic  27.8 us (4%)
  local copies, waits for them, and re-layouts  20.1 us (3%)
    ppermute x69, waiting for transfers between devices, swap(): return lax.ppermute(value, AXES, perm)  219 us
    ppermute x69, starting transfers between devices, swap(): return lax.ppermute(value, AXES, perm)  68.1 us
    pallas_call x5, Pallas kernels, weight_grads(): pl.pallas_call(kernel, grid=(total,), in_specs=specs, out_specs=[block, b...  63.2 us
    pallas_call x4, Pallas kernels, feed_forward(): pl.pallas_call(kernel, grid=(steps,), in_specs=[whole_block(normed.shape)...  61.8 us
    pallas_call x4, Pallas kernels, attend(): pl.pallas_call(attend_kernel, grid=(seqs, blocks), in_specs=specs, out_sp...  45 us
    pallas_call x4, Pallas kernels, attend_back(): pl.pallas_call(kernel, grid=(blocks,), in_specs=specs + [block] + [pl.Blo...  41.7 us
    pallas_call x2, Pallas kernels, feed_back(): pl.pallas_call(kernel, grid=(steps,), in_specs=[full, column, full, whole...  36 us
    pallas_call x4, Pallas kernels, norm_project(): pl.pallas_call(kernel, grid=(steps,), in_specs=[whole_block(states.shape)...  27 us
  transfers between devices with their start and end apart: 69, of which 36 were waited for; matrix products, arithmetic and copies ran while one was open for 2% of the time, Pallas kernels for 41%

profile of v7, /device:TPU:0, one launch (start us, length us, event | category | flops | bytes accessed | tf_op | source)
XLA Modules:
  0.0 689.4 jit_solution(11805714121368053280)
XLA Ops:
  22.6 11.3 %collective-permute-done.1 = bf16[24,6144]{1,0:T(8,128)(2,1)S(1)} collective-permute-done((bf16[24,6144]{1,0:T(8,128)(2,1)S(1)}, bf16[24,6144]{1,0:T(8,128)(2,1)S(1)}, u32[]{:S(2)}, u32[]{:S(2)}) %collective-permute-start.1) | collective-permute-done | bytes 294944 | tf_op jit(solution)/shard_map/ppermute | solution.py:769
  42.2 9.1 %collective-permute-done.5 = bf16[96,4352]{1,0:T(8,128)(2,1)S(1)} collective-permute-done((bf16[96,4352]{1,0:T(8,128)(2,1)S(1)}, bf16[96,4352]{1,0:T(8,128)(2,1)S(1)}, u32[]{:S(2)}, u32[]{:S(2)}) %collective-permute-start.5) | collective-permute-done | bytes 835616 | tf_op jit(solution)/shard_map/ppermute | solution.py:769
  67.6 12.6 %collective-permute-done.9.refs_3_.refs_7_.refs_11_.own2_ref = bf16[192,4352]{1,0:T(8,128)(2,1)S(1)} collective-permute-done((bf16[192,4352]{1,0:T(8,128)(2,1)S(1)}, bf16[192,4352]{1,0:T(8,128)(2,1)S(1)}, u32[]{:S(2)}, u32[]{:S(2)}) %collective-permute-start.9) | collective-permute-done | bytes 1671200 | tf_op jit(solution)/shard_map/ppermute | solution.py:769
  101.4 11.2 %attend.4 = bf16[2,448,768]{2,1,0:T(8,128)(2,1)S(1)} custom-call(bf16[2,448,2304]{2,1,0:T(8,128)(2,1)S(1)} %bitcast.28, bf16[2,448,2304]{2,1,0:T(8,128)(2,1)S(1)} %bitcast.29, bf16[2,448,2304]{2,1,0:T(8,128)(2,1)S(1)} %bitcast.30), custom_call_target="tpu_custom_call" | custom-call | flops 4932501504 | bytes 5505024 | tf_op jit(solution)/shard_map/attend/pallas_call | solution.py:121
  123.7 10.7 %collective-permute-done.14 = bf16[24,16128]{1,0:T(8,128)(2,1)S(1)} collective-permute-done((bf16[24,16128]{1,0:T(8,128)(2,1)S(1)}, bf16[24,16128]{1,0:T(8,128)(2,1)S(1)}, u32[]{:S(2)}, u32[]{:S(2)}) %collective-permute-start.14) | collective-permute-done | bytes 774176 | tf_op jit(solution)/shard_map/ppermute | solution.py:769
  156.1 14.2 %feed_forward.4.h_ref.one_ref = f32[896,768]{1,0:T(8,128)S(1)} custom-call(bf16[896,768]{1,0:T(8,128)(2,1)S(1)} %get-tuple-element.278.b_ref, f32[896,768]{1,0:T(8,128)S(1)} %get-tuple-element.279.m_ref, bf16[192,6144]{1,0:T(8,128)(2,1)} %copy-done.61, bf16[192,6144]{1,0:T(8,128)(2,1)} %copy-done.63, ...), custom_call_target="tpu_custom_call" | custom-call | flops 8455716864 | bytes 46006272 | tf_op jit(solution)/shard_map/feed_forward/pallas_call | solution.py:405
  170.3 14.0 %collective-permute-done.18 = bf16[48,16128]{1,0:T(8,128)(2,1)S(1)} collective-permute-done((bf16[48,16128]{1,0:T(8,128)(2,1)S(1)}, bf16[48,16128]{1,0:T(8,128)(2,1)S(1)}, u32[]{:S(2)}, u32[]{:S(2)}) %collective-permute-start.18) | collective-permute-done | bytes 1548320 | tf_op jit(solution)/shard_map/ppermute | solution.py:769
  184.3 10.6 %collective-permute-done.20.own2_ref.uown2_ref.down2_ref = bf16[192,9216]{1,0:T(8,128)(2,1)S(1)} collective-permute-done((bf16[192,9216]{1,0:T(8,128)(2,1)S(1)}, bf16[192,9216]{1,0:T(8,128)(2,1)S(1)}, u32[]{:S(2)}, u32[]{:S(2)}) %collective-permute-start.20) | collective-permute-done | bytes 3538976 | tf_op jit(solution)/shard_map/ppermute | solution.py:769
  207.4 11.2 %attend.5 = bf16[2,448,768]{2,1,0:T(8,128)(2,1)S(1)} custom-call(bf16[2,448,2304]{2,1,0:T(8,128)(2,1)S(1)} %bitcast.31, bf16[2,448,2304]{2,1,0:T(8,128)(2,1)S(1)} %bitcast.32, bf16[2,448,2304]{2,1,0:T(8,128)(2,1)S(1)} %bitcast.33), custom_call_target="tpu_custom_call" | custom-call | flops 4932501504 | bytes 5505024 | tf_op jit(solution)/shard_map/attend/pallas_call | solution.py:121
  224.2 13.8 %feed_forward.5.two_ref = f32[896,768]{1,0:T(8,128)S(1)} custom-call(bf16[896,768]{1,0:T(8,128)(2,1)S(1)} %get-tuple-element.290.b_ref, f32[896,768]{1,0:T(8,128)S(1)} %get-tuple-element.291.m_ref, bf16[192,9216]{1,0:T(8,128)(2,1)} %copy-done.42, bf16[192,9216]{1,0:T(8,128)(2,1)} %copy-done.44, bf16[192,9216]{1,0:T(8,128)(2,1)} %copy-done.45, ...), custom_call_target="tpu_custom_call" | custom-call | flops 8455716864 | bytes 46006272 | tf_op jit(solution)/shard_map/feed_forward/pallas_call | solution.py:405
  259.5 11.2 %attend.6 = bf16[2,448,768]{2,1,0:T(8,128)(2,1)S(1)} custom-call(bf16[2,448,2304]{2,1,0:T(8,128)(2,1)S(1)} %bitcast.41, bf16[2,448,2304]{2,1,0:T(8,128)(2,1)S(1)} %bitcast.42, bf16[2,448,2304]{2,1,0:T(8,128)(2,1)S(1)} %bitcast.43), custom_call_target="tpu_custom_call" | custom-call | flops 4932501504 | bytes 5505024 | tf_op jit(solution)/shard_map/attend/pallas_call | solution.py:121
  284.8 16.9 %feed_forward.6 = (f32[896,768]{1,0:T(8,128)S(1)}, bf16[896,3072]{1,0:T(8,128)(2,1)}, f32[896,3072]{1,0:T(8,128)}) custom-call(bf16[896,768]{1,0:T(8,128)(2,1)S(1)} %get-tuple-element.310.b_ref.refs_0_, f32[896,768]{1,0:T(8,128)S(1)} %get-tuple-element.311.m_ref, bf16[192,6144]{1,0:T(8,128)(2,1)} %pad_maximum_fusion.uown_ref.down_ref, ...), custom_call_target="tpu_custom_call" | custom-call | flops 8455716864 | bytes 46006272 | tf_op jit(solution)/shard_map/feed_forward/pallas_call | solution.py:405
  301.7 9.4 %collective-permute-done.31 = bf16[96,6144]{1,0:T(8,128)(2,1)S(1)} collective-permute-done((bf16[96,6144]{1,0:T(8,128)(2,1)S(1)}, bf16[96,6144]{1,0:T(8,128)(2,1)S(1)}, u32[]{:S(2)}, u32[]{:S(2)}) %collective-permute-start.31) | collective-permute-done | bytes 1179680 | tf_op jit(solution)/shard_map/ppermute | solution.py:769
  322.7 11.4 %attend.7 = bf16[2,448,768]{2,1,0:T(8,128)(2,1)S(1)} custom-call(bf16[2,448,2304]{2,1,0:T(8,128)(2,1)S(1)} %bitcast.50, bf16[2,448,2304]{2,1,0:T(8,128)(2,1)S(1)} %bitcast.51, bf16[2,448,2304]{2,1,0:T(8,128)(2,1)S(1)} %bitcast.52), custom_call_target="tpu_custom_call" | custom-call | flops 4932501504 | bytes 5505024 | tf_op jit(solution)/shard_map/attend/pallas_call | solution.py:121
  345.9 16.9 %feed_forward.7 = (f32[896,768]{1,0:T(8,128)S(1)}, bf16[896,3072]{1,0:T(8,128)(2,1)}, f32[896,3072]{1,0:T(8,128)}) custom-call(bf16[896,768]{1,0:T(8,128)(2,1)S(1)} %get-tuple-element.325.b_ref.refs_0_, f32[896,768]{1,0:T(8,128)S(1)} %get-tuple-element.326.m_ref, bf16[192,6144]{1,0:T(8,128)(2,1)} %copy-done.49, bf16[192,6144]{1,0:T(8,128)(2,1)} %copy-done.52, ...), custom_call_target="tpu_custom_call" | custom-call | flops 8455716864 | bytes 46006272 | tf_op jit(solution)/shard_map/feed_forward/pallas_call | solution.py:405
  372.5 17.9 %feed_back.2 = (bf16[896,3072]{1,0:T(8,128)(2,1)}, bf16[896,768]{1,0:T(8,128)(2,1)}, f32[896,768]{1,0:T(8,128)S(1)}, bf16[896,768]{1,0:T(8,128)(2,1)S(1)}, f32[1,768]{1,0:T(1,128)S(1)}) custom-call(f32[896,768]{1,0:T(8,128)S(1)} %get-tuple-element.336.flow_ref, f32[896,3072]{1,0:T(8,128)} %get-tuple-element.337.slope_ref, f32[896,768]{1,0:T(8,128)S(1)} %copy-done.9, ...), custom_call_target="tpu_custom_call" | custom-call | flops 8455716864 | bytes 46399488 | tf_op jit(solution)/shard_map/feed_back/pallas_call | solution.py:547
  390.4 16.9 %weight_grads.5 = (f32[384,6144]{1,0:T(8,128)}, bf16[384,6144]{1,0:T(8,128)(2,1)S(1)}) custom-call(bf16[896,768]{1,0:T(8,128)(2,1)} %copy-done.38, bf16[896,768]{1,0:T(8,128)(2,1)} %get-tuple-element.342.refs_1_, bf16[896,3072]{1,0:T(8,128)(2,1)} %get-tuple-element.343.refs_2_, bf16[896,3072]{1,0:T(8,128)(2,1)} %get-tuple-element.344.refs_3_), custom_call_target="tpu_custom_call" | custom-call | flops 8455716864 | bytes 29884416 | tf_op jit(solution)/shard_map/weight_grads/pallas_call | solution.py:705
  411.9 10.2 %attend_back.4 = (bf16[2,448,768]{2,1,0:T(8,128)(2,1)}, bf16[2,448,768]{2,1,0:T(8,128)(2,1)}, bf16[2,448,768]{2,1,0:T(8,128)(2,1)}) custom-call(bf16[2,448,2304]{2,1,0:T(8,128)(2,1)S(1)} %bitcast.53, bf16[2,448,2304]{2,1,0:T(8,128)(2,1)S(1)} %bitcast.54, bf16[2,448,2304]{2,1,0:T(8,128)(2,1)S(1)} %bitcast.55, bf16[2,448,768]{2,1,0:T(8,128)(2,1)S(1)} %bitcast.61), custom_call_target="tpu_custom_call" | custom-call | flops 4932501504 | bytes 4816896 | tf_op jit(solution)/shard_map/attend_back/pallas_call | solution.py:158
  424.3 8.6 %convert_add_fusion.1 = (f32[192,6144]{1,0:T(8,128)}, bf16[192,6144]{1,0:T(8,128)(2,1)}) fusion(f32[384,6144]{1,0:T(8,128)} %get-tuple-element.348, bf16[384,6144]{1,0:T(8,128)(2,1)} %copy-done.56), kind=kLoop, calls=%fused_computation.2 | loop fusion | flops 5898240 | bytes 21233664 | tf_op jit(solution)/shard_map/add | solution.py:849
  434.8 10.7 %attend_back.5 = (bf16[2,448,768]{2,1,0:T(8,128)(2,1)}, bf16[2,448,768]{2,1,0:T(8,128)(2,1)}, bf16[2,448,768]{2,1,0:T(8,128)(2,1)}) custom-call(bf16[2,448,2304]{2,1,0:T(8,128)(2,1)S(1)} %bitcast.56, bf16[2,448,2304]{2,1,0:T(8,128)(2,1)S(1)} %bitcast.57, ...), custom_call_target="tpu_custom_call", output_to_operand_aliasing={{0}: (4, {}), {1}: (5, {}), {2}: (6, {})} | custom-call | flops 4932501504 | bytes 4816896 | tf_op jit(solution)/shard_map/attend_back/pallas_call | solution.py:158
  452.5 14.0 %weight_grads.6 = (f32[384,3840]{1,0:T(8,128)}, bf16[384,3840]{1,0:T(8,128)(2,1)S(1)}) custom-call(bf16[896,768]{1,0:T(8,128)(2,1)} %get-tuple-element.358.refs_0_, bf16[896,768]{1,0:T(8,128)(2,1)} %get-tuple-element.359.refs_1_, bf16[896,768]{1,0:T(8,128)(2,1)} %get-tuple-element.360.refs_2_, bf16[896,768]{1,0:T(8,128)(2,1)} %bitcast.79, ...), custom_call_target="tpu_custom_call" | custom-call | flops 5284823040 | bytes 18677760 | tf_op jit(solution)/shard_map/weight_grads/pallas_call | solution.py:705
  470.5 18.0 %feed_back.3 = (bf16[896,3072]{1,0:T(8,128)(2,1)}, bf16[896,768]{1,0:T(8,128)(2,1)}, f32[896,768]{1,0:T(8,128)S(1)}, bf16[896,768]{1,0:T(8,128)(2,1)S(1)}, f32[1,768]{1,0:T(1,128)S(1)}) custom-call(f32[896,768]{1,0:T(8,128)S(1)} %get-tuple-element.381.flow_ref, f32[896,3072]{1,0:T(8,128)} %get-tuple-element.382.slope_ref, ...), custom_call_target="tpu_custom_call" | custom-call | flops 8455716864 | bytes 46399488 | tf_op jit(solution)/shard_map/feed_back/pallas_call | solution.py:547
  496.9 16.8 %weight_grads.7 = (f32[384,6144]{1,0:T(8,128)}, bf16[384,6144]{1,0:T(8,128)(2,1)S(1)}) custom-call(bf16[896,768]{1,0:T(8,128)(2,1)} %copy-done.32, bf16[896,768]{1,0:T(8,128)(2,1)} %get-tuple-element.389.refs_1_, bf16[896,3072]{1,0:T(8,128)(2,1)} %get-tuple-element.390.refs_2_, bf16[896,3072]{1,0:T(8,128)(2,1)} %get-tuple-element.391.refs_3_), custom_call_target="tpu_custom_call" | custom-call | flops 8455716864 | bytes 29884416 | tf_op jit(solution)/shard_map/weight_grads/pallas_call | solution.py:705
  519.5 10.6 %attend_back.6 = (bf16[2,448,768]{2,1,0:T(8,128)(2,1)}, bf16[2,448,768]{2,1,0:T(8,128)(2,1)}, bf16[2,448,768]{2,1,0:T(8,128)(2,1)}) custom-call(bf16[2,448,2304]{2,1,0:T(8,128)(2,1)S(1)} %bitcast.44, bf16[2,448,2304]{2,1,0:T(8,128)(2,1)S(1)} %bitcast.45, bf16[2,448,2304]{2,1,0:T(8,128)(2,1)S(1)} %bitcast.46, bf16[2,448,768]{2,1,0:T(8,128)(2,1)S(1)} %bitcast.59), custom_call_target="tpu_custom_call" | custom-call | flops 4932501504 | bytes 4816896 | tf_op jit(solution)/shard_map/attend_back/pallas_call | solution.py:158
  538.6 10.3 %attend_back.7 = (bf16[2,448,768]{2,1,0:T(8,128)(2,1)}, bf16[2,448,768]{2,1,0:T(8,128)(2,1)}, bf16[2,448,768]{2,1,0:T(8,128)(2,1)}) custom-call(bf16[2,448,2304]{2,1,0:T(8,128)(2,1)S(1)} %bitcast.47, bf16[2,448,2304]{2,1,0:T(8,128)(2,1)S(1)} %bitcast.48, ...), custom_call_target="tpu_custom_call", output_to_operand_aliasing={{0}: (4, {}), {1}: (5, {}), {2}: (6, {})} | custom-call | flops 4932501504 | bytes 4816896 | tf_op jit(solution)/shard_map/attend_back/pallas_call | solution.py:158
  548.9 11.3 %weight_grads.8 = (f32[384,3072]{1,0:T(8,128)}, bf16[384,3072]{1,0:T(8,128)(2,1)S(1)}) custom-call(bf16[896,768]{1,0:T(8,128)(2,1)} %get-tuple-element.408.refs_0_, bf16[896,768]{1,0:T(8,128)(2,1)} %get-tuple-element.409.refs_1_, bf16[896,768]{1,0:T(8,128)(2,1)} %bitcast.72, bf16[896,768]{1,0:T(8,128)(2,1)} %bitcast.74, bf16[896,768]{1,0:T(8,128)(2,1)} %bitcast.76, ...), custom_call_target="tpu_custom_call" | custom-call | flops 4227858432 | bytes 14942208 | tf_op jit(solution)/shard_map/weight_grads/pallas_call | solution.py:705
  572.3 11.1 %project_back.3 = (f32[896,768]{1,0:T(8,128)S(1)}, f32[1,768]{1,0:T(1,128)S(1)}, bf16[896,768]{1,0:T(8,128)(2,1)}, f32[1,768]{1,0:T(1,128)S(1)}) custom-call(bf16[896,768]{1,0:T(8,128)(2,1)} %bitcast.73, bf16[896,768]{1,0:T(8,128)(2,1)} %bitcast.75, bf16[896,768]{1,0:T(8,128)(2,1)} %bitcast.77, bf16[192,4352]{1,0:T(8,128)(2,1)} %copy-done.40, ...), custom_call_target="tpu_custom_call" | custom-call | flops 3170893824 | bytes 15138816 | tf_op jit(solution)/shard_map/project_back/pallas_call | solution.py:645
  594.0 10.4 %collective-permute-done.54 = bf16[48,6144]{1,0:T(8,128)(2,1)S(1)} collective-permute-done((bf16[48,6144]{1,0:T(8,128)(2,1)S(1)}, bf16[48,6144]{1,0:T(8,128)(2,1)S(1)}, u32[]{:S(2)}, u32[]{:S(2)}) %collective-permute-start.54) | collective-permute-done | bytes 589856 | tf_op jit(solution)/shard_map/ppermute | solution.py:769
  604.4 8.1 %collective-permute-done.56 = bf16[192,1280]{1,0:T(8,128)(2,1)S(1)} collective-permute-done((bf16[192,1280]{1,0:T(8,128)(2,1)S(1)}, bf16[192,1280]{1,0:T(8,128)(2,1)S(1)}, u32[]{:S(2)}, u32[]{:S(2)}) %collective-permute-start.56) | collective-permute-done | bytes 491552 | tf_op jit(solution)/shard_map/ppermute | solution.py:769
  620.9 8.5 %collective-permute-done.59 = f32[48,1280]{1,0:T(8,128)S(1)} collective-permute-done((f32[48,1280]{1,0:T(8,128)S(1)}, f32[48,1280]{1,0:T(8,128)S(1)}, u32[]{:S(2)}, u32[]{:S(2)}) %collective-permute-start.59) | collective-permute-done | bytes 245792 | tf_op jit(solution)/shard_map/ppermute | solution.py:769
  631.6 20.2 %collective-permute-done.60 = f32[24,1280]{1,0:T(8,128)S(1)} collective-permute-done((f32[24,1280]{1,0:T(8,128)S(1)}, f32[24,1280]{1,0:T(8,128)S(1)}, u32[]{:S(2)}, u32[]{:S(2)}) %collective-permute-start.60) | collective-permute-done | bytes 122912 | tf_op jit(solution)/shard_map/ppermute | solution.py:769
  652.2 12.6 %collective-permute-done.63 = f32[24,3072]{1,0:T(8,128)S(1)} collective-permute-done((f32[24,3072]{1,0:T(8,128)S(1)}, f32[24,3072]{1,0:T(8,128)S(1)}, u32[]{:S(2)}, u32[]{:S(2)}) %collective-permute-start.63) | collective-permute-done | bytes 294944 | tf_op jit(solution)/shard_map/ppermute | solution.py:769
  (388 shorter events, 284.4 us)
Async XLA Ops:
  40.3 23.0 %collective-permute-start.3 = (bf16[48,6144]{1,0:T(8,128)(2,1)S(1)}, bf16[48,6144]{1,0:T(8,128)(2,1)S(1)}, u32[]{:S(2)}, u32[]{:S(2)}) collective-permute-start(bf16[48,6144]{1,0:T(8,128)(2,1)S(1)} %pad_maximum_fusion.9), channel_id=1, source_target_pairs={{0,8},{1,9},{2,10},{3,11},{4,12},{5,13},{6,14},{7,15},{8,0},{9,1},... | collective-permute-start | bytes 1769480 | tf_op jit(solution)/shard_map/ppermute | solution.py:769
  51.4 28.8 %collective-permute-start.10 = (bf16[192,4352]{1,0:T(8,128)(2,1)S(1)}, bf16[192,4352]{1,0:T(8,128)(2,1)S(1)}, u32[]{:S(2)}, u32[]{:S(2)}) collective-permute-start(bf16[192,4352]{1,0:T(8,128)(2,1)S(1)} %pad_maximum_fusion.2.refs_2_.refs_6_.refs_10_.own_ref), channel_id=1, source_target_pairs={{0,2},{1,3},{2,0},{3,1},{4,6},{5,7},{6,4},{7,5},{8,10},{9,11},{10,... | collective-permute-start | bytes 5013512 | tf_op jit(solution)/shard_map/ppermute | solution.py:769
  51.5 28.6 %collective-permute-start.9 = (bf16[192,4352]{1,0:T(8,128)(2,1)S(1)}, bf16[192,4352]{1,0:T(8,128)(2,1)S(1)}, u32[]{:S(2)}, u32[]{:S(2)}) collective-permute-start(bf16[192,4352]{1,0:T(8,128)(2,1)S(1)} %pad_maximum_fusion.2.refs_2_.refs_6_.refs_10_.own_ref), channel_id=1, source_target_pairs={{0,1},{1,0},{2,6},{3,7},{4,5},{5,4},{6,2},{7,3},{8,9},{9,8},{10,14... | collective-permute-start | bytes 5013512 | tf_op jit(solution)/shard_map/ppermute | solution.py:769
  63.4 31.2 %collective-permute-start.7 = (bf16[24,4352]{1,0:T(8,128)(2,1)S(1)}, bf16[24,4352]{1,0:T(8,128)(2,1)S(1)}, u32[]{:S(2)}, u32[]{:S(2)}) collective-permute-start(bf16[24,4352]{1,0:T(8,128)(2,1)S(1)} %pad_maximum_fusion.16), channel_id=1, source_target_pairs={{0,16},{1,17},{2,18},{3,19},{4,20},{5,21},{6,22},{7,23},{8,24},{9,... | collective-permute-start | bytes 626696 | tf_op jit(solution)/shard_map/ppermute | solution.py:769
  63.4 31.1 %collective-permute-start.6 = (bf16[48,9216]{1,0:T(8,128)(2,1)S(1)}, bf16[48,9216]{1,0:T(8,128)(2,1)S(1)}, u32[]{:S(2)}, u32[]{:S(2)}) collective-permute-start(bf16[48,9216]{1,0:T(8,128)(2,1)S(1)} %pad_maximum_fusion.5), channel_id=1, source_target_pairs={{0,8},{1,9},{2,10},{3,11},{4,12},{5,13},{6,14},{7,15},{8,0},{9,1},... | collective-permute-start | bytes 2654216 | tf_op jit(solution)/shard_map/ppermute | solution.py:769
  66.0 28.6 %collective-permute-start.8 = (bf16[96,6144]{1,0:T(8,128)(2,1)S(1)}, bf16[96,6144]{1,0:T(8,128)(2,1)S(1)}, u32[]{:S(2)}, u32[]{:S(2)}) collective-permute-start(bf16[96,6144]{1,0:T(8,128)(2,1)S(1)} %pad_maximum_fusion.4), channel_id=1, source_target_pairs={{0,4},{1,5},{2,3},{3,2},{4,0},{5,1},{6,7},{7,6},{8,12},{9,13},{10,... | collective-permute-start | bytes 3538952 | tf_op jit(solution)/shard_map/ppermute | solution.py:769
  94.7 48.3 %collective-permute-start.16 = (bf16[192,6144]{1,0:T(8,128)(2,1)S(1)}, bf16[192,6144]{1,0:T(8,128)(2,1)S(1)}, u32[]{:S(2)}, u32[]{:S(2)}) collective-permute-start(bf16[192,6144]{1,0:T(8,128)(2,1)S(1)} %constant_dynamic-update-slice_fusion.uown_ref.down_ref), channel_id=1, source_target_pairs={{0,1},{1,0},{2,6},{3,7},{4,5},{5,4},{6,2},{7,3},{8,9},{9,8},{10,14... | collective-permute-start | bytes 7077896 | tf_op jit(solution)/shard_map/ppermute | solution.py:769
  97.2 45.8 %collective-permute-start.12 = (bf16[192,6144]{1,0:T(8,128)(2,1)S(1)}, bf16[192,6144]{1,0:T(8,128)(2,1)}, u32[]{:S(2)}, u32[]{:S(2)}) collective-permute-start(bf16[192,6144]{1,0:T(8,128)(2,1)S(1)} %constant_dynamic-update-slice_fusion.uown_ref.down_ref), channel_id=1, source_target_pairs={{0,2},{1,3},{2,0},{3,1},{4,6},{5,7},{6,4},{7,5},{8,10},{9,11},{10,... | collective-permute-start | bytes 7077896 | tf_op jit(solution)/shard_map/ppermute | solution.py:769
  97.2 37.2 %collective-permute-start.14 = (bf16[24,16128]{1,0:T(8,128)(2,1)S(1)}, bf16[24,16128]{1,0:T(8,128)(2,1)S(1)}, u32[]{:S(2)}, u32[]{:S(2)}) collective-permute-start(bf16[24,16128]{1,0:T(8,128)(2,1)S(1)} %pad_maximum_fusion.8), channel_id=1, source_target_pairs={{0,16},{1,17},{2,18},{3,19},{4,20},{5,21},{6,22},{7,23},{8,24},{9,... | collective-permute-start | bytes 2322440 | tf_op jit(solution)/shard_map/ppermute | solution.py:769
  97.5 41.6 %collective-permute-start.15 = (bf16[96,9216]{1,0:T(8,128)(2,1)S(1)}, bf16[96,9216]{1,0:T(8,128)(2,1)S(1)}, u32[]{:S(2)}, u32[]{:S(2)}) collective-permute-start(bf16[96,9216]{1,0:T(8,128)(2,1)S(1)} %pad_maximum_fusion.1), channel_id=1, source_target_pairs={{0,4},{1,5},{2,3},{3,2},{4,0},{5,1},{6,7},{7,6},{8,12},{9,13},{10,... | collective-permute-start | bytes 5308424 | tf_op jit(solution)/shard_map/ppermute | solution.py:769
  98.7 25.0 %collective-permute-start.13 = (bf16[48,4352]{1,0:T(8,128)(2,1)S(1)}, bf16[48,4352]{1,0:T(8,128)(2,1)S(1)}, u32[]{:S(2)}, u32[]{:S(2)}) collective-permute-start(bf16[48,4352]{1,0:T(8,128)(2,1)S(1)} %pad_maximum_fusion.14), channel_id=1, source_target_pairs={{0,8},{1,9},{2,10},{3,11},{4,12},{5,13},{6,14},{7,15},{8,0},{9,1},... | collective-permute-start | bytes 1253384 | tf_op jit(solution)/shard_map/ppermute | solution.py:769
  144.5 50.4 %collective-permute-start.20 = (bf16[192,9216]{1,0:T(8,128)(2,1)S(1)}, bf16[192,9216]{1,0:T(8,128)(2,1)S(1)}, u32[]{:S(2)}, u32[]{:S(2)}) collective-permute-start(bf16[192,9216]{1,0:T(8,128)(2,1)S(1)} %constant_dynamic-update-slice_fusion.4.own_ref.uown_ref.down_ref), channel_id=1, source_target_pairs={{0,1},{1,0},{2,6},{3,7},{4,5},{5,4},{6,2},{7,3},{8,9},{9,8},{10,14... | collective-permute-start | bytes 10616840 | tf_op jit(solution)/shard_map/ppermute | solution.py:769
  146.5 48.4 %collective-permute-start.17 = (bf16[192,9216]{1,0:T(8,128)(2,1)S(1)}, bf16[192,9216]{1,0:T(8,128)(2,1)S(1)}, u32[]{:S(2)}, u32[]{:S(2)}) collective-permute-start(bf16[192,9216]{1,0:T(8,128)(2,1)S(1)} %constant_dynamic-update-slice_fusion.4.own_ref.uown_ref.down_ref), channel_id=1, source_target_pairs={{0,2},{1,3},{2,0},{3,1},{4,6},{5,7},{6,4},{7,5},{8,10},{9,11},{10,... | collective-permute-start | bytes 10616840 | tf_op jit(solution)/shard_map/ppermute | solution.py:769
  146.6 23.7 %collective-permute-start.19 = (bf16[96,4352]{1,0:T(8,128)(2,1)S(1)}, bf16[96,4352]{1,0:T(8,128)(2,1)S(1)}, u32[]{:S(2)}, u32[]{:S(2)}) collective-permute-start(bf16[96,4352]{1,0:T(8,128)(2,1)S(1)} %pad_maximum_fusion.7), channel_id=1, source_target_pairs={{0,4},{1,5},{2,3},{3,2},{4,0},{5,1},{6,7},{7,6},{8,12},{9,13},{10,... | collective-permute-start | bytes 2506760 | tf_op jit(solution)/shard_map/ppermute | solution.py:769
  147.2 37.1 %collective-permute-start.18 = (bf16[48,16128]{1,0:T(8,128)(2,1)S(1)}, bf16[48,16128]{1,0:T(8,128)(2,1)S(1)}, u32[]{:S(2)}, u32[]{:S(2)}) collective-permute-start(bf16[48,16128]{1,0:T(8,128)(2,1)S(1)} %pad_maximum_fusion.3), channel_id=1, source_target_pairs={{0,8},{1,9},{2,10},{3,11},{4,12},{5,13},{6,14},{7,15},{8,0},{9,1},... | collective-permute-start | bytes 4644872 | tf_op jit(solution)/shard_map/ppermute | solution.py:769
  195.1 45.1 %collective-permute-start.24 = (bf16[192,4352]{1,0:T(8,128)(2,1)S(1)}, bf16[192,4352]{1,0:T(8,128)(2,1)}, u32[]{:S(2)}, u32[]{:S(2)}) collective-permute-start(bf16[192,4352]{1,0:T(8,128)(2,1)S(1)} %constant_dynamic-update-slice_fusion.11.refs_2_.refs_6_.refs_10_.own_ref.refs_3_.refs_7_.refs_11_), channel_id=1, source_target_pairs={{0,1},{1,0},{2,6},{3,7},{4,5},{5,4},{6,2},{7,3},{8,9},{9,8},{10,14... | collective-permute-start | bytes 5013512 | tf_op jit(solution)/shard_map/ppermute | solution.py:769
  197.2 43.0 %collective-permute-start.22 = (bf16[192,4352]{1,0:T(8,128)(2,1)S(1)}, bf16[192,4352]{1,0:T(8,128)(2,1)S(1)}, u32[]{:S(2)}, u32[]{:S(2)}) collective-permute-start(bf16[192,4352]{1,0:T(8,128)(2,1)S(1)} %constant_dynamic-update-slice_fusion.11.refs_2_.refs_6_.refs_10_.own_ref.refs_3_.refs_7_.refs_11_), channel_id=1, source_target_pairs={{0,2},{1,3},{2,0},{3,1},{4,6},{5,7},{6,4},{7,5},{8,10},{9,11},{10,... | collective-permute-start | bytes 5013512 | tf_op jit(solution)/shard_map/ppermute | solution.py:769
  199.8 40.3 %collective-permute-start.23 = (bf16[96,6144]{1,0:T(8,128)(2,1)S(1)}, bf16[96,6144]{1,0:T(8,128)(2,1)S(1)}, u32[]{:S(2)}, u32[]{:S(2)}) collective-permute-start(bf16[96,6144]{1,0:T(8,128)(2,1)S(1)} %get-tuple-element.498), channel_id=1, source_target_pairs={{0,4},{1,5},{2,3},{3,2},{4,0},{5,1},{6,7},{7,6},{8,12},{9,13},{10,... | collective-permute-start | bytes 3538952 | tf_op jit(solution)/shard_map/ppermute | solution.py:769
  243.0 37.1 %collective-permute-start.28 = (bf16[192,6144]{1,0:T(8,128)(2,1)}, bf16[192,6144]{1,0:T(8,128)(2,1)}, u32[]{:S(2)}, u32[]{:S(2)}) collective-permute-start(bf16[192,6144]{1,0:T(8,128)(2,1)} %pad_maximum_fusion.uown_ref.down_ref), channel_id=1, source_target_pairs={{0,1},{1,0},{2,6},{3,7},{4,5},{5,4},{6,2},{7,3},{8,9},{9,8},{10,14... | collective-permute-start | bytes 7077896 | tf_op jit(solution)/shard_map/ppermute | solution.py:769
  245.0 35.1 %collective-permute-start.26 = (bf16[192,6144]{1,0:T(8,128)(2,1)}, bf16[192,6144]{1,0:T(8,128)(2,1)}, u32[]{:S(2)}, u32[]{:S(2)}) collective-permute-start(bf16[192,6144]{1,0:T(8,128)(2,1)} %pad_maximum_fusion.uown_ref.down_ref), channel_id=1, source_target_pairs={{0,2},{1,3},{2,0},{3,1},{4,6},{5,7},{6,4},{7,5},{8,10},{9,11},{10,... | collective-permute-start | bytes 7077896 | tf_op jit(solution)/shard_map/ppermute | solution.py:769
  245.3 32.0 %collective-permute-start.27 = (bf16[96,3840]{1,0:T(8,128)(2,1)}, bf16[96,3840]{1,0:T(8,128)(2,1)S(1)}, u32[]{:S(2)}, u32[]{:S(2)}) collective-permute-start(bf16[96,3840]{1,0:T(8,128)(2,1)} %slice.419), channel_id=1, source_target_pairs={{0,4},{1,5},{2,3},{3,2},{4,0},{5,1},{6,7},{7,6},{8,12},{9,13},{10,... | collective-permute-start | bytes 2211848 | tf_op jit(solution)/shard_map/ppermute | solution.py:769
  280.2 32.1 %collective-permute-start.32 = (bf16[192,3840]{1,0:T(8,128)(2,1)S(1)}, bf16[192,3840]{1,0:T(8,128)(2,1)S(1)}, u32[]{:S(2)}, u32[]{:S(2)}) collective-permute-start(bf16[192,3840]{1,0:T(8,128)(2,1)S(1)} %constant_dynamic-update-slice_fusion.15.own_ref.refs_3_.refs_7_.refs_11_), channel_id=1, source_target_pairs={{0,1},{1,0},{2,6},{3,7},{4,5},{5,4},{6,2},{7,3},{8,9},{9,8},{10,14... | collective-permute-start | bytes 4423688 | tf_op jit(solution)/shard_map/ppermute | solution.py:769
  282.2 30.0 %collective-permute-start.30 = (bf16[192,3840]{1,0:T(8,128)(2,1)S(1)}, bf16[192,3840]{1,0:T(8,128)(2,1)S(1)}, u32[]{:S(2)}, u32[]{:S(2)}) collective-permute-start(bf16[192,3840]{1,0:T(8,128)(2,1)S(1)} %constant_dynamic-update-slice_fusion.15.own_ref.refs_3_.refs_7_.refs_11_), channel_id=1, source_target_pairs={{0,2},{1,3},{2,0},{3,1},{4,6},{5,7},{6,4},{7,5},{8,10},{9,11},{10,... | collective-permute-start | bytes 4423688 | tf_op jit(solution)/shard_map/ppermute | solution.py:769
  282.2 28.9 %collective-permute-start.31 = (bf16[96,6144]{1,0:T(8,128)(2,1)S(1)}, bf16[96,6144]{1,0:T(8,128)(2,1)S(1)}, u32[]{:S(2)}, u32[]{:S(2)}) collective-permute-start(bf16[96,6144]{1,0:T(8,128)(2,1)S(1)} %copy-done.54), channel_id=1, source_target_pairs={{0,4},{1,5},{2,3},{3,2},{4,0},{5,1},{6,7},{7,6},{8,12},{9,13},{10,... | collective-permute-start | bytes 3538952 | tf_op jit(solution)/shard_map/ppermute | solution.py:769
  312.4 28.9 %collective-permute-start.35 = (bf16[192,6144]{1,0:T(8,128)(2,1)S(1)}, bf16[192,6144]{1,0:T(8,128)(2,1)S(1)}, u32[]{:S(2)}, u32[]{:S(2)}) collective-permute-start(bf16[192,6144]{1,0:T(8,128)(2,1)S(1)} %constant_dynamic-update-slice_fusion.17.uown_ref.down_ref), channel_id=1, source_target_pairs={{0,1},{1,0},{2,6},{3,7},{4,5},{5,4},{6,2},{7,3},{8,9},{9,8},{10,14... | collective-permute-start | bytes 7077896 | tf_op jit(solution)/shard_map/ppermute | solution.py:769
  314.3 27.0 %collective-permute-start.34 = (bf16[192,6144]{1,0:T(8,128)(2,1)S(1)}, bf16[192,6144]{1,0:T(8,128)(2,1)S(1)}, u32[]{:S(2)}, u32[]{:S(2)}) collective-permute-start(bf16[192,6144]{1,0:T(8,128)(2,1)S(1)} %constant_dynamic-update-slice_fusion.17.uown_ref.down_ref), channel_id=1, source_target_pairs={{0,2},{1,3},{2,0},{3,1},{4,6},{5,7},{6,4},{7,5},{8,10},{9,11},{10,... | collective-permute-start | bytes 7077896 | tf_op jit(solution)/shard_map/ppermute | solution.py:769
  432.9 33.5 %collective-permute-start.39 = (bf16[192,6144]{1,0:T(8,128)(2,1)}, bf16[192,6144]{1,0:T(8,128)(2,1)}, u32[]{:S(2)}, u32[]{:S(2)}) collective-permute-start(bf16[192,6144]{1,0:T(8,128)(2,1)} %get-tuple-element.480), channel_id=1, source_target_pairs={{0,1},{1,0},{2,6},{3,7},{4,5},{5,4},{6,2},{7,3},{8,9},{9,8},{10,14... | collective-permute-start | bytes 7077896 | tf_op jit(solution)/shard_map/ppermute | solution.py:769
  536.0 32.4 %collective-permute-start.48 = (bf16[192,6144]{1,0:T(8,128)(2,1)}, bf16[192,6144]{1,0:T(8,128)(2,1)S(1)}, u32[]{:S(2)}, u32[]{:S(2)}) collective-permute-start(bf16[192,6144]{1,0:T(8,128)(2,1)} %get-tuple-element.478), channel_id=1, source_target_pairs={{0,1},{1,0},{2,6},{3,7},{4,5},{5,4},{6,2},{7,3},{8,9},{9,8},{10,14... | collective-permute-start | bytes 7077896 | tf_op jit(solution)/shard_map/ppermute | solution.py:769
  537.2 28.9 %collective-permute-start.46 = (f32[24,6144]{1,0:T(8,128)S(1)}, f32[24,6144]{1,0:T(8,128)S(1)}, u32[]{:S(2)}, u32[]{:S(2)}) collective-permute-start(f32[24,6144]{1,0:T(8,128)S(1)} %slice_add_fusion.19), channel_id=1, source_target_pairs={{0,16},{1,17},{2,18},{3,19},{4,20},{5,21},{6,22},{7,23},{8,24},{9,... | collective-permute-start | bytes 1769480 | tf_op jit(solution)/shard_map/ppermute | solution.py:769
  537.4 31.1 %collective-permute-start.47 = (f32[48,3840]{1,0:T(8,128)S(1)}, f32[48,3840]{1,0:T(8,128)S(1)}, u32[]{:S(2)}, u32[]{:S(2)}) collective-permute-start(f32[48,3840]{1,0:T(8,128)S(1)} %get-tuple-element.499), channel_id=1, source_target_pairs={{0,8},{1,9},{2,10},{3,11},{4,12},{5,13},{6,14},{7,15},{8,0},{9,1},... | collective-permute-start | bytes 2211848 | tf_op jit(solution)/shard_map/ppermute | solution.py:769
  619.7 32.1 %collective-permute-start.61 = (f32[24,6144]{1,0:T(8,128)S(1)}, f32[24,6144]{1,0:T(8,128)S(1)}, u32[]{:S(2)}, u32[]{:S(2)}) collective-permute-start(f32[24,6144]{1,0:T(8,128)S(1)} %slice_add_fusion.17), channel_id=1, source_target_pairs={{0,16},{1,17},{2,18},{3,19},{4,20},{5,21},{6,22},{7,23},{8,24},{9,... | collective-permute-start | bytes 1769480 | tf_op jit(solution)/shard_map/ppermute | solution.py:769
  629.4 22.4 %collective-permute-start.60 = (f32[24,1280]{1,0:T(8,128)S(1)}, f32[24,1280]{1,0:T(8,128)S(1)}, u32[]{:S(2)}, u32[]{:S(2)}) collective-permute-start(f32[24,1280]{1,0:T(8,128)S(1)} %slice_add_fusion.26), channel_id=1, source_target_pairs={{0,16},{1,17},{2,18},{3,19},{4,20},{5,21},{6,22},{7,23},{8,24},{9,... | collective-permute-start | bytes 368648 | tf_op jit(solution)/shard_map/ppermute | solution.py:769
  (111 other events, 1658.1 us)

commit v8 on v7

--- a/solution.py
+++ b/solution.py
@@ -1096,6 +1096,7 @@
     own = [None] * len(chunks)
     blocks = [None] * len(chunks)
     values = ()
+    ahead = {}
     for tick in range(len(chunks) + early + 1):
         sends = {}
         for group, start in enumerate(group_start):
@@ -1104,16 +1105,28 @@
         for chunk in range(len(chunks)):
             if tick == chunk + early:
                 sends["first", chunk] = (own[chunk], plan.stages[early])
-            if tick == chunk + early + 1:
+            if tick == chunk + early + 1 and ("second", chunk) not in ahead:
                 sends["second", chunk] = (own[chunk], plan.stages[early + 1])
                 sends["core", chunk] = (own[chunk], plan.core_stage)
         gots = {key: plan.swap(value, perm) for key, (value, perm) in sends.items()}
+        if tick == early + 2:
+            gots.update(ahead)
         place = tick - early - 2
         if 0 <= place < len(segments):
             values = segments[place](values, finish(blocks[place]))
         if tick == early + 1:
-            first_blocks = (own[0], gots["second", 0], gots["core", 0])
-            values = segment_t0(values, finish(first_blocks))
+            lead = [gots.pop(key) for key in (("second", 0), ("core", 0), ("first", 1))]
+            later = [g for g in range(len(groups)) if group_start[g] > tick]
+            lead, held = lax.optimization_barrier((lead, [group_values[g] for g in later]))
+            for g, value in zip(later, held):
+                group_values[g] = value
+            own[1] = jnp.concatenate([own[1], lead[2]], axis=0)
+            ahead = {
+                ("second", 1): plan.swap(own[1], plan.stages[early + 1]),
+                ("core", 1): plan.swap(own[1], plan.core_stage),
+            }
+            blocks[0] = (own[0], lead[0], lead[1])
+            values = segment_t0(values, finish(blocks[0]))
         apart = {key: got for key, got in gots.items() if FAST_LANE and key[1] == 0 and tick}
         gots = {key: got for key, got in gots.items() if key not in apart}
         later = [g for g in range(len(groups)) if group_start[g] > tick]

time: 695 us -> 686 us (0.987)
  transfers between devices with their start and end apart: 69 -> 69, of which waited for: 36 -> 34; matrix products, arithmetic and copies ran while one was open for 2% -> 2% of each run, Pallas kernels for 41% -> 42%
where the time goes in v8:
time: 686 us; the launch traced here: 680 us
  Pallas kernels  350 us (51%)
  waiting for transfers between devices  214 us (31%)
  starting transfers between devices  63.6 us (9%)
  other arithmetic  27.8 us (4%)
  local copies, waits for them, and re-layouts  19.6 us (3%)
    ppermute x69, waiting for transfers between devices, swap(): return lax.ppermute(value, AXES, perm)  214 us
    ppermute x69, starting transfers between devices, swap(): return lax.ppermute(value, AXES, perm)  63.6 us
    pallas_call x5, Pallas kernels, weight_grads(): pl.pallas_call(kernel, grid=(total,), in_specs=specs, out_specs=[block, b...  63.5 us
    pallas_call x4, Pallas kernels, feed_forward(): pl.pallas_call(kernel, grid=(steps,), in_specs=[whole_block(normed.shape)...  61.8 us
    pallas_call x4, Pallas kernels, attend(): pl.pallas_call(attend_kernel, grid=(seqs, blocks), in_specs=specs, out_sp...  45.5 us
    pallas_call x4, Pallas kernels, attend_back(): pl.pallas_call(kernel, grid=(blocks,), in_specs=specs + [block] + [pl.Blo...  41.3 us
    pallas_call x2, Pallas kernels, feed_back(): pl.pallas_call(kernel, grid=(steps,), in_specs=[full, column, full, whole...  35.8 us
    pallas_call x4, Pallas kernels, norm_project(): pl.pallas_call(kernel, grid=(steps,), in_specs=[whole_block(states.shape)...  26.4 us
  transfers between devices with their start and end apart: 69, of which 34 were waited for; matrix products, arithmetic and copies ran while one was open for 2% of the time, Pallas kernels for 42%

profile of v8, /device:TPU:0, one launch (start us, length us, event | category | flops | bytes accessed | tf_op | source)
XLA Modules:
  0.0 680.0 jit_solution(16235319818839796316)
XLA Ops:
  22.6 11.3 %collective-permute-done.1 = bf16[24,6144]{1,0:T(8,128)(2,1)S(1)} collective-permute-done((bf16[24,6144]{1,0:T(8,128)(2,1)S(1)}, bf16[24,6144]{1,0:T(8,128)(2,1)S(1)}, u32[]{:S(2)}, u32[]{:S(2)}) %collective-permute-start.1) | collective-permute-done | bytes 294944 | tf_op jit(solution)/shard_map/ppermute | solution.py:769
  42.2 9.1 %collective-permute-done.5 = bf16[96,4352]{1,0:T(8,128)(2,1)S(1)} collective-permute-done((bf16[96,4352]{1,0:T(8,128)(2,1)S(1)}, bf16[96,4352]{1,0:T(8,128)(2,1)S(1)}, u32[]{:S(2)}, u32[]{:S(2)}) %collective-permute-start.5) | collective-permute-done | bytes 835616 | tf_op jit(solution)/shard_map/ppermute | solution.py:769
  67.6 17.5 %collective-permute-done.10 = bf16[96,6144]{1,0:T(8,128)(2,1)S(1)} collective-permute-done((bf16[96,6144]{1,0:T(8,128)(2,1)S(1)}, bf16[96,6144]{1,0:T(8,128)(2,1)S(1)}, u32[]{:S(2)}, u32[]{:S(2)}) %collective-permute-start.10) | collective-permute-done | bytes 1179680 | tf_op jit(solution)/shard_map/ppermute | solution.py:769
  103.8 11.2 %attend.4 = bf16[2,448,768]{2,1,0:T(8,128)(2,1)S(1)} custom-call(bf16[2,448,2304]{2,1,0:T(8,128)(2,1)S(1)} %bitcast.28, bf16[2,448,2304]{2,1,0:T(8,128)(2,1)S(1)} %bitcast.29, bf16[2,448,2304]{2,1,0:T(8,128)(2,1)S(1)} %bitcast.30), custom_call_target="tpu_custom_call" | custom-call | flops 4932501504 | bytes 5505024 | tf_op jit(solution)/shard_map/attend/pallas_call | solution.py:121
  127.0 10.0 %collective-permute-done.14 = bf16[24,16128]{1,0:T(8,128)(2,1)S(1)} collective-permute-done((bf16[24,16128]{1,0:T(8,128)(2,1)S(1)}, bf16[24,16128]{1,0:T(8,128)(2,1)S(1)}, u32[]{:S(2)}, u32[]{:S(2)}) %collective-permute-start.14) | collective-permute-done | bytes 774176 | tf_op jit(solution)/shard_map/ppermute | solution.py:769
  148.3 14.2 %feed_forward.4.h_ref.one_ref = f32[896,768]{1,0:T(8,128)S(1)} custom-call(bf16[896,768]{1,0:T(8,128)(2,1)S(1)} %get-tuple-element.284.b_ref, f32[896,768]{1,0:T(8,128)S(1)} %get-tuple-element.285.m_ref, bf16[192,6144]{1,0:T(8,128)(2,1)} %copy-done.61, bf16[192,6144]{1,0:T(8,128)(2,1)} %copy-done.63, ...), custom_call_target="tpu_custom_call" | custom-call | flops 8455716864 | bytes 46006272 | tf_op jit(solution)/shard_map/feed_forward/pallas_call | solution.py:405
  162.6 13.0 %collective-permute-done.18 = bf16[48,16128]{1,0:T(8,128)(2,1)S(1)} collective-permute-done((bf16[48,16128]{1,0:T(8,128)(2,1)S(1)}, bf16[48,16128]{1,0:T(8,128)(2,1)S(1)}, u32[]{:S(2)}, u32[]{:S(2)}) %collective-permute-start.18) | collective-permute-done | bytes 1548320 | tf_op jit(solution)/shard_map/ppermute | solution.py:769
  175.6 12.1 %collective-permute-done.20.own2_ref.uown2_ref.down2_ref = bf16[192,9216]{1,0:T(8,128)(2,1)S(1)} collective-permute-done((bf16[192,9216]{1,0:T(8,128)(2,1)S(1)}, bf16[192,9216]{1,0:T(8,128)(2,1)S(1)}, u32[]{:S(2)}, u32[]{:S(2)}) %collective-permute-start.20) | collective-permute-done | bytes 3538976 | tf_op jit(solution)/shard_map/ppermute | solution.py:769
  200.0 11.4 %attend.5 = bf16[2,448,768]{2,1,0:T(8,128)(2,1)S(1)} custom-call(bf16[2,448,2304]{2,1,0:T(8,128)(2,1)S(1)} %bitcast.31, bf16[2,448,2304]{2,1,0:T(8,128)(2,1)S(1)} %bitcast.32, bf16[2,448,2304]{2,1,0:T(8,128)(2,1)S(1)} %bitcast.33), custom_call_target="tpu_custom_call" | custom-call | flops 4932501504 | bytes 5505024 | tf_op jit(solution)/shard_map/attend/pallas_call | solution.py:121
  217.1 13.8 %feed_forward.5.two_ref = f32[896,768]{1,0:T(8,128)S(1)} custom-call(bf16[896,768]{1,0:T(8,128)(2,1)S(1)} %get-tuple-element.296.b_ref, f32[896,768]{1,0:T(8,128)S(1)} %get-tuple-element.297.m_ref, bf16[192,9216]{1,0:T(8,128)(2,1)} %copy-done.42, bf16[192,9216]{1,0:T(8,128)(2,1)} %copy-done.44, bf16[192,9216]{1,0:T(8,128)(2,1)} %copy-done.45, ...), custom_call_target="tpu_custom_call" | custom-call | flops 8455716864 | bytes 46006272 | tf_op jit(solution)/shard_map/feed_forward/pallas_call | solution.py:405
  252.3 11.6 %attend.6 = bf16[2,448,768]{2,1,0:T(8,128)(2,1)S(1)} custom-call(bf16[2,448,2304]{2,1,0:T(8,128)(2,1)S(1)} %bitcast.41, bf16[2,448,2304]{2,1,0:T(8,128)(2,1)S(1)} %bitcast.42, bf16[2,448,2304]{2,1,0:T(8,128)(2,1)S(1)} %bitcast.43), custom_call_target="tpu_custom_call" | custom-call | flops 4932501504 | bytes 5505024 | tf_op jit(solution)/shard_map/attend/pallas_call | solution.py:121
  277.6 16.9 %feed_forward.6 = (f32[896,768]{1,0:T(8,128)S(1)}, bf16[896,3072]{1,0:T(8,128)(2,1)}, f32[896,3072]{1,0:T(8,128)}) custom-call(bf16[896,768]{1,0:T(8,128)(2,1)S(1)} %get-tuple-element.316.b_ref.refs_0_, f32[896,768]{1,0:T(8,128)S(1)} %get-tuple-element.317.m_ref, bf16[192,6144]{1,0:T(8,128)(2,1)} %pad_maximum_fusion.uown_ref.down_ref, ...), custom_call_target="tpu_custom_call" | custom-call | flops 8455716864 | bytes 46006272 | tf_op jit(solution)/shard_map/feed_forward/pallas_call | solution.py:405
  294.6 9.1 %collective-permute-done.31 = bf16[96,6144]{1,0:T(8,128)(2,1)S(1)} collective-permute-done((bf16[96,6144]{1,0:T(8,128)(2,1)S(1)}, bf16[96,6144]{1,0:T(8,128)(2,1)S(1)}, u32[]{:S(2)}, u32[]{:S(2)}) %collective-permute-start.31) | collective-permute-done | bytes 1179680 | tf_op jit(solution)/shard_map/ppermute | solution.py:769
  315.5 11.2 %attend.7 = bf16[2,448,768]{2,1,0:T(8,128)(2,1)S(1)} custom-call(bf16[2,448,2304]{2,1,0:T(8,128)(2,1)S(1)} %bitcast.50, bf16[2,448,2304]{2,1,0:T(8,128)(2,1)S(1)} %bitcast.51, bf16[2,448,2304]{2,1,0:T(8,128)(2,1)S(1)} %bitcast.52), custom_call_target="tpu_custom_call" | custom-call | flops 4932501504 | bytes 5505024 | tf_op jit(solution)/shard_map/attend/pallas_call | solution.py:121
  338.8 16.9 %feed_forward.7 = (f32[896,768]{1,0:T(8,128)S(1)}, bf16[896,3072]{1,0:T(8,128)(2,1)}, f32[896,3072]{1,0:T(8,128)}) custom-call(bf16[896,768]{1,0:T(8,128)(2,1)S(1)} %get-tuple-element.331.b_ref.refs_0_, f32[896,768]{1,0:T(8,128)S(1)} %get-tuple-element.332.m_ref, bf16[192,6144]{1,0:T(8,128)(2,1)} %copy-done.49, bf16[192,6144]{1,0:T(8,128)(2,1)} %copy-done.52, ...), custom_call_target="tpu_custom_call" | custom-call | flops 8455716864 | bytes 46006272 | tf_op jit(solution)/shard_map/feed_forward/pallas_call | solution.py:405
  365.3 17.7 %feed_back.2 = (bf16[896,3072]{1,0:T(8,128)(2,1)}, bf16[896,768]{1,0:T(8,128)(2,1)}, f32[896,768]{1,0:T(8,128)S(1)}, bf16[896,768]{1,0:T(8,128)(2,1)S(1)}, f32[1,768]{1,0:T(1,128)S(1)}) custom-call(f32[896,768]{1,0:T(8,128)S(1)} %get-tuple-element.342.flow_ref, f32[896,3072]{1,0:T(8,128)} %get-tuple-element.343.slope_ref, f32[896,768]{1,0:T(8,128)S(1)} %copy-done.9, ...), custom_call_target="tpu_custom_call" | custom-call | flops 8455716864 | bytes 46399488 | tf_op jit(solution)/shard_map/feed_back/pallas_call | solution.py:547
  383.1 17.1 %weight_grads.5 = (f32[384,6144]{1,0:T(8,128)}, bf16[384,6144]{1,0:T(8,128)(2,1)S(1)}) custom-call(bf16[896,768]{1,0:T(8,128)(2,1)} %copy-done.38, bf16[896,768]{1,0:T(8,128)(2,1)} %get-tuple-element.348.refs_1_, bf16[896,3072]{1,0:T(8,128)(2,1)} %get-tuple-element.349.refs_2_, bf16[896,3072]{1,0:T(8,128)(2,1)} %get-tuple-element.350.refs_3_), custom_call_target="tpu_custom_call" | custom-call | flops 8455716864 | bytes 29884416 | tf_op jit(solution)/shard_map/weight_grads/pallas_call | solution.py:705
  404.8 10.2 %attend_back.4 = (bf16[2,448,768]{2,1,0:T(8,128)(2,1)}, bf16[2,448,768]{2,1,0:T(8,128)(2,1)}, bf16[2,448,768]{2,1,0:T(8,128)(2,1)}) custom-call(bf16[2,448,2304]{2,1,0:T(8,128)(2,1)S(1)} %bitcast.53, bf16[2,448,2304]{2,1,0:T(8,128)(2,1)S(1)} %bitcast.54, bf16[2,448,2304]{2,1,0:T(8,128)(2,1)S(1)} %bitcast.55, bf16[2,448,768]{2,1,0:T(8,128)(2,1)S(1)} %bitcast.61), custom_call_target="tpu_custom_call" | custom-call | flops 4932501504 | bytes 4816896 | tf_op jit(solution)/shard_map/attend_back/pallas_call | solution.py:158
  417.2 8.6 %convert_add_fusion.1 = (f32[192,6144]{1,0:T(8,128)}, bf16[192,6144]{1,0:T(8,128)(2,1)}) fusion(f32[384,6144]{1,0:T(8,128)} %get-tuple-element.354, bf16[384,6144]{1,0:T(8,128)(2,1)} %copy-done.56), kind=kLoop, calls=%fused_computation.2 | loop fusion | flops 5898240 | bytes 21233664 | tf_op jit(solution)/shard_map/add | solution.py:849
  427.3 10.2 %attend_back.5 = (bf16[2,448,768]{2,1,0:T(8,128)(2,1)}, bf16[2,448,768]{2,1,0:T(8,128)(2,1)}, bf16[2,448,768]{2,1,0:T(8,128)(2,1)}) custom-call(bf16[2,448,2304]{2,1,0:T(8,128)(2,1)S(1)} %bitcast.56, bf16[2,448,2304]{2,1,0:T(8,128)(2,1)S(1)} %bitcast.57, ...), custom_call_target="tpu_custom_call", output_to_operand_aliasing={{0}: (4, {}), {1}: (5, {}), {2}: (6, {})} | custom-call | flops 4932501504 | bytes 4816896 | tf_op jit(solution)/shard_map/attend_back/pallas_call | solution.py:158
  445.0 14.0 %weight_grads.6 = (f32[384,3840]{1,0:T(8,128)}, bf16[384,3840]{1,0:T(8,128)(2,1)S(1)}) custom-call(bf16[896,768]{1,0:T(8,128)(2,1)} %get-tuple-element.364.refs_0_, bf16[896,768]{1,0:T(8,128)(2,1)} %get-tuple-element.365.refs_1_, bf16[896,768]{1,0:T(8,128)(2,1)} %get-tuple-element.366.refs_2_, bf16[896,768]{1,0:T(8,128)(2,1)} %bitcast.79, ...), custom_call_target="tpu_custom_call" | custom-call | flops 5284823040 | bytes 18677760 | tf_op jit(solution)/shard_map/weight_grads/pallas_call | solution.py:705
  463.7 18.0 %feed_back.3 = (bf16[896,3072]{1,0:T(8,128)(2,1)}, bf16[896,768]{1,0:T(8,128)(2,1)}, f32[896,768]{1,0:T(8,128)S(1)}, bf16[896,768]{1,0:T(8,128)(2,1)S(1)}, f32[1,768]{1,0:T(1,128)S(1)}) custom-call(f32[896,768]{1,0:T(8,128)S(1)} %get-tuple-element.387.flow_ref, f32[896,3072]{1,0:T(8,128)} %get-tuple-element.388.slope_ref, ...), custom_call_target="tpu_custom_call" | custom-call | flops 8455716864 | bytes 46399488 | tf_op jit(solution)/shard_map/feed_back/pallas_call | solution.py:547
  486.4 16.8 %weight_grads.7 = (f32[384,6144]{1,0:T(8,128)}, bf16[384,6144]{1,0:T(8,128)(2,1)S(1)}) custom-call(bf16[896,768]{1,0:T(8,128)(2,1)} %copy-done.32, bf16[896,768]{1,0:T(8,128)(2,1)} %get-tuple-element.395.refs_1_, bf16[896,3072]{1,0:T(8,128)(2,1)} %get-tuple-element.396.refs_2_, bf16[896,3072]{1,0:T(8,128)(2,1)} %get-tuple-element.397.refs_3_), custom_call_target="tpu_custom_call" | custom-call | flops 8455716864 | bytes 29884416 | tf_op jit(solution)/shard_map/weight_grads/pallas_call | solution.py:705
  510.6 10.6 %attend_back.6 = (bf16[2,448,768]{2,1,0:T(8,128)(2,1)}, bf16[2,448,768]{2,1,0:T(8,128)(2,1)}, bf16[2,448,768]{2,1,0:T(8,128)(2,1)}) custom-call(bf16[2,448,2304]{2,1,0:T(8,128)(2,1)S(1)} %bitcast.44, bf16[2,448,2304]{2,1,0:T(8,128)(2,1)S(1)} %bitcast.45, bf16[2,448,2304]{2,1,0:T(8,128)(2,1)S(1)} %bitcast.46, bf16[2,448,768]{2,1,0:T(8,128)(2,1)S(1)} %bitcast.59), custom_call_target="tpu_custom_call" | custom-call | flops 4932501504 | bytes 4816896 | tf_op jit(solution)/shard_map/attend_back/pallas_call | solution.py:158
  530.5 10.3 %attend_back.7 = (bf16[2,448,768]{2,1,0:T(8,128)(2,1)}, bf16[2,448,768]{2,1,0:T(8,128)(2,1)}, bf16[2,448,768]{2,1,0:T(8,128)(2,1)}) custom-call(bf16[2,448,2304]{2,1,0:T(8,128)(2,1)S(1)} %bitcast.47, bf16[2,448,2304]{2,1,0:T(8,128)(2,1)S(1)} %bitcast.48, ...), custom_call_target="tpu_custom_call", output_to_operand_aliasing={{0}: (4, {}), {1}: (5, {}), {2}: (6, {})} | custom-call | flops 4932501504 | bytes 4816896 | tf_op jit(solution)/shard_map/attend_back/pallas_call | solution.py:158
  540.7 11.3 %weight_grads.8 = (f32[384,3072]{1,0:T(8,128)}, bf16[384,3072]{1,0:T(8,128)(2,1)S(1)}) custom-call(bf16[896,768]{1,0:T(8,128)(2,1)} %get-tuple-element.414.refs_0_, bf16[896,768]{1,0:T(8,128)(2,1)} %get-tuple-element.415.refs_1_, bf16[896,768]{1,0:T(8,128)(2,1)} %bitcast.72, bf16[896,768]{1,0:T(8,128)(2,1)} %bitcast.74, bf16[896,768]{1,0:T(8,128)(2,1)} %bitcast.76, ...), custom_call_target="tpu_custom_call" | custom-call | flops 4227858432 | bytes 14942208 | tf_op jit(solution)/shard_map/weight_grads/pallas_call | solution.py:705
  562.9 11.1 %project_back.3 = (f32[896,768]{1,0:T(8,128)S(1)}, f32[1,768]{1,0:T(1,128)S(1)}, bf16[896,768]{1,0:T(8,128)(2,1)}, f32[1,768]{1,0:T(1,128)S(1)}) custom-call(bf16[896,768]{1,0:T(8,128)(2,1)} %bitcast.73, bf16[896,768]{1,0:T(8,128)(2,1)} %bitcast.75, bf16[896,768]{1,0:T(8,128)(2,1)} %bitcast.77, bf16[192,4352]{1,0:T(8,128)(2,1)} %copy-done.40, ...), custom_call_target="tpu_custom_call" | custom-call | flops 3170893824 | bytes 15138816 | tf_op jit(solution)/shard_map/project_back/pallas_call | solution.py:645
  584.4 10.6 %collective-permute-done.54 = bf16[48,6144]{1,0:T(8,128)(2,1)S(1)} collective-permute-done((bf16[48,6144]{1,0:T(8,128)(2,1)S(1)}, bf16[48,6144]{1,0:T(8,128)(2,1)S(1)}, u32[]{:S(2)}, u32[]{:S(2)}) %collective-permute-start.54) | collective-permute-done | bytes 589856 | tf_op jit(solution)/shard_map/ppermute | solution.py:769
  595.1 8.4 %collective-permute-done.56 = bf16[192,1280]{1,0:T(8,128)(2,1)S(1)} collective-permute-done((bf16[192,1280]{1,0:T(8,128)(2,1)S(1)}, bf16[192,1280]{1,0:T(8,128)(2,1)S(1)}, u32[]{:S(2)}, u32[]{:S(2)}) %collective-permute-start.56) | collective-permute-done | bytes 491552 | tf_op jit(solution)/shard_map/ppermute | solution.py:769
  612.1 8.1 %collective-permute-done.59 = f32[48,1280]{1,0:T(8,128)S(1)} collective-permute-done((f32[48,1280]{1,0:T(8,128)S(1)}, f32[48,1280]{1,0:T(8,128)S(1)}, u32[]{:S(2)}, u32[]{:S(2)}) %collective-permute-start.59) | collective-permute-done | bytes 245792 | tf_op jit(solution)/shard_map/ppermute | solution.py:769
  623.0 19.5 %collective-permute-done.60 = f32[24,1280]{1,0:T(8,128)S(1)} collective-permute-done((f32[24,1280]{1,0:T(8,128)S(1)}, f32[24,1280]{1,0:T(8,128)S(1)}, u32[]{:S(2)}, u32[]{:S(2)}) %collective-permute-start.60) | collective-permute-done | bytes 122912 | tf_op jit(solution)/shard_map/ppermute | solution.py:769
  642.9 12.5 %collective-permute-done.63 = f32[24,3072]{1,0:T(8,128)S(1)} collective-permute-done((f32[24,3072]{1,0:T(8,128)S(1)}, f32[24,3072]{1,0:T(8,128)S(1)}, u32[]{:S(2)}, u32[]{:S(2)}) %collective-permute-start.63) | collective-permute-done | bytes 294944 | tf_op jit(solution)/shard_map/ppermute | solution.py:769
  (388 shorter events, 271.2 us)
Async XLA Ops:
  40.3 23.0 %collective-permute-start.3 = (bf16[48,6144]{1,0:T(8,128)(2,1)S(1)}, bf16[48,6144]{1,0:T(8,128)(2,1)S(1)}, u32[]{:S(2)}, u32[]{:S(2)}) collective-permute-start(bf16[48,6144]{1,0:T(8,128)(2,1)S(1)} %pad_maximum_fusion.9), channel_id=1, source_target_pairs={{0,8},{1,9},{2,10},{3,11},{4,12},{5,13},{6,14},{7,15},{8,0},{9,1},... | collective-permute-start | bytes 1769480 | tf_op jit(solution)/shard_map/ppermute | solution.py:769
  51.4 33.7 %collective-permute-start.9 = (bf16[192,4352]{1,0:T(8,128)(2,1)S(1)}, bf16[192,4352]{1,0:T(8,128)(2,1)S(1)}, u32[]{:S(2)}, u32[]{:S(2)}) collective-permute-start(bf16[192,4352]{1,0:T(8,128)(2,1)S(1)} %pad_maximum_fusion.2.refs_2_.refs_6_.refs_10_.own_ref), channel_id=1, source_target_pairs={{0,2},{1,3},{2,0},{3,1},{4,6},{5,7},{6,4},{7,5},{8,10},{9,11},{10,... | collective-permute-start | bytes 5013512 | tf_op jit(solution)/shard_map/ppermute | solution.py:769
  51.5 33.6 %collective-permute-start.8 = (bf16[192,4352]{1,0:T(8,128)(2,1)S(1)}, bf16[192,4352]{1,0:T(8,128)(2,1)S(1)}, u32[]{:S(2)}, u32[]{:S(2)}) collective-permute-start(bf16[192,4352]{1,0:T(8,128)(2,1)S(1)} %pad_maximum_fusion.2.refs_2_.refs_6_.refs_10_.own_ref), channel_id=1, source_target_pairs={{0,1},{1,0},{2,6},{3,7},{4,5},{5,4},{6,2},{7,3},{8,9},{9,8},{10,14... | collective-permute-start | bytes 5013512 | tf_op jit(solution)/shard_map/ppermute | solution.py:769
  63.4 36.5 %collective-permute-start.7 = (bf16[24,4352]{1,0:T(8,128)(2,1)S(1)}, bf16[24,4352]{1,0:T(8,128)(2,1)S(1)}, u32[]{:S(2)}, u32[]{:S(2)}) collective-permute-start(bf16[24,4352]{1,0:T(8,128)(2,1)S(1)} %pad_maximum_fusion.16), channel_id=1, source_target_pairs={{0,16},{1,17},{2,18},{3,19},{4,20},{5,21},{6,22},{7,23},{8,24},{9,... | collective-permute-start | bytes 626696 | tf_op jit(solution)/shard_map/ppermute | solution.py:769
  63.4 36.5 %collective-permute-start.6 = (bf16[48,9216]{1,0:T(8,128)(2,1)S(1)}, bf16[48,9216]{1,0:T(8,128)(2,1)S(1)}, u32[]{:S(2)}, u32[]{:S(2)}) collective-permute-start(bf16[48,9216]{1,0:T(8,128)(2,1)S(1)} %pad_maximum_fusion.5), channel_id=1, source_target_pairs={{0,8},{1,9},{2,10},{3,11},{4,12},{5,13},{6,14},{7,15},{8,0},{9,1},... | collective-permute-start | bytes 2654216 | tf_op jit(solution)/shard_map/ppermute | solution.py:769
  86.0 41.0 %collective-permute-start.16 = (bf16[192,6144]{1,0:T(8,128)(2,1)S(1)}, bf16[192,6144]{1,0:T(8,128)(2,1)S(1)}, u32[]{:S(2)}, u32[]{:S(2)}) collective-permute-start(bf16[192,6144]{1,0:T(8,128)(2,1)S(1)} %constant_dynamic-update-slice_fusion.uown_ref.down_ref), channel_id=1, source_target_pairs={{0,1},{1,0},{2,6},{3,7},{4,5},{5,4},{6,2},{7,3},{8,9},{9,8},{10,14... | collective-permute-start | bytes 7077896 | tf_op jit(solution)/shard_map/ppermute | solution.py:769
  87.6 39.5 %collective-permute-start.12 = (bf16[192,6144]{1,0:T(8,128)(2,1)S(1)}, bf16[192,6144]{1,0:T(8,128)(2,1)}, u32[]{:S(2)}, u32[]{:S(2)}) collective-permute-start(bf16[192,6144]{1,0:T(8,128)(2,1)S(1)} %constant_dynamic-update-slice_fusion.uown_ref.down_ref), channel_id=1, source_target_pairs={{0,2},{1,3},{2,0},{3,1},{4,6},{5,7},{6,4},{7,5},{8,10},{9,11},{10,... | collective-permute-start | bytes 7077896 | tf_op jit(solution)/shard_map/ppermute | solution.py:769
  99.9 37.1 %collective-permute-start.14 = (bf16[24,16128]{1,0:T(8,128)(2,1)S(1)}, bf16[24,16128]{1,0:T(8,128)(2,1)S(1)}, u32[]{:S(2)}, u32[]{:S(2)}) collective-permute-start(bf16[24,16128]{1,0:T(8,128)(2,1)S(1)} %pad_maximum_fusion.8), channel_id=1, source_target_pairs={{0,16},{1,17},{2,18},{3,19},{4,20},{5,21},{6,22},{7,23},{8,24},{9,... | collective-permute-start | bytes 2322440 | tf_op jit(solution)/shard_map/ppermute | solution.py:769
  101.2 35.8 %collective-permute-start.15 = (bf16[96,9216]{1,0:T(8,128)(2,1)S(1)}, bf16[96,9216]{1,0:T(8,128)(2,1)S(1)}, u32[]{:S(2)}, u32[]{:S(2)}) collective-permute-start(bf16[96,9216]{1,0:T(8,128)(2,1)S(1)} %pad_maximum_fusion.1), channel_id=1, source_target_pairs={{0,4},{1,5},{2,3},{3,2},{4,0},{5,1},{6,7},{7,6},{8,12},{9,13},{10,... | collective-permute-start | bytes 5308424 | tf_op jit(solution)/shard_map/ppermute | solution.py:769
  102.6 24.4 %collective-permute-start.13 = (bf16[48,4352]{1,0:T(8,128)(2,1)S(1)}, bf16[48,4352]{1,0:T(8,128)(2,1)S(1)}, u32[]{:S(2)}, u32[]{:S(2)}) collective-permute-start(bf16[48,4352]{1,0:T(8,128)(2,1)S(1)} %pad_maximum_fusion.14), channel_id=1, source_target_pairs={{0,8},{1,9},{2,10},{3,11},{4,12},{5,13},{6,14},{7,15},{8,0},{9,1},... | collective-permute-start | bytes 1253384 | tf_op jit(solution)/shard_map/ppermute | solution.py:769
  137.2 50.5 %collective-permute-start.20 = (bf16[192,9216]{1,0:T(8,128)(2,1)S(1)}, bf16[192,9216]{1,0:T(8,128)(2,1)S(1)}, u32[]{:S(2)}, u32[]{:S(2)}) collective-permute-start(bf16[192,9216]{1,0:T(8,128)(2,1)S(1)} %constant_dynamic-update-slice_fusion.4.own_ref.uown_ref.down_ref), channel_id=1, source_target_pairs={{0,1},{1,0},{2,6},{3,7},{4,5},{5,4},{6,2},{7,3},{8,9},{9,8},{10,14... | collective-permute-start | bytes 10616840 | tf_op jit(solution)/shard_map/ppermute | solution.py:769
  138.7 49.0 %collective-permute-start.17 = (bf16[192,9216]{1,0:T(8,128)(2,1)S(1)}, bf16[192,9216]{1,0:T(8,128)(2,1)S(1)}, u32[]{:S(2)}, u32[]{:S(2)}) collective-permute-start(bf16[192,9216]{1,0:T(8,128)(2,1)S(1)} %constant_dynamic-update-slice_fusion.4.own_ref.uown_ref.down_ref), channel_id=1, source_target_pairs={{0,2},{1,3},{2,0},{3,1},{4,6},{5,7},{6,4},{7,5},{8,10},{9,11},{10,... | collective-permute-start | bytes 10616840 | tf_op jit(solution)/shard_map/ppermute | solution.py:769
  138.8 23.7 %collective-permute-start.19 = (bf16[96,4352]{1,0:T(8,128)(2,1)S(1)}, bf16[96,4352]{1,0:T(8,128)(2,1)S(1)}, u32[]{:S(2)}, u32[]{:S(2)}) collective-permute-start(bf16[96,4352]{1,0:T(8,128)(2,1)S(1)} %pad_maximum_fusion.7), channel_id=1, source_target_pairs={{0,4},{1,5},{2,3},{3,2},{4,0},{5,1},{6,7},{7,6},{8,12},{9,13},{10,... | collective-permute-start | bytes 2506760 | tf_op jit(solution)/shard_map/ppermute | solution.py:769
  140.5 35.1 %collective-permute-start.18 = (bf16[48,16128]{1,0:T(8,128)(2,1)S(1)}, bf16[48,16128]{1,0:T(8,128)(2,1)S(1)}, u32[]{:S(2)}, u32[]{:S(2)}) collective-permute-start(bf16[48,16128]{1,0:T(8,128)(2,1)S(1)} %pad_maximum_fusion.3), channel_id=1, source_target_pairs={{0,8},{1,9},{2,10},{3,11},{4,12},{5,13},{6,14},{7,15},{8,0},{9,1},... | collective-permute-start | bytes 4644872 | tf_op jit(solution)/shard_map/ppermute | solution.py:769
  187.8 45.2 %collective-permute-start.24 = (bf16[192,4352]{1,0:T(8,128)(2,1)S(1)}, bf16[192,4352]{1,0:T(8,128)(2,1)}, u32[]{:S(2)}, u32[]{:S(2)}) collective-permute-start(bf16[192,4352]{1,0:T(8,128)(2,1)S(1)} %constant_dynamic-update-slice_fusion.11.refs_2_.refs_6_.refs_10_.own_ref.refs_3_.refs_7_.refs_11_), channel_id=1, source_target_pairs={{0,1},{1,0},{2,6},{3,7},{4,5},{5,4},{6,2},{7,3},{8,9},{9,8},{10,14... | collective-permute-start | bytes 5013512 | tf_op jit(solution)/shard_map/ppermute | solution.py:769
  189.4 43.6 %collective-permute-start.22 = (bf16[192,4352]{1,0:T(8,128)(2,1)S(1)}, bf16[192,4352]{1,0:T(8,128)(2,1)S(1)}, u32[]{:S(2)}, u32[]{:S(2)}) collective-permute-start(bf16[192,4352]{1,0:T(8,128)(2,1)S(1)} %constant_dynamic-update-slice_fusion.11.refs_2_.refs_6_.refs_10_.own_ref.refs_3_.refs_7_.refs_11_), channel_id=1, source_target_pairs={{0,2},{1,3},{2,0},{3,1},{4,6},{5,7},{6,4},{7,5},{8,10},{9,11},{10,... | collective-permute-start | bytes 5013512 | tf_op jit(solution)/shard_map/ppermute | solution.py:769
  192.5 40.5 %collective-permute-start.23 = (bf16[96,6144]{1,0:T(8,128)(2,1)S(1)}, bf16[96,6144]{1,0:T(8,128)(2,1)S(1)}, u32[]{:S(2)}, u32[]{:S(2)}) collective-permute-start(bf16[96,6144]{1,0:T(8,128)(2,1)S(1)} %get-tuple-element.504), channel_id=1, source_target_pairs={{0,4},{1,5},{2,3},{3,2},{4,0},{5,1},{6,7},{7,6},{8,12},{9,13},{10,... | collective-permute-start | bytes 3538952 | tf_op jit(solution)/shard_map/ppermute | solution.py:769
  235.8 37.1 %collective-permute-start.28 = (bf16[192,6144]{1,0:T(8,128)(2,1)}, bf16[192,6144]{1,0:T(8,128)(2,1)}, u32[]{:S(2)}, u32[]{:S(2)}) collective-permute-start(bf16[192,6144]{1,0:T(8,128)(2,1)} %pad_maximum_fusion.uown_ref.down_ref), channel_id=1, source_target_pairs={{0,1},{1,0},{2,6},{3,7},{4,5},{5,4},{6,2},{7,3},{8,9},{9,8},{10,14... | collective-permute-start | bytes 7077896 | tf_op jit(solution)/shard_map/ppermute | solution.py:769
  237.3 35.6 %collective-permute-start.26 = (bf16[192,6144]{1,0:T(8,128)(2,1)}, bf16[192,6144]{1,0:T(8,128)(2,1)}, u32[]{:S(2)}, u32[]{:S(2)}) collective-permute-start(bf16[192,6144]{1,0:T(8,128)(2,1)} %pad_maximum_fusion.uown_ref.down_ref), channel_id=1, source_target_pairs={{0,2},{1,3},{2,0},{3,1},{4,6},{5,7},{6,4},{7,5},{8,10},{9,11},{10,... | collective-permute-start | bytes 7077896 | tf_op jit(solution)/shard_map/ppermute | solution.py:769
  237.7 32.8 %collective-permute-start.27 = (bf16[96,3840]{1,0:T(8,128)(2,1)}, bf16[96,3840]{1,0:T(8,128)(2,1)S(1)}, u32[]{:S(2)}, u32[]{:S(2)}) collective-permute-start(bf16[96,3840]{1,0:T(8,128)(2,1)} %slice.419), channel_id=1, source_target_pairs={{0,4},{1,5},{2,3},{3,2},{4,0},{5,1},{6,7},{7,6},{8,12},{9,13},{10,... | collective-permute-start | bytes 2211848 | tf_op jit(solution)/shard_map/ppermute | solution.py:769
  273.0 32.1 %collective-permute-start.32 = (bf16[192,3840]{1,0:T(8,128)(2,1)S(1)}, bf16[192,3840]{1,0:T(8,128)(2,1)S(1)}, u32[]{:S(2)}, u32[]{:S(2)}) collective-permute-start(bf16[192,3840]{1,0:T(8,128)(2,1)S(1)} %constant_dynamic-update-slice_fusion.15.own_ref.refs_3_.refs_7_.refs_11_), channel_id=1, source_target_pairs={{0,1},{1,0},{2,6},{3,7},{4,5},{5,4},{6,2},{7,3},{8,9},{9,8},{10,14... | collective-permute-start | bytes 4423688 | tf_op jit(solution)/shard_map/ppermute | solution.py:769
  274.6 30.5 %collective-permute-start.30 = (bf16[192,3840]{1,0:T(8,128)(2,1)S(1)}, bf16[192,3840]{1,0:T(8,128)(2,1)S(1)}, u32[]{:S(2)}, u32[]{:S(2)}) collective-permute-start(bf16[192,3840]{1,0:T(8,128)(2,1)S(1)} %constant_dynamic-update-slice_fusion.15.own_ref.refs_3_.refs_7_.refs_11_), channel_id=1, source_target_pairs={{0,2},{1,3},{2,0},{3,1},{4,6},{5,7},{6,4},{7,5},{8,10},{9,11},{10,... | collective-permute-start | bytes 4423688 | tf_op jit(solution)/shard_map/ppermute | solution.py:769
  274.7 28.9 %collective-permute-start.31 = (bf16[96,6144]{1,0:T(8,128)(2,1)S(1)}, bf16[96,6144]{1,0:T(8,128)(2,1)S(1)}, u32[]{:S(2)}, u32[]{:S(2)}) collective-permute-start(bf16[96,6144]{1,0:T(8,128)(2,1)S(1)} %copy-done.54), channel_id=1, source_target_pairs={{0,4},{1,5},{2,3},{3,2},{4,0},{5,1},{6,7},{7,6},{8,12},{9,13},{10,... | collective-permute-start | bytes 3538952 | tf_op jit(solution)/shard_map/ppermute | solution.py:769
  305.3 28.9 %collective-permute-start.35 = (bf16[192,6144]{1,0:T(8,128)(2,1)S(1)}, bf16[192,6144]{1,0:T(8,128)(2,1)S(1)}, u32[]{:S(2)}, u32[]{:S(2)}) collective-permute-start(bf16[192,6144]{1,0:T(8,128)(2,1)S(1)} %constant_dynamic-update-slice_fusion.17.uown_ref.down_ref), channel_id=1, source_target_pairs={{0,1},{1,0},{2,6},{3,7},{4,5},{5,4},{6,2},{7,3},{8,9},{9,8},{10,14... | collective-permute-start | bytes 7077896 | tf_op jit(solution)/shard_map/ppermute | solution.py:769
  306.8 27.4 %collective-permute-start.34 = (bf16[192,6144]{1,0:T(8,128)(2,1)S(1)}, bf16[192,6144]{1,0:T(8,128)(2,1)S(1)}, u32[]{:S(2)}, u32[]{:S(2)}) collective-permute-start(bf16[192,6144]{1,0:T(8,128)(2,1)S(1)} %constant_dynamic-update-slice_fusion.17.uown_ref.down_ref), channel_id=1, source_target_pairs={{0,2},{1,3},{2,0},{3,1},{4,6},{5,7},{6,4},{7,5},{8,10},{9,11},{10,... | collective-permute-start | bytes 7077896 | tf_op jit(solution)/shard_map/ppermute | solution.py:769
  425.8 33.2 %collective-permute-start.39 = (bf16[192,6144]{1,0:T(8,128)(2,1)}, bf16[192,6144]{1,0:T(8,128)(2,1)}, u32[]{:S(2)}, u32[]{:S(2)}) collective-permute-start(bf16[192,6144]{1,0:T(8,128)(2,1)} %get-tuple-element.486), channel_id=1, source_target_pairs={{0,1},{1,0},{2,6},{3,7},{4,5},{5,4},{6,2},{7,3},{8,9},{9,8},{10,14... | collective-permute-start | bytes 7077896 | tf_op jit(solution)/shard_map/ppermute | solution.py:769
  459.0 22.8 %collective-permute-start.41 = (bf16[384,3840]{1,0:T(8,128)(2,1)S(1)}, bf16[384,3840]{1,0:T(8,128)(2,1)}, u32[]{:S(2)}, u32[]{:S(2)}) collective-permute-start(bf16[384,3840]{1,0:T(8,128)(2,1)S(1)} %get-tuple-element.386), channel_id=1, source_target_pairs={{0,2},{1,3},{2,0},{3,1},{4,6},{5,7},{6,4},{7,5},{8,10},{9,11},{10,... | collective-permute-start | bytes 8847368 | tf_op jit(solution)/shard_map/ppermute | solution.py:769
  527.1 33.0 %collective-permute-start.48 = (bf16[192,6144]{1,0:T(8,128)(2,1)}, bf16[192,6144]{1,0:T(8,128)(2,1)S(1)}, u32[]{:S(2)}, u32[]{:S(2)}) collective-permute-start(bf16[192,6144]{1,0:T(8,128)(2,1)} %get-tuple-element.484), channel_id=1, source_target_pairs={{0,1},{1,0},{2,6},{3,7},{4,5},{5,4},{6,2},{7,3},{8,9},{9,8},{10,14... | collective-permute-start | bytes 7077896 | tf_op jit(solution)/shard_map/ppermute | solution.py:769
  528.3 28.9 %collective-permute-start.46 = (f32[24,6144]{1,0:T(8,128)S(1)}, f32[24,6144]{1,0:T(8,128)S(1)}, u32[]{:S(2)}, u32[]{:S(2)}) collective-permute-start(f32[24,6144]{1,0:T(8,128)S(1)} %slice_add_fusion.19), channel_id=1, source_target_pairs={{0,16},{1,17},{2,18},{3,19},{4,20},{5,21},{6,22},{7,23},{8,24},{9,... | collective-permute-start | bytes 1769480 | tf_op jit(solution)/shard_map/ppermute | solution.py:769
  529.0 31.1 %collective-permute-start.47 = (f32[48,3840]{1,0:T(8,128)S(1)}, f32[48,3840]{1,0:T(8,128)S(1)}, u32[]{:S(2)}, u32[]{:S(2)}) collective-permute-start(f32[48,3840]{1,0:T(8,128)S(1)} %get-tuple-element.505), channel_id=1, source_target_pairs={{0,8},{1,9},{2,10},{3,11},{4,12},{5,13},{6,14},{7,15},{8,0},{9,1},... | collective-permute-start | bytes 2211848 | tf_op jit(solution)/shard_map/ppermute | solution.py:769
  610.3 32.2 %collective-permute-start.61 = (f32[24,6144]{1,0:T(8,128)S(1)}, f32[24,6144]{1,0:T(8,128)S(1)}, u32[]{:S(2)}, u32[]{:S(2)}) collective-permute-start(f32[24,6144]{1,0:T(8,128)S(1)} %slice_add_fusion.17), channel_id=1, source_target_pairs={{0,16},{1,17},{2,18},{3,19},{4,20},{5,21},{6,22},{7,23},{8,24},{9,... | collective-permute-start | bytes 1769480 | tf_op jit(solution)/shard_map/ppermute | solution.py:769
  620.3 22.2 %collective-permute-start.60 = (f32[24,1280]{1,0:T(8,128)S(1)}, f32[24,1280]{1,0:T(8,128)S(1)}, u32[]{:S(2)}, u32[]{:S(2)}) collective-permute-start(f32[24,1280]{1,0:T(8,128)S(1)} %slice_add_fusion.26), channel_id=1, source_target_pairs={{0,16},{1,17},{2,18},{3,19},{4,20},{5,21},{6,22},{7,23},{8,24},{9,... | collective-permute-start | bytes 368648 | tf_op jit(solution)/shard_map/ppermute | solution.py:769
  (111 other events, 1662.7 us)

commit v9 on v8

--- a/solution.py
+++ b/solution.py
@@ -1192,7 +1192,7 @@
         piece = weight_grads([(normed_two, [grad_hidden]), (grad_down, [active])])
         piece, grad_branch = pump.end((piece, grad_branch))
         send_off(
-            ("mlp", layer), [piece], 3, {1: 2, last_stage: 2} if layer else {last_stage: 2}
+            ("mlp", layer), [piece], 2, {1: 2, last_stage: 2} if layer else {last_stage: 2}
         )
         pump.begin()
         grad_mixed, branch_whole = mix_back(grad_branch, w_out_rel, mover)
@@ -1208,7 +1208,7 @@
         if layer == 0:
             piece = weight_grads(pairs)
             piece, grad_proj = pump.end((piece, grad_proj))
-            send_off(("attn", 0), [piece], 3)
+            send_off(("attn", 0), [piece], 2)
             pump.begin()
         results = project_back(
             grad_proj,

time: 686 us -> 696 us (1.015)
  waiting for transfers between devices: 214 us -> 231 us
    ppermute x69, waiting for transfers between devices: 214 us -> 231 us  [swap(): return lax.ppermute(value, AXES, perm)]
    unnamed x161 -> x163, local copies, waits for them, and re-layouts: 14.6 us -> 10.6 us
  transfers between devices with their start and end apart: 69 -> 69, of which waited for: 34 -> 36; matrix products, arithmetic and copies ran while one was open for 2% -> 2% of each run, Pallas kernels for 42% -> 41%
where the time goes in v9:
time: 696 us; the launch traced here: 690 us
  Pallas kernels  351 us (50%)
  waiting for transfers between devices  231 us (33%)
  starting transfers between devices  64 us (9%)
  other arithmetic  24.5 us (4%)
  local copies, waits for them, and re-layouts  15.7 us (2%)
    ppermute x69, waiting for transfers between devices, swap(): return lax.ppermute(value, AXES, perm)  231 us
    ppermute x69, starting transfers between devices, swap(): return lax.ppermute(value, AXES, perm)  64 us
    pallas_call x5, Pallas kernels, weight_grads(): pl.pallas_call(kernel, grid=(total,), in_specs=specs, out_specs=[block, b...  63.7 us
    pallas_call x4, Pallas kernels, feed_forward(): pl.pallas_call(kernel, grid=(steps,), in_specs=[whole_block(normed.shape)...  62.2 us
    pallas_call x4, Pallas kernels, attend(): pl.pallas_call(attend_kernel, grid=(seqs, blocks), in_specs=specs, out_sp...  45.5 us
    pallas_call x4, Pallas kernels, attend_back(): pl.pallas_call(kernel, grid=(blocks,), in_specs=specs + [block] + [pl.Blo...  41.2 us
    pallas_call x2, Pallas kernels, feed_back(): pl.pallas_call(kernel, grid=(steps,), in_specs=[full, column, full, whole...  35.7 us
    pallas_call x4, Pallas kernels, norm_project(): pl.pallas_call(kernel, grid=(steps,), in_specs=[whole_block(states.shape)...  26.4 us
  transfers between devices with their start and end apart: 69, of which 36 were waited for; matrix products, arithmetic and copies ran while one was open for 2% of the time, Pallas kernels for 41%

profile of v9, /device:TPU:0, one launch (start us, length us, event | category | flops | bytes accessed | tf_op | source)
XLA Modules:
  0.0 690.3 jit_solution(15872609252753634345)
XLA Ops:
  22.6 11.3 %collective-permute-done.1 = bf16[24,6144]{1,0:T(8,128)(2,1)S(1)} collective-permute-done((bf16[24,6144]{1,0:T(8,128)(2,1)S(1)}, bf16[24,6144]{1,0:T(8,128)(2,1)S(1)}, u32[]{:S(2)}, u32[]{:S(2)}) %collective-permute-start.1) | collective-permute-done | bytes 294944 | tf_op jit(solution)/shard_map/ppermute | solution.py:769
  42.2 9.1 %collective-permute-done.5 = bf16[96,4352]{1,0:T(8,128)(2,1)S(1)} collective-permute-done((bf16[96,4352]{1,0:T(8,128)(2,1)S(1)}, bf16[96,4352]{1,0:T(8,128)(2,1)S(1)}, u32[]{:S(2)}, u32[]{:S(2)}) %collective-permute-start.5) | collective-permute-done | bytes 835616 | tf_op jit(solution)/shard_map/ppermute | solution.py:769
  67.6 17.5 %collective-permute-done.10 = bf16[96,6144]{1,0:T(8,128)(2,1)S(1)} collective-permute-done((bf16[96,6144]{1,0:T(8,128)(2,1)S(1)}, bf16[96,6144]{1,0:T(8,128)(2,1)S(1)}, u32[]{:S(2)}, u32[]{:S(2)}) %collective-permute-start.10) | collective-permute-done | bytes 1179680 | tf_op jit(solution)/shard_map/ppermute | solution.py:769
  103.8 11.2 %attend.4 = bf16[2,448,768]{2,1,0:T(8,128)(2,1)S(1)} custom-call(bf16[2,448,2304]{2,1,0:T(8,128)(2,1)S(1)} %bitcast.28, bf16[2,448,2304]{2,1,0:T(8,128)(2,1)S(1)} %bitcast.29, bf16[2,448,2304]{2,1,0:T(8,128)(2,1)S(1)} %bitcast.30), custom_call_target="tpu_custom_call" | custom-call | flops 4932501504 | bytes 5505024 | tf_op jit(solution)/shard_map/attend/pallas_call | solution.py:121
  127.0 10.0 %collective-permute-done.14 = bf16[24,16128]{1,0:T(8,128)(2,1)S(1)} collective-permute-done((bf16[24,16128]{1,0:T(8,128)(2,1)S(1)}, bf16[24,16128]{1,0:T(8,128)(2,1)S(1)}, u32[]{:S(2)}, u32[]{:S(2)}) %collective-permute-start.14) | collective-permute-done | bytes 774176 | tf_op jit(solution)/shard_map/ppermute | solution.py:769
  148.3 14.2 %feed_forward.4.h_ref.one_ref = f32[896,768]{1,0:T(8,128)S(1)} custom-call(bf16[896,768]{1,0:T(8,128)(2,1)S(1)} %get-tuple-element.284.b_ref, f32[896,768]{1,0:T(8,128)S(1)} %get-tuple-element.285.m_ref, bf16[192,6144]{1,0:T(8,128)(2,1)} %copy-done.62, bf16[192,6144]{1,0:T(8,128)(2,1)} %copy-done.64, bf16[192,6144]{1,0:T(8,128)(2,1)} %copy-done.65, ...), custom_call_target="tpu_custom_call" | custom-call | flops 8455716864 | bytes 46006272 | tf_op jit(solution)/shard_map/feed_forward/pallas_call | solution.py:405
  162.5 13.0 %collective-permute-done.18 = bf16[48,16128]{1,0:T(8,128)(2,1)S(1)} collective-permute-done((bf16[48,16128]{1,0:T(8,128)(2,1)S(1)}, bf16[48,16128]{1,0:T(8,128)(2,1)S(1)}, u32[]{:S(2)}, u32[]{:S(2)}) %collective-permute-start.18) | collective-permute-done | bytes 1548320 | tf_op jit(solution)/shard_map/ppermute | solution.py:769
  175.6 12.1 %collective-permute-done.20.own2_ref.uown2_ref.down2_ref = bf16[192,9216]{1,0:T(8,128)(2,1)S(1)} collective-permute-done((bf16[192,9216]{1,0:T(8,128)(2,1)S(1)}, bf16[192,9216]{1,0:T(8,128)(2,1)S(1)}, u32[]{:S(2)}, u32[]{:S(2)}) %collective-permute-start.20) | collective-permute-done | bytes 3538976 | tf_op jit(solution)/shard_map/ppermute | solution.py:769
  200.0 11.4 %attend.5 = bf16[2,448,768]{2,1,0:T(8,128)(2,1)S(1)} custom-call(bf16[2,448,2304]{2,1,0:T(8,128)(2,1)S(1)} %bitcast.31, bf16[2,448,2304]{2,1,0:T(8,128)(2,1)S(1)} %bitcast.32, bf16[2,448,2304]{2,1,0:T(8,128)(2,1)S(1)} %bitcast.33), custom_call_target="tpu_custom_call" | custom-call | flops 4932501504 | bytes 5505024 | tf_op jit(solution)/shard_map/attend/pallas_call | solution.py:121
  217.1 14.1 %feed_forward.5.two_ref = f32[896,768]{1,0:T(8,128)S(1)} custom-call(bf16[896,768]{1,0:T(8,128)(2,1)S(1)} %get-tuple-element.296.b_ref, f32[896,768]{1,0:T(8,128)S(1)} %get-tuple-element.297.m_ref, bf16[192,9216]{1,0:T(8,128)(2,1)} %copy-done.42, bf16[192,9216]{1,0:T(8,128)(2,1)} %copy-done.44, bf16[192,9216]{1,0:T(8,128)(2,1)} %copy-done.45, ...), custom_call_target="tpu_custom_call" | custom-call | flops 8455716864 | bytes 46006272 | tf_op jit(solution)/shard_map/feed_forward/pallas_call | solution.py:405
  252.7 11.6 %attend.6 = bf16[2,448,768]{2,1,0:T(8,128)(2,1)S(1)} custom-call(bf16[2,448,2304]{2,1,0:T(8,128)(2,1)S(1)} %bitcast.41, bf16[2,448,2304]{2,1,0:T(8,128)(2,1)S(1)} %bitcast.42, bf16[2,448,2304]{2,1,0:T(8,128)(2,1)S(1)} %bitcast.43), custom_call_target="tpu_custom_call" | custom-call | flops 4932501504 | bytes 5505024 | tf_op jit(solution)/shard_map/attend/pallas_call | solution.py:121
  278.0 16.9 %feed_forward.6 = (f32[896,768]{1,0:T(8,128)S(1)}, bf16[896,3072]{1,0:T(8,128)(2,1)}, f32[896,3072]{1,0:T(8,128)}) custom-call(bf16[896,768]{1,0:T(8,128)(2,1)S(1)} %get-tuple-element.316.b_ref.refs_0_, f32[896,768]{1,0:T(8,128)S(1)} %get-tuple-element.317.m_ref, bf16[192,6144]{1,0:T(8,128)(2,1)} %pad_maximum_fusion.uown_ref.down_ref, ...), custom_call_target="tpu_custom_call" | custom-call | flops 8455716864 | bytes 46006272 | tf_op jit(solution)/shard_map/feed_forward/pallas_call | solution.py:405
  295.0 9.1 %collective-permute-done.31 = bf16[96,6144]{1,0:T(8,128)(2,1)S(1)} collective-permute-done((bf16[96,6144]{1,0:T(8,128)(2,1)S(1)}, bf16[96,6144]{1,0:T(8,128)(2,1)S(1)}, u32[]{:S(2)}, u32[]{:S(2)}) %collective-permute-start.31) | collective-permute-done | bytes 1179680 | tf_op jit(solution)/shard_map/ppermute | solution.py:769
  315.9 11.2 %attend.7 = bf16[2,448,768]{2,1,0:T(8,128)(2,1)S(1)} custom-call(bf16[2,448,2304]{2,1,0:T(8,128)(2,1)S(1)} %bitcast.50, bf16[2,448,2304]{2,1,0:T(8,128)(2,1)S(1)} %bitcast.51, bf16[2,448,2304]{2,1,0:T(8,128)(2,1)S(1)} %bitcast.52), custom_call_target="tpu_custom_call" | custom-call | flops 4932501504 | bytes 5505024 | tf_op jit(solution)/shard_map/attend/pallas_call | solution.py:121
  339.2 16.9 %feed_forward.7 = (f32[896,768]{1,0:T(8,128)S(1)}, bf16[896,3072]{1,0:T(8,128)(2,1)}, f32[896,3072]{1,0:T(8,128)}) custom-call(bf16[896,768]{1,0:T(8,128)(2,1)S(1)} %get-tuple-element.331.b_ref.refs_0_, f32[896,768]{1,0:T(8,128)S(1)} %get-tuple-element.332.m_ref, bf16[192,6144]{1,0:T(8,128)(2,1)} %copy-done.49, bf16[192,6144]{1,0:T(8,128)(2,1)} %copy-done.52, ...), custom_call_target="tpu_custom_call" | custom-call | flops 8455716864 | bytes 46006272 | tf_op jit(solution)/shard_map/feed_forward/pallas_call | solution.py:405
  356.1 7.8 %head_step.1 = (f32[896,768]{1,0:T(8,128)S(1)}, bf16[896,768]{1,0:T(8,128)(2,1)}, bf16[896,768]{1,0:T(8,128)(2,1)}, f32[1,768]{1,0:T(1,128)S(1)}, f32[1,768]{1,0:T(1,128)S(1)}) custom-call(f32[896,768]{1,0:T(8,128)S(1)} %get-tuple-element.335.h_ref, f32[8,768]{1,0:T(8,128)S(1)} %get-tuple-element.336.table_ref.refs_17_, ...), custom_call_target="tpu_custom_call" | custom-call | flops 4227858432 | bytes 11010048 | tf_op jit(solution)/shard_map/head_step/pallas_call | solution.py:486
  365.7 17.7 %feed_back.2 = (bf16[896,3072]{1,0:T(8,128)(2,1)}, bf16[896,768]{1,0:T(8,128)(2,1)}, f32[896,768]{1,0:T(8,128)S(1)}, bf16[896,768]{1,0:T(8,128)(2,1)S(1)}, f32[1,768]{1,0:T(1,128)S(1)}) custom-call(f32[896,768]{1,0:T(8,128)S(1)} %get-tuple-element.342.flow_ref, f32[896,3072]{1,0:T(8,128)} %get-tuple-element.343.slope_ref, f32[896,768]{1,0:T(8,128)S(1)} %copy-done.9, ...), custom_call_target="tpu_custom_call" | custom-call | flops 8455716864 | bytes 46399488 | tf_op jit(solution)/shard_map/feed_back/pallas_call | solution.py:547
  383.4 17.2 %weight_grads.5 = (f32[384,6144]{1,0:T(8,128)}, bf16[384,6144]{1,0:T(8,128)(2,1)S(1)}) custom-call(bf16[896,768]{1,0:T(8,128)(2,1)} %copy-done.38, bf16[896,768]{1,0:T(8,128)(2,1)} %get-tuple-element.348.refs_1_, bf16[896,3072]{1,0:T(8,128)(2,1)} %get-tuple-element.349.refs_2_, bf16[896,3072]{1,0:T(8,128)(2,1)} %get-tuple-element.350.refs_3_), custom_call_target="tpu_custom_call" | custom-call | flops 8455716864 | bytes 29884416 | tf_op jit(solution)/shard_map/weight_grads/pallas_call | solution.py:705
  405.3 10.2 %attend_back.4 = (bf16[2,448,768]{2,1,0:T(8,128)(2,1)}, bf16[2,448,768]{2,1,0:T(8,128)(2,1)}, bf16[2,448,768]{2,1,0:T(8,128)(2,1)}) custom-call(bf16[2,448,2304]{2,1,0:T(8,128)(2,1)S(1)} %bitcast.53, bf16[2,448,2304]{2,1,0:T(8,128)(2,1)S(1)} %bitcast.54, bf16[2,448,2304]{2,1,0:T(8,128)(2,1)S(1)} %bitcast.55, bf16[2,448,768]{2,1,0:T(8,128)(2,1)S(1)} %bitcast.61), custom_call_target="tpu_custom_call" | custom-call | flops 4932501504 | bytes 4816896 | tf_op jit(solution)/shard_map/attend_back/pallas_call | solution.py:158
  424.8 10.2 %attend_back.5 = (bf16[2,448,768]{2,1,0:T(8,128)(2,1)}, bf16[2,448,768]{2,1,0:T(8,128)(2,1)}, bf16[2,448,768]{2,1,0:T(8,128)(2,1)}) custom-call(bf16[2,448,2304]{2,1,0:T(8,128)(2,1)S(1)} %bitcast.56, bf16[2,448,2304]{2,1,0:T(8,128)(2,1)S(1)} %bitcast.57, ...), custom_call_target="tpu_custom_call", output_to_operand_aliasing={{0}: (4, {}), {1}: (5, {}), {2}: (6, {})} | custom-call | flops 4932501504 | bytes 4816896 | tf_op jit(solution)/shard_map/attend_back/pallas_call | solution.py:158
  442.5 14.0 %weight_grads.6 = (f32[384,3840]{1,0:T(8,128)}, bf16[384,3840]{1,0:T(8,128)(2,1)S(1)}) custom-call(bf16[896,768]{1,0:T(8,128)(2,1)} %get-tuple-element.364.refs_0_, bf16[896,768]{1,0:T(8,128)(2,1)} %get-tuple-element.365.refs_1_, bf16[896,768]{1,0:T(8,128)(2,1)} %get-tuple-element.366.refs_2_, bf16[896,768]{1,0:T(8,128)(2,1)} %bitcast.79, ...), custom_call_target="tpu_custom_call" | custom-call | flops 5284823040 | bytes 18677760 | tf_op jit(solution)/shard_map/weight_grads/pallas_call | solution.py:705
  458.6 18.0 %feed_back.3 = (bf16[896,3072]{1,0:T(8,128)(2,1)}, bf16[896,768]{1,0:T(8,128)(2,1)}, f32[896,768]{1,0:T(8,128)S(1)}, bf16[896,768]{1,0:T(8,128)(2,1)S(1)}, f32[1,768]{1,0:T(1,128)S(1)}) custom-call(f32[896,768]{1,0:T(8,128)S(1)} %get-tuple-element.387.flow_ref, f32[896,3072]{1,0:T(8,128)} %get-tuple-element.388.slope_ref, ...), custom_call_target="tpu_custom_call" | custom-call | flops 8455716864 | bytes 46399488 | tf_op jit(solution)/shard_map/feed_back/pallas_call | solution.py:547
  481.3 16.8 %weight_grads.7 = (f32[384,6144]{1,0:T(8,128)}, bf16[384,6144]{1,0:T(8,128)(2,1)S(1)}) custom-call(bf16[896,768]{1,0:T(8,128)(2,1)} %copy-done.32, bf16[896,768]{1,0:T(8,128)(2,1)} %get-tuple-element.395.refs_1_, bf16[896,3072]{1,0:T(8,128)(2,1)} %get-tuple-element.396.refs_2_, bf16[896,3072]{1,0:T(8,128)(2,1)} %get-tuple-element.397.refs_3_), custom_call_target="tpu_custom_call" | custom-call | flops 8455716864 | bytes 29884416 | tf_op jit(solution)/shard_map/weight_grads/pallas_call | solution.py:705
  498.1 10.8 %collective-permute-done.42 = f32[48,6144]{1,0:T(8,128)S(1)} collective-permute-done((f32[48,6144]{1,0:T(8,128)S(1)}, f32[48,6144]{1,0:T(8,128)S(1)}, u32[]{:S(2)}, u32[]{:S(2)}) %collective-permute-start.42) | collective-permute-done | bytes 1179680 | tf_op jit(solution)/shard_map/ppermute | solution.py:769
  515.6 10.6 %attend_back.6 = (bf16[2,448,768]{2,1,0:T(8,128)(2,1)}, bf16[2,448,768]{2,1,0:T(8,128)(2,1)}, bf16[2,448,768]{2,1,0:T(8,128)(2,1)}) custom-call(bf16[2,448,2304]{2,1,0:T(8,128)(2,1)S(1)} %bitcast.44, bf16[2,448,2304]{2,1,0:T(8,128)(2,1)S(1)} %bitcast.45, bf16[2,448,2304]{2,1,0:T(8,128)(2,1)S(1)} %bitcast.46, bf16[2,448,768]{2,1,0:T(8,128)(2,1)S(1)} %bitcast.59), custom_call_target="tpu_custom_call" | custom-call | flops 4932501504 | bytes 4816896 | tf_op jit(solution)/shard_map/attend_back/pallas_call | solution.py:158
  533.5 10.2 %attend_back.7 = (bf16[2,448,768]{2,1,0:T(8,128)(2,1)}, bf16[2,448,768]{2,1,0:T(8,128)(2,1)}, bf16[2,448,768]{2,1,0:T(8,128)(2,1)}) custom-call(bf16[2,448,2304]{2,1,0:T(8,128)(2,1)S(1)} %bitcast.47, bf16[2,448,2304]{2,1,0:T(8,128)(2,1)S(1)} %bitcast.48, ...), custom_call_target="tpu_custom_call", output_to_operand_aliasing={{0}: (4, {}), {1}: (5, {}), {2}: (6, {})} | custom-call | flops 4932501504 | bytes 4816896 | tf_op jit(solution)/shard_map/attend_back/pallas_call | solution.py:158
  543.7 11.4 %weight_grads.8 = (f32[384,3072]{1,0:T(8,128)}, bf16[384,3072]{1,0:T(8,128)(2,1)S(1)}) custom-call(bf16[896,768]{1,0:T(8,128)(2,1)} %get-tuple-element.414.refs_0_, bf16[896,768]{1,0:T(8,128)(2,1)} %get-tuple-element.415.refs_1_, bf16[896,768]{1,0:T(8,128)(2,1)} %bitcast.72, bf16[896,768]{1,0:T(8,128)(2,1)} %bitcast.74, bf16[896,768]{1,0:T(8,128)(2,1)} %bitcast.76, ...), custom_call_target="tpu_custom_call" | custom-call | flops 4227858432 | bytes 14942208 | tf_op jit(solution)/shard_map/weight_grads/pallas_call | solution.py:705
  565.0 11.1 %project_back.3 = (f32[896,768]{1,0:T(8,128)S(1)}, f32[1,768]{1,0:T(1,128)S(1)}, bf16[896,768]{1,0:T(8,128)(2,1)}, f32[1,768]{1,0:T(1,128)S(1)}) custom-call(bf16[896,768]{1,0:T(8,128)(2,1)} %bitcast.73, bf16[896,768]{1,0:T(8,128)(2,1)} %bitcast.75, bf16[896,768]{1,0:T(8,128)(2,1)} %bitcast.77, bf16[192,4352]{1,0:T(8,128)(2,1)} %copy-done.40, ...), custom_call_target="tpu_custom_call" | custom-call | flops 3170893824 | bytes 15138816 | tf_op jit(solution)/shard_map/project_back/pallas_call | solution.py:645
  587.2 18.9 %collective-permute-done.56 = bf16[192,1280]{1,0:T(8,128)(2,1)S(1)} collective-permute-done((bf16[192,1280]{1,0:T(8,128)(2,1)S(1)}, bf16[192,1280]{1,0:T(8,128)(2,1)S(1)}, u32[]{:S(2)}, u32[]{:S(2)}) %collective-permute-start.56) | collective-permute-done | bytes 491552 | tf_op jit(solution)/shard_map/ppermute | solution.py:769
  621.1 8.0 %collective-permute-done.59 = f32[48,1280]{1,0:T(8,128)S(1)} collective-permute-done((f32[48,1280]{1,0:T(8,128)S(1)}, f32[48,1280]{1,0:T(8,128)S(1)}, u32[]{:S(2)}, u32[]{:S(2)}) %collective-permute-start.59) | collective-permute-done | bytes 245792 | tf_op jit(solution)/shard_map/ppermute | solution.py:769
  631.6 19.6 %collective-permute-done.60 = f32[24,1280]{1,0:T(8,128)S(1)} collective-permute-done((f32[24,1280]{1,0:T(8,128)S(1)}, f32[24,1280]{1,0:T(8,128)S(1)}, u32[]{:S(2)}, u32[]{:S(2)}) %collective-permute-start.60) | collective-permute-done | bytes 122912 | tf_op jit(solution)/shard_map/ppermute | solution.py:769
  656.2 9.4 %collective-permute-done.63 = f32[24,3072]{1,0:T(8,128)S(1)} collective-permute-done((f32[24,3072]{1,0:T(8,128)S(1)}, f32[24,3072]{1,0:T(8,128)S(1)}, u32[]{:S(2)}, u32[]{:S(2)}) %collective-permute-start.63) | collective-permute-done | bytes 294944 | tf_op jit(solution)/shard_map/ppermute | solution.py:769
  (390 shorter events, 274.1 us)
Async XLA Ops:
  51.4 33.7 %collective-permute-start.9 = (bf16[192,4352]{1,0:T(8,128)(2,1)S(1)}, bf16[192,4352]{1,0:T(8,128)(2,1)S(1)}, u32[]{:S(2)}, u32[]{:S(2)}) collective-permute-start(bf16[192,4352]{1,0:T(8,128)(2,1)S(1)} %pad_maximum_fusion.2.refs_2_.refs_6_.refs_10_.own_ref), channel_id=1, source_target_pairs={{0,2},{1,3},{2,0},{3,1},{4,6},{5,7},{6,4},{7,5},{8,10},{9,11},{10,... | collective-permute-start | bytes 5013512 | tf_op jit(solution)/shard_map/ppermute | solution.py:769
  51.5 33.6 %collective-permute-start.8 = (bf16[192,4352]{1,0:T(8,128)(2,1)S(1)}, bf16[192,4352]{1,0:T(8,128)(2,1)S(1)}, u32[]{:S(2)}, u32[]{:S(2)}) collective-permute-start(bf16[192,4352]{1,0:T(8,128)(2,1)S(1)} %pad_maximum_fusion.2.refs_2_.refs_6_.refs_10_.own_ref), channel_id=1, source_target_pairs={{0,1},{1,0},{2,6},{3,7},{4,5},{5,4},{6,2},{7,3},{8,9},{9,8},{10,14... | collective-permute-start | bytes 5013512 | tf_op jit(solution)/shard_map/ppermute | solution.py:769
  63.4 36.5 %collective-permute-start.7 = (bf16[24,4352]{1,0:T(8,128)(2,1)S(1)}, bf16[24,4352]{1,0:T(8,128)(2,1)S(1)}, u32[]{:S(2)}, u32[]{:S(2)}) collective-permute-start(bf16[24,4352]{1,0:T(8,128)(2,1)S(1)} %pad_maximum_fusion.16), channel_id=1, source_target_pairs={{0,16},{1,17},{2,18},{3,19},{4,20},{5,21},{6,22},{7,23},{8,24},{9,... | collective-permute-start | bytes 626696 | tf_op jit(solution)/shard_map/ppermute | solution.py:769
  63.4 36.5 %collective-permute-start.6 = (bf16[48,9216]{1,0:T(8,128)(2,1)S(1)}, bf16[48,9216]{1,0:T(8,128)(2,1)S(1)}, u32[]{:S(2)}, u32[]{:S(2)}) collective-permute-start(bf16[48,9216]{1,0:T(8,128)(2,1)S(1)} %pad_maximum_fusion.5), channel_id=1, source_target_pairs={{0,8},{1,9},{2,10},{3,11},{4,12},{5,13},{6,14},{7,15},{8,0},{9,1},... | collective-permute-start | bytes 2654216 | tf_op jit(solution)/shard_map/ppermute | solution.py:769
  86.0 41.0 %collective-permute-start.16 = (bf16[192,6144]{1,0:T(8,128)(2,1)S(1)}, bf16[192,6144]{1,0:T(8,128)(2,1)S(1)}, u32[]{:S(2)}, u32[]{:S(2)}) collective-permute-start(bf16[192,6144]{1,0:T(8,128)(2,1)S(1)} %constant_dynamic-update-slice_fusion.uown_ref.down_ref), channel_id=1, source_target_pairs={{0,1},{1,0},{2,6},{3,7},{4,5},{5,4},{6,2},{7,3},{8,9},{9,8},{10,14... | collective-permute-start | bytes 7077896 | tf_op jit(solution)/shard_map/ppermute | solution.py:769
  87.6 39.5 %collective-permute-start.12 = (bf16[192,6144]{1,0:T(8,128)(2,1)S(1)}, bf16[192,6144]{1,0:T(8,128)(2,1)S(1)}, u32[]{:S(2)}, u32[]{:S(2)}) collective-permute-start(bf16[192,6144]{1,0:T(8,128)(2,1)S(1)} %constant_dynamic-update-slice_fusion.uown_ref.down_ref), channel_id=1, source_target_pairs={{0,2},{1,3},{2,0},{3,1},{4,6},{5,7},{6,4},{7,5},{8,10},{9,11},{10,... | collective-permute-start | bytes 7077896 | tf_op jit(solution)/shard_map/ppermute | solution.py:769
  99.9 37.1 %collective-permute-start.14 = (bf16[24,16128]{1,0:T(8,128)(2,1)S(1)}, bf16[24,16128]{1,0:T(8,128)(2,1)S(1)}, u32[]{:S(2)}, u32[]{:S(2)}) collective-permute-start(bf16[24,16128]{1,0:T(8,128)(2,1)S(1)} %pad_maximum_fusion.8), channel_id=1, source_target_pairs={{0,16},{1,17},{2,18},{3,19},{4,20},{5,21},{6,22},{7,23},{8,24},{9,... | collective-permute-start | bytes 2322440 | tf_op jit(solution)/shard_map/ppermute | solution.py:769
  101.2 35.8 %collective-permute-start.15 = (bf16[96,9216]{1,0:T(8,128)(2,1)S(1)}, bf16[96,9216]{1,0:T(8,128)(2,1)S(1)}, u32[]{:S(2)}, u32[]{:S(2)}) collective-permute-start(bf16[96,9216]{1,0:T(8,128)(2,1)S(1)} %pad_maximum_fusion.1), channel_id=1, source_target_pairs={{0,4},{1,5},{2,3},{3,2},{4,0},{5,1},{6,7},{7,6},{8,12},{9,13},{10,... | collective-permute-start | bytes 5308424 | tf_op jit(solution)/shard_map/ppermute | solution.py:769
  137.2 50.5 %collective-permute-start.20 = (bf16[192,9216]{1,0:T(8,128)(2,1)S(1)}, bf16[192,9216]{1,0:T(8,128)(2,1)S(1)}, u32[]{:S(2)}, u32[]{:S(2)}) collective-permute-start(bf16[192,9216]{1,0:T(8,128)(2,1)S(1)} %constant_dynamic-update-slice_fusion.4.own_ref.uown_ref.down_ref), channel_id=1, source_target_pairs={{0,1},{1,0},{2,6},{3,7},{4,5},{5,4},{6,2},{7,3},{8,9},{9,8},{10,14... | collective-permute-start | bytes 10616840 | tf_op jit(solution)/shard_map/ppermute | solution.py:769
  138.7 48.9 %collective-permute-start.17 = (bf16[192,9216]{1,0:T(8,128)(2,1)S(1)}, bf16[192,9216]{1,0:T(8,128)(2,1)S(1)}, u32[]{:S(2)}, u32[]{:S(2)}) collective-permute-start(bf16[192,9216]{1,0:T(8,128)(2,1)S(1)} %constant_dynamic-update-slice_fusion.4.own_ref.uown_ref.down_ref), channel_id=1, source_target_pairs={{0,2},{1,3},{2,0},{3,1},{4,6},{5,7},{6,4},{7,5},{8,10},{9,11},{10,... | collective-permute-start | bytes 10616840 | tf_op jit(solution)/shard_map/ppermute | solution.py:769
  140.5 35.1 %collective-permute-start.18 = (bf16[48,16128]{1,0:T(8,128)(2,1)S(1)}, bf16[48,16128]{1,0:T(8,128)(2,1)S(1)}, u32[]{:S(2)}, u32[]{:S(2)}) collective-permute-start(bf16[48,16128]{1,0:T(8,128)(2,1)S(1)} %pad_maximum_fusion.3), channel_id=1, source_target_pairs={{0,8},{1,9},{2,10},{3,11},{4,12},{5,13},{6,14},{7,15},{8,0},{9,1},... | collective-permute-start | bytes 4644872 | tf_op jit(solution)/shard_map/ppermute | solution.py:769
  187.8 45.6 %collective-permute-start.24 = (bf16[192,4352]{1,0:T(8,128)(2,1)S(1)}, bf16[192,4352]{1,0:T(8,128)(2,1)}, u32[]{:S(2)}, u32[]{:S(2)}) collective-permute-start(bf16[192,4352]{1,0:T(8,128)(2,1)S(1)} %constant_dynamic-update-slice_fusion.11.refs_2_.refs_6_.refs_10_.own_ref.refs_3_.refs_7_.refs_11_), channel_id=1, source_target_pairs={{0,1},{1,0},{2,6},{3,7},{4,5},{5,4},{6,2},{7,3},{8,9},{9,8},{10,14... | collective-permute-start | bytes 5013512 | tf_op jit(solution)/shard_map/ppermute | solution.py:769
  189.4 44.0 %collective-permute-start.22 = (bf16[192,4352]{1,0:T(8,128)(2,1)S(1)}, bf16[192,4352]{1,0:T(8,128)(2,1)S(1)}, u32[]{:S(2)}, u32[]{:S(2)}) collective-permute-start(bf16[192,4352]{1,0:T(8,128)(2,1)S(1)} %constant_dynamic-update-slice_fusion.11.refs_2_.refs_6_.refs_10_.own_ref.refs_3_.refs_7_.refs_11_), channel_id=1, source_target_pairs={{0,2},{1,3},{2,0},{3,1},{4,6},{5,7},{6,4},{7,5},{8,10},{9,11},{10,... | collective-permute-start | bytes 5013512 | tf_op jit(solution)/shard_map/ppermute | solution.py:769
  192.5 40.8 %collective-permute-start.23 = (bf16[96,6144]{1,0:T(8,128)(2,1)S(1)}, bf16[96,6144]{1,0:T(8,128)(2,1)S(1)}, u32[]{:S(2)}, u32[]{:S(2)}) collective-permute-start(bf16[96,6144]{1,0:T(8,128)(2,1)S(1)} %get-tuple-element.504), channel_id=1, source_target_pairs={{0,4},{1,5},{2,3},{3,2},{4,0},{5,1},{6,7},{7,6},{8,12},{9,13},{10,... | collective-permute-start | bytes 3538952 | tf_op jit(solution)/shard_map/ppermute | solution.py:769
  236.2 37.1 %collective-permute-start.28 = (bf16[192,6144]{1,0:T(8,128)(2,1)}, bf16[192,6144]{1,0:T(8,128)(2,1)}, u32[]{:S(2)}, u32[]{:S(2)}) collective-permute-start(bf16[192,6144]{1,0:T(8,128)(2,1)} %pad_maximum_fusion.uown_ref.down_ref), channel_id=1, source_target_pairs={{0,1},{1,0},{2,6},{3,7},{4,5},{5,4},{6,2},{7,3},{8,9},{9,8},{10,14... | collective-permute-start | bytes 7077896 | tf_op jit(solution)/shard_map/ppermute | solution.py:769
  237.7 35.6 %collective-permute-start.26 = (bf16[192,6144]{1,0:T(8,128)(2,1)}, bf16[192,6144]{1,0:T(8,128)(2,1)}, u32[]{:S(2)}, u32[]{:S(2)}) collective-permute-start(bf16[192,6144]{1,0:T(8,128)(2,1)} %pad_maximum_fusion.uown_ref.down_ref), channel_id=1, source_target_pairs={{0,2},{1,3},{2,0},{3,1},{4,6},{5,7},{6,4},{7,5},{8,10},{9,11},{10,... | collective-permute-start | bytes 7077896 | tf_op jit(solution)/shard_map/ppermute | solution.py:769
  238.0 32.8 %collective-permute-start.27 = (bf16[96,3840]{1,0:T(8,128)(2,1)}, bf16[96,3840]{1,0:T(8,128)(2,1)S(1)}, u32[]{:S(2)}, u32[]{:S(2)}) collective-permute-start(bf16[96,3840]{1,0:T(8,128)(2,1)} %slice.419), channel_id=1, source_target_pairs={{0,4},{1,5},{2,3},{3,2},{4,0},{5,1},{6,7},{7,6},{8,12},{9,13},{10,... | collective-permute-start | bytes 2211848 | tf_op jit(solution)/shard_map/ppermute | solution.py:769
  273.4 32.1 %collective-permute-start.32 = (bf16[192,3840]{1,0:T(8,128)(2,1)S(1)}, bf16[192,3840]{1,0:T(8,128)(2,1)S(1)}, u32[]{:S(2)}, u32[]{:S(2)}) collective-permute-start(bf16[192,3840]{1,0:T(8,128)(2,1)S(1)} %constant_dynamic-update-slice_fusion.15.own_ref.refs_3_.refs_7_.refs_11_), channel_id=1, source_target_pairs={{0,1},{1,0},{2,6},{3,7},{4,5},{5,4},{6,2},{7,3},{8,9},{9,8},{10,14... | collective-permute-start | bytes 4423688 | tf_op jit(solution)/shard_map/ppermute | solution.py:769
  275.0 30.5 %collective-permute-start.30 = (bf16[192,3840]{1,0:T(8,128)(2,1)S(1)}, bf16[192,3840]{1,0:T(8,128)(2,1)S(1)}, u32[]{:S(2)}, u32[]{:S(2)}) collective-permute-start(bf16[192,3840]{1,0:T(8,128)(2,1)S(1)} %constant_dynamic-update-slice_fusion.15.own_ref.refs_3_.refs_7_.refs_11_), channel_id=1, source_target_pairs={{0,2},{1,3},{2,0},{3,1},{4,6},{5,7},{6,4},{7,5},{8,10},{9,11},{10,... | collective-permute-start | bytes 4423688 | tf_op jit(solution)/shard_map/ppermute | solution.py:769
  275.1 28.9 %collective-permute-start.31 = (bf16[96,6144]{1,0:T(8,128)(2,1)S(1)}, bf16[96,6144]{1,0:T(8,128)(2,1)S(1)}, u32[]{:S(2)}, u32[]{:S(2)}) collective-permute-start(bf16[96,6144]{1,0:T(8,128)(2,1)S(1)} %copy-done.54), channel_id=1, source_target_pairs={{0,4},{1,5},{2,3},{3,2},{4,0},{5,1},{6,7},{7,6},{8,12},{9,13},{10,... | collective-permute-start | bytes 3538952 | tf_op jit(solution)/shard_map/ppermute | solution.py:769
  305.6 28.9 %collective-permute-start.35 = (bf16[192,6144]{1,0:T(8,128)(2,1)S(1)}, bf16[192,6144]{1,0:T(8,128)(2,1)S(1)}, u32[]{:S(2)}, u32[]{:S(2)}) collective-permute-start(bf16[192,6144]{1,0:T(8,128)(2,1)S(1)} %constant_dynamic-update-slice_fusion.17.uown_ref.down_ref), channel_id=1, source_target_pairs={{0,1},{1,0},{2,6},{3,7},{4,5},{5,4},{6,2},{7,3},{8,9},{9,8},{10,14... | collective-permute-start | bytes 7077896 | tf_op jit(solution)/shard_map/ppermute | solution.py:769
  307.2 27.4 %collective-permute-start.34 = (bf16[192,6144]{1,0:T(8,128)(2,1)S(1)}, bf16[192,6144]{1,0:T(8,128)(2,1)S(1)}, u32[]{:S(2)}, u32[]{:S(2)}) collective-permute-start(bf16[192,6144]{1,0:T(8,128)(2,1)S(1)} %constant_dynamic-update-slice_fusion.17.uown_ref.down_ref), channel_id=1, source_target_pairs={{0,2},{1,3},{2,0},{3,1},{4,6},{5,7},{6,4},{7,5},{8,10},{9,11},{10,... | collective-permute-start | bytes 7077896 | tf_op jit(solution)/shard_map/ppermute | solution.py:769
  423.3 33.2 %collective-permute-start.39 = (bf16[192,6144]{1,0:T(8,128)(2,1)S(1)}, bf16[192,6144]{1,0:T(8,128)(2,1)S(1)}, u32[]{:S(2)}, u32[]{:S(2)}) collective-permute-start(bf16[192,6144]{1,0:T(8,128)(2,1)S(1)} %get-tuple-element.486), channel_id=1, source_target_pairs={{0,1},{1,0},{2,6},{3,7},{4,5},{5,4},{6,2},{7,3},{8,9},{9,8},{10,14... | collective-permute-start | bytes 7077896 | tf_op jit(solution)/shard_map/ppermute | solution.py:769
  480.3 28.7 %collective-permute-start.43 = (bf16[192,3840]{1,0:T(8,128)(2,1)S(1)}, bf16[192,3840]{1,0:T(8,128)(2,1)S(1)}, u32[]{:S(2)}, u32[]{:S(2)}) collective-permute-start(bf16[192,3840]{1,0:T(8,128)(2,1)S(1)} %get-tuple-element.487), channel_id=1, source_target_pairs={{0,1},{1,0},{2,6},{3,7},{4,5},{5,4},{6,2},{7,3},{8,9},{9,8},{10,14... | collective-permute-start | bytes 4423688 | tf_op jit(solution)/shard_map/ppermute | solution.py:769
  481.2 27.7 %collective-permute-start.42 = (f32[48,6144]{1,0:T(8,128)S(1)}, f32[48,6144]{1,0:T(8,128)S(1)}, u32[]{:S(2)}, u32[]{:S(2)}) collective-permute-start(f32[48,6144]{1,0:T(8,128)S(1)} %get-tuple-element.502), channel_id=1, source_target_pairs={{0,8},{1,9},{2,10},{3,11},{4,12},{5,13},{6,14},{7,15},{8,0},{9,1},... | collective-permute-start | bytes 3538952 | tf_op jit(solution)/shard_map/ppermute | solution.py:769
  530.2 31.9 %collective-permute-start.48 = (bf16[192,6144]{1,0:T(8,128)(2,1)}, bf16[192,6144]{1,0:T(8,128)(2,1)S(1)}, u32[]{:S(2)}, u32[]{:S(2)}) collective-permute-start(bf16[192,6144]{1,0:T(8,128)(2,1)} %get-tuple-element.484), channel_id=1, source_target_pairs={{0,1},{1,0},{2,6},{3,7},{4,5},{5,4},{6,2},{7,3},{8,9},{9,8},{10,14... | collective-permute-start | bytes 7077896 | tf_op jit(solution)/shard_map/ppermute | solution.py:769
  531.3 28.1 %collective-permute-start.46 = (f32[24,6144]{1,0:T(8,128)S(1)}, f32[24,6144]{1,0:T(8,128)S(1)}, u32[]{:S(2)}, u32[]{:S(2)}) collective-permute-start(f32[24,6144]{1,0:T(8,128)S(1)} %slice_add_fusion.19), channel_id=1, source_target_pairs={{0,16},{1,17},{2,18},{3,19},{4,20},{5,21},{6,22},{7,23},{8,24},{9,... | collective-permute-start | bytes 1769480 | tf_op jit(solution)/shard_map/ppermute | solution.py:769
  531.7 30.4 %collective-permute-start.47 = (f32[48,3840]{1,0:T(8,128)S(1)}, f32[48,3840]{1,0:T(8,128)S(1)}, u32[]{:S(2)}, u32[]{:S(2)}) collective-permute-start(f32[48,3840]{1,0:T(8,128)S(1)} %get-tuple-element.505), channel_id=1, source_target_pairs={{0,8},{1,9},{2,10},{3,11},{4,12},{5,13},{6,14},{7,15},{8,0},{9,1},... | collective-permute-start | bytes 2211848 | tf_op jit(solution)/shard_map/ppermute | solution.py:769
  583.7 28.0 %collective-permute-start.54 = (f32[48,6144]{1,0:T(8,128)S(1)}, f32[48,6144]{1,0:T(8,128)S(1)}, u32[]{:S(2)}, u32[]{:S(2)}) collective-permute-start(f32[48,6144]{1,0:T(8,128)S(1)} %get-tuple-element.498), channel_id=1, source_target_pairs={{0,8},{1,9},{2,10},{3,11},{4,12},{5,13},{6,14},{7,15},{8,0},{9,1},... | collective-permute-start | bytes 3538952 | tf_op jit(solution)/shard_map/ppermute | solution.py:769
  584.5 27.1 %collective-permute-start.55 = (bf16[192,3072]{1,0:T(8,128)(2,1)S(1)}, bf16[192,3072]{1,0:T(8,128)(2,1)S(1)}, u32[]{:S(2)}, u32[]{:S(2)}) collective-permute-start(bf16[192,3072]{1,0:T(8,128)(2,1)S(1)} %get-tuple-element.490), channel_id=1, source_target_pairs={{0,1},{1,0},{2,6},{3,7},{4,5},{5,4},{6,2},{7,3},{8,9},{9,8},{10,14... | collective-permute-start | bytes 3538952 | tf_op jit(solution)/shard_map/ppermute | solution.py:769
  618.6 32.7 %collective-permute-start.61 = (f32[24,6144]{1,0:T(8,128)S(1)}, f32[24,6144]{1,0:T(8,128)S(1)}, u32[]{:S(2)}, u32[]{:S(2)}) collective-permute-start(f32[24,6144]{1,0:T(8,128)S(1)} %slice_add_fusion.17), channel_id=1, source_target_pairs={{0,16},{1,17},{2,18},{3,19},{4,20},{5,21},{6,22},{7,23},{8,24},{9,... | collective-permute-start | bytes 1769480 | tf_op jit(solution)/shard_map/ppermute | solution.py:769
  629.4 26.5 %collective-permute-start.62 = (f32[48,3072]{1,0:T(8,128)S(1)}, f32[48,3072]{1,0:T(8,128)S(1)}, u32[]{:S(2)}, u32[]{:S(2)}) collective-permute-start(f32[48,3072]{1,0:T(8,128)S(1)} %get-tuple-element.507), channel_id=1, source_target_pairs={{0,8},{1,9},{2,10},{3,11},{4,12},{5,13},{6,14},{7,15},{8,0},{9,1},... | collective-permute-start | bytes 1769480 | tf_op jit(solution)/shard_map/ppermute | solution.py:769
  (112 other events, 1659.9 us)

commit v10 on v8

--- a/solution.py
+++ b/solution.py
@@ -9,7 +9,7 @@
 LAYERS = 2
 TOPK = 2
 LANES = 128
-FF_TILE = 512
+FF_TILE = 1024
 SMALL_TILE = 256
 ROW_TILE = 64
 PAIRS = 2
@@ -411,7 +411,7 @@
         out_specs=out_specs,
         out_shape=outs,
         cost_estimate=cost(4 * rows * width * w_up.cols, 12 * rows * width + 16 * width * w_up.cols),
-        compiler_params=grant(30),
+        compiler_params=grant(42),
         name="feed_forward",
     )(normed, middle, *w_up.refs(), *w_down.refs())
 

time: 686 us -> 689 us (level)
  local copies, waits for them, and re-layouts: 19.6 us -> 27.9 us
    unnamed x161 -> x177, local copies, waits for them, and re-layouts: 14.6 us -> 18.2 us
  transfers between devices with their start and end apart: 69 -> 69, of which waited for: 34 -> 35; matrix products, arithmetic and copies ran while one was open for 2% -> 4% of each run, Pallas kernels for 42% -> 41%
where the time goes in v10:
time: 689 us; the launch traced here: 683 us
  Pallas kernels  344 us (50%)
  waiting for transfers between devices  217 us (31%)
  starting transfers between devices  60.7 us (9%)
  other arithmetic  29.9 us (4%)
  local copies, waits for them, and re-layouts  27.9 us (4%)
    ppermute x69, waiting for transfers between devices, swap(): return lax.ppermute(value, AXES, perm)  217 us
    pallas_call x5, Pallas kernels, weight_grads(): pl.pallas_call(kernel, grid=(total,), in_specs=specs, out_specs=[block, b...  63.3 us
    ppermute x69, starting transfers between devices, swap(): return lax.ppermute(value, AXES, perm)  60.7 us
    pallas_call x4, Pallas kernels, feed_forward(): pl.pallas_call(kernel, grid=(steps,), in_specs=[whole_block(normed.shape)...  57.1 us
    pallas_call x4, Pallas kernels, attend(): pl.pallas_call(attend_kernel, grid=(seqs, blocks), in_specs=specs, out_sp...  44.9 us
    pallas_call x4, Pallas kernels, attend_back(): pl.pallas_call(kernel, grid=(blocks,), in_specs=specs + [block] + [pl.Blo...  41.4 us
    pallas_call x2, Pallas kernels, feed_back(): pl.pallas_call(kernel, grid=(steps,), in_specs=[full, column, full, whole...  34.3 us
    pallas_call x4, Pallas kernels, norm_project(): pl.pallas_call(kernel, grid=(steps,), in_specs=[whole_block(states.shape)...  26.8 us
  transfers between devices with their start and end apart: 69, of which 35 were waited for; matrix products, arithmetic and copies ran while one was open for 4% of the time, Pallas kernels for 41%

profile of v10, /device:TPU:0, one launch (start us, length us, event | category | flops | bytes accessed | tf_op | source)
XLA Modules:
  0.0 683.5 jit_solution(6668800237434756358)
XLA Ops:
  10.9 7.4 %collective-permute-done = bf16[24,4352]{1,0:T(8,128)(2,1)S(1)} collective-permute-done((bf16[24,4352]{1,0:T(8,128)(2,1)S(1)}, bf16[24,4352]{1,0:T(8,128)(2,1)S(1)}, u32[]{:S(2)}, u32[]{:S(2)}) %collective-permute-start) | collective-permute-done | bytes 208928 | tf_op jit(solution)/shard_map/ppermute | solution.py:769
  22.6 11.3 %collective-permute-done.1 = bf16[24,6144]{1,0:T(8,128)(2,1)S(1)} collective-permute-done((bf16[24,6144]{1,0:T(8,128)(2,1)S(1)}, bf16[24,6144]{1,0:T(8,128)(2,1)S(1)}, u32[]{:S(2)}, u32[]{:S(2)}) %collective-permute-start.1) | collective-permute-done | bytes 294944 | tf_op jit(solution)/shard_map/ppermute | solution.py:769
  42.2 9.1 %collective-permute-done.5 = bf16[96,4352]{1,0:T(8,128)(2,1)S(1)} collective-permute-done((bf16[96,4352]{1,0:T(8,128)(2,1)S(1)}, bf16[96,4352]{1,0:T(8,128)(2,1)S(1)}, u32[]{:S(2)}, u32[]{:S(2)}) %collective-permute-start.5) | collective-permute-done | bytes 835616 | tf_op jit(solution)/shard_map/ppermute | solution.py:769
  67.6 17.5 %collective-permute-done.10 = bf16[96,6144]{1,0:T(8,128)(2,1)S(1)} collective-permute-done((bf16[96,6144]{1,0:T(8,128)(2,1)S(1)}, bf16[96,6144]{1,0:T(8,128)(2,1)S(1)}, u32[]{:S(2)}, u32[]{:S(2)}) %collective-permute-start.10) | collective-permute-done | bytes 1179680 | tf_op jit(solution)/shard_map/ppermute | solution.py:769
  104.9 11.2 %attend.4 = bf16[2,448,768]{2,1,0:T(8,128)(2,1)S(1)} custom-call(bf16[2,448,2304]{2,1,0:T(8,128)(2,1)S(1)} %bitcast.28, bf16[2,448,2304]{2,1,0:T(8,128)(2,1)S(1)} %bitcast.29, bf16[2,448,2304]{2,1,0:T(8,128)(2,1)S(1)} %bitcast.30), custom_call_target="tpu_custom_call" | custom-call | flops 4932501504 | bytes 5505024 | tf_op jit(solution)/shard_map/attend/pallas_call | solution.py:121
  127.1 10.0 %collective-permute-done.14 = bf16[24,16128]{1,0:T(8,128)(2,1)S(1)} collective-permute-done((bf16[24,16128]{1,0:T(8,128)(2,1)S(1)}, bf16[24,16128]{1,0:T(8,128)(2,1)S(1)}, u32[]{:S(2)}, u32[]{:S(2)}) %collective-permute-start.14) | collective-permute-done | bytes 774176 | tf_op jit(solution)/shard_map/ppermute | solution.py:769
  148.4 12.4 %feed_forward.4.h_ref.one_ref = f32[896,768]{1,0:T(8,128)S(1)} custom-call(bf16[896,768]{1,0:T(8,128)(2,1)S(1)} %get-tuple-element.284.b_ref, f32[896,768]{1,0:T(8,128)S(1)} %get-tuple-element.285.m_ref, bf16[192,6144]{1,0:T(8,128)(2,1)} %copy-done.73, bf16[192,6144]{1,0:T(8,128)(2,1)} %copy-done.75, bf16[192,6144]{1,0:T(8,128)(2,1)} %copy-done.76, ...), custom_call_target="tpu_custom_call" | custom-call | flops 8455716864 | bytes 46006272 | tf_op jit(solution)/shard_map/feed_forward/pallas_call | solution.py:405
  161.6 16.3 %collective-permute-done.18 = bf16[48,16128]{1,0:T(8,128)(2,1)S(1)} collective-permute-done((bf16[48,16128]{1,0:T(8,128)(2,1)}, bf16[48,16128]{1,0:T(8,128)(2,1)S(1)}, u32[]{:S(2)}, u32[]{:S(2)}) %collective-permute-start.18) | collective-permute-done | bytes 1548320 | tf_op jit(solution)/shard_map/ppermute | solution.py:769
  177.8 10.0 %collective-permute-done.20.own2_ref.uown2_ref.down2_ref = bf16[192,9216]{1,0:T(8,128)(2,1)S(1)} collective-permute-done((bf16[192,9216]{1,0:T(8,128)(2,1)S(1)}, bf16[192,9216]{1,0:T(8,128)(2,1)S(1)}, u32[]{:S(2)}, u32[]{:S(2)}) %collective-permute-start.20) | collective-permute-done | bytes 3538976 | tf_op jit(solution)/shard_map/ppermute | solution.py:769
  203.5 11.2 %attend.5 = bf16[2,448,768]{2,1,0:T(8,128)(2,1)S(1)} custom-call(bf16[2,448,2304]{2,1,0:T(8,128)(2,1)S(1)} %bitcast.31, bf16[2,448,2304]{2,1,0:T(8,128)(2,1)S(1)} %bitcast.32, bf16[2,448,2304]{2,1,0:T(8,128)(2,1)S(1)} %bitcast.33), custom_call_target="tpu_custom_call" | custom-call | flops 4932501504 | bytes 5505024 | tf_op jit(solution)/shard_map/attend/pallas_call | solution.py:121
  220.4 12.3 %feed_forward.5.two_ref = f32[896,768]{1,0:T(8,128)S(1)} custom-call(bf16[896,768]{1,0:T(8,128)(2,1)S(1)} %get-tuple-element.296.b_ref, f32[896,768]{1,0:T(8,128)S(1)} %get-tuple-element.297.m_ref, bf16[192,9216]{1,0:T(8,128)(2,1)} %copy-done.48, bf16[192,9216]{1,0:T(8,128)(2,1)} %copy-done.50, ...), custom_call_target="tpu_custom_call" | custom-call | flops 8455716864 | bytes 46006272 | tf_op jit(solution)/shard_map/feed_forward/pallas_call | solution.py:405
  255.7 11.2 %attend.6 = bf16[2,448,768]{2,1,0:T(8,128)(2,1)S(1)} custom-call(bf16[2,448,2304]{2,1,0:T(8,128)(2,1)S(1)} %bitcast.41, bf16[2,448,2304]{2,1,0:T(8,128)(2,1)S(1)} %bitcast.42, bf16[2,448,2304]{2,1,0:T(8,128)(2,1)S(1)} %bitcast.43), custom_call_target="tpu_custom_call" | custom-call | flops 4932501504 | bytes 5505024 | tf_op jit(solution)/shard_map/attend/pallas_call | solution.py:121
  281.8 16.1 %feed_forward.6 = (f32[896,768]{1,0:T(8,128)S(1)}, bf16[896,3072]{1,0:T(8,128)(2,1)}, f32[896,3072]{1,0:T(8,128)}) custom-call(bf16[896,768]{1,0:T(8,128)(2,1)S(1)} %get-tuple-element.316.b_ref.refs_0_, f32[896,768]{1,0:T(8,128)S(1)} %get-tuple-element.317.m_ref, bf16[192,6144]{1,0:T(8,128)(2,1)} %pad_maximum_fusion.uown_ref.down_ref, ...), custom_call_target="tpu_custom_call" | custom-call | flops 8455716864 | bytes 46006272 | tf_op jit(solution)/shard_map/feed_forward/pallas_call | solution.py:405
  297.9 9.4 %collective-permute-done.31 = bf16[96,6144]{1,0:T(8,128)(2,1)S(1)} collective-permute-done((bf16[96,6144]{1,0:T(8,128)(2,1)S(1)}, bf16[96,6144]{1,0:T(8,128)(2,1)S(1)}, u32[]{:S(2)}, u32[]{:S(2)}) %collective-permute-start.31) | collective-permute-done | bytes 1179680 | tf_op jit(solution)/shard_map/ppermute | solution.py:769
  319.6 11.2 %attend.7 = bf16[2,448,768]{2,1,0:T(8,128)(2,1)S(1)} custom-call(bf16[2,448,2304]{2,1,0:T(8,128)(2,1)S(1)} %bitcast.50, bf16[2,448,2304]{2,1,0:T(8,128)(2,1)S(1)} %bitcast.51, bf16[2,448,2304]{2,1,0:T(8,128)(2,1)S(1)} %bitcast.52), custom_call_target="tpu_custom_call" | custom-call | flops 4932501504 | bytes 5505024 | tf_op jit(solution)/shard_map/attend/pallas_call | solution.py:121
  344.2 16.2 %feed_forward.7 = (f32[896,768]{1,0:T(8,128)S(1)}, bf16[896,3072]{1,0:T(8,128)(2,1)}, f32[896,3072]{1,0:T(8,128)}) custom-call(bf16[896,768]{1,0:T(8,128)(2,1)S(1)} %get-tuple-element.331.b_ref.refs_0_, f32[896,768]{1,0:T(8,128)S(1)} %get-tuple-element.332.m_ref, bf16[192,6144]{1,0:T(8,128)(2,1)} %constant_dynamic-update-slice_fusion.17.uown_ref.down_ref, ...), custom_call_target="tpu_custom_call" | custom-call | flops 8455716864 | bytes 46006272 | tf_op jit(solution)/shard_map/feed_forward/pallas_call | solution.py:405
  365.6 7.8 %head_step.1 = (f32[896,768]{1,0:T(8,128)S(1)}, bf16[896,768]{1,0:T(8,128)(2,1)}, bf16[896,768]{1,0:T(8,128)(2,1)}, f32[1,768]{1,0:T(1,128)S(1)}, f32[1,768]{1,0:T(1,128)S(1)}) custom-call(f32[896,768]{1,0:T(8,128)S(1)} %copy-done.45, f32[8,768]{1,0:T(8,128)S(1)} %get-tuple-element.336.table_ref.refs_17_, ...), custom_call_target="tpu_custom_call" | custom-call | flops 4227858432 | bytes 11010048 | tf_op jit(solution)/shard_map/head_step/pallas_call | solution.py:486
  373.4 17.2 %feed_back.2 = (bf16[896,3072]{1,0:T(8,128)(2,1)}, bf16[896,768]{1,0:T(8,128)(2,1)}, f32[896,768]{1,0:T(8,128)S(1)}, bf16[896,768]{1,0:T(8,128)(2,1)S(1)}, f32[1,768]{1,0:T(1,128)S(1)}) custom-call(f32[896,768]{1,0:T(8,128)S(1)} %get-tuple-element.342.flow_ref, f32[896,3072]{1,0:T(8,128)} %get-tuple-element.343.slope_ref, f32[896,768]{1,0:T(8,128)S(1)} %copy-done.13, ...), custom_call_target="tpu_custom_call" | custom-call | flops 8455716864 | bytes 46399488 | tf_op jit(solution)/shard_map/feed_back/pallas_call | solution.py:547
  390.6 16.9 %weight_grads.5 = (f32[384,6144]{1,0:T(8,128)}, bf16[384,6144]{1,0:T(8,128)(2,1)S(1)}) custom-call(bf16[896,768]{1,0:T(8,128)(2,1)} %copy-done.42, bf16[896,768]{1,0:T(8,128)(2,1)} %get-tuple-element.348.refs_1_, bf16[896,3072]{1,0:T(8,128)(2,1)} %get-tuple-element.349.refs_2_, bf16[896,3072]{1,0:T(8,128)(2,1)} %get-tuple-element.350.refs_3_), custom_call_target="tpu_custom_call" | custom-call | flops 8455716864 | bytes 29884416 | tf_op jit(solution)/shard_map/weight_grads/pallas_call | solution.py:705
  412.1 10.5 %attend_back.4 = (bf16[2,448,768]{2,1,0:T(8,128)(2,1)}, bf16[2,448,768]{2,1,0:T(8,128)(2,1)}, bf16[2,448,768]{2,1,0:T(8,128)(2,1)}) custom-call(bf16[2,448,2304]{2,1,0:T(8,128)(2,1)S(1)} %bitcast.53, bf16[2,448,2304]{2,1,0:T(8,128)(2,1)S(1)} %bitcast.54, bf16[2,448,2304]{2,1,0:T(8,128)(2,1)S(1)} %bitcast.55, bf16[2,448,768]{2,1,0:T(8,128)(2,1)S(1)} %bitcast.61), custom_call_target="tpu_custom_call" | custom-call | flops 4932501504 | bytes 4816896 | tf_op jit(solution)/shard_map/attend_back/pallas_call | solution.py:158
  429.3 10.2 %attend_back.5 = (bf16[2,448,768]{2,1,0:T(8,128)(2,1)}, bf16[2,448,768]{2,1,0:T(8,128)(2,1)}, bf16[2,448,768]{2,1,0:T(8,128)(2,1)}) custom-call(bf16[2,448,2304]{2,1,0:T(8,128)(2,1)S(1)} %bitcast.56, bf16[2,448,2304]{2,1,0:T(8,128)(2,1)S(1)} %bitcast.57, ...), custom_call_target="tpu_custom_call", output_to_operand_aliasing={{0}: (4, {}), {1}: (5, {}), {2}: (6, {})} | custom-call | flops 4932501504 | bytes 4816896 | tf_op jit(solution)/shard_map/attend_back/pallas_call | solution.py:158
  446.5 14.3 %weight_grads.6 = (f32[384,3840]{1,0:T(8,128)}, bf16[384,3840]{1,0:T(8,128)(2,1)S(1)}) custom-call(bf16[896,768]{1,0:T(8,128)(2,1)} %get-tuple-element.364.refs_0_, bf16[896,768]{1,0:T(8,128)(2,1)} %get-tuple-element.365.refs_1_, bf16[896,768]{1,0:T(8,128)(2,1)} %get-tuple-element.366.refs_2_, bf16[896,768]{1,0:T(8,128)(2,1)} %bitcast.75, ...), custom_call_target="tpu_custom_call" | custom-call | flops 5284823040 | bytes 18677760 | tf_op jit(solution)/shard_map/weight_grads/pallas_call | solution.py:705
  465.7 17.1 %feed_back.3 = (bf16[896,3072]{1,0:T(8,128)(2,1)}, bf16[896,768]{1,0:T(8,128)(2,1)}, f32[896,768]{1,0:T(8,128)S(1)}, bf16[896,768]{1,0:T(8,128)(2,1)S(1)}, f32[1,768]{1,0:T(1,128)S(1)}) custom-call(f32[896,768]{1,0:T(8,128)S(1)} %get-tuple-element.387.flow_ref, f32[896,3072]{1,0:T(8,128)} %get-tuple-element.388.slope_ref, f32[896,768]{1,0:T(8,128)S(1)} %copy-done.9, ...), custom_call_target="tpu_custom_call" | custom-call | flops 8455716864 | bytes 46399488 | tf_op jit(solution)/shard_map/feed_back/pallas_call | solution.py:547
  488.0 16.8 %weight_grads.7 = (f32[384,6144]{1,0:T(8,128)}, bf16[384,6144]{1,0:T(8,128)(2,1)S(1)}) custom-call(bf16[896,768]{1,0:T(8,128)(2,1)} %copy-done.36, bf16[896,768]{1,0:T(8,128)(2,1)} %get-tuple-element.395.refs_1_, bf16[896,3072]{1,0:T(8,128)(2,1)} %get-tuple-element.396.refs_2_, bf16[896,3072]{1,0:T(8,128)(2,1)} %get-tuple-element.397.refs_3_), custom_call_target="tpu_custom_call" | custom-call | flops 8455716864 | bytes 29884416 | tf_op jit(solution)/shard_map/weight_grads/pallas_call | solution.py:705
  511.5 10.2 %attend_back.6 = (bf16[2,448,768]{2,1,0:T(8,128)(2,1)}, bf16[2,448,768]{2,1,0:T(8,128)(2,1)}, bf16[2,448,768]{2,1,0:T(8,128)(2,1)}) custom-call(bf16[2,448,2304]{2,1,0:T(8,128)(2,1)S(1)} %bitcast.44, bf16[2,448,2304]{2,1,0:T(8,128)(2,1)S(1)} %bitcast.45, bf16[2,448,2304]{2,1,0:T(8,128)(2,1)S(1)} %bitcast.46, bf16[2,448,768]{2,1,0:T(8,128)(2,1)S(1)} %bitcast.59), custom_call_target="tpu_custom_call" | custom-call | flops 4932501504 | bytes 4816896 | tf_op jit(solution)/shard_map/attend_back/pallas_call | solution.py:158
  531.4 10.5 %attend_back.7 = (bf16[2,448,768]{2,1,0:T(8,128)(2,1)}, bf16[2,448,768]{2,1,0:T(8,128)(2,1)}, bf16[2,448,768]{2,1,0:T(8,128)(2,1)}) custom-call(bf16[2,448,2304]{2,1,0:T(8,128)(2,1)S(1)} %bitcast.47, bf16[2,448,2304]{2,1,0:T(8,128)(2,1)S(1)} %bitcast.48, ...), custom_call_target="tpu_custom_call", output_to_operand_aliasing={{0}: (4, {}), {1}: (5, {}), {2}: (6, {})} | custom-call | flops 4932501504 | bytes 4816896 | tf_op jit(solution)/shard_map/attend_back/pallas_call | solution.py:158
  541.8 11.1 %weight_grads.8 = (f32[384,3072]{1,0:T(8,128)}, bf16[384,3072]{1,0:T(8,128)(2,1)S(1)}) custom-call(bf16[896,768]{1,0:T(8,128)(2,1)} %get-tuple-element.414.refs_0_, bf16[896,768]{1,0:T(8,128)(2,1)} %get-tuple-element.415.refs_1_, bf16[896,768]{1,0:T(8,128)(2,1)} %bitcast.68, bf16[896,768]{1,0:T(8,128)(2,1)} %bitcast.70, bf16[896,768]{1,0:T(8,128)(2,1)} %bitcast.72, ...), custom_call_target="tpu_custom_call" | custom-call | flops 4227858432 | bytes 14942208 | tf_op jit(solution)/shard_map/weight_grads/pallas_call | solution.py:705
  564.8 11.2 %project_back.3 = (f32[896,768]{1,0:T(8,128)S(1)}, f32[1,768]{1,0:T(1,128)S(1)}, bf16[896,768]{1,0:T(8,128)(2,1)}, f32[1,768]{1,0:T(1,128)S(1)}) custom-call(bf16[896,768]{1,0:T(8,128)(2,1)} %bitcast.69, bf16[896,768]{1,0:T(8,128)(2,1)} %bitcast.71, bf16[896,768]{1,0:T(8,128)(2,1)} %bitcast.73, bf16[192,4352]{1,0:T(8,128)(2,1)} %copy-done.46, ...), custom_call_target="tpu_custom_call" | custom-call | flops 3170893824 | bytes 15138816 | tf_op jit(solution)/shard_map/project_back/pallas_call | solution.py:645
  586.1 11.3 %collective-permute-done.54 = bf16[48,6144]{1,0:T(8,128)(2,1)S(1)} collective-permute-done((bf16[48,6144]{1,0:T(8,128)(2,1)S(1)}, bf16[48,6144]{1,0:T(8,128)(2,1)S(1)}, u32[]{:S(2)}, u32[]{:S(2)}) %collective-permute-start.54) | collective-permute-done | bytes 589856 | tf_op jit(solution)/shard_map/ppermute | solution.py:769
  597.4 7.5 %collective-permute-done.56 = bf16[192,1280]{1,0:T(8,128)(2,1)S(1)} collective-permute-done((bf16[192,1280]{1,0:T(8,128)(2,1)S(1)}, bf16[192,1280]{1,0:T(8,128)(2,1)S(1)}, u32[]{:S(2)}, u32[]{:S(2)}) %collective-permute-start.56) | collective-permute-done | bytes 491552 | tf_op jit(solution)/shard_map/ppermute | solution.py:769
  614.1 7.4 %collective-permute-done.59 = f32[48,1280]{1,0:T(8,128)S(1)} collective-permute-done((f32[48,1280]{1,0:T(8,128)S(1)}, f32[48,1280]{1,0:T(8,128)S(1)}, u32[]{:S(2)}, u32[]{:S(2)}) %collective-permute-start.59) | collective-permute-done | bytes 245792 | tf_op jit(solution)/shard_map/ppermute | solution.py:769
  625.1 26.2 %collective-permute-done.60 = f32[24,1280]{1,0:T(8,128)S(1)} collective-permute-done((f32[24,1280]{1,0:T(8,128)S(1)}, f32[24,1280]{1,0:T(8,128)S(1)}, u32[]{:S(2)}, u32[]{:S(2)}) %collective-permute-start.60) | collective-permute-done | bytes 122912 | tf_op jit(solution)/shard_map/ppermute | solution.py:769
  (402 shorter events, 280.2 us)
Async XLA Ops:
  40.3 23.0 %collective-permute-start.3 = (bf16[48,6144]{1,0:T(8,128)(2,1)S(1)}, bf16[48,6144]{1,0:T(8,128)(2,1)S(1)}, u32[]{:S(2)}, u32[]{:S(2)}) collective-permute-start(bf16[48,6144]{1,0:T(8,128)(2,1)S(1)} %pad_maximum_fusion.9), channel_id=1, source_target_pairs={{0,8},{1,9},{2,10},{3,11},{4,12},{5,13},{6,14},{7,15},{8,0},{9,1},... | collective-permute-start | bytes 1769480 | tf_op jit(solution)/shard_map/ppermute | solution.py:769
  51.4 33.7 %collective-permute-start.9 = (bf16[192,4352]{1,0:T(8,128)(2,1)S(1)}, bf16[192,4352]{1,0:T(8,128)(2,1)S(1)}, u32[]{:S(2)}, u32[]{:S(2)}) collective-permute-start(bf16[192,4352]{1,0:T(8,128)(2,1)S(1)} %pad_maximum_fusion.2.refs_2_.refs_6_.refs_10_.own_ref), channel_id=1, source_target_pairs={{0,2},{1,3},{2,0},{3,1},{4,6},{5,7},{6,4},{7,5},{8,10},{9,11},{10,... | collective-permute-start | bytes 5013512 | tf_op jit(solution)/shard_map/ppermute | solution.py:769
  51.5 33.6 %collective-permute-start.8 = (bf16[192,4352]{1,0:T(8,128)(2,1)S(1)}, bf16[192,4352]{1,0:T(8,128)(2,1)S(1)}, u32[]{:S(2)}, u32[]{:S(2)}) collective-permute-start(bf16[192,4352]{1,0:T(8,128)(2,1)S(1)} %pad_maximum_fusion.2.refs_2_.refs_6_.refs_10_.own_ref), channel_id=1, source_target_pairs={{0,1},{1,0},{2,6},{3,7},{4,5},{5,4},{6,2},{7,3},{8,9},{9,8},{10,14... | collective-permute-start | bytes 5013512 | tf_op jit(solution)/shard_map/ppermute | solution.py:769
  63.4 36.7 %collective-permute-start.7 = (bf16[24,4352]{1,0:T(8,128)(2,1)S(1)}, bf16[24,4352]{1,0:T(8,128)(2,1)S(1)}, u32[]{:S(2)}, u32[]{:S(2)}) collective-permute-start(bf16[24,4352]{1,0:T(8,128)(2,1)S(1)} %pad_maximum_fusion.16), channel_id=1, source_target_pairs={{0,16},{1,17},{2,18},{3,19},{4,20},{5,21},{6,22},{7,23},{8,24},{9,... | collective-permute-start | bytes 626696 | tf_op jit(solution)/shard_map/ppermute | solution.py:769
  63.4 36.6 %collective-permute-start.6 = (bf16[48,9216]{1,0:T(8,128)(2,1)S(1)}, bf16[48,9216]{1,0:T(8,128)(2,1)S(1)}, u32[]{:S(2)}, u32[]{:S(2)}) collective-permute-start(bf16[48,9216]{1,0:T(8,128)(2,1)S(1)} %pad_maximum_fusion.5), channel_id=1, source_target_pairs={{0,8},{1,9},{2,10},{3,11},{4,12},{5,13},{6,14},{7,15},{8,0},{9,1},... | collective-permute-start | bytes 2654216 | tf_op jit(solution)/shard_map/ppermute | solution.py:769
  86.0 41.1 %collective-permute-start.16 = (bf16[192,6144]{1,0:T(8,128)(2,1)S(1)}, bf16[192,6144]{1,0:T(8,128)(2,1)S(1)}, u32[]{:S(2)}, u32[]{:S(2)}) collective-permute-start(bf16[192,6144]{1,0:T(8,128)(2,1)S(1)} %constant_dynamic-update-slice_fusion.uown_ref.down_ref), channel_id=1, source_target_pairs={{0,1},{1,0},{2,6},{3,7},{4,5},{5,4},{6,2},{7,3},{8,9},{9,8},{10,14... | collective-permute-start | bytes 7077896 | tf_op jit(solution)/shard_map/ppermute | solution.py:769
  87.6 39.6 %collective-permute-start.12 = (bf16[192,6144]{1,0:T(8,128)(2,1)S(1)}, bf16[192,6144]{1,0:T(8,128)(2,1)S(1)}, u32[]{:S(2)}, u32[]{:S(2)}) collective-permute-start(bf16[192,6144]{1,0:T(8,128)(2,1)S(1)} %constant_dynamic-update-slice_fusion.uown_ref.down_ref), channel_id=1, source_target_pairs={{0,2},{1,3},{2,0},{3,1},{4,6},{5,7},{6,4},{7,5},{8,10},{9,11},{10,... | collective-permute-start | bytes 7077896 | tf_op jit(solution)/shard_map/ppermute | solution.py:769
  100.0 37.1 %collective-permute-start.14 = (bf16[24,16128]{1,0:T(8,128)(2,1)S(1)}, bf16[24,16128]{1,0:T(8,128)(2,1)S(1)}, u32[]{:S(2)}, u32[]{:S(2)}) collective-permute-start(bf16[24,16128]{1,0:T(8,128)(2,1)S(1)} %pad_maximum_fusion.8), channel_id=1, source_target_pairs={{0,16},{1,17},{2,18},{3,19},{4,20},{5,21},{6,22},{7,23},{8,24},{9,... | collective-permute-start | bytes 2322440 | tf_op jit(solution)/shard_map/ppermute | solution.py:769
  102.3 34.8 %collective-permute-start.15 = (bf16[96,9216]{1,0:T(8,128)(2,1)S(1)}, bf16[96,9216]{1,0:T(8,128)(2,1)S(1)}, u32[]{:S(2)}, u32[]{:S(2)}) collective-permute-start(bf16[96,9216]{1,0:T(8,128)(2,1)S(1)} %pad_maximum_fusion.1), channel_id=1, source_target_pairs={{0,4},{1,5},{2,3},{3,2},{4,0},{5,1},{6,7},{7,6},{8,12},{9,13},{10,... | collective-permute-start | bytes 5308424 | tf_op jit(solution)/shard_map/ppermute | solution.py:769
  103.7 23.4 %collective-permute-start.13 = (bf16[48,4352]{1,0:T(8,128)(2,1)S(1)}, bf16[48,4352]{1,0:T(8,128)(2,1)S(1)}, u32[]{:S(2)}, u32[]{:S(2)}) collective-permute-start(bf16[48,4352]{1,0:T(8,128)(2,1)S(1)} %pad_maximum_fusion.14), channel_id=1, source_target_pairs={{0,8},{1,9},{2,10},{3,11},{4,12},{5,13},{6,14},{7,15},{8,0},{9,1},... | collective-permute-start | bytes 1253384 | tf_op jit(solution)/shard_map/ppermute | solution.py:769
  137.3 50.5 %collective-permute-start.20 = (bf16[192,9216]{1,0:T(8,128)(2,1)S(1)}, bf16[192,9216]{1,0:T(8,128)(2,1)S(1)}, u32[]{:S(2)}, u32[]{:S(2)}) collective-permute-start(bf16[192,9216]{1,0:T(8,128)(2,1)S(1)} %constant_dynamic-update-slice_fusion.4.own_ref.uown_ref.down_ref), channel_id=1, source_target_pairs={{0,1},{1,0},{2,6},{3,7},{4,5},{5,4},{6,2},{7,3},{8,9},{9,8},{10,14... | collective-permute-start | bytes 10616840 | tf_op jit(solution)/shard_map/ppermute | solution.py:769
  138.8 48.9 %collective-permute-start.17 = (bf16[192,9216]{1,0:T(8,128)(2,1)S(1)}, bf16[192,9216]{1,0:T(8,128)(2,1)}, u32[]{:S(2)}, u32[]{:S(2)}) collective-permute-start(bf16[192,9216]{1,0:T(8,128)(2,1)S(1)} %constant_dynamic-update-slice_fusion.4.own_ref.uown_ref.down_ref), channel_id=1, source_target_pairs={{0,2},{1,3},{2,0},{3,1},{4,6},{5,7},{6,4},{7,5},{8,10},{9,11},{10,... | collective-permute-start | bytes 10616840 | tf_op jit(solution)/shard_map/ppermute | solution.py:769
  142.6 35.2 %collective-permute-start.18 = (bf16[48,16128]{1,0:T(8,128)(2,1)}, bf16[48,16128]{1,0:T(8,128)(2,1)S(1)}, u32[]{:S(2)}, u32[]{:S(2)}) collective-permute-start(bf16[48,16128]{1,0:T(8,128)(2,1)} %pad_maximum_fusion.3), channel_id=1, source_target_pairs={{0,8},{1,9},{2,10},{3,11},{4,12},{5,13},{6,14},{7,15},{8,0},{9,1},... | collective-permute-start | bytes 4644872 | tf_op jit(solution)/shard_map/ppermute | solution.py:769
  187.9 47.2 %collective-permute-start.24 = (bf16[192,4352]{1,0:T(8,128)(2,1)S(1)}, bf16[192,4352]{1,0:T(8,128)(2,1)}, u32[]{:S(2)}, u32[]{:S(2)}) collective-permute-start(bf16[192,4352]{1,0:T(8,128)(2,1)S(1)} %constant_dynamic-update-slice_fusion.11.refs_2_.refs_6_.refs_10_.own_ref.refs_3_.refs_7_.refs_11_), channel_id=1, source_target_pairs={{0,1},{1,0},{2,6},{3,7},{4,5},{5,4},{6,2},{7,3},{8,9},{9,8},{10,14... | collective-permute-start | bytes 5013512 | tf_op jit(solution)/shard_map/ppermute | solution.py:769
  189.4 45.7 %collective-permute-start.22 = (bf16[192,4352]{1,0:T(8,128)(2,1)S(1)}, bf16[192,4352]{1,0:T(8,128)(2,1)S(1)}, u32[]{:S(2)}, u32[]{:S(2)}) collective-permute-start(bf16[192,4352]{1,0:T(8,128)(2,1)S(1)} %constant_dynamic-update-slice_fusion.11.refs_2_.refs_6_.refs_10_.own_ref.refs_3_.refs_7_.refs_11_), channel_id=1, source_target_pairs={{0,2},{1,3},{2,0},{3,1},{4,6},{5,7},{6,4},{7,5},{8,10},{9,11},{10,... | collective-permute-start | bytes 5013512 | tf_op jit(solution)/shard_map/ppermute | solution.py:769
  195.8 39.3 %collective-permute-start.23 = (bf16[96,6144]{1,0:T(8,128)(2,1)S(1)}, bf16[96,6144]{1,0:T(8,128)(2,1)S(1)}, u32[]{:S(2)}, u32[]{:S(2)}) collective-permute-start(bf16[96,6144]{1,0:T(8,128)(2,1)S(1)} %get-tuple-element.504), channel_id=1, source_target_pairs={{0,4},{1,5},{2,3},{3,2},{4,0},{5,1},{6,7},{7,6},{8,12},{9,13},{10,... | collective-permute-start | bytes 3538952 | tf_op jit(solution)/shard_map/ppermute | solution.py:769
  239.9 37.1 %collective-permute-start.28 = (bf16[192,6144]{1,0:T(8,128)(2,1)}, bf16[192,6144]{1,0:T(8,128)(2,1)}, u32[]{:S(2)}, u32[]{:S(2)}) collective-permute-start(bf16[192,6144]{1,0:T(8,128)(2,1)} %pad_maximum_fusion.uown_ref.down_ref), channel_id=1, source_target_pairs={{0,1},{1,0},{2,6},{3,7},{4,5},{5,4},{6,2},{7,3},{8,9},{9,8},{10,14... | collective-permute-start | bytes 7077896 | tf_op jit(solution)/shard_map/ppermute | solution.py:769
  241.2 35.8 %collective-permute-start.26 = (bf16[192,6144]{1,0:T(8,128)(2,1)}, bf16[192,6144]{1,0:T(8,128)(2,1)}, u32[]{:S(2)}, u32[]{:S(2)}) collective-permute-start(bf16[192,6144]{1,0:T(8,128)(2,1)} %pad_maximum_fusion.uown_ref.down_ref), channel_id=1, source_target_pairs={{0,2},{1,3},{2,0},{3,1},{4,6},{5,7},{6,4},{7,5},{8,10},{9,11},{10,... | collective-permute-start | bytes 7077896 | tf_op jit(solution)/shard_map/ppermute | solution.py:769
  241.5 31.9 %collective-permute-start.27 = (bf16[96,3840]{1,0:T(8,128)(2,1)}, bf16[96,3840]{1,0:T(8,128)(2,1)S(1)}, u32[]{:S(2)}, u32[]{:S(2)}) collective-permute-start(bf16[96,3840]{1,0:T(8,128)(2,1)} %slice.419), channel_id=1, source_target_pairs={{0,4},{1,5},{2,3},{3,2},{4,0},{5,1},{6,7},{7,6},{8,12},{9,13},{10,... | collective-permute-start | bytes 2211848 | tf_op jit(solution)/shard_map/ppermute | solution.py:769
  277.1 32.1 %collective-permute-start.32 = (bf16[192,3840]{1,0:T(8,128)(2,1)S(1)}, bf16[192,3840]{1,0:T(8,128)(2,1)S(1)}, u32[]{:S(2)}, u32[]{:S(2)}) collective-permute-start(bf16[192,3840]{1,0:T(8,128)(2,1)S(1)} %constant_dynamic-update-slice_fusion.15.own_ref.refs_3_.refs_7_.refs_11_), channel_id=1, source_target_pairs={{0,1},{1,0},{2,6},{3,7},{4,5},{5,4},{6,2},{7,3},{8,9},{9,8},{10,14... | collective-permute-start | bytes 4423688 | tf_op jit(solution)/shard_map/ppermute | solution.py:769
  278.4 30.8 %collective-permute-start.30 = (bf16[192,3840]{1,0:T(8,128)(2,1)S(1)}, bf16[192,3840]{1,0:T(8,128)(2,1)S(1)}, u32[]{:S(2)}, u32[]{:S(2)}) collective-permute-start(bf16[192,3840]{1,0:T(8,128)(2,1)S(1)} %constant_dynamic-update-slice_fusion.15.own_ref.refs_3_.refs_7_.refs_11_), channel_id=1, source_target_pairs={{0,2},{1,3},{2,0},{3,1},{4,6},{5,7},{6,4},{7,5},{8,10},{9,11},{10,... | collective-permute-start | bytes 4423688 | tf_op jit(solution)/shard_map/ppermute | solution.py:769
  278.4 28.9 %collective-permute-start.31 = (bf16[96,6144]{1,0:T(8,128)(2,1)S(1)}, bf16[96,6144]{1,0:T(8,128)(2,1)S(1)}, u32[]{:S(2)}, u32[]{:S(2)}) collective-permute-start(bf16[96,6144]{1,0:T(8,128)(2,1)S(1)} %copy-done.58), channel_id=1, source_target_pairs={{0,4},{1,5},{2,3},{3,2},{4,0},{5,1},{6,7},{7,6},{8,12},{9,13},{10,... | collective-permute-start | bytes 3538952 | tf_op jit(solution)/shard_map/ppermute | solution.py:769
  310.6 29.1 %collective-permute-start.35 = (bf16[192,6144]{1,0:T(8,128)(2,1)}, bf16[192,6144]{1,0:T(8,128)(2,1)S(1)}, u32[]{:S(2)}, u32[]{:S(2)}) collective-permute-start(bf16[192,6144]{1,0:T(8,128)(2,1)} %constant_dynamic-update-slice_fusion.17.uown_ref.down_ref), channel_id=1, source_target_pairs={{0,1},{1,0},{2,6},{3,7},{4,5},{5,4},{6,2},{7,3},{8,9},{9,8},{10,14... | collective-permute-start | bytes 7077896 | tf_op jit(solution)/shard_map/ppermute | solution.py:769
  311.8 27.8 %collective-permute-start.34 = (bf16[192,6144]{1,0:T(8,128)(2,1)}, bf16[192,6144]{1,0:T(8,128)(2,1)S(1)}, u32[]{:S(2)}, u32[]{:S(2)}) collective-permute-start(bf16[192,6144]{1,0:T(8,128)(2,1)} %constant_dynamic-update-slice_fusion.17.uown_ref.down_ref), channel_id=1, source_target_pairs={{0,2},{1,3},{2,0},{3,1},{4,6},{5,7},{6,4},{7,5},{8,10},{9,11},{10,... | collective-permute-start | bytes 7077896 | tf_op jit(solution)/shard_map/ppermute | solution.py:769
  428.1 32.7 %collective-permute-start.39 = (bf16[192,6144]{1,0:T(8,128)(2,1)}, bf16[192,6144]{1,0:T(8,128)(2,1)S(1)}, u32[]{:S(2)}, u32[]{:S(2)}) collective-permute-start(bf16[192,6144]{1,0:T(8,128)(2,1)} %get-tuple-element.486), channel_id=1, source_target_pairs={{0,1},{1,0},{2,6},{3,7},{4,5},{5,4},{6,2},{7,3},{8,9},{9,8},{10,14... | collective-permute-start | bytes 7077896 | tf_op jit(solution)/shard_map/ppermute | solution.py:769
  460.8 22.0 %collective-permute-start.41 = (bf16[384,3840]{1,0:T(8,128)(2,1)S(1)}, bf16[384,3840]{1,0:T(8,128)(2,1)S(1)}, u32[]{:S(2)}, u32[]{:S(2)}) collective-permute-start(bf16[384,3840]{1,0:T(8,128)(2,1)S(1)} %get-tuple-element.386), channel_id=1, source_target_pairs={{0,2},{1,3},{2,0},{3,1},{4,6},{5,7},{6,4},{7,5},{8,10},{9,11},{10,... | collective-permute-start | bytes 8847368 | tf_op jit(solution)/shard_map/ppermute | solution.py:769
  528.2 33.3 %collective-permute-start.48 = (bf16[192,6144]{1,0:T(8,128)(2,1)}, bf16[192,6144]{1,0:T(8,128)(2,1)S(1)}, u32[]{:S(2)}, u32[]{:S(2)}) collective-permute-start(bf16[192,6144]{1,0:T(8,128)(2,1)} %get-tuple-element.484), channel_id=1, source_target_pairs={{0,1},{1,0},{2,6},{3,7},{4,5},{5,4},{6,2},{7,3},{8,9},{9,8},{10,14... | collective-permute-start | bytes 7077896 | tf_op jit(solution)/shard_map/ppermute | solution.py:769
  529.1 29.4 %collective-permute-start.46 = (f32[24,6144]{1,0:T(8,128)S(1)}, f32[24,6144]{1,0:T(8,128)S(1)}, u32[]{:S(2)}, u32[]{:S(2)}) collective-permute-start(f32[24,6144]{1,0:T(8,128)S(1)} %slice_add_fusion.19), channel_id=1, source_target_pairs={{0,16},{1,17},{2,18},{3,19},{4,20},{5,21},{6,22},{7,23},{8,24},{9,... | collective-permute-start | bytes 1769480 | tf_op jit(solution)/shard_map/ppermute | solution.py:769
  531.1 30.4 %collective-permute-start.47 = (f32[48,3840]{1,0:T(8,128)S(1)}, f32[48,3840]{1,0:T(8,128)S(1)}, u32[]{:S(2)}, u32[]{:S(2)}) collective-permute-start(f32[48,3840]{1,0:T(8,128)S(1)} %get-tuple-element.505), channel_id=1, source_target_pairs={{0,8},{1,9},{2,10},{3,11},{4,12},{5,13},{6,14},{7,15},{8,0},{9,1},... | collective-permute-start | bytes 2211848 | tf_op jit(solution)/shard_map/ppermute | solution.py:769
  612.6 38.7 %collective-permute-start.61 = (f32[24,6144]{1,0:T(8,128)S(1)}, f32[24,6144]{1,0:T(8,128)S(1)}, u32[]{:S(2)}, u32[]{:S(2)}) collective-permute-start(f32[24,6144]{1,0:T(8,128)S(1)} %slice_add_fusion.17), channel_id=1, source_target_pairs={{0,16},{1,17},{2,18},{3,19},{4,20},{5,21},{6,22},{7,23},{8,24},{9,... | collective-permute-start | bytes 1769480 | tf_op jit(solution)/shard_map/ppermute | solution.py:769
  621.6 29.8 %collective-permute-start.60 = (f32[24,1280]{1,0:T(8,128)S(1)}, f32[24,1280]{1,0:T(8,128)S(1)}, u32[]{:S(2)}, u32[]{:S(2)}) collective-permute-start(f32[24,1280]{1,0:T(8,128)S(1)} %slice_add_fusion.26), channel_id=1, source_target_pairs={{0,16},{1,17},{2,18},{3,19},{4,20},{5,21},{6,22},{7,23},{8,24},{9,... | collective-permute-start | bytes 368648 | tf_op jit(solution)/shard_map/ppermute | solution.py:769
  622.6 28.8 %collective-permute-start.62 = (bf16[48,3072]{1,0:T(8,128)(2,1)S(1)}, bf16[48,3072]{1,0:T(8,128)(2,1)S(1)}, u32[]{:S(2)}, u32[]{:S(2)}) collective-permute-start(bf16[48,3072]{1,0:T(8,128)(2,1)S(1)} %get-tuple-element.507), channel_id=1, source_target_pairs={{0,8},{1,9},{2,10},{3,11},{4,12},{5,13},{6,14},{7,15},{8,0},{9,1},... | collective-permute-start | bytes 884744 | tf_op jit(solution)/shard_map/ppermute | solution.py:769
  (119 other events, 1613.2 us)
